TPU v7x, 512 devices: a whole 4x4x16 slice. The times are simulated.
512 devices in a mesh: half: 2 (over core), row: 64 (over z, x), col: 4 (over y).
Axes of the slice: x: 4, y: 4, z: 16, core: 2. Of those that a mesh axis runs over, the one named last changes fastest.
Arguments:
- samples: bfloat16 [262144, 512], P(('half', 'row'), 'col'), may hold values from -6 to 6
- couplings: bfloat16 [4096, 64, 512], P(('half', 'row')), may hold values from -0.25 to 0.25
- coupling_cols: int32 [4096, 8], P(('half', 'row')), may hold values from 0 to 4095, as said below
- child_map: int32 [2, 64, 64], P('half', 'row'), may hold values from 0 to 63, each once within a row
- gen_left: bfloat16 [2, 256, 262144], P('half', 'col', 'row'), may hold values from -0.375 to 0.375
- gen_right: bfloat16 [2, 256, 262144], P('half', 'col', 'row'), may hold values from -0.01171875 to 0.01171875
Outputs:
- range_samples: bfloat16 [262144, 512], P(('half', 'row'), 'col')
- row_samples: bfloat16 [262144, 512], P(('half', 'row'), 'col')
Inputs may be any that keep to these rules, and one draw needn't show every extreme that they name: `coupling_cols`: slot 0 of block row b is b itself, and every entry lies within 8 blocks of its block row. `child_map`: for each child and row group, the last dimension is a permutation.
All inputs are finite; a program needn't handle non-finite values.
Results may differ from a plain program's by a relative error of at most 0.0075.
Values may be sent and summed in bfloat16 or wider, within the bound.
No kernel may reach another device: no remote copies, remote signals or barrier semaphores. Data moves between devices by JAX's collectives and lax.ppermute only.
A program may use at most 64 MiB of HBM per device.

v0:
```python
import jax
import jax.numpy as jnp
from jax import lax
from jax.sharding import PartitionSpec as P

BS = 64
NB = 8
HB = 8


def with_halo(x, sides, width):
    edges = {}
    for axis, dim in sides:
        count, length = (lax.axis_size(axis), x.shape[dim])
        up = [(i, (i + 1) % count) for i in range(count - 1)]
        last = lax.slice_in_dim(x, length - width, length, axis=dim)
        leading = lax.slice_in_dim(x, 0, width, axis=dim)
        edges[dim] = (
            lax.ppermute(last, axis, up),
            lax.ppermute(leading, axis, [(b, a) for a, b in up]),
        )
    done = []
    for _, dim in sides:
        low, high = edges[dim]
        around = [(width, width) if d in done else (0, 0) for d in range(x.ndim)]
        x = jnp.concatenate([jnp.pad(low, around), x, jnp.pad(high, around)], axis=dim)
        done.append(dim)
    return x


def shifted(x, axis, by):
    count = lax.axis_size(axis)
    pairs = [(i, i + by) for i in range(count) if 0 <= i + by < count]
    return lax.ppermute(x, axis, pairs)


def in_order(parts, dim):
    lengths = list(parts.shape[1:])
    lengths[dim] *= parts.shape[0]
    return jnp.moveaxis(parts, 0, dim).reshape(lengths)


def copy_for_each(x, axis):
    copies = jnp.broadcast_to(x, (lax.axis_size(axis), *x.shape))
    return lax.all_to_all(copies, axis, split_axis=0, concat_axis=0, tiled=True)


def gathered_copies(x, axis, dim):
    return in_order(copy_for_each(x, axis), dim)


def sent_together(arrays, axis, split_dim, concat_dim, along):
    widths = [a.shape[along] for a in arrays]
    both = jnp.concatenate(arrays, axis=along)
    filled = lax.all_to_all(both, axis, split_axis=split_dim, concat_axis=concat_dim, tiled=True)
    return tuple(jnp.split(filled, [sum(widths[:k]) for k in range(1, len(widths))], axis=along))


def side_by_side(arrays, axis, dim, along):
    ends, at = ([], 0)
    for a in arrays[:-1]:
        at += a.shape[along]
        ends.append(at)
    both = jnp.concatenate(arrays, axis=along)
    return tuple(jnp.split(lax.all_gather(both, axis, axis=dim, tiled=True), ends, axis=along))


def rows_for(lines, count):
    spare = -lines.shape[0] % count
    if not spare:
        return lines
    return jnp.concatenate([lines, jnp.zeros((spare, *lines.shape[1:]), lines.dtype)])


def in_blocks(x, dim, count):
    before, after = (x.shape[:dim], x.shape[dim + 1 :])
    return jnp.moveaxis(x.reshape(*before, count, -1, *after), dim, 0)


def sum_at_owner(x, axis, dim):
    count = lax.axis_size(axis)
    parts = lax.all_to_all(in_blocks(x, dim, count), axis, 0, 0, tiled=True)
    return jnp.sum(parts, axis=0)


def sum_by_parts(x, axes):
    padded = rows_for(x, lax.axis_size(axes))
    whole = gathered_copies(sum_at_owner(padded, axes, 0), axes, 0)
    return lax.slice_in_dim(whole, 0, len(x)).reshape(x.shape)


def in_one(arrays, axis):
    line, at, outs = (jnp.concatenate([a.reshape(-1) for a in arrays]), 0, [])
    so_far = sum_by_parts(line, axis)
    for a in arrays:
        outs.append(so_far[at : at + a.size].reshape(a.shape))
        at += a.size
    return tuple(outs)


def summed_on_arrival(x, axis, dim):
    parts = in_blocks(x, dim, lax.axis_size(axis))
    arrived = lax.all_to_all(parts, axis, split_axis=0, concat_axis=0, tiled=True)
    return arrived.astype(jnp.float32).sum(axis=0)


def side_by_side_2(arrays, axis, dim, along):
    widths = [a.shape[along] for a in arrays]
    both = jnp.concatenate(arrays, axis=along)
    filled = summed_on_arrival(both, axis, dim)
    return tuple(jnp.split(filled, [sum(widths[:k]) for k in range(1, len(widths))], axis=along))


def shards(samples, couplings, coupling_cols, child_map, gen_left, gen_right):
    block_count = couplings.shape[0]
    panel_cols = samples.shape[1]
    sample_blocks = samples.reshape(block_count, BS, panel_cols)
    first_block = lax.axis_index(("half", "row")) * block_count
    padded = with_halo(sample_blocks, ((("half", "row"), 0),), HB)
    local_cols = coupling_cols - first_block + HB
    picked = padded[local_cols].reshape(block_count, NB * BS, panel_cols)
    sparse_range = jnp.einsum("bik,bks->bis", couplings, picked, preferred_element_type=jnp.float32)
    pieces = jnp.einsum(
        "bik,bis->bks", couplings, sample_blocks, preferred_element_type=jnp.float32
    )
    pieces = pieces.reshape(block_count * NB, BS, panel_cols)
    spread = jnp.zeros((block_count + 2 * HB, BS, panel_cols), jnp.float32)
    spread = spread.at[local_cols.reshape(-1)].add(pieces)
    from_below = shifted(
        spread[block_count + HB :].astype(jnp.bfloat16), ("half", "row"), 1
    ).astype(jnp.float32)
    from_above = shifted(spread[:HB].astype(jnp.bfloat16), ("half", "row"), -1).astype(jnp.float32)
    sparse_rows = spread[HB : block_count + HB]
    sparse_rows = sparse_rows.at[:HB].add(from_below)
    sparse_rows = sparse_rows.at[block_count - HB :].add(from_above)
    order_map = child_map[0, 0]
    pair_blocks = order_map.shape[0]
    inverse = (
        jnp.zeros((pair_blocks,), jnp.int32)
        .at[order_map]
        .set(jnp.arange(pair_blocks, dtype=jnp.int32))
    )
    left_gen = gen_left[0]
    right_gen = gen_right[0]
    rows_pair = gathered_copies(samples, "half", 0)

    def reorder(matrix):
        ranks = matrix.shape[0]
        return matrix.reshape(ranks, pair_blocks, BS)[:, inverse].reshape(ranks, pair_blocks * BS)

    left_gen, right_gen = sent_together((reorder(left_gen), reorder(right_gen)), "row", 1, 1, 0)
    full_left, full_right = side_by_side((left_gen, right_gen), "col", 0, 1)
    partials = (
        jnp.dot(full_right, rows_pair, preferred_element_type=jnp.float32),
        jnp.dot(full_left, rows_pair, preferred_element_type=jnp.float32),
    )
    w_total, g_total = in_one((partials[0], partials[1]), "row")
    w_half = w_total.astype(jnp.bfloat16)
    g_half = g_total.astype(jnp.bfloat16)
    range_child = jnp.einsum(
        "kr,ks->rs", full_left, w_half, preferred_element_type=jnp.float32
    ).astype(jnp.bfloat16)
    rows_child = jnp.einsum(
        "kr,ks->rs", full_right, g_half, preferred_element_type=jnp.float32
    ).astype(jnp.bfloat16)
    range_child = lax.optimization_barrier(range_child).astype(jnp.float32)
    rows_child = lax.optimization_barrier(rows_child).astype(jnp.float32)
    range_both, rows_both = side_by_side_2(
        (range_child.astype(jnp.bfloat16), rows_child.astype(jnp.bfloat16)), "half", 0, 1
    )
    range_samples = (sparse_range.reshape(block_count * BS, panel_cols) + range_both).astype(
        jnp.bfloat16
    )
    row_samples = (sparse_rows.reshape(block_count * BS, panel_cols) + rows_both).astype(
        jnp.bfloat16
    )
    return (range_samples, row_samples)


def solution(mesh):
    placed = (
        P(("half", "row"), "col"),
        P(("half", "row"), None, None),
        P(("half", "row"), None),
        P("half", "row", None),
        P("half", "col", "row"),
        P("half", "col", "row"),
    )
    return jax.shard_map(
        shards,
        mesh=mesh,
        in_specs=placed,
        out_specs=(P(("half", "row"), "col"), P(("half", "row"), "col")),
        check_vma=False,
    )
```

profile of v0, /device:TPU:1, one launch (start us, length us, event | category | flops | bytes accessed | tf_op | source)
XLA Modules:
  0.0 264.6 jit_solution(9092162941843981921)
XLA Ops:
  7.2 0.0 all-gather.2.cloned.1.call-start
  7.2 0.8 fusion.10
  8.0 0.8 scatter_custom_fusion
  8.8 2.8 %reshape_squeeze.6 = bf16[64,64,64]{2,1,0:T(8,128)(2,1)} reshape(bf16[1,64,4096]{2,1,0:T(8,128)(2,1)} %param.14) | data formatting | bytes 1048576 | tf_op jit(solution)/shard_map/reshape;squeeze | solution.py:149
  11.6 1.9 copy.17
  13.5 2.8 %reshape_squeeze.7 = bf16[64,64,64]{2,1,0:T(8,128)(2,1)} reshape(bf16[1,64,4096]{2,1,0:T(8,128)(2,1)} %param.15) | data formatting | bytes 1048576 | tf_op jit(solution)/shard_map/reshape;squeeze | solution.py:149
  16.3 2.9 %copy.18 = bf16[64,64,64]{2,0,1:T(8,128)(2,1)} copy(bf16[64,64,64]{2,1,0:T(8,128)(2,1)} %reshape_squeeze.7) | data formatting | bytes 1048576 | tf_op jit(solution)/shard_map/reshape;squeeze | solution.py:149
  19.2 1.7 gather_fusion.1
  20.9 3.0 %gather_fusion.2 = bf16[64,64,64]{2,1,0:T(8,128)(2,1)} fusion(bf16[64,64,64]{2,0,1:T(8,128)(2,1)} %copy.18, s32[1024]{0:T(1024)S(1)} %pad_clamp_fusion), kind=kCustom, calls=%fused_computation.2 | custom fusion | bytes 1048832 | tf_op jit(solution)/shard_map/gather | solution.py:149
  23.9 3.3 %pad_maximum_fusion = bf16[128,64,64]{2,0,1:T(8,128)(2,1)} fusion(bf16[64,64,64]{2,0,1:T(8,128)(2,1)} %bitcast.36, bf16[64,64,64]{2,0,1:T(8,128)(2,1)S(1)} %bitcast.35), kind=kLoop, calls=%fused_computation.8 | loop fusion | flops 2097152 | bytes 2097152 | tf_op jit(solution)/shard_map/concatenate | solution.py:54
  27.2 2.0 copy.19
  29.2 70.5 %all_to_all.31 = bf16[128,64,64]{0,2,1:T(8,128)(2,1)S(1)} all-to-all(bf16[128,64,64]{0,2,1:T(8,128)(2,1)S(1)} %copy.19), channel_id=1, replica_groups=mesh['half'=2,'row'=64,'col'=4] {'row'}, dimensions={1} | all-to-all | bytes 2097152 | tf_op jit(solution)/shard_map/all_to_all | solution.py:55
  99.7 1.5 fusion.13
  101.2 1.1 copy.23
  102.3 1.6 copy.24
  103.9 2.1 pad_maximum_fusion.2
  106.0 0.0 all-gather.2.cloned.1.call-update
  106.1 1.0 broadcast_in_dim.20
  107.1 9.0 %all-to-all-start.1 = ((bf16[2,2048,128]{2,1,0:T(8,128)(2,1)}), bf16[2,2048,128]{2,1,0:T(8,128)(2,1)}, u32[]{:S(2)}, u32[]{:S(2)}) async-start(bf16[2,2048,128]{2,1,0:T(8,128)(2,1)} %broadcast_in_dim.20), calls=%async_computation.1 | async-start | bytes 2097152 | tf_op jit(solution)/shard_map/all_to_all | solution.py:45
  116.2 0.1 copy.22
  116.2 0.1 reshape.187
  116.4 4.9 %fusion.16 = f32[32,512,128]{2,1,0:T(8,128)} fusion(bf16[32,64,512]{2,1,0:T(8,128)(2,1)S(1)} %copy-done, bf16[32,64,128]{2,1,0:T(8,128)(2,1)S(1)} %bitcast.33), kind=kOutput, calls=%fused_computation.42 | convolution fusion | flops 268435456 | bytes 11010048 | tf_op jit(solution)/shard_map/bik,bis->bks/dot_general | solution.py:123
  121.2 1.4 broadcast_in_dim.22
  122.6 39.6 %scatter_fusion = f32[48,64,128]{2,1,0:T(8,128)} fusion(f32[48,64,128]{2,1,0:T(8,128)} %broadcast_in_dim.22, s32[256]{0:T(256)S(1)} %bitcast.39, f32[256,64,128]{2,1,0:T(8,128)} %bitcast.30), kind=kCustom, calls=%fused_computation.4 | custom fusion | flops 2097152 | bytes 25166848 | tf_op jit(solution)/shard_map/scatter-add | solution.py:128
  162.2 1.5 convert.9
  163.7 0.0 all-gather.2.cloned.1.call-done
  163.8 3.2 %fusion.1 = f32[256,128]{1,0:T(8,128)} fusion(bf16[4096,128]{1,0:T(8,128)(2,1)} %bitcast.12, bf16[256,8192]{1,0:T(8,128)(2,1)} %all-gather.2.cloned.1.call-done), kind=kOutput, calls=%fused_computation.11 | convolution fusion | flops 268435456 | bytes 3276800 | tf_op jit(solution)/shard_map/dot_general | solution.py:154
  167.0 0.9 concatenate.28
  167.9 3.2 %fusion.4 = f32[256,128]{1,0:T(8,128)} fusion(bf16[4096,128]{1,0:T(8,128)(2,1)} %bitcast.12, bf16[256,8192]{1,0:T(8,128)(2,1)} %all-gather.2.cloned.1.call-done), kind=kOutput, calls=%fused_computation.14 | convolution fusion | flops 268435456 | bytes 3276800 | tf_op jit(solution)/shard_map/dot_general | solution.py:155
  171.1 1.6 concatenate.29
  172.7 0.9 pad_maximum_fusion.4
  173.6 0.9 all_to_all.22
  174.5 9.4 %all-to-all-start.2 = ((f32[64,1,1024]{2,1,0:T(1,128)}), f32[64,1,1024]{2,1,0:T(1,128)}, u32[]{:S(2)}, u32[]{:S(2)}) async-start(f32[64,1,1024]{2,1,0:T(1,128)} %all_to_all.22), calls=%async_computation.2 | async-start | bytes 524288 | tf_op jit(solution)/shard_map/all_to_all | solution.py:82
  184.0 0.7 fusion.14
  184.7 2.8 %collective-permute-start.2 = (bf16[8,64,128]{2,1,0:T(8,128)(2,1)}, bf16[8,64,128]{2,1,0:T(8,128)(2,1)S(1)}, u32[]{:S(2)}, u32[]{:S(2)}) collective-permute-start(bf16[8,64,128]{2,1,0:T(8,128)(2,1)} %get-tuple-element.33), channel_id=1, source_target_pairs={{0,4},{4,8},{8,12},{12,16},{16,20},{20,24},{24,28},{28,32},{32,36}... | collective-permute-start | bytes 393224 | tf_op jit(solution)/shard_map/ppermute | solution.py:34
  187.5 6.8 %collective-permute-start.3 = (bf16[8,64,128]{2,1,0:T(8,128)(2,1)S(1)}, bf16[8,64,128]{2,1,0:T(8,128)(2,1)S(1)}, u32[]{:S(2)}, u32[]{:S(2)}) collective-permute-start(bf16[8,64,128]{2,1,0:T(8,128)(2,1)S(1)} %get-tuple-element.32), channel_id=1, source_target_pairs={{4,0},{8,4},{12,8},{16,12},{20,16},{24,20},{28,24},{32,28},{36,32}... | collective-permute-start | bytes 393224 | tf_op jit(solution)/shard_map/ppermute | solution.py:34
  194.3 0.7 fusion.15
  195.1 1.9 collective-permute-start
  197.0 7.0 %collective-permute-start.1 = (bf16[8,64,128]{2,1,0:T(8,128)(2,1)}, bf16[8,64,128]{2,1,0:T(8,128)(2,1)}, u32[]{:S(2)}, u32[]{:S(2)}) collective-permute-start(bf16[8,64,128]{2,1,0:T(8,128)(2,1)} %bitcast.2), channel_id=1, source_target_pairs={{4,0},{8,4},{12,8},{16,12},{20,16},{24,20},{28,24},{32,28},{36,32}... | collective-permute-start | bytes 393224 | tf_op jit(solution)/shard_map/ppermute | solution.py:20
  204.0 2.3 slice.105
  206.3 0.1 copy.16
  206.4 0.1 reshape.192
  206.5 1.7 fusion.9
  208.2 1.7 fusion.8
  209.9 1.1 reduce_sum.18
  211.0 0.1 broadcast_in_dim.21
  211.1 0.5 broadcast.102
  211.7 1.4 reduce.9
  213.0 0.7 reshape.239
  213.8 10.7 %all-to-all-start.3 = ((bf16[64,2,512]{2,1,0:T(2,128)(2,1)}), bf16[64,2,512]{2,1,0:T(2,128)(2,1)S(1)}, u32[]{:S(2)}, u32[]{:S(2)}) async-start(bf16[64,2,512]{2,1,0:T(2,128)(2,1)} %reshape.239), calls=%async_computation.3 | async-start | bytes 262144 | tf_op jit(solution)/shard_map/all_to_all | solution.py:45
  224.5 0.6 copy-done.5
  225.1 1.1 pad_maximum_fusion.3
  226.2 3.0 %gather_fusion = bf16[256,64,128]{2,1,0:T(8,128)(2,1)} fusion(bf16[48,64,128]{2,1,0:T(8,128)(2,1)S(1)} %pad_maximum_fusion.3, s32[1024]{0:T(1024)S(1)} %pad_clamp_fusion.1), kind=kCustom, calls=%fused_computation | custom fusion | bytes 8389632 | tf_op jit(solution)/shard_map/gather | solution.py:121
  229.2 3.1 %fusion.17 = f32[32,128,64]{1,2,0:T(8,128)S(1)} fusion(bf16[32,64,512]{2,1,0:T(8,128)(2,1)S(1)} %copy-done, bf16[32,512,128]{2,1,0:T(8,128)(2,1)} %bitcast.31), kind=kOutput, calls=%fused_computation.43 | convolution fusion | flops 268435456 | bytes 7340032 | tf_op jit(solution)/shard_map/bik,bks->bis/dot_general | solution.py:122
  232.3 7.1 %all-to-all-done.3 = bf16[64,2,512]{2,1,0:T(2,128)(2,1)S(1)} async-done(((bf16[64,2,512]{2,1,0:T(2,128)(2,1)}), bf16[64,2,512]{2,1,0:T(2,128)(2,1)S(1)}, u32[]{:S(2)}, u32[]{:S(2)}) %all-to-all-start.3) | async-done | bytes 131104 | tf_op jit(solution)/shard_map/all_to_all | solution.py:45
  239.4 0.1 reshape.240
  239.5 0.5 slice_reduce_fusion.1
  240.1 3.4 %convolution_convert_fusion.1 = bf16[4096,128]{1,0:T(8,128)(2,1)} fusion(bf16[256,128]{1,0:T(8,128)(2,1)S(1)} %convert_element_type.35, bf16[256,8192]{1,0:T(8,128)(2,1)} %all-gather.2.cloned.1.call-done), kind=kOutput, calls=%fused_computation.6 | convolution fusion | flops 268959744 | bytes 3211264 | tf_op jit(solution)/shard_map/kr,ks->rs/dot_general | solution.py:160
  243.5 2.4 convolution_convert_fusion
  246.0 0.2 pad_maximum_fusion.1
  246.2 9.1 %all_to_all.32 = bf16[2,2048,256]{2,1,0:T(8,128)(2,1)S(1)} all-to-all(bf16[2,2048,256]{2,1,0:T(8,128)(2,1)S(1)} %bitcast.32), channel_id=1, replica_groups=mesh['half'=2,'row'=64,'col'=4] {'half'}, dimensions={0} | all-to-all | bytes 4194304 | tf_op jit(solution)/shard_map/all_to_all | solution.py:103
  255.3 0.4 convert_reduce_fusion
  255.7 0.8 copy-done.2
  256.6 1.2 fusion.6
  (26 shorter events, 0.1 us)
Async XLA Ops:
  7.2 109.2 %copy-start = (bf16[32,64,512]{2,1,0:T(8,128)(2,1)S(1)}, bf16[32,64,512]{2,1,0:T(8,128)(2,1)}, u32[]{:S(2)}) copy-start(bf16[32,64,512]{2,1,0:T(8,128)(2,1)} %param.11) | copy-start | bytes 6291460
  7.2 156.6 %all-gather.2.cloned.1.call-start = ((), (), s32[]{:S(2)}) async-start(), calls=%async_computation.5 | async-start | bytes 5242880 | tf_op jit(solution)/shard_map/all_gather | solution.py:65
  20.9 3.0 %copy-start.3 = (bf16[64,64,64]{2,1,0:T(8,128)(2,1)S(1)}, bf16[64,64,64]{2,1,0:T(8,128)(2,1)}, u32[]{:S(2)}) copy-start(bf16[64,64,64]{2,1,0:T(8,128)(2,1)} %gather_fusion.1) | copy-start | bytes 1572868
  102.3 3.7 %copy-start.1 = (bf16[2048,128]{1,0:T(8,128)(2,1)S(1)}, bf16[2048,128]{1,0:T(8,128)(2,1)}, u32[]{:S(2)}) copy-start(bf16[2048,128]{1,0:T(8,128)(2,1)} %param.10) | copy-start | bytes 1572868
  106.1 10.1 %copy-start.6 = (s32[32,8]{0,1:T(8,128)S(1)}, s32[32,8]{0,1:T(8,128)}, u32[]{:S(2)}) copy-start(s32[32,8]{0,1:T(8,128)} %param.12) | copy-start | bytes 3076
  107.1 56.6 %all-to-all-start.1 = ((bf16[2,2048,128]{2,1,0:T(8,128)(2,1)}), bf16[2,2048,128]{2,1,0:T(8,128)(2,1)}, u32[]{:S(2)}, u32[]{:S(2)}) async-start(bf16[2,2048,128]{2,1,0:T(8,128)(2,1)} %broadcast_in_dim.20), calls=%async_computation.1 | async-start | bytes 2097152 | tf_op jit(solution)/shard_map/all_to_all | solution.py:45
  174.5 35.3 %all-to-all-start.2 = ((f32[64,1,1024]{2,1,0:T(1,128)}), f32[64,1,1024]{2,1,0:T(1,128)}, u32[]{:S(2)}, u32[]{:S(2)}) async-start(f32[64,1,1024]{2,1,0:T(1,128)} %all_to_all.22), calls=%async_computation.2 | async-start | bytes 524288 | tf_op jit(solution)/shard_map/all_to_all | solution.py:82
  184.7 21.8 %collective-permute-start.2 = (bf16[8,64,128]{2,1,0:T(8,128)(2,1)}, bf16[8,64,128]{2,1,0:T(8,128)(2,1)S(1)}, u32[]{:S(2)}, u32[]{:S(2)}) collective-permute-start(bf16[8,64,128]{2,1,0:T(8,128)(2,1)} %get-tuple-element.33), channel_id=1, source_target_pairs={{0,4},{4,8},{8,12},{12,16},{16,20},{20,24},{24,28},{28,32},{32,36}... | collective-permute-start | bytes 393224 | tf_op jit(solution)/shard_map/ppermute | solution.py:34
  187.5 20.7 %collective-permute-start.3 = (bf16[8,64,128]{2,1,0:T(8,128)(2,1)S(1)}, bf16[8,64,128]{2,1,0:T(8,128)(2,1)S(1)}, u32[]{:S(2)}, u32[]{:S(2)}) collective-permute-start(bf16[8,64,128]{2,1,0:T(8,128)(2,1)S(1)} %get-tuple-element.32), channel_id=1, source_target_pairs={{4,0},{8,4},{12,8},{16,12},{20,16},{24,20},{28,24},{32,28},{36,32}... | collective-permute-start | bytes 393224 | tf_op jit(solution)/shard_map/ppermute | solution.py:34
  195.1 29.4 %collective-permute-start = (bf16[8,64,128]{2,1,0:T(8,128)(2,1)}, bf16[8,64,128]{2,1,0:T(8,128)(2,1)S(1)}, u32[]{:S(2)}, u32[]{:S(2)}) collective-permute-start(bf16[8,64,128]{2,1,0:T(8,128)(2,1)} %bitcast), channel_id=1, source_target_pairs={{0,4},{4,8},{8,12},{12,16},{16,20},{20,24},{24,28},{28,32},{32,36}... | collective-permute-start | bytes 393224 | tf_op jit(solution)/shard_map/ppermute | solution.py:19
  197.0 28.1 %collective-permute-start.1 = (bf16[8,64,128]{2,1,0:T(8,128)(2,1)}, bf16[8,64,128]{2,1,0:T(8,128)(2,1)}, u32[]{:S(2)}, u32[]{:S(2)}) collective-permute-start(bf16[8,64,128]{2,1,0:T(8,128)(2,1)} %bitcast.2), channel_id=1, source_target_pairs={{4,0},{8,4},{12,8},{16,12},{20,16},{24,20},{28,24},{32,28},{36,32}... | collective-permute-start | bytes 393224 | tf_op jit(solution)/shard_map/ppermute | solution.py:20
  213.8 25.7 %all-to-all-start.3 = ((bf16[64,2,512]{2,1,0:T(2,128)(2,1)}), bf16[64,2,512]{2,1,0:T(2,128)(2,1)S(1)}, u32[]{:S(2)}, u32[]{:S(2)}) async-start(bf16[64,2,512]{2,1,0:T(2,128)(2,1)} %reshape.239), calls=%async_computation.3 | async-start | bytes 262144 | tf_op jit(solution)/shard_map/all_to_all | solution.py:45
  224.5 0.7 copy-start.5
  243.5 2.5 copy-start.4
  255.3 1.2 copy-start.2
Sparse Core Ops, SparseCore 0:
  106.2 51.4 all-gather.1
where the time goes:
time: 266 us; the launch traced here: 265 us
  blocking collectives  79.6 us (30%)
  other arithmetic  57 us (21%)
  starting transfers between devices  47.7 us (18%)
  local copies, waits for them, and re-layouts  38.5 us (14%)
  matrix products  20.2 us (8%)
  between operations  14.3 us (5%)
  waiting for transfers between devices  7.19 us (3%)
    all_to_all x1, blocking collectives, sent_together(): lax.all_to_all(both, axis, split_axis=split_dim, concat_axis=concat_dim,...  70.5 us
    scatter-add x1, other arithmetic, shards(): spread = spread.at[local_cols.reshape(-1)].add(pieces)  39.6 us
    all_to_all x2, starting transfers between devices, copy_for_each(): return lax.all_to_all(copies, axis, split_axis=0, concat_axis=0, tiled=True)  19.7 us
    another operation x4, local copies, waits for them, and re-layouts, reorder(): matrix.reshape(ranks, pair_blocks, BS)[:, inverse]  10.3 us
    ppermute x2, starting transfers between devices, shifted(): return lax.ppermute(x, axis, pairs)  9.67 us
    all_to_all x1, starting transfers between devices, sum_at_owner(): parts = lax.all_to_all(in_blocks(x, dim, count), axis, 0, 0, tiled=True)  9.45 us
    all_to_all x1, blocking collectives, summed_on_arrival(): lax.all_to_all(parts, axis, split_axis=0, concat_axis=0, tiled=True)  9.09 us
    all_to_all x2, waiting for transfers between devices, copy_for_each(): return lax.all_to_all(copies, axis, split_axis=0, concat_axis=0, tiled=True)  7.14 us
  transfers between devices with their start and end apart: 8, of which 1 were waited for; matrix products, arithmetic and copies ran while one was open for 25% of the time, Pallas kernels for 0%

commit v1 on v0

v1 whole, which is shorter than its diff:
```python
import functools

import jax
import jax.numpy as jnp
from jax import lax
from jax.experimental import pallas as pl
from jax.experimental.pallas import tpu as pltpu
from jax.sharding import Mesh
from jax.sharding import PartitionSpec as P

BS = 64
NB = 8
HB = 8
LANES = 128
CHUNKS = 1
FRONT = ("half", "z", "x")
F32 = jnp.float32
BF16 = jnp.bfloat16
VMEM = pltpu.VMEM
SMEM = pltpu.SMEM


def whole(space):
    return pl.BlockSpec(memory_space=space)


def cost(flops, moved):
    return pl.CostEstimate(flops=flops, bytes_accessed=moved, transcendentals=0)


def swapped_halves(x):
    return pltpu.roll(x.astype(F32), BS, 1).astype(BF16)


def low_lanes(shape):
    return lax.broadcasted_iota(jnp.int32, shape, 1) < BS


def pack_kernel(map_ref, left_ref, right_ref, *out_refs):
    ranks = left_ref.shape[0] // len(out_refs)
    low = low_lanes((ranks, LANES))
    for k in range(left_ref.shape[1] // LANES):
        one, two = map_ref[2 * k], map_ref[2 * k + 1]
        for part, out_ref in enumerate(out_refs):
            rows = slice(part * ranks, (part + 1) * ranks)
            left = left_ref[rows, k * LANES : (k + 1) * LANES]
            right = right_ref[rows, k * LANES : (k + 1) * LANES]
            out_ref[one] = jnp.where(low, left, swapped_halves(right))
            out_ref[two] = jnp.where(low, swapped_halves(left), right)


def pack(order_map, left, right):
    ranks, width = left.shape
    out = jax.ShapeDtypeStruct((width // BS, ranks // CHUNKS, LANES), BF16)
    return pl.pallas_call(
        pack_kernel,
        out_shape=(out,) * CHUNKS,
        in_specs=[whole(SMEM), whole(VMEM), whole(VMEM)],
        out_specs=(whole(VMEM),) * CHUNKS,
        cost_estimate=cost(0, 8 * ranks * width),
        name="pack",
    )(order_map, left, right)


def sparse_kernel(
    cols_ref, a_ref, own_ref, low_ref, high_ref, range_ref, rows_ref, up_ref, down_ref, padded, spread
):
    per = a_ref.shape[0]
    count = own_ref.shape[0]
    step = pl.program_id(0)

    @pl.when(step == 0)
    def _():
        padded[:HB] = low_ref[...]
        padded[HB : HB + count] = own_ref[...]
        padded[HB + count :] = high_ref[...]
        spread[...] = jnp.zeros_like(spread)

    for i in range(per):
        b = step * per + i
        at = [cols_ref[b, t] for t in range(NB)]
        picked = jnp.concatenate([padded[c] for c in at], axis=0)
        a = a_ref[i]
        range_ref[i] = jnp.dot(a, picked, preferred_element_type=F32)
        terms = lax.dot_general(
            a, own_ref[b], (((0,), (0,)), ((), ())), preferred_element_type=F32
        )
        for t in range(NB):
            spread[at[t]] += terms[t * BS : (t + 1) * BS]

    @pl.when(step == pl.num_programs(0) - 1)
    def _():
        rows_ref[...] = spread[HB : HB + count]
        up_ref[...] = spread[HB + count :].astype(BF16)
        down_ref[...] = spread[:HB].astype(BF16)


def sparse(local_cols, couplings, blocks, low, high):
    count, _, width = blocks.shape
    per = 8
    edge = jax.ShapeDtypeStruct((HB, BS, width), BF16)
    return pl.pallas_call(
        sparse_kernel,
        grid=(count // per,),
        out_shape=(
            jax.ShapeDtypeStruct((count, BS, width), F32),
            jax.ShapeDtypeStruct((count, BS, width), F32),
            edge,
            edge,
        ),
        in_specs=[
            whole(SMEM),
            pl.BlockSpec((per, BS, NB * BS), lambda i: (i, 0, 0)),
            whole(VMEM),
            whole(VMEM),
            whole(VMEM),
        ],
        out_specs=(
            pl.BlockSpec((per, BS, width), lambda i: (i, 0, 0)),
            whole(VMEM),
            whole(VMEM),
            whole(VMEM),
        ),
        scratch_shapes=[
            pltpu.VMEM((count + 2 * HB, BS, width), BF16),
            pltpu.VMEM((count + 2 * HB, BS, width), F32),
        ],
        compiler_params=pltpu.CompilerParams(dimension_semantics=("arbitrary",)),
        cost_estimate=cost(4 * count * BS * BS * NB * width, 6 << 20),
        name="sparse",
    )(local_cols, couplings, blocks, low, high)


def reduce_kernel(at_ref, *refs):
    gen_refs, (own_ref, other_ref, out_ref, lhs) = refs[:CHUNKS], refs[CHUNKS:]
    half, me = at_ref[0], at_ref[1]
    blocks, ranks, _ = gen_refs[0].shape
    count = blocks // 2
    parts = own_ref.shape[0]
    low = low_lanes((ranks, LANES))
    for side, first in ((0, half * count), (1, (1 - half) * count)):
        for part, gen_ref in enumerate(gen_refs):
            left = slice(part * ranks, (part + 1) * ranks)
            right = slice((CHUNKS + part) * ranks, (CHUNKS + part + 1) * ranks)
            for k in range(count // 2):
                one, two = gen_ref[first + 2 * k], gen_ref[first + 2 * k + 1]
                lanes = slice(k * LANES, (k + 1) * LANES)
                lhs[side, left, lanes] = jnp.where(low, one, swapped_halves(two))
                lhs[side, right, lanes] = jnp.where(low, swapped_halves(one), two)
    for pair in range(0, parts, 2):
        total = 0.0
        for side, ref in ((0, own_ref), (1, other_ref)):
            rhs = jnp.concatenate([ref[pair], ref[pair + 1]], axis=1)
            total += jnp.dot(lhs[side], rhs, preferred_element_type=F32)
        for k in range(2):
            piece = total[:, k * LANES : (k + 1) * LANES]
            slot = lax.rem(me + parts - (pair + k), parts)
            out_ref[:, slot] = piece.reshape(out_ref.shape[0], -1, LANES).astype(BF16)


def reduced(at, gens, own, other, splits):
    ranks = CHUNKS * gens[0].shape[1]
    parts, rows, _ = own.shape
    return pl.pallas_call(
        reduce_kernel,
        out_shape=jax.ShapeDtypeStruct((splits, parts, 2 * ranks // splits, LANES), BF16),
        in_specs=[whole(SMEM)] + [whole(VMEM)] * (CHUNKS + 2),
        out_specs=whole(VMEM),
        scratch_shapes=[pltpu.VMEM((2, 2 * ranks, rows), BF16)],
        cost_estimate=cost(8 * ranks * rows * parts * LANES, 6 << 20),
        name="partials",
    )(at, *gens, own, other)


def low_rank_kernel(mine, at_ref, own, up, far_a, far_b, down, w_ref, *refs):
    me, step, steps = at_ref[1], pl.program_id(0), pl.num_programs(0)
    per, ranks, _ = own.shape
    rhs = refs[-1]
    parts = rhs.shape[0] // ranks

    @pl.when(step == 0)
    def _():
        for k in range(parts):
            both = w_ref[:, lax.rem(me + parts - k, parts)].reshape(2 * ranks, LANES)
            rows = slice(k * ranks, (k + 1) * ranks)
            rhs[rows, :LANES] = both[ranks:]
            rhs[rows, LANES:] = both[:ranks]

    for i in range(per):
        lhs = jnp.concatenate([g[i] for g in (own, up, far_a, far_b, down)], axis=0)
        both = lax.dot_general(
            lhs, rhs[...], (((0,), (0,)), ((), ())), preferred_element_type=F32
        )
        for_range, for_rows = both[:BS, :LANES], both[BS:, LANES:]
        if mine:
            sr_ref, sp_ref, below_ref, above_ref, out_ref = refs[:-1]
            for_range += sr_ref[i]
            for_rows += sp_ref[i]
            for_rows += jnp.where(step == 0, below_ref[i].astype(F32), 0.0)
            for_rows += jnp.where(step == steps - 1, above_ref[i].astype(F32), 0.0)
        else:
            out_ref = refs[0]
        out_ref[0, i] = for_range.astype(out_ref.dtype)
        out_ref[1, i] = for_rows.astype(out_ref.dtype)


def low_rank(at, gens, w, added=()):
    blocks, ranks, _ = gens[0].shape
    count, per = blocks // 2, HB
    steps = count // per
    mine = bool(added)
    depth = sum(g.shape[1] for g in gens)

    def place(i, at_ref):
        half = at_ref[0] if mine else 1 - at_ref[0]
        return (half * steps + i, 0, 0)

    def tiles(rows):
        return pl.BlockSpec((per, rows, LANES), place)

    edges = [pl.BlockSpec((per, BS, LANES), lambda i, at_ref: (i, 0, 0))] * 2 + [whole(VMEM)] * 2
    return pl.pallas_call(
        functools.partial(low_rank_kernel, mine),
        grid_spec=pltpu.PrefetchScalarGridSpec(
            num_scalar_prefetch=1,
            grid=(steps,),
            in_specs=[tiles(g.shape[1]) for g in gens] + [whole(VMEM)] + (edges if mine else []),
            out_specs=pl.BlockSpec((2, per, BS, LANES), lambda i, at_ref: (0, i, 0, 0)),
            scratch_shapes=[pltpu.VMEM((depth, 2 * LANES), BF16)],
        ),
        out_shape=jax.ShapeDtypeStruct((2, count, BS, LANES), F32 if mine else BF16),
        compiler_params=pltpu.CompilerParams(dimension_semantics=("arbitrary",)),
        cost_estimate=cost(4 * count * LANES * depth * LANES, 4 << 20),
        name="mine" if mine else "theirs",
    )(at, *gens, w, *added)


def around(x, axis, by):
    count = lax.axis_size(axis)
    return lax.ppermute(x, axis, [(i, (i + by) % count) for i in range(count)])


def along_front(x, by):
    count = lax.axis_size(FRONT)
    pairs = [(i, i + by) for i in range(count) if 0 <= i + by < count]
    return lax.ppermute(x, FRONT, pairs)


def spread_out(x, axis):
    return lax.all_to_all(x, axis, split_axis=0, concat_axis=0, tiled=True)


def shards(samples, couplings, coupling_cols, child_map, gen_left, gen_right):
    count = couplings.shape[0]
    width = samples.shape[1]
    half, me = lax.axis_index("half"), lax.axis_index("col")
    at = jnp.stack([half, me]).astype(jnp.int32)
    n_z, n_x, n_col = (lax.axis_size(a) for a in ("z", "x", "col"))
    blocks = samples.reshape(count, BS, width)

    (packed,) = pack(child_map[0, 0], gen_left[0], gen_right[0])
    gens = spread_out(packed, ("z", "x"))

    shifted = [around(samples, "col", k) for k in range(1, n_col)]
    low = along_front(blocks[count - HB :], 1)
    high = along_front(blocks[:HB], -1)
    local_cols = coupling_cols - lax.axis_index(FRONT) * count + HB
    sparse_range, sparse_rows, up, down = sparse(local_cols, couplings, blocks, low, high)
    shifted, up, down = lax.optimization_barrier((shifted, up, down))
    panels = jnp.stack([samples, *shifted])
    others = around(panels, "half", 1)
    below, above = along_front(up, 1), along_front(down, -1)

    gens, panels, others, *added = lax.optimization_barrier(
        (gens, panels, others, sparse_range, sparse_rows, below, above)
    )
    partial = reduced(at, (gens,), panels, others, n_z)
    from_up, from_down = around(gens, "col", 1), around(gens, "col", -1)
    middle = gens.shape[1] // 2
    far_a = around(from_up[:, :middle], "col", 1)
    far_b = around(from_down[:, middle:], "col", -1)

    by_z = jnp.sum(spread_out(partial, "z").astype(F32), axis=0)
    copies = jnp.broadcast_to(by_z, (n_x, *by_z.shape)).reshape(n_x * n_col, *by_z.shape[1:])
    arrived = spread_out(copies, ("x", "col")).reshape(n_x, n_col, *by_z.shape[1:])
    slice_sum = jnp.sum(arrived, axis=0).astype(BF16)
    w = spread_out(jnp.broadcast_to(slice_sum, (n_z, *slice_sum.shape)), "z")

    everyone = (gens, from_up, far_a, far_b, from_down)
    received = around(low_rank(at, everyone, w), "half", 1)
    total = low_rank(at, everyone, w, added) + received.astype(F32)
    range_out, rows_out = total[0].astype(BF16), total[1].astype(BF16)
    return range_out.reshape(samples.shape), rows_out.reshape(samples.shape)


def solution(mesh):
    n_half, n_row, n_col = (mesh.shape[a] for a in ("half", "row", "col"))
    n_x = n_col
    fine = Mesh(
        mesh.devices.reshape(n_half, n_row // n_x, n_x, n_col), ("half", "z", "x", "col")
    )
    row = ("z", "x")
    placed = (
        P(FRONT, "col"),
        P(FRONT, None, None),
        P(FRONT, None),
        P("half", row, None),
        P("half", "col", row),
        P("half", "col", row),
    )
    return jax.shard_map(
        shards,
        mesh=fine,
        in_specs=placed,
        out_specs=(P(FRONT, "col"), P(FRONT, "col")),
        check_vma=False,
    )
```

time: 266 us -> 188 us (0.71)
  other arithmetic: 57 us -> 5.03 us
  blocking collectives: 79.6 us -> 42.1 us
  local copies, waits for them, and re-layouts: 38.5 us -> 8.72 us
  starting transfers between devices: 47.7 us -> 76.2 us
  Pallas kernels: 0 us -> 23.6 us
  waiting for transfers between devices: 7.19 us -> 30.1 us
  matrix products: 20.2 us -> 0 us
  between operations: 14.3 us -> 0.94 us
    scatter-add x3 -> x0, other arithmetic: 43 us -> none  [the longest x1 39.6 us: shards(): spread = spread.at[local_cols.reshape(-1)].add(pieces)]
    all_to_all x2, blocking collectives: 79.6 us -> 42.1 us  [spread_out(): return lax.all_to_all(x, axis, split_axis=0, concat_axis=0, tiled=True)]
    ppermute x4 -> x13, starting transfers between devices: 18.5 us -> 49.9 us  [the longest x9 30.6 us: around(): return lax.ppermute(x, axis, [(i, (i + by) % count) for i in range(count)])]
    ppermute x4 -> x13, waiting for transfers between devices: 0.01 us -> 30.1 us  [the longest x4 30 us: along_front(): return lax.ppermute(x, FRONT, pairs)]
    pallas_call x0 -> x5, Pallas kernels: none -> 23.6 us  [the longest x2 11.1 us: low_rank(): pl.pallas_call(functools.partial(low_rank_kernel, mine), grid_spec=pltpu....]
    dot_general x6 -> x0, matrix products: 20.2 us -> none  [the longest x1 4.89 us: shards(): jnp.einsum('bik,bis->bks', couplings, sample_blocks, preferred_element_ty...]
    another operation x4 -> x0, local copies, waits for them, and re-layouts: 10.3 us -> none  [reorder(): matrix.reshape(ranks, pair_blocks, BS)[:, inverse]]
    gather x3 -> x0, local copies, waits for them, and re-layouts: 7.75 us -> none  [the longest x2 4.71 us: reorder(): matrix.reshape(ranks, pair_blocks, BS)[:, inverse]]
  transfers between devices with their start and end apart: 8 -> 15, of which waited for: 1 -> 3; matrix products, arithmetic and copies ran while one was open for 25% -> 4% of each run, Pallas kernels for 0% -> 8%
where the time goes in v1:
time: 188 us; the launch traced here: 187 us
  starting transfers between devices  76.2 us (41%)
  blocking collectives  42.1 us (22%)
  waiting for transfers between devices  30.1 us (16%)
  Pallas kernels  23.6 us (13%)
  local copies, waits for them, and re-layouts  8.72 us (5%)
  other arithmetic  5.03 us (3%)
    all_to_all x2, blocking collectives, spread_out(): return lax.all_to_all(x, axis, split_axis=0, concat_axis=0, tiled=True)  42.1 us
    ppermute x9, starting transfers between devices, around(): return lax.ppermute(x, axis, [(i, (i + by) % count) for i in range(count)])  30.6 us
    ppermute x4, waiting for transfers between devices, along_front(): return lax.ppermute(x, FRONT, pairs)  30 us
    all_to_all x2, starting transfers between devices, spread_out(): return lax.all_to_all(x, axis, split_axis=0, concat_axis=0, tiled=True)  26.3 us
    ppermute x4, starting transfers between devices, along_front(): return lax.ppermute(x, FRONT, pairs)  19.3 us
    pallas_call x2, Pallas kernels, low_rank(): pl.pallas_call(functools.partial(low_rank_kernel, mine), grid_spec=pltpu....  11.1 us
    pallas_call x1, Pallas kernels, sparse(): pl.pallas_call(sparse_kernel, grid=(count // per,), out_shape=(jax.ShapeD...  5.83 us
    unnamed x29, local copies, waits for them, and re-layouts  4.18 us
  transfers between devices with their start and end apart: 15, of which 3 were waited for; matrix products, arithmetic and copies ran while one was open for 4% of the time, Pallas kernels for 8%

profile of v1, /device:TPU:1, one launch (start us, length us, event | category | flops | bytes accessed | tf_op | source)
XLA Modules:
  0.0 186.7 jit_solution(16418608819249176043)
XLA Ops:
  0.6 0.0 copy-start.2
  0.6 2.6 %pack.1 = bf16[64,64,128]{2,1,0:T(8,128)(2,1)} custom-call(s32[64]{0:T(128)} %bitcast.27, bf16[64,4096]{1,0:T(8,128)(2,1)} %bitcast.18, bf16[64,4096]{1,0:T(8,128)(2,1)} %bitcast.19), custom_call_target="tpu_custom_call" | custom-call | bytes 2097152 | tf_op jit(solution)/shard_map/pack/pallas_call | solution.py:55
  3.3 19.1 %all-to-all-start = ((bf16[64,64,128]{2,1,0:T(8,128)(2,1)}), bf16[64,64,128]{2,1,0:T(8,128)(2,1)S(1)}, u32[]{:S(2)}, u32[]{:S(2)}) async-start(bf16[64,64,128]{2,1,0:T(8,128)(2,1)} %pack.1), calls=%async_computation | async-start | bytes 2097152 | tf_op jit(solution)/shard_map/all_to_all | solution.py:250
  22.4 0.0 copy-done.2
  22.4 4.6 %collective-permute-start.2 = (bf16[2048,128]{1,0:T(8,128)(2,1)S(1)}, bf16[2048,128]{1,0:T(8,128)(2,1)S(1)}, u32[]{:S(2)}, u32[]{:S(2)}) collective-permute-start(bf16[2048,128]{1,0:T(8,128)(2,1)S(1)} %copy-done.2), channel_id=1, source_target_pairs={{0,3},{1,0},{2,1},{3,2},{4,7},{5,4},{6,5},{7,6},{8,11},{9,8},{10,9... | collective-permute-start | bytes 1572872 | tf_op jit(solution)/shard_map/ppermute | solution.py:240
  27.0 2.3 %collective-permute-start.1 = (bf16[2048,128]{1,0:T(8,128)(2,1)S(1)}, bf16[2048,128]{1,0:T(8,128)(2,1)S(1)}, u32[]{:S(2)}, u32[]{:S(2)}) collective-permute-start(bf16[2048,128]{1,0:T(8,128)(2,1)S(1)} %copy-done.2), channel_id=1, source_target_pairs={{0,2},{1,3},{2,0},{3,1},{4,6},{5,7},{6,4},{7,5},{8,10},{9,11},{10,... | collective-permute-start | bytes 1572872 | tf_op jit(solution)/shard_map/ppermute | solution.py:240
  29.3 2.6 %collective-permute-start = (bf16[2048,128]{1,0:T(8,128)(2,1)S(1)}, bf16[2048,128]{1,0:T(8,128)(2,1)S(1)}, u32[]{:S(2)}, u32[]{:S(2)}) collective-permute-start(bf16[2048,128]{1,0:T(8,128)(2,1)S(1)} %copy-done.2), channel_id=1, source_target_pairs={{0,1},{1,2},{2,3},{3,0},{4,5},{5,6},{6,7},{7,4},{8,9},{9,10},{10,1... | collective-permute-start | bytes 1572872 | tf_op jit(solution)/shard_map/ppermute | solution.py:240
  31.9 0.7 fusion.1
  32.6 2.9 %collective-permute-start.3 = (bf16[8,64,128]{2,1,0:T(8,128)(2,1)}, bf16[8,64,128]{2,1,0:T(8,128)(2,1)S(1)}, u32[]{:S(2)}, u32[]{:S(2)}) collective-permute-start(bf16[8,64,128]{2,1,0:T(8,128)(2,1)} %bitcast.7), channel_id=1, source_target_pairs={{0,4},{4,8},{8,12},{12,16},{16,20},{20,24},{24,28},{28,32},{32,36}... | collective-permute-start | bytes 393224 | tf_op jit(solution)/shard_map/ppermute | solution.py:246
  35.5 7.5 %collective-permute-start.4 = (bf16[8,64,128]{2,1,0:T(8,128)(2,1)S(1)}, bf16[8,64,128]{2,1,0:T(8,128)(2,1)S(1)}, u32[]{:S(2)}, u32[]{:S(2)}) collective-permute-start(bf16[8,64,128]{2,1,0:T(8,128)(2,1)S(1)} %bitcast.26), channel_id=1, source_target_pairs={{4,0},{8,4},{12,8},{16,12},{20,16},{24,20},{28,24},{32,28},{36,32}... | collective-permute-start | bytes 393224 | tf_op jit(solution)/shard_map/ppermute | solution.py:246
  43.0 0.8 copy.10
  43.8 0.6 subtract_add_fusion.cols_ref
  44.4 28.1 %collective-permute-done.3.low_ref = bf16[8,64,128]{2,1,0:T(8,128)(2,1)S(1)} collective-permute-done((bf16[8,64,128]{2,1,0:T(8,128)(2,1)}, bf16[8,64,128]{2,1,0:T(8,128)(2,1)S(1)}, u32[]{:S(2)}, u32[]{:S(2)}) %collective-permute-start.3) | collective-permute-done | bytes 131104 | tf_op jit(solution)/shard_map/ppermute | solution.py:246
  72.5 0.0 collective-permute-done.4.high_ref
  72.5 0.6 copy-done.10
  73.2 0.0 copy-done.11
  73.2 5.8 %sparse.1 = (f32[32,64,128]{2,1,0:T(8,128)}, f32[32,64,128]{2,1,0:T(8,128)}, bf16[8,64,128]{2,1,0:T(8,128)(2,1)}, bf16[8,64,128]{2,1,0:T(8,128)(2,1)}) custom-call(s32[32,8]{1,0:T(8,128)} %subtract_add_fusion.cols_ref, bf16[32,64,512]{2,1,0:T(8,128)(2,1)} %a_ref.1, bf16[32,64,128]{2,1,0:T(8,128)(2,1)} %bitcast.16, bf16[8,64,128]{2,1,0:T(8,128)(2,1)} %copy-done.10, ...), custom_call_target="tpu_custom_call" | custom-call | flops 536870912 | bytes 6291456 | tf_op jit(solution)/shard_map/sparse/pallas_call | solution.py:102
  79.0 0.0 collective-permute-done.2
  79.0 0.0 copy-start.5
  79.0 0.0 collective-permute-done.1
  79.1 0.0 copy-start.6
  79.1 0.0 collective-permute-done
  79.1 0.0 copy-start.7
  79.1 0.7 copy-done.5
  79.8 0.2 copy-done.6
  80.0 0.2 copy-done.7
  80.2 1.8 pad_maximum_fusion.refs_1_
  82.0 0.0 copy-start.1
  82.0 1.9 %collective-permute-start.5 = (bf16[4,2048,128]{2,1,0:T(8,128)(2,1)S(1)}, bf16[4,2048,128]{2,1,0:T(8,128)(2,1)}, u32[]{:S(2)}, u32[]{:S(2)}) collective-permute-start(bf16[4,2048,128]{2,1,0:T(8,128)(2,1)S(1)} %pad_maximum_fusion.refs_1_), channel_id=1, source_target_pairs={{0,256},{256,0},{1,257},{257,1},{2,258},{258,2},{3,259},{259,3},{4... | collective-permute-start | bytes 6291464 | tf_op jit(solution)/shard_map/ppermute | solution.py:240
  84.0 0.0 copy-done.13
  84.0 1.9 %collective-permute-start.6 = (bf16[8,64,128]{2,1,0:T(8,128)(2,1)S(1)}, bf16[8,64,128]{2,1,0:T(8,128)(2,1)S(1)}, u32[]{:S(2)}, u32[]{:S(2)}) collective-permute-start(bf16[8,64,128]{2,1,0:T(8,128)(2,1)S(1)} %copy-done.13), channel_id=1, source_target_pairs={{0,4},{4,8},{8,12},{12,16},{16,20},{20,24},{24,28},{28,32},{32,36}... | collective-permute-start | bytes 393224 | tf_op jit(solution)/shard_map/ppermute | solution.py:246
  85.9 0.0 copy-done.12
  85.9 7.0 %collective-permute-start.7 = (bf16[8,64,128]{2,1,0:T(8,128)(2,1)S(1)}, bf16[8,64,128]{2,1,0:T(8,128)(2,1)S(1)}, u32[]{:S(2)}, u32[]{:S(2)}) collective-permute-start(bf16[8,64,128]{2,1,0:T(8,128)(2,1)S(1)} %copy-done.12), channel_id=1, source_target_pairs={{4,0},{8,4},{12,8},{16,12},{20,16},{24,20},{28,24},{32,28},{36,32}... | collective-permute-start | bytes 393224 | tf_op jit(solution)/shard_map/ppermute | solution.py:246
  92.9 0.7 collective-permute-done.6.refs_2_
  93.6 1.2 collective-permute-done.7.refs_3_
  94.8 0.0 collective-permute-done.5.refs_2_
  94.8 0.0 all-to-all-done.refs_0_.own
  94.8 4.6 %collective-permute-start.10 = (bf16[64,64,128]{2,1,0:T(8,128)(2,1)S(1)}, bf16[64,64,128]{2,1,0:T(8,128)(2,1)}, u32[]{:S(2)}, u32[]{:S(2)}) collective-permute-start(bf16[64,64,128]{2,1,0:T(8,128)(2,1)S(1)} %all-to-all-done.refs_0_.own), channel_id=1, source_target_pairs={{0,3},{1,0},{2,1},{3,2},{4,7},{5,4},{6,5},{7,6},{8,11},{9,8},{10,9... | collective-permute-start | bytes 3145736 | tf_op jit(solution)/shard_map/ppermute | solution.py:240
  99.5 1.9 %collective-permute-start.8 = (bf16[64,64,128]{2,1,0:T(8,128)(2,1)S(1)}, bf16[64,64,128]{2,1,0:T(8,128)(2,1)}, u32[]{:S(2)}, u32[]{:S(2)}) collective-permute-start(bf16[64,64,128]{2,1,0:T(8,128)(2,1)S(1)} %all-to-all-done.refs_0_.own), channel_id=1, source_target_pairs={{0,1},{1,2},{2,3},{3,0},{4,5},{5,6},{6,7},{7,4},{8,9},{9,10},{10,1... | collective-permute-start | bytes 3145736 | tf_op jit(solution)/shard_map/ppermute | solution.py:240
  101.4 0.7 pad_add_fusion.at_ref
  102.1 0.0 copy-done.1
  102.1 0.0 copy-done
  102.1 4.1 %partials.1 = bf16[16,4,8,128]{3,2,1,0:T(8,128)(2,1)} custom-call(s32[2]{0:T(128)} %pad_add_fusion.at_ref, bf16[64,64,128]{2,1,0:T(8,128)(2,1)} %copy-done, bf16[4,2048,128]{2,1,0:T(8,128)(2,1)} %copy-done.1, bf16[4,2048,128]{2,1,0:T(8,128)(2,1)} %collective-permute-done.5.refs_2_), custom_call_target="tpu_custom_call" | custom-call | flops 536870912 | bytes 6291456 | tf_op jit(solution)/shard_map/partials/pallas_call | solution.py:164
  106.2 24.9 %all_to_all.20 = bf16[16,4,8,128]{3,2,1,0:T(8,128)(2,1)S(1)} all-to-all(bf16[16,4,8,128]{3,2,1,0:T(8,128)(2,1)} %partials.1), channel_id=1, replica_groups=mesh['half'=2,'z'=16,'x'=4,'col'=4] {'z'}, dimensions={0} | all-to-all | bytes 262144 | tf_op jit(solution)/shard_map/all_to_all | solution.py:250
  131.1 0.6 broadcast_in_dim.6
  131.8 7.2 %all-to-all-start.2 = ((f32[16,8,128]{2,1,0:T(8,128)}), f32[16,8,128]{2,1,0:T(8,128)S(1)}, u32[]{:S(2)}, u32[]{:S(2)}) async-start(f32[16,8,128]{2,1,0:T(8,128)} %bitcast.12), calls=%async_computation.2 | async-start | bytes 131072 | tf_op jit(solution)/shard_map/all_to_all | solution.py:250
  139.0 0.0 collective-permute-done.10.down
  139.0 1.1 slice.35
  140.1 4.5 %collective-permute-start.11 = (bf16[64,32,128]{2,1,0:T(8,128)(2,1)S(1)}, bf16[64,32,128]{2,1,0:T(8,128)(2,1)S(1)}, u32[]{:S(2)}, u32[]{:S(2)}) collective-permute-start(bf16[64,32,128]{2,1,0:T(8,128)(2,1)S(1)} %slice.35), channel_id=1, source_target_pairs={{0,3},{1,0},{2,1},{3,2},{4,7},{5,4},{6,5},{7,6},{8,11},{9,8},{10,9... | collective-permute-start | bytes 1572872 | tf_op jit(solution)/shard_map/ppermute | solution.py:240
  144.6 0.0 collective-permute-done.8.up
  144.6 1.1 slice.34
  145.7 1.9 %collective-permute-start.9 = (bf16[64,32,128]{2,1,0:T(8,128)(2,1)S(1)}, bf16[64,32,128]{2,1,0:T(8,128)(2,1)S(1)}, u32[]{:S(2)}, u32[]{:S(2)}) collective-permute-start(bf16[64,32,128]{2,1,0:T(8,128)(2,1)S(1)} %slice.34), channel_id=1, source_target_pairs={{0,1},{1,2},{2,3},{3,0},{4,5},{5,6},{6,7},{7,4},{8,9},{9,10},{10,1... | collective-permute-start | bytes 1572872 | tf_op jit(solution)/shard_map/ppermute | solution.py:240
  147.6 0.0 all-to-all-done.2
  147.6 17.2 %all_to_all.21.w_ref = bf16[16,4,8,128]{3,2,1,0:T(8,128)(2,1)} all-to-all(bf16[16,4,8,128]{3,2,1,0:T(8,128)(2,1)S(1)} %broadcast_in_dim.7), channel_id=1, replica_groups=mesh['half'=2,'z'=16,'x'=4,'col'=4] {'z'}, dimensions={0} | all-to-all | bytes 262144 | tf_op jit(solution)/shard_map/all_to_all | solution.py:250
  164.8 0.0 collective-permute-done.11.far_b
  164.9 0.0 collective-permute-done.9.far_a
  164.9 0.8 copy-done.3
  165.6 0.8 copy-done.4
  166.4 5.2 %theirs.1 = bf16[2,32,64,128]{3,2,1,0:T(8,128)(2,1)} custom-call(s32[2]{0:T(128)} %pad_add_fusion.at_ref, bf16[64,64,128]{2,1,0:T(8,128)(2,1)} %copy-done, bf16[64,64,128]{2,1,0:T(8,128)(2,1)} %collective-permute-done.8.up, bf16[64,32,128]{2,1,0:T(8,128)(2,1)} %copy-done.4, bf16[64,32,128]{2,1,0:T(8,128)(2,1)} %copy-done.3, ...), custom_call_target="tpu_custom_call" | custom-call | flops 536870912 | bytes 4194304 | tf_op jit(solution)/shard_map/theirs/pallas_call | solution.py:222
  171.6 6.2 %collective-permute-start.12 = (bf16[2,32,64,128]{3,2,1,0:T(8,128)(2,1)}, bf16[2,32,64,128]{3,2,1,0:T(8,128)(2,1)S(1)}, u32[]{:S(2)}, u32[]{:S(2)}) collective-permute-start(bf16[2,32,64,128]{3,2,1,0:T(8,128)(2,1)} %theirs.1), channel_id=1, source_target_pairs={{0,256},{256,0},{1,257},{257,1},{2,258},{258,2},{3,259},{259,3},{4... | collective-permute-start | bytes 3145736 | tf_op jit(solution)/shard_map/ppermute | solution.py:240
  177.9 5.9 %mine.1 = f32[2,32,64,128]{3,2,1,0:T(8,128)} custom-call(s32[2]{0:T(128)} %pad_add_fusion.at_ref, bf16[64,64,128]{2,1,0:T(8,128)(2,1)} %copy-done, bf16[64,64,128]{2,1,0:T(8,128)(2,1)} %collective-permute-done.8.up, bf16[64,32,128]{2,1,0:T(8,128)(2,1)} %copy-done.4, bf16[64,32,128]{2,1,0:T(8,128)(2,1)} %copy-done.3, ...), custom_call_target="tpu_custom_call" | custom-call | flops 536870912 | bytes 4194304 | tf_op jit(solution)/shard_map/mine/pallas_call | solution.py:222
  183.7 0.0 collective-permute-done.12
  183.7 1.9 %add_convert_fusion = bf16[2,32,64,128]{3,2,1,0:T(8,128)(2,1)S(1)} fusion(f32[2,32,64,128]{3,2,1,0:T(8,128)} %mine.1, bf16[2,32,64,128]{3,2,1,0:T(8,128)(2,1)S(1)} %collective-permute-done.12), kind=kLoop, calls=%fused_computation.1 | loop fusion | flops 1572864 | bytes 4194304 | tf_op jit(solution)/shard_map/convert.1
  185.7 1.0 fusion
  (14 shorter events, 0.1 us)
Async XLA Ops:
  0.6 21.7 %copy-start.2 = (bf16[2048,128]{1,0:T(8,128)(2,1)S(1)}, bf16[2048,128]{1,0:T(8,128)(2,1)}, u32[]{:S(2)}) copy-start(bf16[2048,128]{1,0:T(8,128)(2,1)} %param.6) | copy-start | bytes 1572868
  3.3 91.6 %all-to-all-start = ((bf16[64,64,128]{2,1,0:T(8,128)(2,1)}), bf16[64,64,128]{2,1,0:T(8,128)(2,1)S(1)}, u32[]{:S(2)}, u32[]{:S(2)}) async-start(bf16[64,64,128]{2,1,0:T(8,128)(2,1)} %pack.1), calls=%async_computation | async-start | bytes 2097152 | tf_op jit(solution)/shard_map/all_to_all | solution.py:250
  22.4 56.7 %collective-permute-start.2 = (bf16[2048,128]{1,0:T(8,128)(2,1)S(1)}, bf16[2048,128]{1,0:T(8,128)(2,1)S(1)}, u32[]{:S(2)}, u32[]{:S(2)}) collective-permute-start(bf16[2048,128]{1,0:T(8,128)(2,1)S(1)} %copy-done.2), channel_id=1, source_target_pairs={{0,3},{1,0},{2,1},{3,2},{4,7},{5,4},{6,5},{7,6},{8,11},{9,8},{10,9... | collective-permute-start | bytes 1572872 | tf_op jit(solution)/shard_map/ppermute | solution.py:240
  27.0 52.0 %collective-permute-start.1 = (bf16[2048,128]{1,0:T(8,128)(2,1)S(1)}, bf16[2048,128]{1,0:T(8,128)(2,1)S(1)}, u32[]{:S(2)}, u32[]{:S(2)}) collective-permute-start(bf16[2048,128]{1,0:T(8,128)(2,1)S(1)} %copy-done.2), channel_id=1, source_target_pairs={{0,2},{1,3},{2,0},{3,1},{4,6},{5,7},{6,4},{7,5},{8,10},{9,11},{10,... | collective-permute-start | bytes 1572872 | tf_op jit(solution)/shard_map/ppermute | solution.py:240
  29.3 49.8 %collective-permute-start = (bf16[2048,128]{1,0:T(8,128)(2,1)S(1)}, bf16[2048,128]{1,0:T(8,128)(2,1)S(1)}, u32[]{:S(2)}, u32[]{:S(2)}) collective-permute-start(bf16[2048,128]{1,0:T(8,128)(2,1)S(1)} %copy-done.2), channel_id=1, source_target_pairs={{0,1},{1,2},{2,3},{3,0},{4,5},{5,6},{6,7},{7,4},{8,9},{9,10},{10,1... | collective-permute-start | bytes 1572872 | tf_op jit(solution)/shard_map/ppermute | solution.py:240
  32.6 39.9 %collective-permute-start.3 = (bf16[8,64,128]{2,1,0:T(8,128)(2,1)}, bf16[8,64,128]{2,1,0:T(8,128)(2,1)S(1)}, u32[]{:S(2)}, u32[]{:S(2)}) collective-permute-start(bf16[8,64,128]{2,1,0:T(8,128)(2,1)} %bitcast.7), channel_id=1, source_target_pairs={{0,4},{4,8},{8,12},{12,16},{16,20},{20,24},{24,28},{28,32},{32,36}... | collective-permute-start | bytes 393224 | tf_op jit(solution)/shard_map/ppermute | solution.py:246
  35.5 37.0 %collective-permute-start.4 = (bf16[8,64,128]{2,1,0:T(8,128)(2,1)S(1)}, bf16[8,64,128]{2,1,0:T(8,128)(2,1)S(1)}, u32[]{:S(2)}, u32[]{:S(2)}) collective-permute-start(bf16[8,64,128]{2,1,0:T(8,128)(2,1)S(1)} %bitcast.26), channel_id=1, source_target_pairs={{4,0},{8,4},{12,8},{16,12},{20,16},{24,20},{28,24},{32,28},{36,32}... | collective-permute-start | bytes 393224 | tf_op jit(solution)/shard_map/ppermute | solution.py:246
  72.5 0.7 copy-start.10
  72.5 0.7 copy-start.11
  79.0 0.8 copy-start.5
  79.1 0.9 copy-start.6
  79.1 1.1 copy-start.7
  80.2 3.8 %copy-start.13 = (bf16[8,64,128]{2,1,0:T(8,128)(2,1)S(1)}, bf16[8,64,128]{2,1,0:T(8,128)(2,1)}, u32[]{:S(2)}) copy-start(bf16[8,64,128]{2,1,0:T(8,128)(2,1)} %get-tuple-element.25) | copy-start | bytes 393220
  80.2 5.7 %copy-start.12 = (bf16[8,64,128]{2,1,0:T(8,128)(2,1)S(1)}, bf16[8,64,128]{2,1,0:T(8,128)(2,1)}, u32[]{:S(2)}) copy-start(bf16[8,64,128]{2,1,0:T(8,128)(2,1)} %get-tuple-element.26) | copy-start | bytes 393220
  82.0 20.0 %copy-start.1 = (bf16[4,2048,128]{2,1,0:T(8,128)(2,1)}, bf16[4,2048,128]{2,1,0:T(8,128)(2,1)S(1)}, u32[]{:S(2)}) copy-start(bf16[4,2048,128]{2,1,0:T(8,128)(2,1)S(1)} %pad_maximum_fusion.refs_1_) | copy-start | bytes 6291460
  82.0 12.8 %collective-permute-start.5 = (bf16[4,2048,128]{2,1,0:T(8,128)(2,1)S(1)}, bf16[4,2048,128]{2,1,0:T(8,128)(2,1)}, u32[]{:S(2)}, u32[]{:S(2)}) collective-permute-start(bf16[4,2048,128]{2,1,0:T(8,128)(2,1)S(1)} %pad_maximum_fusion.refs_1_), channel_id=1, source_target_pairs={{0,256},{256,0},{1,257},{257,1},{2,258},{258,2},{3,259},{259,3},{4... | collective-permute-start | bytes 6291464 | tf_op jit(solution)/shard_map/ppermute | solution.py:240
  84.0 9.6 %collective-permute-start.6 = (bf16[8,64,128]{2,1,0:T(8,128)(2,1)S(1)}, bf16[8,64,128]{2,1,0:T(8,128)(2,1)S(1)}, u32[]{:S(2)}, u32[]{:S(2)}) collective-permute-start(bf16[8,64,128]{2,1,0:T(8,128)(2,1)S(1)} %copy-done.13), channel_id=1, source_target_pairs={{0,4},{4,8},{8,12},{12,16},{16,20},{20,24},{24,28},{28,32},{32,36}... | collective-permute-start | bytes 393224 | tf_op jit(solution)/shard_map/ppermute | solution.py:246
  85.9 8.9 %collective-permute-start.7 = (bf16[8,64,128]{2,1,0:T(8,128)(2,1)S(1)}, bf16[8,64,128]{2,1,0:T(8,128)(2,1)S(1)}, u32[]{:S(2)}, u32[]{:S(2)}) collective-permute-start(bf16[8,64,128]{2,1,0:T(8,128)(2,1)S(1)} %copy-done.12), channel_id=1, source_target_pairs={{4,0},{8,4},{12,8},{16,12},{20,16},{24,20},{28,24},{32,28},{36,32}... | collective-permute-start | bytes 393224 | tf_op jit(solution)/shard_map/ppermute | solution.py:246
  93.6 78.0 %copy-start.8 = (bf16[8,64,128]{2,1,0:T(8,128)(2,1)}, bf16[8,64,128]{2,1,0:T(8,128)(2,1)S(1)}, u32[]{:S(2)}) copy-start(bf16[8,64,128]{2,1,0:T(8,128)(2,1)S(1)} %collective-permute-done.6.refs_2_) | copy-start | bytes 393220
  94.8 76.8 %copy-start.9 = (bf16[8,64,128]{2,1,0:T(8,128)(2,1)}, bf16[8,64,128]{2,1,0:T(8,128)(2,1)S(1)}, u32[]{:S(2)}) copy-start(bf16[8,64,128]{2,1,0:T(8,128)(2,1)S(1)} %collective-permute-done.7.refs_3_) | copy-start | bytes 393220
  94.8 7.2 %copy-start = (bf16[64,64,128]{2,1,0:T(8,128)(2,1)}, bf16[64,64,128]{2,1,0:T(8,128)(2,1)S(1)}, u32[]{:S(2)}) copy-start(bf16[64,64,128]{2,1,0:T(8,128)(2,1)S(1)} %all-to-all-done.refs_0_.own) | copy-start | bytes 3145732
  94.8 44.1 %collective-permute-start.10 = (bf16[64,64,128]{2,1,0:T(8,128)(2,1)S(1)}, bf16[64,64,128]{2,1,0:T(8,128)(2,1)}, u32[]{:S(2)}, u32[]{:S(2)}) collective-permute-start(bf16[64,64,128]{2,1,0:T(8,128)(2,1)S(1)} %all-to-all-done.refs_0_.own), channel_id=1, source_target_pairs={{0,3},{1,0},{2,1},{3,2},{4,7},{5,4},{6,5},{7,6},{8,11},{9,8},{10,9... | collective-permute-start | bytes 3145736 | tf_op jit(solution)/shard_map/ppermute | solution.py:240
  99.5 45.1 %collective-permute-start.8 = (bf16[64,64,128]{2,1,0:T(8,128)(2,1)S(1)}, bf16[64,64,128]{2,1,0:T(8,128)(2,1)}, u32[]{:S(2)}, u32[]{:S(2)}) collective-permute-start(bf16[64,64,128]{2,1,0:T(8,128)(2,1)S(1)} %all-to-all-done.refs_0_.own), channel_id=1, source_target_pairs={{0,1},{1,2},{2,3},{3,0},{4,5},{5,6},{6,7},{7,4},{8,9},{9,10},{10,1... | collective-permute-start | bytes 3145736 | tf_op jit(solution)/shard_map/ppermute | solution.py:240
  131.8 15.8 %all-to-all-start.2 = ((f32[16,8,128]{2,1,0:T(8,128)}), f32[16,8,128]{2,1,0:T(8,128)S(1)}, u32[]{:S(2)}, u32[]{:S(2)}) async-start(f32[16,8,128]{2,1,0:T(8,128)} %bitcast.12), calls=%async_computation.2 | async-start | bytes 131072 | tf_op jit(solution)/shard_map/all_to_all | solution.py:250
  140.1 24.8 %collective-permute-start.11 = (bf16[64,32,128]{2,1,0:T(8,128)(2,1)S(1)}, bf16[64,32,128]{2,1,0:T(8,128)(2,1)S(1)}, u32[]{:S(2)}, u32[]{:S(2)}) collective-permute-start(bf16[64,32,128]{2,1,0:T(8,128)(2,1)S(1)} %slice.35), channel_id=1, source_target_pairs={{0,3},{1,0},{2,1},{3,2},{4,7},{5,4},{6,5},{7,6},{8,11},{9,8},{10,9... | collective-permute-start | bytes 1572872 | tf_op jit(solution)/shard_map/ppermute | solution.py:240
  145.7 19.2 %collective-permute-start.9 = (bf16[64,32,128]{2,1,0:T(8,128)(2,1)S(1)}, bf16[64,32,128]{2,1,0:T(8,128)(2,1)S(1)}, u32[]{:S(2)}, u32[]{:S(2)}) collective-permute-start(bf16[64,32,128]{2,1,0:T(8,128)(2,1)S(1)} %slice.34), channel_id=1, source_target_pairs={{0,1},{1,2},{2,3},{3,0},{4,5},{5,6},{6,7},{7,4},{8,9},{9,10},{10,1... | collective-permute-start | bytes 1572872 | tf_op jit(solution)/shard_map/ppermute | solution.py:240
  164.9 0.8 copy-start.3
  165.6 0.8 copy-start.4
  171.6 12.1 %collective-permute-start.12 = (bf16[2,32,64,128]{3,2,1,0:T(8,128)(2,1)}, bf16[2,32,64,128]{3,2,1,0:T(8,128)(2,1)S(1)}, u32[]{:S(2)}, u32[]{:S(2)}) collective-permute-start(bf16[2,32,64,128]{3,2,1,0:T(8,128)(2,1)} %theirs.1), channel_id=1, source_target_pairs={{0,256},{256,0},{1,257},{257,1},{2,258},{258,2},{3,259},{259,3},{4... | collective-permute-start | bytes 3145736 | tf_op jit(solution)/shard_map/ppermute | solution.py:240

commit v2 on v1

--- a/solution.py
+++ b/solution.py
@@ -131,26 +131,26 @@
     )(local_cols, couplings, blocks, low, high)
 
 
-def reduce_kernel(at_ref, *refs):
-    gen_refs, (own_ref, other_ref, out_ref, lhs) = refs[:CHUNKS], refs[CHUNKS:]
+def reduce_kernel(at_ref, gen_ref, *refs):
+    panels, (out_ref, first_ref, second_ref, lhs) = refs[:-4], refs[-4:]
     half, me = at_ref[0], at_ref[1]
-    blocks, ranks, _ = gen_refs[0].shape
+    blocks, ranks, _ = gen_ref.shape
     count = blocks // 2
-    parts = own_ref.shape[0]
+    parts = len(panels) // 2
     low = low_lanes((ranks, LANES))
+    first_ref[...] = gen_ref[:, : ranks // 2]
+    second_ref[...] = gen_ref[:, ranks // 2 :]
     for side, first in ((0, half * count), (1, (1 - half) * count)):
-        for part, gen_ref in enumerate(gen_refs):
-            left = slice(part * ranks, (part + 1) * ranks)
-            right = slice((CHUNKS + part) * ranks, (CHUNKS + part + 1) * ranks)
-            for k in range(count // 2):
-                one, two = gen_ref[first + 2 * k], gen_ref[first + 2 * k + 1]
-                lanes = slice(k * LANES, (k + 1) * LANES)
-                lhs[side, left, lanes] = jnp.where(low, one, swapped_halves(two))
-                lhs[side, right, lanes] = jnp.where(low, swapped_halves(one), two)
+        for k in range(count // 2):
+            one, two = gen_ref[first + 2 * k], gen_ref[first + 2 * k + 1]
+            lanes = slice(k * LANES, (k + 1) * LANES)
+            lhs[side, :ranks, lanes] = jnp.where(low, one, swapped_halves(two))
+            lhs[side, ranks:, lanes] = jnp.where(low, swapped_halves(one), two)
     for pair in range(0, parts, 2):
         total = 0.0
-        for side, ref in ((0, own_ref), (1, other_ref)):
-            rhs = jnp.concatenate([ref[pair], ref[pair + 1]], axis=1)
+        for side in range(2):
+            ours = panels[side * parts + pair : side * parts + pair + 2]
+            rhs = jnp.concatenate([p[0] for p in ours], axis=1)
             total += jnp.dot(lhs[side], rhs, preferred_element_type=F32)
         for k in range(2):
             piece = total[:, k * LANES : (k + 1) * LANES]
@@ -158,21 +158,36 @@
             out_ref[:, slot] = piece.reshape(out_ref.shape[0], -1, LANES).astype(BF16)
 
 
-def reduced(at, gens, own, other, splits):
-    ranks = CHUNKS * gens[0].shape[1]
-    parts, rows, _ = own.shape
+def reduced(at, gens, panels, splits):
+    blocks, ranks, _ = gens.shape
+    rows = blocks * BS // 2
+    parts = len(panels) // 2
+    half_ranks = jax.ShapeDtypeStruct((blocks, ranks // 2, LANES), BF16)
+
+    def side(p, which):
+        which = which if p.shape[0] == 2 else 0
+        return pl.BlockSpec((1, rows, LANES), lambda i: (which, 0, 0))
+
+    def same(shape):
+        return pl.BlockSpec(shape, lambda i: (0,) * len(shape))
+
+    out = (splits, parts, 2 * ranks // splits, LANES)
     return pl.pallas_call(
         reduce_kernel,
-        out_shape=jax.ShapeDtypeStruct((splits, parts, 2 * ranks // splits, LANES), BF16),
-        in_specs=[whole(SMEM)] + [whole(VMEM)] * (CHUNKS + 2),
-        out_specs=whole(VMEM),
+        grid=(1,),
+        out_shape=(jax.ShapeDtypeStruct(out, BF16), half_ranks, half_ranks),
+        in_specs=[whole(SMEM), same(gens.shape)]
+        + [side(p, k // parts) for k, p in enumerate(panels)],
+        out_specs=(same(out), same(half_ranks.shape), same(half_ranks.shape)),
         scratch_shapes=[pltpu.VMEM((2, 2 * ranks, rows), BF16)],
         cost_estimate=cost(8 * ranks * rows * parts * LANES, 6 << 20),
         name="partials",
-    )(at, *gens, own, other)
-
-
-def low_rank_kernel(mine, at_ref, own, up, far_a, far_b, down, w_ref, *refs):
+    )(at, gens, *panels)
+
+
+def low_rank_kernel(mine, pieces, at_ref, *refs):
+    gens, w_ref, refs = refs[:pieces], refs[pieces], refs[pieces + 1 :]
+    own = gens[0]
     me, step, steps = at_ref[1], pl.program_id(0), pl.num_programs(0)
     per, ranks, _ = own.shape
     rhs = refs[-1]
@@ -187,7 +202,7 @@
             rhs[rows, LANES:] = both[:ranks]
 
     for i in range(per):
-        lhs = jnp.concatenate([g[i] for g in (own, up, far_a, far_b, down)], axis=0)
+        lhs = jnp.concatenate([g[i] for g in gens], axis=0)
         both = lax.dot_general(
             lhs, rhs[...], (((0,), (0,)), ((), ())), preferred_element_type=F32
         )
@@ -205,7 +220,7 @@
 
 
 def low_rank(at, gens, w, added=()):
-    blocks, ranks, _ = gens[0].shape
+    blocks, _, _ = gens[0].shape
     count, per = blocks // 2, HB
     steps = count // per
     mine = bool(added)
@@ -220,7 +235,7 @@
 
     edges = [pl.BlockSpec((per, BS, LANES), lambda i, at_ref: (i, 0, 0))] * 2 + [whole(VMEM)] * 2
     return pl.pallas_call(
-        functools.partial(low_rank_kernel, mine),
+        functools.partial(low_rank_kernel, mine, len(gens)),
         grid_spec=pltpu.PrefetchScalarGridSpec(
             num_scalar_prefetch=1,
             grid=(steps,),
@@ -258,35 +273,39 @@
     n_z, n_x, n_col = (lax.axis_size(a) for a in ("z", "x", "col"))
     blocks = samples.reshape(count, BS, width)
 
+    low = along_front(blocks[count - HB :], 1)
+    high = along_front(blocks[:HB], -1)
+    other = around(samples, "half", 1)
     (packed,) = pack(child_map[0, 0], gen_left[0], gen_right[0])
     gens = spread_out(packed, ("z", "x"))
 
-    shifted = [around(samples, "col", k) for k in range(1, n_col)]
-    low = along_front(blocks[count - HB :], 1)
-    high = along_front(blocks[:HB], -1)
+    both = jnp.stack([samples, other])
+    s_up, s_down = around(both, "col", 1), around(both, "col", -1)
     local_cols = coupling_cols - lax.axis_index(FRONT) * count + HB
     sparse_range, sparse_rows, up, down = sparse(local_cols, couplings, blocks, low, high)
-    shifted, up, down = lax.optimization_barrier((shifted, up, down))
-    panels = jnp.stack([samples, *shifted])
-    others = around(panels, "half", 1)
+    s_up, s_down, up, down = lax.optimization_barrier((s_up, s_down, up, down))
+    s_far, o_far = around(s_up[:1], "col", 1), around(s_down[1:], "col", -1)
     below, above = along_front(up, 1), along_front(down, -1)
-
-    gens, panels, others, *added = lax.optimization_barrier(
-        (gens, panels, others, sparse_range, sparse_rows, below, above)
+    panels = (both, s_up, s_far, s_down, both, s_up, o_far, s_down)
+
+    gens, panels, sparse_range, sparse_rows = lax.optimization_barrier(
+        (gens, panels, sparse_range, sparse_rows)
     )
-    partial = reduced(at, (gens,), panels, others, n_z)
-    from_up, from_down = around(gens, "col", 1), around(gens, "col", -1)
-    middle = gens.shape[1] // 2
-    far_a = around(from_up[:, :middle], "col", 1)
-    far_b = around(from_down[:, middle:], "col", -1)
-
-    by_z = jnp.sum(spread_out(partial, "z").astype(F32), axis=0)
+    added = (sparse_range, sparse_rows, below, above)
+    partial, first, second = reduced(at, gens, panels, n_z)
+    up_a, down_b = around(first, "col", 1), around(second, "col", -1)
+    up_b, down_a = around(second, "col", 1), around(first, "col", -1)
+    far_a, far_b = around(up_a, "col", 1), around(down_b, "col", -1)
+
+    by_z = spread_out(partial, "z")
+    by_z = jnp.sum(by_z.astype(F32), axis=0)
     copies = jnp.broadcast_to(by_z, (n_x, *by_z.shape)).reshape(n_x * n_col, *by_z.shape[1:])
-    arrived = spread_out(copies, ("x", "col")).reshape(n_x, n_col, *by_z.shape[1:])
-    slice_sum = jnp.sum(arrived, axis=0).astype(BF16)
-    w = spread_out(jnp.broadcast_to(slice_sum, (n_z, *slice_sum.shape)), "z")
-
-    everyone = (gens, from_up, far_a, far_b, from_down)
+    arrived = spread_out(copies, ("x", "col"))
+    slice_sum = jnp.sum(arrived.reshape(n_x, n_col, *by_z.shape[1:]), axis=0).astype(BF16)
+    copies = jnp.broadcast_to(slice_sum, (n_z, *slice_sum.shape))
+    w = spread_out(copies, "z")
+
+    everyone = (gens, up_a, up_b, far_a, far_b, down_a, down_b)
     received = around(low_rank(at, everyone, w), "half", 1)
     total = low_rank(at, everyone, w, added) + received.astype(F32)
     range_out, rows_out = total[0].astype(BF16), total[1].astype(BF16)

time: 188 us -> 204 us (1.085)
  blocking collectives: 42.1 us -> 0 us
  starting transfers between devices: 76.2 us -> 106 us
  waiting for transfers between devices: 30.1 us -> 57.2 us
  local copies, waits for them, and re-layouts: 8.72 us -> 11.1 us
    all_to_all x2 -> x0, blocking collectives: 42.1 us -> none  [spread_out(): return lax.all_to_all(x, axis, split_axis=0, concat_axis=0, tiled=True)]
    all_to_all x2 -> x4, starting transfers between devices: 26.3 us -> 44.7 us  [spread_out(): return lax.all_to_all(x, axis, split_axis=0, concat_axis=0, tiled=True)]
    all_to_all x2 -> x4, waiting for transfers between devices: 0.01 us -> 17.4 us  [spread_out(): return lax.all_to_all(x, axis, split_axis=0, concat_axis=0, tiled=True)]
    ppermute x9 -> x12, starting transfers between devices: 30.6 us -> 43.3 us  [around(): return lax.ppermute(x, axis, [(i, (i + by) % count) for i in range(count)])]
    ppermute x9 -> x12, waiting for transfers between devices: 0.02 us -> 10.3 us  [around(): return lax.ppermute(x, axis, [(i, (i + by) % count) for i in range(count)])]
    unnamed x29 -> x41, local copies, waits for them, and re-layouts: 4.18 us -> 5.02 us
  transfers between devices with their start and end apart: 15 -> 20, of which waited for: 3 -> 8; matrix products, arithmetic and copies ran while one was open for 4% -> 4% of each run, Pallas kernels for 8% -> 6%
where the time goes in v2:
time: 204 us; the launch traced here: 203 us
  starting transfers between devices  106 us (52%)
  waiting for transfers between devices  57.2 us (28%)
  Pallas kernels  23.9 us (12%)
  local copies, waits for them, and re-layouts  11.1 us (5%)
  other arithmetic  3.32 us (2%)
    all_to_all x4, starting transfers between devices, spread_out(): return lax.all_to_all(x, axis, split_axis=0, concat_axis=0, tiled=True)  44.7 us
    ppermute x12, starting transfers between devices, around(): return lax.ppermute(x, axis, [(i, (i + by) % count) for i in range(count)])  43.3 us
    ppermute x4, waiting for transfers between devices, along_front(): return lax.ppermute(x, FRONT, pairs)  29.5 us
    ppermute x4, starting transfers between devices, along_front(): return lax.ppermute(x, FRONT, pairs)  18.2 us
    all_to_all x4, waiting for transfers between devices, spread_out(): return lax.all_to_all(x, axis, split_axis=0, concat_axis=0, tiled=True)  17.4 us
    pallas_call x2, Pallas kernels, low_rank(): pl.pallas_call(functools.partial(low_rank_kernel, mine, len(gens)), grid_...  11 us
    ppermute x12, waiting for transfers between devices, around(): return lax.ppermute(x, axis, [(i, (i + by) % count) for i in range(count)])  10.3 us
    pallas_call x1, Pallas kernels, sparse(): pl.pallas_call(sparse_kernel, grid=(count // per,), out_shape=(jax.ShapeD...  5.87 us
  transfers between devices with their start and end apart: 20, of which 8 were waited for; matrix products, arithmetic and copies ran while one was open for 4% of the time, Pallas kernels for 6%

profile of v2, /device:TPU:1, one launch (start us, length us, event | category | flops | bytes accessed | tf_op | source)
XLA Modules:
  0.0 202.8 jit_solution(7211885442137100119)
XLA Ops:
  0.6 0.0 copy-start.3
  0.6 2.7 %pack.1 = bf16[64,64,128]{2,1,0:T(8,128)(2,1)} custom-call(s32[64]{0:T(128)} %bitcast.23, bf16[64,4096]{1,0:T(8,128)(2,1)} %bitcast.16, bf16[64,4096]{1,0:T(8,128)(2,1)} %bitcast.17), custom_call_target="tpu_custom_call" | custom-call | bytes 2097152 | tf_op jit(solution)/shard_map/pack/pallas_call | solution.py:55
  3.3 19.1 %all-to-all-start = ((bf16[64,64,128]{2,1,0:T(8,128)(2,1)}), bf16[64,64,128]{2,1,0:T(8,128)(2,1)S(1)}, u32[]{:S(2)}, u32[]{:S(2)}) async-start(bf16[64,64,128]{2,1,0:T(8,128)(2,1)} %pack.1), calls=%async_computation | async-start | bytes 2097152 | tf_op jit(solution)/shard_map/all_to_all | solution.py:265
  22.4 0.0 copy-start.4
  22.4 3.0 %collective-permute-start = (bf16[2048,128]{1,0:T(8,128)(2,1)S(1)}, bf16[2048,128]{1,0:T(8,128)(2,1)S(1)}, u32[]{:S(2)}, u32[]{:S(2)}) collective-permute-start(bf16[2048,128]{1,0:T(8,128)(2,1)S(1)} %copy-done.3), channel_id=1, source_target_pairs={{0,256},{256,0},{1,257},{257,1},{2,258},{258,2},{3,259},{259,3},{4... | collective-permute-start | bytes 1572872 | tf_op jit(solution)/shard_map/ppermute | solution.py:255
  25.4 1.5 collective-permute-done
  27.0 0.1 pad_maximum_fusion.refs_0_.refs_4_
  27.1 4.6 %collective-permute-start.2 = (bf16[2,2048,128]{2,1,0:T(8,128)(2,1)S(1)}, bf16[2,2048,128]{2,1,0:T(8,128)(2,1)S(1)}, u32[]{:S(2)}, u32[]{:S(2)}) collective-permute-start(bf16[2,2048,128]{2,1,0:T(8,128)(2,1)S(1)} %pad_maximum_fusion.refs_0_.refs_4_), channel_id=1, source_target_pairs={{0,3},{1,0},{2,1},{3,2},{4,7},{5,4},{6,5},{7,6},{8,11},{9,8},{10,9... | collective-permute-start | bytes 3145736 | tf_op jit(solution)/shard_map/ppermute | solution.py:255
  31.7 1.9 collective-permute-start.1
  33.7 0.7 fusion.1
  34.3 3.2 %collective-permute-start.3 = (bf16[8,64,128]{2,1,0:T(8,128)(2,1)}, bf16[8,64,128]{2,1,0:T(8,128)(2,1)S(1)}, u32[]{:S(2)}, u32[]{:S(2)}) collective-permute-start(bf16[8,64,128]{2,1,0:T(8,128)(2,1)} %bitcast.8), channel_id=1, source_target_pairs={{0,4},{4,8},{8,12},{12,16},{16,20},{20,24},{24,28},{28,32},{32,36}... | collective-permute-start | bytes 393224 | tf_op jit(solution)/shard_map/ppermute | solution.py:261
  37.5 6.1 %collective-permute-start.4 = (bf16[8,64,128]{2,1,0:T(8,128)(2,1)S(1)}, bf16[8,64,128]{2,1,0:T(8,128)(2,1)S(1)}, u32[]{:S(2)}, u32[]{:S(2)}) collective-permute-start(bf16[8,64,128]{2,1,0:T(8,128)(2,1)S(1)} %bitcast.22), channel_id=1, source_target_pairs={{4,0},{8,4},{12,8},{16,12},{20,16},{24,20},{28,24},{32,28},{36,32}... | collective-permute-start | bytes 393224 | tf_op jit(solution)/shard_map/ppermute | solution.py:261
  43.6 0.8 copy.10
  44.4 0.6 subtract_add_fusion.cols_ref
  45.0 27.6 %collective-permute-done.3.low_ref = bf16[8,64,128]{2,1,0:T(8,128)(2,1)S(1)} collective-permute-done((bf16[8,64,128]{2,1,0:T(8,128)(2,1)}, bf16[8,64,128]{2,1,0:T(8,128)(2,1)S(1)}, u32[]{:S(2)}, u32[]{:S(2)}) %collective-permute-start.3) | collective-permute-done | bytes 131104 | tf_op jit(solution)/shard_map/ppermute | solution.py:261
  72.6 0.0 collective-permute-done.4.high_ref
  72.6 0.6 copy-done.16
  73.2 0.0 copy-done.17
  73.3 5.9 %sparse.1 = (f32[32,64,128]{2,1,0:T(8,128)}, f32[32,64,128]{2,1,0:T(8,128)}, bf16[8,64,128]{2,1,0:T(8,128)(2,1)}, bf16[8,64,128]{2,1,0:T(8,128)(2,1)}) custom-call(s32[32,8]{1,0:T(8,128)} %subtract_add_fusion.cols_ref, bf16[32,64,512]{2,1,0:T(8,128)(2,1)} %a_ref.1, bf16[32,64,128]{2,1,0:T(8,128)(2,1)} %bitcast.14, bf16[8,64,128]{2,1,0:T(8,128)(2,1)} %copy-done.16, ...), custom_call_target="tpu_custom_call" | custom-call | flops 536870912 | bytes 6291456 | tf_op jit(solution)/shard_map/sparse/pallas_call | solution.py:102
  79.1 0.0 collective-permute-done.2.refs_3_.refs_7_
  79.1 0.0 collective-permute-done.1.refs_1_.refs_5_
  79.2 2.2 %slice.30 = bf16[1,2048,128]{2,1,0:T(8,128)(2,1)} slice(bf16[2,2048,128]{2,1,0:T(8,128)(2,1)} %collective-permute-done.1.refs_1_.refs_5_), slice={[0:1], [0:2048], [0:128]} | slice | bytes 1048576 | tf_op jit(solution)/shard_map/slice | solution.py:287
  81.4 0.8 slice.31
  82.2 4.6 %collective-permute-start.6 = (bf16[1,2048,128]{2,1,0:T(8,128)(2,1)}, bf16[1,2048,128]{2,1,0:T(8,128)(2,1)S(1)}, u32[]{:S(2)}, u32[]{:S(2)}) collective-permute-start(bf16[1,2048,128]{2,1,0:T(8,128)(2,1)} %slice.31), channel_id=1, source_target_pairs={{0,3},{1,0},{2,1},{3,2},{4,7},{5,4},{6,5},{7,6},{8,11},{9,8},{10,9... | collective-permute-start | bytes 1572872 | tf_op jit(solution)/shard_map/ppermute | solution.py:255
  86.9 1.9 collective-permute-start.5
  88.8 0.7 pad_add_fusion.at_ref
  89.5 3.8 %collective-permute-done.6.refs_6_ = bf16[1,2048,128]{2,1,0:T(8,128)(2,1)S(1)} collective-permute-done((bf16[1,2048,128]{2,1,0:T(8,128)(2,1)}, bf16[1,2048,128]{2,1,0:T(8,128)(2,1)S(1)}, u32[]{:S(2)}, u32[]{:S(2)}) %collective-permute-start.6) | collective-permute-done | bytes 524320 | tf_op jit(solution)/shard_map/ppermute | solution.py:255
  93.3 4.9 %collective-permute-done.5.refs_2_ = bf16[1,2048,128]{2,1,0:T(8,128)(2,1)S(1)} collective-permute-done((bf16[1,2048,128]{2,1,0:T(8,128)(2,1)}, bf16[1,2048,128]{2,1,0:T(8,128)(2,1)S(1)}, u32[]{:S(2)}, u32[]{:S(2)}) %collective-permute-start.5) | collective-permute-done | bytes 524320 | tf_op jit(solution)/shard_map/ppermute | solution.py:255
  98.2 0.0 all-to-all-done.gen_ref.refs_0_
  98.2 0.8 copy-done.13
  99.0 0.4 copy-done
  99.4 4.3 %partials.1 = (bf16[16,4,8,128]{3,2,1,0:T(8,128)(2,1)}, bf16[64,32,128]{2,1,0:T(8,128)(2,1)}, bf16[64,32,128]{2,1,0:T(8,128)(2,1)}) custom-call(s32[2]{0:T(128)} %pad_add_fusion.at_ref, bf16[64,64,128]{2,1,0:T(8,128)(2,1)} %copy-done, bf16[2,2048,128]{2,1,0:T(8,128)(2,1)} %copy-done.1, bf16[2,2048,128]{2,1,0:T(8,128)(2,1)} %collective-permute-done.1.refs_1_.refs_5_, ...), custom_call_target="tpu_custom_call" | custom-call | flops 536870912 | bytes 6291456 | tf_op jit(solution)/shard_map/partials/pallas_call | solution.py:175
  103.7 16.1 %all-to-all-start.1 = ((bf16[16,4,8,128]{3,2,1,0:T(8,128)(2,1)}), bf16[16,4,8,128]{3,2,1,0:T(8,128)(2,1)S(1)}, u32[]{:S(2)}, u32[]{:S(2)}) async-start(bf16[16,4,8,128]{3,2,1,0:T(8,128)(2,1)} %get-tuple-element.41), calls=%async_computation.1 | async-start | bytes 262144 | tf_op jit(solution)/shard_map/all_to_all | solution.py:265
  119.9 1.9 collective-permute-start.7
  121.8 4.6 %collective-permute-start.10 = (bf16[64,32,128]{2,1,0:T(8,128)(2,1)}, bf16[64,32,128]{2,1,0:T(8,128)(2,1)S(1)}, u32[]{:S(2)}, u32[]{:S(2)}) collective-permute-start(bf16[64,32,128]{2,1,0:T(8,128)(2,1)} %get-tuple-element.40), channel_id=1, source_target_pairs={{0,3},{1,0},{2,1},{3,2},{4,7},{5,4},{6,5},{7,6},{8,11},{9,8},{10,9... | collective-permute-start | bytes 1572872 | tf_op jit(solution)/shard_map/ppermute | solution.py:255
  126.4 5.5 %all-to-all-done.1 = bf16[16,4,8,128]{3,2,1,0:T(8,128)(2,1)S(1)} async-done(((bf16[16,4,8,128]{3,2,1,0:T(8,128)(2,1)}), bf16[16,4,8,128]{3,2,1,0:T(8,128)(2,1)S(1)}, u32[]{:S(2)}, u32[]{:S(2)}) %all-to-all-start.1) | async-done | bytes 131104 | tf_op jit(solution)/shard_map/all_to_all | solution.py:265
  131.9 0.6 broadcast_in_dim.6
  132.5 3.5 %all-to-all-start.2 = ((f32[16,8,128]{2,1,0:T(8,128)}), f32[16,8,128]{2,1,0:T(8,128)S(1)}, u32[]{:S(2)}, u32[]{:S(2)}) async-start(f32[16,8,128]{2,1,0:T(8,128)} %bitcast.10), calls=%async_computation.2 | async-start | bytes 131072 | tf_op jit(solution)/shard_map/all_to_all | solution.py:265
  136.0 4.4 %collective-permute-start.12 = (bf16[64,32,128]{2,1,0:T(8,128)(2,1)}, bf16[64,32,128]{2,1,0:T(8,128)(2,1)S(1)}, u32[]{:S(2)}, u32[]{:S(2)}) collective-permute-start(bf16[64,32,128]{2,1,0:T(8,128)(2,1)} %get-tuple-element.39), channel_id=1, source_target_pairs={{0,3},{1,0},{2,1},{3,2},{4,7},{5,4},{6,5},{7,6},{8,11},{9,8},{10,9... | collective-permute-start | bytes 1572872 | tf_op jit(solution)/shard_map/ppermute | solution.py:255
  140.4 1.9 collective-permute-start.8
  142.3 0.0 copy-start.5
  142.3 2.1 %collective-permute-start.9 = (bf16[64,32,128]{2,1,0:T(8,128)(2,1)S(1)}, bf16[64,32,128]{2,1,0:T(8,128)(2,1)S(1)}, u32[]{:S(2)}, u32[]{:S(2)}) collective-permute-start(bf16[64,32,128]{2,1,0:T(8,128)(2,1)S(1)} %collective-permute-done.7.refs_1_), channel_id=1, source_target_pairs={{0,1},{1,2},{2,3},{3,0},{4,5},{5,6},{6,7},{7,4},{8,9},{9,10},{10,1... | collective-permute-start | bytes 1572872 | tf_op jit(solution)/shard_map/ppermute | solution.py:255
  144.5 4.4 %collective-permute-start.11 = (bf16[64,32,128]{2,1,0:T(8,128)(2,1)S(1)}, bf16[64,32,128]{2,1,0:T(8,128)(2,1)S(1)}, u32[]{:S(2)}, u32[]{:S(2)}) collective-permute-start(bf16[64,32,128]{2,1,0:T(8,128)(2,1)S(1)} %collective-permute-done.10.refs_6_), channel_id=1, source_target_pairs={{0,3},{1,0},{2,1},{3,2},{4,7},{5,4},{6,5},{7,6},{8,11},{9,8},{10,9... | collective-permute-start | bytes 1572872 | tf_op jit(solution)/shard_map/ppermute | solution.py:255
  148.9 0.0 all-to-all-done.2
  148.9 0.7 broadcast_in_dim.7
  149.6 6.0 %all-to-all-start.3 = ((bf16[16,4,8,128]{3,2,1,0:T(8,128)(2,1)}), bf16[16,4,8,128]{3,2,1,0:T(8,128)(2,1)S(1)}, u32[]{:S(2)}, u32[]{:S(2)}) async-start(bf16[16,4,8,128]{3,2,1,0:T(8,128)(2,1)} %broadcast_in_dim.7), calls=%async_computation.3 | async-start | bytes 262144 | tf_op jit(solution)/shard_map/all_to_all | solution.py:265
  155.6 0.0 collective-permute-done.12.refs_5_
  155.6 0.0 collective-permute-done.8.refs_2_
  155.6 0.0 copy-start.8
  155.7 11.9 %all-to-all-done.3.refs_7_ = bf16[16,4,8,128]{3,2,1,0:T(8,128)(2,1)S(1)} async-done(((bf16[16,4,8,128]{3,2,1,0:T(8,128)(2,1)}), bf16[16,4,8,128]{3,2,1,0:T(8,128)(2,1)S(1)}, u32[]{:S(2)}, u32[]{:S(2)}) %all-to-all-start.3) | async-done | bytes 131104 | tf_op jit(solution)/shard_map/all_to_all | solution.py:265
  167.7 0.6 copy-done.11
  168.3 0.2 copy-done.9
  168.5 0.8 copy-done.10
  169.3 5.1 %theirs.1 = bf16[2,32,64,128]{3,2,1,0:T(8,128)(2,1)} custom-call(s32[2]{0:T(128)} %pad_add_fusion.at_ref, bf16[64,64,128]{2,1,0:T(8,128)(2,1)} %copy-done, bf16[64,32,128]{2,1,0:T(8,128)(2,1)} %copy-done.5, bf16[64,32,128]{2,1,0:T(8,128)(2,1)} %copy-done.8, bf16[64,32,128]{2,1,0:T(8,128)(2,1)} %copy-done.9, bf16[64,32,128]{2,1,0:T(8,128)(2,1)} %copy-done.10, ...), custom_call_target="tpu_custom_call" | custom-call | flops 536870912 | bytes 4194304 | tf_op jit(solution)/shard_map/theirs/pallas_call | solution.py:237
  174.5 7.9 %collective-permute-start.15 = (bf16[2,32,64,128]{3,2,1,0:T(8,128)(2,1)}, bf16[2,32,64,128]{3,2,1,0:T(8,128)(2,1)S(1)}, u32[]{:S(2)}, u32[]{:S(2)}) collective-permute-start(bf16[2,32,64,128]{3,2,1,0:T(8,128)(2,1)} %theirs.1), channel_id=1, source_target_pairs={{0,256},{256,0},{1,257},{257,1},{2,258},{258,2},{3,259},{259,3},{4... | collective-permute-start | bytes 3145736 | tf_op jit(solution)/shard_map/ppermute | solution.py:255
  182.4 2.6 %collective-permute-start.13 = (bf16[8,64,128]{2,1,0:T(8,128)(2,1)S(1)}, bf16[8,64,128]{2,1,0:T(8,128)(2,1)S(1)}, u32[]{:S(2)}, u32[]{:S(2)}) collective-permute-start(bf16[8,64,128]{2,1,0:T(8,128)(2,1)S(1)} %copy-done.19), channel_id=1, source_target_pairs={{0,4},{4,8},{8,12},{12,16},{16,20},{20,24},{24,28},{28,32},{32,36}... | collective-permute-start | bytes 393224 | tf_op jit(solution)/shard_map/ppermute | solution.py:261
  185.1 6.2 %collective-permute-start.14 = (bf16[8,64,128]{2,1,0:T(8,128)(2,1)S(1)}, bf16[8,64,128]{2,1,0:T(8,128)(2,1)S(1)}, u32[]{:S(2)}, u32[]{:S(2)}) collective-permute-start(bf16[8,64,128]{2,1,0:T(8,128)(2,1)S(1)} %copy-done.18), channel_id=1, source_target_pairs={{4,0},{8,4},{12,8},{16,12},{20,16},{24,20},{28,24},{32,28},{36,32}... | collective-permute-start | bytes 393224 | tf_op jit(solution)/shard_map/ppermute | solution.py:261
  191.3 0.7 collective-permute-done.13.refs_10_
  192.0 1.2 collective-permute-done.14.refs_11_
  193.2 0.7 copy-done.15
  193.9 5.9 %mine.1 = f32[2,32,64,128]{3,2,1,0:T(8,128)} custom-call(s32[2]{0:T(128)} %pad_add_fusion.at_ref, bf16[64,64,128]{2,1,0:T(8,128)(2,1)} %copy-done, bf16[64,32,128]{2,1,0:T(8,128)(2,1)} %copy-done.5, bf16[64,32,128]{2,1,0:T(8,128)(2,1)} %copy-done.8, bf16[64,32,128]{2,1,0:T(8,128)(2,1)} %copy-done.9, bf16[64,32,128]{2,1,0:T(8,128)(2,1)} %copy-done.10, ...), custom_call_target="tpu_custom_call" | custom-call | flops 536870912 | bytes 4194304 | tf_op jit(solution)/shard_map/mine/pallas_call | solution.py:237
  199.8 0.0 collective-permute-done.15
  199.8 1.9 add_convert_fusion
  201.7 1.0 fusion
  (34 shorter events, 0.1 us)
Async XLA Ops:
  0.6 21.8 %copy-start.3 = (bf16[2048,128]{1,0:T(8,128)(2,1)S(1)}, bf16[2048,128]{1,0:T(8,128)(2,1)}, u32[]{:S(2)}) copy-start(bf16[2048,128]{1,0:T(8,128)(2,1)} %param.6) | copy-start | bytes 1572868
  3.3 94.9 %all-to-all-start = ((bf16[64,64,128]{2,1,0:T(8,128)(2,1)}), bf16[64,64,128]{2,1,0:T(8,128)(2,1)S(1)}, u32[]{:S(2)}, u32[]{:S(2)}) async-start(bf16[64,64,128]{2,1,0:T(8,128)(2,1)} %pack.1), calls=%async_computation | async-start | bytes 2097152 | tf_op jit(solution)/shard_map/all_to_all | solution.py:265
  22.4 11.2 %copy-start.4 = (bf16[2048,128]{1,0:T(8,128)(2,1)S(1)}, bf16[2048,128]{1,0:T(8,128)(2,1)}, u32[]{:S(2)}) copy-start(bf16[2048,128]{1,0:T(8,128)(2,1)} %param.6) | copy-start | bytes 1572868
  22.4 4.5 %collective-permute-start = (bf16[2048,128]{1,0:T(8,128)(2,1)S(1)}, bf16[2048,128]{1,0:T(8,128)(2,1)S(1)}, u32[]{:S(2)}, u32[]{:S(2)}) collective-permute-start(bf16[2048,128]{1,0:T(8,128)(2,1)S(1)} %copy-done.3), channel_id=1, source_target_pairs={{0,256},{256,0},{1,257},{257,1},{2,258},{258,2},{3,259},{259,3},{4... | collective-permute-start | bytes 1572872 | tf_op jit(solution)/shard_map/ppermute | solution.py:255
  27.1 54.3 %copy-start.1 = (bf16[2,2048,128]{2,1,0:T(8,128)(2,1)}, bf16[2,2048,128]{2,1,0:T(8,128)(2,1)S(1)}, u32[]{:S(2)}) copy-start(bf16[2,2048,128]{2,1,0:T(8,128)(2,1)S(1)} %pad_maximum_fusion.refs_0_.refs_4_) | copy-start | bytes 3145732
  27.1 52.1 %collective-permute-start.2 = (bf16[2,2048,128]{2,1,0:T(8,128)(2,1)S(1)}, bf16[2,2048,128]{2,1,0:T(8,128)(2,1)S(1)}, u32[]{:S(2)}, u32[]{:S(2)}) collective-permute-start(bf16[2,2048,128]{2,1,0:T(8,128)(2,1)S(1)} %pad_maximum_fusion.refs_0_.refs_4_), channel_id=1, source_target_pairs={{0,3},{1,0},{2,1},{3,2},{4,7},{5,4},{6,5},{7,6},{8,11},{9,8},{10,9... | collective-permute-start | bytes 3145736 | tf_op jit(solution)/shard_map/ppermute | solution.py:255
  31.7 47.4 %collective-permute-start.1 = (bf16[2,2048,128]{2,1,0:T(8,128)(2,1)S(1)}, bf16[2,2048,128]{2,1,0:T(8,128)(2,1)}, u32[]{:S(2)}, u32[]{:S(2)}) collective-permute-start(bf16[2,2048,128]{2,1,0:T(8,128)(2,1)S(1)} %pad_maximum_fusion.refs_0_.refs_4_), channel_id=1, source_target_pairs={{0,1},{1,2},{2,3},{3,0},{4,5},{5,6},{6,7},{7,4},{8,9},{9,10},{10,1... | collective-permute-start | bytes 3145736 | tf_op jit(solution)/shard_map/ppermute | solution.py:255
  34.3 38.2 %collective-permute-start.3 = (bf16[8,64,128]{2,1,0:T(8,128)(2,1)}, bf16[8,64,128]{2,1,0:T(8,128)(2,1)S(1)}, u32[]{:S(2)}, u32[]{:S(2)}) collective-permute-start(bf16[8,64,128]{2,1,0:T(8,128)(2,1)} %bitcast.8), channel_id=1, source_target_pairs={{0,4},{4,8},{8,12},{12,16},{16,20},{20,24},{24,28},{28,32},{32,36}... | collective-permute-start | bytes 393224 | tf_op jit(solution)/shard_map/ppermute | solution.py:261
  37.5 35.0 %collective-permute-start.4 = (bf16[8,64,128]{2,1,0:T(8,128)(2,1)S(1)}, bf16[8,64,128]{2,1,0:T(8,128)(2,1)S(1)}, u32[]{:S(2)}, u32[]{:S(2)}) collective-permute-start(bf16[8,64,128]{2,1,0:T(8,128)(2,1)S(1)} %bitcast.22), channel_id=1, source_target_pairs={{4,0},{8,4},{12,8},{16,12},{20,16},{24,20},{28,24},{32,28},{36,32}... | collective-permute-start | bytes 393224 | tf_op jit(solution)/shard_map/ppermute | solution.py:261
  72.6 0.7 copy-start.16
  72.6 0.7 copy-start.17
  79.1 19.1 %copy-start.2 = (bf16[2,2048,128]{2,1,0:T(8,128)(2,1)}, bf16[2,2048,128]{2,1,0:T(8,128)(2,1)S(1)}, u32[]{:S(2)}) copy-start(bf16[2,2048,128]{2,1,0:T(8,128)(2,1)S(1)} %collective-permute-done.2.refs_3_.refs_7_) | copy-start | bytes 3145732
  82.2 11.1 %collective-permute-start.6 = (bf16[1,2048,128]{2,1,0:T(8,128)(2,1)}, bf16[1,2048,128]{2,1,0:T(8,128)(2,1)S(1)}, u32[]{:S(2)}, u32[]{:S(2)}) collective-permute-start(bf16[1,2048,128]{2,1,0:T(8,128)(2,1)} %slice.31), channel_id=1, source_target_pairs={{0,3},{1,0},{2,1},{3,2},{4,7},{5,4},{6,5},{7,6},{8,11},{9,8},{10,9... | collective-permute-start | bytes 1572872 | tf_op jit(solution)/shard_map/ppermute | solution.py:255
  86.9 11.3 %collective-permute-start.5 = (bf16[1,2048,128]{2,1,0:T(8,128)(2,1)}, bf16[1,2048,128]{2,1,0:T(8,128)(2,1)S(1)}, u32[]{:S(2)}, u32[]{:S(2)}) collective-permute-start(bf16[1,2048,128]{2,1,0:T(8,128)(2,1)} %slice.30), channel_id=1, source_target_pairs={{0,1},{1,2},{2,3},{3,0},{4,5},{5,6},{6,7},{7,4},{8,9},{9,10},{10,1... | collective-permute-start | bytes 1572872 | tf_op jit(solution)/shard_map/ppermute | solution.py:255
  93.3 4.9 %copy-start.12 = (bf16[1,2048,128]{2,1,0:T(8,128)(2,1)}, bf16[1,2048,128]{2,1,0:T(8,128)(2,1)S(1)}, u32[]{:S(2)}) copy-start(bf16[1,2048,128]{2,1,0:T(8,128)(2,1)S(1)} %collective-permute-done.6.refs_6_) | copy-start | bytes 1572868
  98.2 0.8 copy-start.13
  98.2 1.2 copy-start
  103.7 28.1 %all-to-all-start.1 = ((bf16[16,4,8,128]{3,2,1,0:T(8,128)(2,1)}), bf16[16,4,8,128]{3,2,1,0:T(8,128)(2,1)S(1)}, u32[]{:S(2)}, u32[]{:S(2)}) async-start(bf16[16,4,8,128]{3,2,1,0:T(8,128)(2,1)} %get-tuple-element.41), calls=%async_computation.1 | async-start | bytes 262144 | tf_op jit(solution)/shard_map/all_to_all | solution.py:265
  119.9 22.4 %collective-permute-start.7 = (bf16[64,32,128]{2,1,0:T(8,128)(2,1)}, bf16[64,32,128]{2,1,0:T(8,128)(2,1)S(1)}, u32[]{:S(2)}, u32[]{:S(2)}) collective-permute-start(bf16[64,32,128]{2,1,0:T(8,128)(2,1)} %get-tuple-element.39), channel_id=1, source_target_pairs={{0,1},{1,2},{2,3},{3,0},{4,5},{5,6},{6,7},{7,4},{8,9},{9,10},{10,1... | collective-permute-start | bytes 1572872 | tf_op jit(solution)/shard_map/ppermute | solution.py:255
  121.8 22.7 %collective-permute-start.10 = (bf16[64,32,128]{2,1,0:T(8,128)(2,1)}, bf16[64,32,128]{2,1,0:T(8,128)(2,1)S(1)}, u32[]{:S(2)}, u32[]{:S(2)}) collective-permute-start(bf16[64,32,128]{2,1,0:T(8,128)(2,1)} %get-tuple-element.40), channel_id=1, source_target_pairs={{0,3},{1,0},{2,1},{3,2},{4,7},{5,4},{6,5},{7,6},{8,11},{9,8},{10,9... | collective-permute-start | bytes 1572872 | tf_op jit(solution)/shard_map/ppermute | solution.py:255
  132.5 16.4 %all-to-all-start.2 = ((f32[16,8,128]{2,1,0:T(8,128)}), f32[16,8,128]{2,1,0:T(8,128)S(1)}, u32[]{:S(2)}, u32[]{:S(2)}) async-start(f32[16,8,128]{2,1,0:T(8,128)} %bitcast.10), calls=%async_computation.2 | async-start | bytes 131072 | tf_op jit(solution)/shard_map/all_to_all | solution.py:265
  136.0 19.6 %collective-permute-start.12 = (bf16[64,32,128]{2,1,0:T(8,128)(2,1)}, bf16[64,32,128]{2,1,0:T(8,128)(2,1)S(1)}, u32[]{:S(2)}, u32[]{:S(2)}) collective-permute-start(bf16[64,32,128]{2,1,0:T(8,128)(2,1)} %get-tuple-element.39), channel_id=1, source_target_pairs={{0,3},{1,0},{2,1},{3,2},{4,7},{5,4},{6,5},{7,6},{8,11},{9,8},{10,9... | collective-permute-start | bytes 1572872 | tf_op jit(solution)/shard_map/ppermute | solution.py:255
  140.4 15.2 %collective-permute-start.8 = (bf16[64,32,128]{2,1,0:T(8,128)(2,1)}, bf16[64,32,128]{2,1,0:T(8,128)(2,1)S(1)}, u32[]{:S(2)}, u32[]{:S(2)}) collective-permute-start(bf16[64,32,128]{2,1,0:T(8,128)(2,1)} %get-tuple-element.40), channel_id=1, source_target_pairs={{0,1},{1,2},{2,3},{3,0},{4,5},{5,6},{6,7},{7,4},{8,9},{9,10},{10,1... | collective-permute-start | bytes 1572872 | tf_op jit(solution)/shard_map/ppermute | solution.py:255
  142.3 25.3 %copy-start.5 = (bf16[64,32,128]{2,1,0:T(8,128)(2,1)}, bf16[64,32,128]{2,1,0:T(8,128)(2,1)S(1)}, u32[]{:S(2)}) copy-start(bf16[64,32,128]{2,1,0:T(8,128)(2,1)S(1)} %collective-permute-done.7.refs_1_) | copy-start | bytes 1572868
  142.3 25.3 %collective-permute-start.9 = (bf16[64,32,128]{2,1,0:T(8,128)(2,1)S(1)}, bf16[64,32,128]{2,1,0:T(8,128)(2,1)S(1)}, u32[]{:S(2)}, u32[]{:S(2)}) collective-permute-start(bf16[64,32,128]{2,1,0:T(8,128)(2,1)S(1)} %collective-permute-done.7.refs_1_), channel_id=1, source_target_pairs={{0,1},{1,2},{2,3},{3,0},{4,5},{5,6},{6,7},{7,4},{8,9},{9,10},{10,1... | collective-permute-start | bytes 1572872 | tf_op jit(solution)/shard_map/ppermute | solution.py:255
  144.5 23.1 %copy-start.6 = (bf16[64,32,128]{2,1,0:T(8,128)(2,1)}, bf16[64,32,128]{2,1,0:T(8,128)(2,1)S(1)}, u32[]{:S(2)}) copy-start(bf16[64,32,128]{2,1,0:T(8,128)(2,1)S(1)} %collective-permute-done.10.refs_6_) | copy-start | bytes 1572868
  144.5 23.1 %collective-permute-start.11 = (bf16[64,32,128]{2,1,0:T(8,128)(2,1)S(1)}, bf16[64,32,128]{2,1,0:T(8,128)(2,1)S(1)}, u32[]{:S(2)}, u32[]{:S(2)}) collective-permute-start(bf16[64,32,128]{2,1,0:T(8,128)(2,1)S(1)} %collective-permute-done.10.refs_6_), channel_id=1, source_target_pairs={{0,3},{1,0},{2,1},{3,2},{4,7},{5,4},{6,5},{7,6},{8,11},{9,8},{10,9... | collective-permute-start | bytes 1572872 | tf_op jit(solution)/shard_map/ppermute | solution.py:255
  149.6 18.0 %all-to-all-start.3 = ((bf16[16,4,8,128]{3,2,1,0:T(8,128)(2,1)}), bf16[16,4,8,128]{3,2,1,0:T(8,128)(2,1)S(1)}, u32[]{:S(2)}, u32[]{:S(2)}) async-start(bf16[16,4,8,128]{3,2,1,0:T(8,128)(2,1)} %broadcast_in_dim.7), calls=%async_computation.3 | async-start | bytes 262144 | tf_op jit(solution)/shard_map/all_to_all | solution.py:265
  155.6 26.8 %copy-start.19 = (bf16[8,64,128]{2,1,0:T(8,128)(2,1)S(1)}, bf16[8,64,128]{2,1,0:T(8,128)(2,1)}, u32[]{:S(2)}) copy-start(bf16[8,64,128]{2,1,0:T(8,128)(2,1)} %get-tuple-element.44) | copy-start | bytes 393220
  155.6 29.5 %copy-start.18 = (bf16[8,64,128]{2,1,0:T(8,128)(2,1)S(1)}, bf16[8,64,128]{2,1,0:T(8,128)(2,1)}, u32[]{:S(2)}) copy-start(bf16[8,64,128]{2,1,0:T(8,128)(2,1)} %get-tuple-element.45) | copy-start | bytes 393220
  155.6 12.0 %copy-start.7 = (bf16[64,32,128]{2,1,0:T(8,128)(2,1)}, bf16[64,32,128]{2,1,0:T(8,128)(2,1)S(1)}, u32[]{:S(2)}) copy-start(bf16[64,32,128]{2,1,0:T(8,128)(2,1)S(1)} %collective-permute-done.12.refs_5_) | copy-start | bytes 1572868
  155.6 12.0 %copy-start.8 = (bf16[64,32,128]{2,1,0:T(8,128)(2,1)}, bf16[64,32,128]{2,1,0:T(8,128)(2,1)S(1)}, u32[]{:S(2)}) copy-start(bf16[64,32,128]{2,1,0:T(8,128)(2,1)S(1)} %collective-permute-done.8.refs_2_) | copy-start | bytes 1572868
  167.6 0.7 copy-start.11
  167.6 0.9 copy-start.9
  168.5 0.8 copy-start.10
  174.5 25.3 %collective-permute-start.15 = (bf16[2,32,64,128]{3,2,1,0:T(8,128)(2,1)}, bf16[2,32,64,128]{3,2,1,0:T(8,128)(2,1)S(1)}, u32[]{:S(2)}, u32[]{:S(2)}) collective-permute-start(bf16[2,32,64,128]{3,2,1,0:T(8,128)(2,1)} %theirs.1), channel_id=1, source_target_pairs={{0,256},{256,0},{1,257},{257,1},{2,258},{258,2},{3,259},{259,3},{4... | collective-permute-start | bytes 3145736 | tf_op jit(solution)/shard_map/ppermute | solution.py:255
  182.4 9.6 %collective-permute-start.13 = (bf16[8,64,128]{2,1,0:T(8,128)(2,1)S(1)}, bf16[8,64,128]{2,1,0:T(8,128)(2,1)S(1)}, u32[]{:S(2)}, u32[]{:S(2)}) collective-permute-start(bf16[8,64,128]{2,1,0:T(8,128)(2,1)S(1)} %copy-done.19), channel_id=1, source_target_pairs={{0,4},{4,8},{8,12},{12,16},{16,20},{20,24},{24,28},{28,32},{32,36}... | collective-permute-start | bytes 393224 | tf_op jit(solution)/shard_map/ppermute | solution.py:261
  185.1 8.2 %collective-permute-start.14 = (bf16[8,64,128]{2,1,0:T(8,128)(2,1)S(1)}, bf16[8,64,128]{2,1,0:T(8,128)(2,1)S(1)}, u32[]{:S(2)}, u32[]{:S(2)}) collective-permute-start(bf16[8,64,128]{2,1,0:T(8,128)(2,1)S(1)} %copy-done.18), channel_id=1, source_target_pairs={{4,0},{8,4},{12,8},{16,12},{20,16},{24,20},{28,24},{32,28},{36,32}... | collective-permute-start | bytes 393224 | tf_op jit(solution)/shard_map/ppermute | solution.py:261
  192.0 1.2 copy-start.14
  193.2 0.7 copy-start.15

commit v3 on v2

--- a/solution.py
+++ b/solution.py
@@ -131,12 +131,11 @@
     )(local_cols, couplings, blocks, low, high)
 
 
-def reduce_kernel(at_ref, gen_ref, *refs):
-    panels, (out_ref, first_ref, second_ref, lhs) = refs[:-4], refs[-4:]
+def reduce_kernel(at_ref, gen_ref, own_ref, other_ref, out_ref, first_ref, second_ref, lhs):
     half, me = at_ref[0], at_ref[1]
     blocks, ranks, _ = gen_ref.shape
     count = blocks // 2
-    parts = len(panels) // 2
+    parts = own_ref.shape[0]
     low = low_lanes((ranks, LANES))
     first_ref[...] = gen_ref[:, : ranks // 2]
     second_ref[...] = gen_ref[:, ranks // 2 :]
@@ -148,9 +147,8 @@
             lhs[side, ranks:, lanes] = jnp.where(low, swapped_halves(one), two)
     for pair in range(0, parts, 2):
         total = 0.0
-        for side in range(2):
-            ours = panels[side * parts + pair : side * parts + pair + 2]
-            rhs = jnp.concatenate([p[0] for p in ours], axis=1)
+        for side, ref in ((0, own_ref), (1, other_ref)):
+            rhs = jnp.concatenate([ref[pair], ref[pair + 1]], axis=1)
             total += jnp.dot(lhs[side], rhs, preferred_element_type=F32)
         for k in range(2):
             piece = total[:, k * LANES : (k + 1) * LANES]
@@ -158,65 +156,59 @@
             out_ref[:, slot] = piece.reshape(out_ref.shape[0], -1, LANES).astype(BF16)
 
 
-def reduced(at, gens, panels, splits):
+def reduced(at, gens, own, other, splits):
     blocks, ranks, _ = gens.shape
-    rows = blocks * BS // 2
-    parts = len(panels) // 2
+    parts, rows, _ = own.shape
     half_ranks = jax.ShapeDtypeStruct((blocks, ranks // 2, LANES), BF16)
-
-    def side(p, which):
-        which = which if p.shape[0] == 2 else 0
-        return pl.BlockSpec((1, rows, LANES), lambda i: (which, 0, 0))
-
-    def same(shape):
-        return pl.BlockSpec(shape, lambda i: (0,) * len(shape))
-
-    out = (splits, parts, 2 * ranks // splits, LANES)
+    out = jax.ShapeDtypeStruct((splits, parts, 2 * ranks // splits, LANES), BF16)
     return pl.pallas_call(
         reduce_kernel,
-        grid=(1,),
-        out_shape=(jax.ShapeDtypeStruct(out, BF16), half_ranks, half_ranks),
-        in_specs=[whole(SMEM), same(gens.shape)]
-        + [side(p, k // parts) for k, p in enumerate(panels)],
-        out_specs=(same(out), same(half_ranks.shape), same(half_ranks.shape)),
+        out_shape=(out, half_ranks, half_ranks),
+        in_specs=[whole(SMEM)] + [whole(VMEM)] * 3,
+        out_specs=(whole(VMEM),) * 3,
         scratch_shapes=[pltpu.VMEM((2, 2 * ranks, rows), BF16)],
         cost_estimate=cost(8 * ranks * rows * parts * LANES, 6 << 20),
         name="partials",
-    )(at, gens, *panels)
+    )(at, gens, own, other)
 
 
 def low_rank_kernel(mine, pieces, at_ref, *refs):
     gens, w_ref, refs = refs[:pieces], refs[pieces], refs[pieces + 1 :]
-    own = gens[0]
     me, step, steps = at_ref[1], pl.program_id(0), pl.num_programs(0)
-    per, ranks, _ = own.shape
-    rhs = refs[-1]
-    parts = rhs.shape[0] // ranks
+    per, ranks, _ = gens[0].shape
+    lhs = refs[-1]
+    parts = lhs.shape[1] // ranks
+    low = low_lanes((LANES, LANES))
 
     @pl.when(step == 0)
     def _():
         for k in range(parts):
             both = w_ref[:, lax.rem(me + parts - k, parts)].reshape(2 * ranks, LANES)
-            rows = slice(k * ranks, (k + 1) * ranks)
-            rhs[rows, :LANES] = both[ranks:]
-            rhs[rows, LANES:] = both[:ranks]
-
-    for i in range(per):
-        lhs = jnp.concatenate([g[i] for g in gens], axis=0)
-        both = lax.dot_general(
-            lhs, rhs[...], (((0,), (0,)), ((), ())), preferred_element_type=F32
+            turned = both.astype(F32).T.astype(BF16)
+            lanes = slice(k * ranks, (k + 1) * ranks)
+            lhs[:LANES, lanes] = turned[:, ranks:]
+            lhs[LANES:, lanes] = turned[:, :ranks]
+
+    for i in range(0, per, 2):
+        rhs = jnp.concatenate(
+            [jnp.concatenate([g[i + j] for g in gens], axis=0) for j in range(2)], axis=1
         )
-        for_range, for_rows = both[:BS, :LANES], both[BS:, LANES:]
-        if mine:
-            sr_ref, sp_ref, below_ref, above_ref, out_ref = refs[:-1]
-            for_range += sr_ref[i]
-            for_rows += sp_ref[i]
-            for_rows += jnp.where(step == 0, below_ref[i].astype(F32), 0.0)
-            for_rows += jnp.where(step == steps - 1, above_ref[i].astype(F32), 0.0)
-        else:
-            out_ref = refs[0]
-        out_ref[0, i] = for_range.astype(out_ref.dtype)
-        out_ref[1, i] = for_rows.astype(out_ref.dtype)
+        both = jnp.dot(lhs[...], rhs, preferred_element_type=F32)
+        for j in range(2):
+            lanes = slice(j * LANES, (j + 1) * LANES)
+            out = jnp.where(low, both[:LANES, lanes], both[LANES:, lanes]).T
+            for_range, for_rows = out[:BS], out[BS:]
+            b = i + j
+            if mine:
+                sr_ref, sp_ref, below_ref, above_ref, range_ref, rows_ref = refs[:-1]
+                range_ref[b] = for_range + sr_ref[b]
+                for_rows += sp_ref[b]
+                for_rows += jnp.where(step == 0, below_ref[b].astype(F32), 0.0)
+                for_rows += jnp.where(step == steps - 1, above_ref[b].astype(F32), 0.0)
+                rows_ref[b] = for_rows
+            else:
+                refs[0][0, b] = for_range.astype(BF16)
+                refs[0][1, b] = for_rows.astype(BF16)
 
 
 def low_rank(at, gens, w, added=()):
@@ -233,17 +225,24 @@
     def tiles(rows):
         return pl.BlockSpec((per, rows, LANES), place)
 
-    edges = [pl.BlockSpec((per, BS, LANES), lambda i, at_ref: (i, 0, 0))] * 2 + [whole(VMEM)] * 2
+    flat = pl.BlockSpec((per, BS, LANES), lambda i, at_ref: (i, 0, 0))
+    edges = [flat] * 2 + [whole(VMEM)] * 2
+    if mine:
+        out_shape = (jax.ShapeDtypeStruct((count, BS, LANES), F32),) * 2
+        out_specs = (flat, flat)
+    else:
+        out_shape = jax.ShapeDtypeStruct((2, count, BS, LANES), BF16)
+        out_specs = pl.BlockSpec((2, per, BS, LANES), lambda i, at_ref: (0, i, 0, 0))
     return pl.pallas_call(
         functools.partial(low_rank_kernel, mine, len(gens)),
         grid_spec=pltpu.PrefetchScalarGridSpec(
             num_scalar_prefetch=1,
             grid=(steps,),
             in_specs=[tiles(g.shape[1]) for g in gens] + [whole(VMEM)] + (edges if mine else []),
-            out_specs=pl.BlockSpec((2, per, BS, LANES), lambda i, at_ref: (0, i, 0, 0)),
-            scratch_shapes=[pltpu.VMEM((depth, 2 * LANES), BF16)],
+            out_specs=out_specs,
+            scratch_shapes=[pltpu.VMEM((2 * LANES, depth), BF16)],
         ),
-        out_shape=jax.ShapeDtypeStruct((2, count, BS, LANES), F32 if mine else BF16),
+        out_shape=out_shape,
         compiler_params=pltpu.CompilerParams(dimension_semantics=("arbitrary",)),
         cost_estimate=cost(4 * count * LANES * depth * LANES, 4 << 20),
         name="mine" if mine else "theirs",
@@ -275,24 +274,22 @@
 
     low = along_front(blocks[count - HB :], 1)
     high = along_front(blocks[:HB], -1)
-    other = around(samples, "half", 1)
     (packed,) = pack(child_map[0, 0], gen_left[0], gen_right[0])
     gens = spread_out(packed, ("z", "x"))
 
-    both = jnp.stack([samples, other])
-    s_up, s_down = around(both, "col", 1), around(both, "col", -1)
+    shifted = [around(samples, "col", k) for k in range(1, n_col)]
     local_cols = coupling_cols - lax.axis_index(FRONT) * count + HB
     sparse_range, sparse_rows, up, down = sparse(local_cols, couplings, blocks, low, high)
-    s_up, s_down, up, down = lax.optimization_barrier((s_up, s_down, up, down))
-    s_far, o_far = around(s_up[:1], "col", 1), around(s_down[1:], "col", -1)
+    shifted, up, down = lax.optimization_barrier((shifted, up, down))
+    panels = jnp.stack([samples, *shifted])
+    others = around(panels, "half", 1)
     below, above = along_front(up, 1), along_front(down, -1)
-    panels = (both, s_up, s_far, s_down, both, s_up, o_far, s_down)
-
-    gens, panels, sparse_range, sparse_rows = lax.optimization_barrier(
-        (gens, panels, sparse_range, sparse_rows)
+
+    gens, panels, others, sparse_range, sparse_rows = lax.optimization_barrier(
+        (gens, panels, others, sparse_range, sparse_rows)
     )
     added = (sparse_range, sparse_rows, below, above)
-    partial, first, second = reduced(at, gens, panels, n_z)
+    partial, first, second = reduced(at, gens, panels, others, n_z)
     up_a, down_b = around(first, "col", 1), around(second, "col", -1)
     up_b, down_a = around(second, "col", 1), around(first, "col", -1)
     far_a, far_b = around(up_a, "col", 1), around(down_b, "col", -1)
@@ -307,8 +304,10 @@
 
     everyone = (gens, up_a, up_b, far_a, far_b, down_a, down_b)
     received = around(low_rank(at, everyone, w), "half", 1)
-    total = low_rank(at, everyone, w, added) + received.astype(F32)
-    range_out, rows_out = total[0].astype(BF16), total[1].astype(BF16)
+    range_out, rows_out = (
+        (ours + theirs.astype(F32)).astype(BF16)
+        for ours, theirs in zip(low_rank(at, everyone, w, added), received)
+    )
     return range_out.reshape(samples.shape), rows_out.reshape(samples.shape)
 
 

time: 204 us -> 190 us (0.931)
  starting transfers between devices: 106 us -> 98.5 us
  waiting for transfers between devices: 57.2 us -> 52.4 us
  local copies, waits for them, and re-layouts: 11.1 us -> 6.32 us
  other arithmetic: 3.32 us -> 5.92 us
    ppermute x12 -> x11, waiting for transfers between devices: 10.3 us -> 3.63 us  [around(): return lax.ppermute(x, axis, [(i, (i + by) % count) for i in range(count)])]
    ppermute x12 -> x11, starting transfers between devices: 43.3 us -> 36.9 us  [around(): return lax.ppermute(x, axis, [(i, (i + by) % count) for i in range(count)])]
    slice x3 -> x0, local copies, waits for them, and re-layouts: 4.11 us -> none  [the longest x2 3.07 us: shards(): s_far, o_far = (around(s_up[:1], 'col', 1), around(s_down[1:], 'col', -1))]
    convert_element_type x0 -> x1, other arithmetic: none -> 2.85 us  [shards(): (ours + theirs.astype(F32)).astype(BF16)]
    all_to_all x4, starting transfers between devices: 44.7 us -> 42.2 us  [spread_out(): return lax.all_to_all(x, axis, split_axis=0, concat_axis=0, tiled=True)]
    unnamed x41 -> x39, local copies, waits for them, and re-layouts: 5.02 us -> 5 us
  transfers between devices with their start and end apart: 20 -> 19, of which waited for: 8 -> 6; matrix products, arithmetic and copies ran while one was open for 4% -> 2% of each run, Pallas kernels for 6% -> 6%
where the time goes in v3:
time: 190 us; the launch traced here: 189 us
  starting transfers between devices  98.5 us (52%)
  waiting for transfers between devices  52.4 us (28%)
  Pallas kernels  24.4 us (13%)
  local copies, waits for them, and re-layouts  6.32 us (3%)
  other arithmetic  5.92 us (3%)
    all_to_all x4, starting transfers between devices, spread_out(): return lax.all_to_all(x, axis, split_axis=0, concat_axis=0, tiled=True)  42.2 us
    ppermute x11, starting transfers between devices, around(): return lax.ppermute(x, axis, [(i, (i + by) % count) for i in range(count)])  36.9 us
    ppermute x4, waiting for transfers between devices, along_front(): return lax.ppermute(x, FRONT, pairs)  31.4 us
    ppermute x4, starting transfers between devices, along_front(): return lax.ppermute(x, FRONT, pairs)  19.3 us
    all_to_all x4, waiting for transfers between devices, spread_out(): return lax.all_to_all(x, axis, split_axis=0, concat_axis=0, tiled=True)  17.4 us
    pallas_call x2, Pallas kernels, low_rank(): pl.pallas_call(functools.partial(low_rank_kernel, mine, len(gens)), grid_...  11.5 us
    pallas_call x1, Pallas kernels, sparse(): pl.pallas_call(sparse_kernel, grid=(count // per,), out_shape=(jax.ShapeD...  5.88 us
    unnamed x39, local copies, waits for them, and re-layouts  5 us
  transfers between devices with their start and end apart: 19, of which 6 were waited for; matrix products, arithmetic and copies ran while one was open for 2% of the time, Pallas kernels for 6%

profile of v3, /device:TPU:1, one launch (start us, length us, event | category | flops | bytes accessed | tf_op | source)
XLA Modules:
  0.0 188.5 jit_solution(2005999748926713781)
XLA Ops:
  0.6 0.0 copy-start.2
  0.6 0.0 copy-start.16
  0.7 2.6 %pack.1 = bf16[64,64,128]{2,1,0:T(8,128)(2,1)} custom-call(s32[64]{0:T(128)} %bitcast.37, bf16[64,4096]{1,0:T(8,128)(2,1)} %bitcast.28, bf16[64,4096]{1,0:T(8,128)(2,1)} %bitcast.29), custom_call_target="tpu_custom_call" | custom-call | bytes 2097152 | tf_op jit(solution)/shard_map/pack/pallas_call | solution.py:55
  3.3 19.1 %all-to-all-start = ((bf16[64,64,128]{2,1,0:T(8,128)(2,1)}), bf16[64,64,128]{2,1,0:T(8,128)(2,1)S(1)}, u32[]{:S(2)}, u32[]{:S(2)}) async-start(bf16[64,64,128]{2,1,0:T(8,128)(2,1)} %pack.1), calls=%async_computation | async-start | bytes 2097152 | tf_op jit(solution)/shard_map/all_to_all | solution.py:264
  22.4 4.6 %collective-permute-start.2 = (bf16[2048,128]{1,0:T(8,128)(2,1)S(1)}, bf16[2048,128]{1,0:T(8,128)(2,1)}, u32[]{:S(2)}, u32[]{:S(2)}) collective-permute-start(bf16[2048,128]{1,0:T(8,128)(2,1)S(1)} %copy-done.2), channel_id=1, source_target_pairs={{0,3},{1,0},{2,1},{3,2},{4,7},{5,4},{6,5},{7,6},{8,11},{9,8},{10,9... | collective-permute-start | bytes 1572872 | tf_op jit(solution)/shard_map/ppermute | solution.py:254
  27.0 2.3 %collective-permute-start.1 = (bf16[2048,128]{1,0:T(8,128)(2,1)S(1)}, bf16[2048,128]{1,0:T(8,128)(2,1)S(1)}, u32[]{:S(2)}, u32[]{:S(2)}) collective-permute-start(bf16[2048,128]{1,0:T(8,128)(2,1)S(1)} %copy-done.2), channel_id=1, source_target_pairs={{0,2},{1,3},{2,0},{3,1},{4,6},{5,7},{6,4},{7,5},{8,10},{9,11},{10,... | collective-permute-start | bytes 1572872 | tf_op jit(solution)/shard_map/ppermute | solution.py:254
  29.3 2.6 %collective-permute-start = (bf16[2048,128]{1,0:T(8,128)(2,1)S(1)}, bf16[2048,128]{1,0:T(8,128)(2,1)S(1)}, u32[]{:S(2)}, u32[]{:S(2)}) collective-permute-start(bf16[2048,128]{1,0:T(8,128)(2,1)S(1)} %copy-done.2), channel_id=1, source_target_pairs={{0,1},{1,2},{2,3},{3,0},{4,5},{5,6},{6,7},{7,4},{8,9},{9,10},{10,1... | collective-permute-start | bytes 1572872 | tf_op jit(solution)/shard_map/ppermute | solution.py:254
  31.9 2.9 %collective-permute-start.3 = (bf16[8,64,128]{2,1,0:T(8,128)(2,1)S(1)}, bf16[8,64,128]{2,1,0:T(8,128)(2,1)S(1)}, u32[]{:S(2)}, u32[]{:S(2)}) collective-permute-start(bf16[8,64,128]{2,1,0:T(8,128)(2,1)S(1)} %bitcast.36), channel_id=1, source_target_pairs={{0,4},{4,8},{8,12},{12,16},{16,20},{20,24},{24,28},{28,32},{32,36}... | collective-permute-start | bytes 393224 | tf_op jit(solution)/shard_map/ppermute | solution.py:260
  34.9 7.5 %collective-permute-start.4 = (bf16[8,64,128]{2,1,0:T(8,128)(2,1)S(1)}, bf16[8,64,128]{2,1,0:T(8,128)(2,1)S(1)}, u32[]{:S(2)}, u32[]{:S(2)}) collective-permute-start(bf16[8,64,128]{2,1,0:T(8,128)(2,1)S(1)} %bitcast.35), channel_id=1, source_target_pairs={{4,0},{8,4},{12,8},{16,12},{20,16},{24,20},{28,24},{32,28},{36,32}... | collective-permute-start | bytes 393224 | tf_op jit(solution)/shard_map/ppermute | solution.py:260
  42.4 0.1 copy.10
  42.5 0.6 subtract_add_fusion.cols_ref
  43.1 29.4 %collective-permute-done.3.low_ref = bf16[8,64,128]{2,1,0:T(8,128)(2,1)S(1)} collective-permute-done((bf16[8,64,128]{2,1,0:T(8,128)(2,1)S(1)}, bf16[8,64,128]{2,1,0:T(8,128)(2,1)S(1)}, u32[]{:S(2)}, u32[]{:S(2)}) %collective-permute-start.3) | collective-permute-done | bytes 131104 | tf_op jit(solution)/shard_map/ppermute | solution.py:260
  72.5 0.0 collective-permute-done.4.high_ref
  72.5 0.6 copy-done.12
  73.2 0.0 copy-done.13
  73.2 5.9 %sparse.1 = (f32[32,64,128]{2,1,0:T(8,128)}, f32[32,64,128]{2,1,0:T(8,128)}, bf16[8,64,128]{2,1,0:T(8,128)(2,1)}, bf16[8,64,128]{2,1,0:T(8,128)(2,1)}) custom-call(s32[32,8]{1,0:T(8,128)} %subtract_add_fusion.cols_ref, bf16[32,64,512]{2,1,0:T(8,128)(2,1)} %a_ref.1, bf16[32,64,128]{2,1,0:T(8,128)(2,1)} %bitcast.26, bf16[8,64,128]{2,1,0:T(8,128)(2,1)} %copy-done.12, ...), custom_call_target="tpu_custom_call" | custom-call | flops 536870912 | bytes 6291456 | tf_op jit(solution)/shard_map/sparse/pallas_call | solution.py:102
  79.1 0.0 collective-permute-done.2
  79.1 0.0 collective-permute-done.1
  79.1 0.0 copy-start.10
  79.1 0.0 collective-permute-done
  79.1 0.0 copy-start.11
  79.1 0.8 copy-done.10
  79.9 0.2 copy-done.11
  80.1 1.8 pad_maximum_fusion.own_ref
  81.9 1.9 %collective-permute-start.5 = (bf16[4,2048,128]{2,1,0:T(8,128)(2,1)S(1)}, bf16[4,2048,128]{2,1,0:T(8,128)(2,1)}, u32[]{:S(2)}, u32[]{:S(2)}) collective-permute-start(bf16[4,2048,128]{2,1,0:T(8,128)(2,1)S(1)} %pad_maximum_fusion.own_ref), channel_id=1, source_target_pairs={{0,256},{256,0},{1,257},{257,1},{2,258},{258,2},{3,259},{259,3},{4... | collective-permute-start | bytes 6291464 | tf_op jit(solution)/shard_map/ppermute | solution.py:254
  83.8 0.7 pad_add_fusion.at_ref
  84.5 3.6 %collective-permute-done.5.other_ref = bf16[4,2048,128]{2,1,0:T(8,128)(2,1)} collective-permute-done((bf16[4,2048,128]{2,1,0:T(8,128)(2,1)S(1)}, bf16[4,2048,128]{2,1,0:T(8,128)(2,1)}, u32[]{:S(2)}, u32[]{:S(2)}) %collective-permute-start.5) | collective-permute-done | bytes 2097184 | tf_op jit(solution)/shard_map/ppermute | solution.py:254
  88.1 0.0 all-to-all-done.gen_ref.refs_0_
  88.1 1.0 copy-done
  89.0 4.3 %partials.1 = (bf16[16,4,8,128]{3,2,1,0:T(8,128)(2,1)}, bf16[64,32,128]{2,1,0:T(8,128)(2,1)}, bf16[64,32,128]{2,1,0:T(8,128)(2,1)}) custom-call(s32[2]{0:T(128)} %pad_add_fusion.at_ref, bf16[64,64,128]{2,1,0:T(8,128)(2,1)} %copy-done, bf16[4,2048,128]{2,1,0:T(8,128)(2,1)} %copy-done.1, bf16[4,2048,128]{2,1,0:T(8,128)(2,1)} %collective-permute-done.5.other_ref), custom_call_target="tpu_custom_call" | custom-call | flops 536870912 | bytes 6291456 | tf_op jit(solution)/shard_map/partials/pallas_call | solution.py:164
  93.4 12.3 %all-to-all-start.1 = ((bf16[16,4,8,128]{3,2,1,0:T(8,128)(2,1)}), bf16[16,4,8,128]{3,2,1,0:T(8,128)(2,1)S(1)}, u32[]{:S(2)}, u32[]{:S(2)}) async-start(bf16[16,4,8,128]{3,2,1,0:T(8,128)(2,1)} %get-tuple-element.33), calls=%async_computation.1 | async-start | bytes 262144 | tf_op jit(solution)/shard_map/all_to_all | solution.py:264
  105.7 3.2 %collective-permute-start.6 = (bf16[64,32,128]{2,1,0:T(8,128)(2,1)}, bf16[64,32,128]{2,1,0:T(8,128)(2,1)S(1)}, u32[]{:S(2)}, u32[]{:S(2)}) collective-permute-start(bf16[64,32,128]{2,1,0:T(8,128)(2,1)} %get-tuple-element.31), channel_id=1, source_target_pairs={{0,1},{1,2},{2,3},{3,0},{4,5},{5,6},{6,7},{7,4},{8,9},{9,10},{10,1... | collective-permute-start | bytes 1572872 | tf_op jit(solution)/shard_map/ppermute | solution.py:254
  108.9 3.4 %collective-permute-start.9 = (bf16[64,32,128]{2,1,0:T(8,128)(2,1)}, bf16[64,32,128]{2,1,0:T(8,128)(2,1)S(1)}, u32[]{:S(2)}, u32[]{:S(2)}) collective-permute-start(bf16[64,32,128]{2,1,0:T(8,128)(2,1)} %get-tuple-element.32), channel_id=1, source_target_pairs={{0,3},{1,0},{2,1},{3,2},{4,7},{5,4},{6,5},{7,6},{8,11},{9,8},{10,9... | collective-permute-start | bytes 1572872 | tf_op jit(solution)/shard_map/ppermute | solution.py:254
  112.3 5.5 %all-to-all-done.1 = bf16[16,4,8,128]{3,2,1,0:T(8,128)(2,1)S(1)} async-done(((bf16[16,4,8,128]{3,2,1,0:T(8,128)(2,1)}), bf16[16,4,8,128]{3,2,1,0:T(8,128)(2,1)S(1)}, u32[]{:S(2)}, u32[]{:S(2)}) %all-to-all-start.1) | async-done | bytes 131104 | tf_op jit(solution)/shard_map/all_to_all | solution.py:264
  117.8 0.6 broadcast_in_dim.6
  118.5 4.3 %all-to-all-start.2 = ((f32[16,8,128]{2,1,0:T(8,128)}), f32[16,8,128]{2,1,0:T(8,128)S(1)}, u32[]{:S(2)}, u32[]{:S(2)}) async-start(f32[16,8,128]{2,1,0:T(8,128)} %bitcast.12), calls=%async_computation.2 | async-start | bytes 131072 | tf_op jit(solution)/shard_map/all_to_all | solution.py:264
  122.8 4.5 %collective-permute-start.11 = (bf16[64,32,128]{2,1,0:T(8,128)(2,1)}, bf16[64,32,128]{2,1,0:T(8,128)(2,1)S(1)}, u32[]{:S(2)}, u32[]{:S(2)}) collective-permute-start(bf16[64,32,128]{2,1,0:T(8,128)(2,1)} %get-tuple-element.31), channel_id=1, source_target_pairs={{0,3},{1,0},{2,1},{3,2},{4,7},{5,4},{6,5},{7,6},{8,11},{9,8},{10,9... | collective-permute-start | bytes 1572872 | tf_op jit(solution)/shard_map/ppermute | solution.py:254
  127.2 1.9 %collective-permute-start.7 = (bf16[64,32,128]{2,1,0:T(8,128)(2,1)}, bf16[64,32,128]{2,1,0:T(8,128)(2,1)S(1)}, u32[]{:S(2)}, u32[]{:S(2)}) collective-permute-start(bf16[64,32,128]{2,1,0:T(8,128)(2,1)} %get-tuple-element.32), channel_id=1, source_target_pairs={{0,1},{1,2},{2,3},{3,0},{4,5},{5,6},{6,7},{7,4},{8,9},{9,10},{10,1... | collective-permute-start | bytes 1572872 | tf_op jit(solution)/shard_map/ppermute | solution.py:254
  129.2 0.0 collective-permute-done.6.refs_1_
  129.2 2.2 %collective-permute-start.8 = (bf16[64,32,128]{2,1,0:T(8,128)(2,1)S(1)}, bf16[64,32,128]{2,1,0:T(8,128)(2,1)S(1)}, u32[]{:S(2)}, u32[]{:S(2)}) collective-permute-start(bf16[64,32,128]{2,1,0:T(8,128)(2,1)S(1)} %collective-permute-done.6.refs_1_), channel_id=1, source_target_pairs={{0,1},{1,2},{2,3},{3,0},{4,5},{5,6},{6,7},{7,4},{8,9},{9,10},{10,1... | collective-permute-start | bytes 1572872 | tf_op jit(solution)/shard_map/ppermute | solution.py:254
  131.3 0.0 collective-permute-done.9.refs_6_
  131.4 4.3 %collective-permute-start.10 = (bf16[64,32,128]{2,1,0:T(8,128)(2,1)S(1)}, bf16[64,32,128]{2,1,0:T(8,128)(2,1)S(1)}, u32[]{:S(2)}, u32[]{:S(2)}) collective-permute-start(bf16[64,32,128]{2,1,0:T(8,128)(2,1)S(1)} %collective-permute-done.9.refs_6_), channel_id=1, source_target_pairs={{0,3},{1,0},{2,1},{3,2},{4,7},{5,4},{6,5},{7,6},{8,11},{9,8},{10,9... | collective-permute-start | bytes 1572872 | tf_op jit(solution)/shard_map/ppermute | solution.py:254
  135.7 0.0 all-to-all-done.2
  135.7 0.7 broadcast_in_dim.7
  136.4 6.5 %all-to-all-start.3 = ((bf16[16,4,8,128]{3,2,1,0:T(8,128)(2,1)}), bf16[16,4,8,128]{3,2,1,0:T(8,128)(2,1)S(1)}, u32[]{:S(2)}, u32[]{:S(2)}) async-start(bf16[16,4,8,128]{3,2,1,0:T(8,128)(2,1)} %broadcast_in_dim.7), calls=%async_computation.3 | async-start | bytes 262144 | tf_op jit(solution)/shard_map/all_to_all | solution.py:264
  143.0 0.0 collective-permute-done.11.refs_5_
  143.0 0.0 collective-permute-done.7.refs_2_
  143.0 0.0 copy-start.6
  143.0 11.9 %all-to-all-done.3.refs_7_ = bf16[16,4,8,128]{3,2,1,0:T(8,128)(2,1)S(1)} async-done(((bf16[16,4,8,128]{3,2,1,0:T(8,128)(2,1)}), bf16[16,4,8,128]{3,2,1,0:T(8,128)(2,1)S(1)}, u32[]{:S(2)}, u32[]{:S(2)}) %all-to-all-start.3) | async-done | bytes 131104 | tf_op jit(solution)/shard_map/all_to_all | solution.py:264
  154.9 0.0 collective-permute-done.8.refs_3_
  154.9 0.0 collective-permute-done.10.refs_4_
  155.0 0.6 copy-done.9
  155.5 0.2 copy-done.7
  155.7 0.8 copy-done.8
  156.6 5.4 %theirs.1 = bf16[2,32,64,128]{3,2,1,0:T(8,128)(2,1)} custom-call(s32[2]{0:T(128)} %pad_add_fusion.at_ref, bf16[64,64,128]{2,1,0:T(8,128)(2,1)} %copy-done, bf16[64,32,128]{2,1,0:T(8,128)(2,1)} %copy-done.3, bf16[64,32,128]{2,1,0:T(8,128)(2,1)} %copy-done.6, bf16[64,32,128]{2,1,0:T(8,128)(2,1)} %copy-done.7, bf16[64,32,128]{2,1,0:T(8,128)(2,1)} %copy-done.8, ...), custom_call_target="tpu_custom_call" | custom-call | flops 536870912 | bytes 4194304 | tf_op jit(solution)/shard_map/theirs/pallas_call | solution.py:236
  162.0 6.1 %collective-permute-start.14 = (bf16[2,32,64,128]{3,2,1,0:T(8,128)(2,1)}, bf16[2,32,64,128]{3,2,1,0:T(8,128)(2,1)S(1)}, u32[]{:S(2)}, u32[]{:S(2)}) collective-permute-start(bf16[2,32,64,128]{3,2,1,0:T(8,128)(2,1)} %theirs.1), channel_id=1, source_target_pairs={{0,256},{256,0},{1,257},{257,1},{2,258},{258,2},{3,259},{259,3},{4... | collective-permute-start | bytes 3145736 | tf_op jit(solution)/shard_map/ppermute | solution.py:254
  168.1 3.1 %collective-permute-start.12 = (bf16[8,64,128]{2,1,0:T(8,128)(2,1)S(1)}, bf16[8,64,128]{2,1,0:T(8,128)(2,1)S(1)}, u32[]{:S(2)}, u32[]{:S(2)}) collective-permute-start(bf16[8,64,128]{2,1,0:T(8,128)(2,1)S(1)} %copy-done.18), channel_id=1, source_target_pairs={{0,4},{4,8},{8,12},{12,16},{16,20},{20,24},{24,28},{28,32},{32,36}... | collective-permute-start | bytes 393224 | tf_op jit(solution)/shard_map/ppermute | solution.py:260
  171.2 5.8 %collective-permute-start.13 = (bf16[8,64,128]{2,1,0:T(8,128)(2,1)S(1)}, bf16[8,64,128]{2,1,0:T(8,128)(2,1)S(1)}, u32[]{:S(2)}, u32[]{:S(2)}) collective-permute-start(bf16[8,64,128]{2,1,0:T(8,128)(2,1)S(1)} %copy-done.17), channel_id=1, source_target_pairs={{4,0},{8,4},{12,8},{16,12},{20,16},{24,20},{28,24},{32,28},{36,32}... | collective-permute-start | bytes 393224 | tf_op jit(solution)/shard_map/ppermute | solution.py:260
  177.0 0.7 collective-permute-done.12.refs_10_
  177.7 1.2 collective-permute-done.13.refs_11_
  178.9 0.6 copy-done.15
  179.5 6.1 %mine.1 = (f32[32,64,128]{2,1,0:T(8,128)}, f32[32,64,128]{2,1,0:T(8,128)}) custom-call(s32[2]{0:T(128)} %pad_add_fusion.at_ref, bf16[64,64,128]{2,1,0:T(8,128)(2,1)} %copy-done, bf16[64,32,128]{2,1,0:T(8,128)(2,1)} %copy-done.3, bf16[64,32,128]{2,1,0:T(8,128)(2,1)} %copy-done.6, bf16[64,32,128]{2,1,0:T(8,128)(2,1)} %copy-done.7, ...), custom_call_target="tpu_custom_call" | custom-call | flops 536870912 | bytes 4194304 | tf_op jit(solution)/shard_map/mine/pallas_call | solution.py:236
  185.7 0.0 collective-permute-done.14
  185.7 2.9 %fusion = (bf16[32,64,128]{2,1,0:T(8,128)(2,1)}, bf16[32,64,128]{2,1,0:T(8,128)(2,1)}) fusion(f32[32,64,128]{2,1,0:T(8,128)} %get-tuple-element.39, bf16[2,32,64,128]{3,2,1,0:T(8,128)(2,1)S(1)} %collective-permute-done.14, f32[32,64,128]{2,1,0:T(8,128)} %get-tuple-element.38), kind=kLoop, calls=%fused_computation.2 | loop fusion | flops 1572864 | bytes 4194304 | tf_op jit(solution)/shard_map/convert_element_type | solution.py:308
  (27 shorter events, 0.1 us)
Async XLA Ops:
  0.6 21.8 %copy-start.2 = (bf16[2048,128]{1,0:T(8,128)(2,1)S(1)}, bf16[2048,128]{1,0:T(8,128)(2,1)}, u32[]{:S(2)}) copy-start(bf16[2048,128]{1,0:T(8,128)(2,1)} %param.6) | copy-start | bytes 1572868
  0.6 41.8 %copy-start.16 = (s32[32,8]{0,1:T(8,128)S(1)}, s32[32,8]{0,1:T(8,128)}, u32[]{:S(2)}) copy-start(s32[32,8]{0,1:T(8,128)} %param.8) | copy-start | bytes 3076
  3.3 84.8 %all-to-all-start = ((bf16[64,64,128]{2,1,0:T(8,128)(2,1)}), bf16[64,64,128]{2,1,0:T(8,128)(2,1)S(1)}, u32[]{:S(2)}, u32[]{:S(2)}) async-start(bf16[64,64,128]{2,1,0:T(8,128)(2,1)} %pack.1), calls=%async_computation | async-start | bytes 2097152 | tf_op jit(solution)/shard_map/all_to_all | solution.py:264
  22.4 56.7 %collective-permute-start.2 = (bf16[2048,128]{1,0:T(8,128)(2,1)S(1)}, bf16[2048,128]{1,0:T(8,128)(2,1)}, u32[]{:S(2)}, u32[]{:S(2)}) collective-permute-start(bf16[2048,128]{1,0:T(8,128)(2,1)S(1)} %copy-done.2), channel_id=1, source_target_pairs={{0,3},{1,0},{2,1},{3,2},{4,7},{5,4},{6,5},{7,6},{8,11},{9,8},{10,9... | collective-permute-start | bytes 1572872 | tf_op jit(solution)/shard_map/ppermute | solution.py:254
  27.0 52.1 %collective-permute-start.1 = (bf16[2048,128]{1,0:T(8,128)(2,1)S(1)}, bf16[2048,128]{1,0:T(8,128)(2,1)S(1)}, u32[]{:S(2)}, u32[]{:S(2)}) collective-permute-start(bf16[2048,128]{1,0:T(8,128)(2,1)S(1)} %copy-done.2), channel_id=1, source_target_pairs={{0,2},{1,3},{2,0},{3,1},{4,6},{5,7},{6,4},{7,5},{8,10},{9,11},{10,... | collective-permute-start | bytes 1572872 | tf_op jit(solution)/shard_map/ppermute | solution.py:254
  29.3 49.8 %collective-permute-start = (bf16[2048,128]{1,0:T(8,128)(2,1)S(1)}, bf16[2048,128]{1,0:T(8,128)(2,1)S(1)}, u32[]{:S(2)}, u32[]{:S(2)}) collective-permute-start(bf16[2048,128]{1,0:T(8,128)(2,1)S(1)} %copy-done.2), channel_id=1, source_target_pairs={{0,1},{1,2},{2,3},{3,0},{4,5},{5,6},{6,7},{7,4},{8,9},{9,10},{10,1... | collective-permute-start | bytes 1572872 | tf_op jit(solution)/shard_map/ppermute | solution.py:254
  31.9 40.6 %collective-permute-start.3 = (bf16[8,64,128]{2,1,0:T(8,128)(2,1)S(1)}, bf16[8,64,128]{2,1,0:T(8,128)(2,1)S(1)}, u32[]{:S(2)}, u32[]{:S(2)}) collective-permute-start(bf16[8,64,128]{2,1,0:T(8,128)(2,1)S(1)} %bitcast.36), channel_id=1, source_target_pairs={{0,4},{4,8},{8,12},{12,16},{16,20},{20,24},{24,28},{28,32},{32,36}... | collective-permute-start | bytes 393224 | tf_op jit(solution)/shard_map/ppermute | solution.py:260
  34.9 37.7 %collective-permute-start.4 = (bf16[8,64,128]{2,1,0:T(8,128)(2,1)S(1)}, bf16[8,64,128]{2,1,0:T(8,128)(2,1)S(1)}, u32[]{:S(2)}, u32[]{:S(2)}) collective-permute-start(bf16[8,64,128]{2,1,0:T(8,128)(2,1)S(1)} %bitcast.35), channel_id=1, source_target_pairs={{4,0},{8,4},{12,8},{16,12},{20,16},{24,20},{28,24},{32,28},{36,32}... | collective-permute-start | bytes 393224 | tf_op jit(solution)/shard_map/ppermute | solution.py:260
  72.5 0.7 copy-start.12
  72.5 0.7 copy-start.13
  79.1 0.8 copy-start.10
  79.1 0.9 copy-start.11
  81.9 6.2 %copy-start.1 = (bf16[4,2048,128]{2,1,0:T(8,128)(2,1)}, bf16[4,2048,128]{2,1,0:T(8,128)(2,1)S(1)}, u32[]{:S(2)}) copy-start(bf16[4,2048,128]{2,1,0:T(8,128)(2,1)S(1)} %pad_maximum_fusion.own_ref) | copy-start | bytes 6291460
  81.9 6.2 %collective-permute-start.5 = (bf16[4,2048,128]{2,1,0:T(8,128)(2,1)S(1)}, bf16[4,2048,128]{2,1,0:T(8,128)(2,1)}, u32[]{:S(2)}, u32[]{:S(2)}) collective-permute-start(bf16[4,2048,128]{2,1,0:T(8,128)(2,1)S(1)} %pad_maximum_fusion.own_ref), channel_id=1, source_target_pairs={{0,256},{256,0},{1,257},{257,1},{2,258},{258,2},{3,259},{259,3},{4... | collective-permute-start | bytes 6291464 | tf_op jit(solution)/shard_map/ppermute | solution.py:254
  88.1 1.0 copy-start
  93.4 24.4 %all-to-all-start.1 = ((bf16[16,4,8,128]{3,2,1,0:T(8,128)(2,1)}), bf16[16,4,8,128]{3,2,1,0:T(8,128)(2,1)S(1)}, u32[]{:S(2)}, u32[]{:S(2)}) async-start(bf16[16,4,8,128]{3,2,1,0:T(8,128)(2,1)} %get-tuple-element.33), calls=%async_computation.1 | async-start | bytes 262144 | tf_op jit(solution)/shard_map/all_to_all | solution.py:264
  105.7 23.5 %collective-permute-start.6 = (bf16[64,32,128]{2,1,0:T(8,128)(2,1)}, bf16[64,32,128]{2,1,0:T(8,128)(2,1)S(1)}, u32[]{:S(2)}, u32[]{:S(2)}) collective-permute-start(bf16[64,32,128]{2,1,0:T(8,128)(2,1)} %get-tuple-element.31), channel_id=1, source_target_pairs={{0,1},{1,2},{2,3},{3,0},{4,5},{5,6},{6,7},{7,4},{8,9},{9,10},{10,1... | collective-permute-start | bytes 1572872 | tf_op jit(solution)/shard_map/ppermute | solution.py:254
  108.9 22.4 %collective-permute-start.9 = (bf16[64,32,128]{2,1,0:T(8,128)(2,1)}, bf16[64,32,128]{2,1,0:T(8,128)(2,1)S(1)}, u32[]{:S(2)}, u32[]{:S(2)}) collective-permute-start(bf16[64,32,128]{2,1,0:T(8,128)(2,1)} %get-tuple-element.32), channel_id=1, source_target_pairs={{0,3},{1,0},{2,1},{3,2},{4,7},{5,4},{6,5},{7,6},{8,11},{9,8},{10,9... | collective-permute-start | bytes 1572872 | tf_op jit(solution)/shard_map/ppermute | solution.py:254
  118.5 17.3 %all-to-all-start.2 = ((f32[16,8,128]{2,1,0:T(8,128)}), f32[16,8,128]{2,1,0:T(8,128)S(1)}, u32[]{:S(2)}, u32[]{:S(2)}) async-start(f32[16,8,128]{2,1,0:T(8,128)} %bitcast.12), calls=%async_computation.2 | async-start | bytes 131072 | tf_op jit(solution)/shard_map/all_to_all | solution.py:264
  122.8 20.2 %collective-permute-start.11 = (bf16[64,32,128]{2,1,0:T(8,128)(2,1)}, bf16[64,32,128]{2,1,0:T(8,128)(2,1)S(1)}, u32[]{:S(2)}, u32[]{:S(2)}) collective-permute-start(bf16[64,32,128]{2,1,0:T(8,128)(2,1)} %get-tuple-element.31), channel_id=1, source_target_pairs={{0,3},{1,0},{2,1},{3,2},{4,7},{5,4},{6,5},{7,6},{8,11},{9,8},{10,9... | collective-permute-start | bytes 1572872 | tf_op jit(solution)/shard_map/ppermute | solution.py:254
  127.2 15.7 %collective-permute-start.7 = (bf16[64,32,128]{2,1,0:T(8,128)(2,1)}, bf16[64,32,128]{2,1,0:T(8,128)(2,1)S(1)}, u32[]{:S(2)}, u32[]{:S(2)}) collective-permute-start(bf16[64,32,128]{2,1,0:T(8,128)(2,1)} %get-tuple-element.32), channel_id=1, source_target_pairs={{0,1},{1,2},{2,3},{3,0},{4,5},{5,6},{6,7},{7,4},{8,9},{9,10},{10,1... | collective-permute-start | bytes 1572872 | tf_op jit(solution)/shard_map/ppermute | solution.py:254
  129.2 25.7 %copy-start.3 = (bf16[64,32,128]{2,1,0:T(8,128)(2,1)}, bf16[64,32,128]{2,1,0:T(8,128)(2,1)S(1)}, u32[]{:S(2)}) copy-start(bf16[64,32,128]{2,1,0:T(8,128)(2,1)S(1)} %collective-permute-done.6.refs_1_) | copy-start | bytes 1572868
  129.2 25.7 %collective-permute-start.8 = (bf16[64,32,128]{2,1,0:T(8,128)(2,1)S(1)}, bf16[64,32,128]{2,1,0:T(8,128)(2,1)S(1)}, u32[]{:S(2)}, u32[]{:S(2)}) collective-permute-start(bf16[64,32,128]{2,1,0:T(8,128)(2,1)S(1)} %collective-permute-done.6.refs_1_), channel_id=1, source_target_pairs={{0,1},{1,2},{2,3},{3,0},{4,5},{5,6},{6,7},{7,4},{8,9},{9,10},{10,1... | collective-permute-start | bytes 1572872 | tf_op jit(solution)/shard_map/ppermute | solution.py:254
  131.4 23.6 %copy-start.4 = (bf16[64,32,128]{2,1,0:T(8,128)(2,1)}, bf16[64,32,128]{2,1,0:T(8,128)(2,1)S(1)}, u32[]{:S(2)}) copy-start(bf16[64,32,128]{2,1,0:T(8,128)(2,1)S(1)} %collective-permute-done.9.refs_6_) | copy-start | bytes 1572868
  131.4 23.5 %collective-permute-start.10 = (bf16[64,32,128]{2,1,0:T(8,128)(2,1)S(1)}, bf16[64,32,128]{2,1,0:T(8,128)(2,1)S(1)}, u32[]{:S(2)}, u32[]{:S(2)}) collective-permute-start(bf16[64,32,128]{2,1,0:T(8,128)(2,1)S(1)} %collective-permute-done.9.refs_6_), channel_id=1, source_target_pairs={{0,3},{1,0},{2,1},{3,2},{4,7},{5,4},{6,5},{7,6},{8,11},{9,8},{10,9... | collective-permute-start | bytes 1572872 | tf_op jit(solution)/shard_map/ppermute | solution.py:254
  136.4 18.5 %all-to-all-start.3 = ((bf16[16,4,8,128]{3,2,1,0:T(8,128)(2,1)}), bf16[16,4,8,128]{3,2,1,0:T(8,128)(2,1)S(1)}, u32[]{:S(2)}, u32[]{:S(2)}) async-start(bf16[16,4,8,128]{3,2,1,0:T(8,128)(2,1)} %broadcast_in_dim.7), calls=%async_computation.3 | async-start | bytes 262144 | tf_op jit(solution)/shard_map/all_to_all | solution.py:264
  142.9 25.1 %copy-start.18 = (bf16[8,64,128]{2,1,0:T(8,128)(2,1)S(1)}, bf16[8,64,128]{2,1,0:T(8,128)(2,1)}, u32[]{:S(2)}) copy-start(bf16[8,64,128]{2,1,0:T(8,128)(2,1)} %get-tuple-element.36) | copy-start | bytes 393220
  142.9 28.2 %copy-start.17 = (bf16[8,64,128]{2,1,0:T(8,128)(2,1)S(1)}, bf16[8,64,128]{2,1,0:T(8,128)(2,1)}, u32[]{:S(2)}) copy-start(bf16[8,64,128]{2,1,0:T(8,128)(2,1)} %get-tuple-element.37) | copy-start | bytes 393220
  143.0 12.0 %copy-start.5 = (bf16[64,32,128]{2,1,0:T(8,128)(2,1)}, bf16[64,32,128]{2,1,0:T(8,128)(2,1)S(1)}, u32[]{:S(2)}) copy-start(bf16[64,32,128]{2,1,0:T(8,128)(2,1)S(1)} %collective-permute-done.11.refs_5_) | copy-start | bytes 1572868
  143.0 12.0 %copy-start.6 = (bf16[64,32,128]{2,1,0:T(8,128)(2,1)}, bf16[64,32,128]{2,1,0:T(8,128)(2,1)S(1)}, u32[]{:S(2)}) copy-start(bf16[64,32,128]{2,1,0:T(8,128)(2,1)S(1)} %collective-permute-done.7.refs_2_) | copy-start | bytes 1572868
  154.9 0.6 copy-start.9
  154.9 0.8 copy-start.7
  155.7 0.8 copy-start.8
  162.0 23.7 %collective-permute-start.14 = (bf16[2,32,64,128]{3,2,1,0:T(8,128)(2,1)}, bf16[2,32,64,128]{3,2,1,0:T(8,128)(2,1)S(1)}, u32[]{:S(2)}, u32[]{:S(2)}) collective-permute-start(bf16[2,32,64,128]{3,2,1,0:T(8,128)(2,1)} %theirs.1), channel_id=1, source_target_pairs={{0,256},{256,0},{1,257},{257,1},{2,258},{258,2},{3,259},{259,3},{4... | collective-permute-start | bytes 3145736 | tf_op jit(solution)/shard_map/ppermute | solution.py:254
  168.1 9.6 %collective-permute-start.12 = (bf16[8,64,128]{2,1,0:T(8,128)(2,1)S(1)}, bf16[8,64,128]{2,1,0:T(8,128)(2,1)S(1)}, u32[]{:S(2)}, u32[]{:S(2)}) collective-permute-start(bf16[8,64,128]{2,1,0:T(8,128)(2,1)S(1)} %copy-done.18), channel_id=1, source_target_pairs={{0,4},{4,8},{8,12},{12,16},{16,20},{20,24},{24,28},{28,32},{32,36}... | collective-permute-start | bytes 393224 | tf_op jit(solution)/shard_map/ppermute | solution.py:260
  171.2 7.7 %collective-permute-start.13 = (bf16[8,64,128]{2,1,0:T(8,128)(2,1)S(1)}, bf16[8,64,128]{2,1,0:T(8,128)(2,1)S(1)}, u32[]{:S(2)}, u32[]{:S(2)}) collective-permute-start(bf16[8,64,128]{2,1,0:T(8,128)(2,1)S(1)} %copy-done.17), channel_id=1, source_target_pairs={{4,0},{8,4},{12,8},{16,12},{20,16},{24,20},{28,24},{32,28},{36,32}... | collective-permute-start | bytes 393224 | tf_op jit(solution)/shard_map/ppermute | solution.py:260
  177.7 1.2 copy-start.14
  178.9 0.7 copy-start.15

commit v4 on v3

--- a/solution.py
+++ b/solution.py
@@ -26,6 +26,10 @@
 
 def cost(flops, moved):
     return pl.CostEstimate(flops=flops, bytes_accessed=moved, transcendentals=0)
+
+
+def grant(mib, **more):
+    return pltpu.CompilerParams(vmem_limit_bytes=mib << 20, **more)
 
 
 def swapped_halves(x):
@@ -57,6 +61,7 @@
         out_shape=(out,) * CHUNKS,
         in_specs=[whole(SMEM), whole(VMEM), whole(VMEM)],
         out_specs=(whole(VMEM),) * CHUNKS,
+        compiler_params=grant(6),
         cost_estimate=cost(0, 8 * ranks * width),
         name="pack",
     )(order_map, left, right)
@@ -125,7 +130,7 @@
             pltpu.VMEM((count + 2 * HB, BS, width), BF16),
             pltpu.VMEM((count + 2 * HB, BS, width), F32),
         ],
-        compiler_params=pltpu.CompilerParams(dimension_semantics=("arbitrary",)),
+        compiler_params=grant(12, dimension_semantics=("arbitrary",)),
         cost_estimate=cost(4 * count * BS * BS * NB * width, 6 << 20),
         name="sparse",
     )(local_cols, couplings, blocks, low, high)
@@ -167,6 +172,7 @@
         in_specs=[whole(SMEM)] + [whole(VMEM)] * 3,
         out_specs=(whole(VMEM),) * 3,
         scratch_shapes=[pltpu.VMEM((2, 2 * ranks, rows), BF16)],
+        compiler_params=grant(14),
         cost_estimate=cost(8 * ranks * rows * parts * LANES, 6 << 20),
         name="partials",
     )(at, gens, own, other)
@@ -243,7 +249,7 @@
             scratch_shapes=[pltpu.VMEM((2 * LANES, depth), BF16)],
         ),
         out_shape=out_shape,
-        compiler_params=pltpu.CompilerParams(dimension_semantics=("arbitrary",)),
+        compiler_params=grant(10, dimension_semantics=("arbitrary",)),
         cost_estimate=cost(4 * count * LANES * depth * LANES, 4 << 20),
         name="mine" if mine else "theirs",
     )(at, *gens, w, *added)

time: 190 us -> 184 us (0.968)
  Pallas kernels: 24.4 us -> 16.5 us
  local copies, waits for them, and re-layouts: 6.32 us -> 10.2 us
  other arithmetic: 5.92 us -> 3.19 us
    unnamed x39 -> x29, local copies, waits for them, and re-layouts: 5 us -> 8.89 us
    pallas_call x2, Pallas kernels: 11.5 us -> 7.76 us  [low_rank(): pl.pallas_call(functools.partial(low_rank_kernel, mine, len(gens)), grid_...]
    pallas_call x1, Pallas kernels: 5.88 us -> 3.63 us  [sparse(): pl.pallas_call(sparse_kernel, grid=(count // per,), out_shape=(jax.ShapeD...]
  transfers between devices with their start and end apart: 19 -> 19, of which waited for: 6 -> 6; matrix products, arithmetic and copies ran while one was open for 2% -> 2% of each run, Pallas kernels for 6% -> 4%
where the time goes in v4:
time: 184 us; the launch traced here: 183 us
  starting transfers between devices  98.5 us (54%)
  waiting for transfers between devices  53.6 us (29%)
  Pallas kernels  16.5 us (9%)
  local copies, waits for them, and re-layouts  10.2 us (6%)
  other arithmetic  3.19 us (2%)
    all_to_all x4, starting transfers between devices, spread_out(): return lax.all_to_all(x, axis, split_axis=0, concat_axis=0, tiled=True)  42.2 us
    ppermute x11, starting transfers between devices, around(): return lax.ppermute(x, axis, [(i, (i + by) % count) for i in range(count)])  36.9 us
    ppermute x4, waiting for transfers between devices, along_front(): return lax.ppermute(x, FRONT, pairs)  32 us
    ppermute x4, starting transfers between devices, along_front(): return lax.ppermute(x, FRONT, pairs)  19.3 us
    all_to_all x4, waiting for transfers between devices, spread_out(): return lax.all_to_all(x, axis, split_axis=0, concat_axis=0, tiled=True)  17.5 us
    unnamed x29, local copies, waits for them, and re-layouts  8.89 us
    pallas_call x2, Pallas kernels, low_rank(): pl.pallas_call(functools.partial(low_rank_kernel, mine, len(gens)), grid_...  7.76 us
    ppermute x11, waiting for transfers between devices, around(): return lax.ppermute(x, axis, [(i, (i + by) % count) for i in range(count)])  4.2 us
  transfers between devices with their start and end apart: 19, of which 6 were waited for; matrix products, arithmetic and copies ran while one was open for 2% of the time, Pallas kernels for 4%

profile of v4, /device:TPU:1, one launch (start us, length us, event | category | flops | bytes accessed | tf_op | source)
XLA Modules:
  0.0 183.0 jit_solution(15184168578464284739)
XLA Ops:
  0.6 0.0 copy-start.6
  0.6 1.0 copy-done.6
  1.7 1.0 copy-done.7
  2.7 0.7 copy-done.8
  3.4 2.0 %pack.1 = bf16[64,64,128]{2,1,0:T(8,128)(2,1)} custom-call(s32[64]{0:T(128)S(1)} %bitcast.30, bf16[64,4096]{1,0:T(8,128)(2,1)S(1)} %bitcast.28, bf16[64,4096]{1,0:T(8,128)(2,1)S(1)} %bitcast.29), custom_call_target="tpu_custom_call" | custom-call | bytes 2097152 | tf_op jit(solution)/shard_map/pack/pallas_call | solution.py:59
  5.3 19.1 %all-to-all-start = ((bf16[64,64,128]{2,1,0:T(8,128)(2,1)}), bf16[64,64,128]{2,1,0:T(8,128)(2,1)S(1)}, u32[]{:S(2)}, u32[]{:S(2)}) async-start(bf16[64,64,128]{2,1,0:T(8,128)(2,1)} %pack.1), calls=%async_computation | async-start | bytes 2097152 | tf_op jit(solution)/shard_map/all_to_all | solution.py:270
  24.5 0.0 copy-done
  24.5 4.6 %collective-permute-start.2 = (bf16[2048,128]{1,0:T(8,128)(2,1)S(1)}, bf16[2048,128]{1,0:T(8,128)(2,1)}, u32[]{:S(2)}, u32[]{:S(2)}) collective-permute-start(bf16[2048,128]{1,0:T(8,128)(2,1)S(1)} %copy-done), channel_id=1, source_target_pairs={{0,3},{1,0},{2,1},{3,2},{4,7},{5,4},{6,5},{7,6},{8,11},{9,8},{10,9... | collective-permute-start | bytes 1572872 | tf_op jit(solution)/shard_map/ppermute | solution.py:260
  29.1 2.3 %collective-permute-start.1 = (bf16[2048,128]{1,0:T(8,128)(2,1)S(1)}, bf16[2048,128]{1,0:T(8,128)(2,1)S(1)}, u32[]{:S(2)}, u32[]{:S(2)}) collective-permute-start(bf16[2048,128]{1,0:T(8,128)(2,1)S(1)} %copy-done), channel_id=1, source_target_pairs={{0,2},{1,3},{2,0},{3,1},{4,6},{5,7},{6,4},{7,5},{8,10},{9,11},{10,... | collective-permute-start | bytes 1572872 | tf_op jit(solution)/shard_map/ppermute | solution.py:260
  31.4 2.6 %collective-permute-start = (bf16[2048,128]{1,0:T(8,128)(2,1)S(1)}, bf16[2048,128]{1,0:T(8,128)(2,1)S(1)}, u32[]{:S(2)}, u32[]{:S(2)}) collective-permute-start(bf16[2048,128]{1,0:T(8,128)(2,1)S(1)} %copy-done), channel_id=1, source_target_pairs={{0,1},{1,2},{2,3},{3,0},{4,5},{5,6},{6,7},{7,4},{8,9},{9,10},{10,1... | collective-permute-start | bytes 1572872 | tf_op jit(solution)/shard_map/ppermute | solution.py:260
  34.0 2.9 %collective-permute-start.3 = (bf16[8,64,128]{2,1,0:T(8,128)(2,1)S(1)}, bf16[8,64,128]{2,1,0:T(8,128)(2,1)S(1)}, u32[]{:S(2)}, u32[]{:S(2)}) collective-permute-start(bf16[8,64,128]{2,1,0:T(8,128)(2,1)S(1)} %bitcast.37), channel_id=1, source_target_pairs={{0,4},{4,8},{8,12},{12,16},{16,20},{20,24},{24,28},{28,32},{32,36}... | collective-permute-start | bytes 393224 | tf_op jit(solution)/shard_map/ppermute | solution.py:266
  36.9 7.5 %collective-permute-start.4 = (bf16[8,64,128]{2,1,0:T(8,128)(2,1)S(1)}, bf16[8,64,128]{2,1,0:T(8,128)(2,1)S(1)}, u32[]{:S(2)}, u32[]{:S(2)}) collective-permute-start(bf16[8,64,128]{2,1,0:T(8,128)(2,1)S(1)} %bitcast.36), channel_id=1, source_target_pairs={{4,0},{8,4},{12,8},{16,12},{20,16},{24,20},{28,24},{32,28},{36,32}... | collective-permute-start | bytes 393224 | tf_op jit(solution)/shard_map/ppermute | solution.py:266
  44.5 0.0 copy-done.13
  44.5 0.1 copy.10
  44.6 30.0 %collective-permute-done.3.low_ref = bf16[8,64,128]{2,1,0:T(8,128)(2,1)S(1)} collective-permute-done((bf16[8,64,128]{2,1,0:T(8,128)(2,1)S(1)}, bf16[8,64,128]{2,1,0:T(8,128)(2,1)S(1)}, u32[]{:S(2)}, u32[]{:S(2)}) %collective-permute-start.3) | collective-permute-done | bytes 131104 | tf_op jit(solution)/shard_map/ppermute | solution.py:266
  74.6 0.0 collective-permute-done.4.high_ref
  74.6 1.6 copy-done.1
  76.2 3.6 %sparse.1 = (f32[32,64,128]{2,1,0:T(8,128)S(1)}, f32[32,64,128]{2,1,0:T(8,128)S(1)}, bf16[8,64,128]{2,1,0:T(8,128)(2,1)S(1)}, bf16[8,64,128]{2,1,0:T(8,128)(2,1)S(1)}) custom-call(s32[32,8]{1,0:T(8,128)S(1)} %subtract_add_fusion.cols_ref, bf16[32,64,512]{2,1,0:T(8,128)(2,1)S(1)} %copy-done.1, bf16[32,64,128]{2,1,0:T(8,128)(2,1)S(1)} %bitcast.27, ...), custom_call_target="tpu_custom_call" | custom-call | flops 536870912 | bytes 6291456 | tf_op jit(solution)/shard_map/sparse/pallas_call | solution.py:107
  79.8 0.0 copy-start.2
  79.8 1.0 copy-done.2
  80.8 1.0 copy-done.4
  81.8 0.0 collective-permute-done.2
  81.8 0.0 collective-permute-done.1
  81.8 0.0 collective-permute-done
  81.8 0.0 copy-start.12
  81.8 0.8 copy-done.11
  82.6 0.2 copy-done.12
  82.8 1.8 pad_maximum_fusion.own_ref
  84.5 1.9 %collective-permute-start.5 = (bf16[4,2048,128]{2,1,0:T(8,128)(2,1)S(1)}, bf16[4,2048,128]{2,1,0:T(8,128)(2,1)}, u32[]{:S(2)}, u32[]{:S(2)}) collective-permute-start(bf16[4,2048,128]{2,1,0:T(8,128)(2,1)S(1)} %pad_maximum_fusion.own_ref), channel_id=1, source_target_pairs={{0,256},{256,0},{1,257},{257,1},{2,258},{258,2},{3,259},{259,3},{4... | collective-permute-start | bytes 6291464 | tf_op jit(solution)/shard_map/ppermute | solution.py:260
  86.5 0.1 pad_add_fusion.at_ref
  86.5 4.2 %collective-permute-done.5.other_ref = bf16[4,2048,128]{2,1,0:T(8,128)(2,1)} collective-permute-done((bf16[4,2048,128]{2,1,0:T(8,128)(2,1)S(1)}, bf16[4,2048,128]{2,1,0:T(8,128)(2,1)}, u32[]{:S(2)}, u32[]{:S(2)}) %collective-permute-start.5) | collective-permute-done | bytes 2097184 | tf_op jit(solution)/shard_map/ppermute | solution.py:260
  90.7 0.0 all-to-all-done.gen_ref.refs_0_
  90.7 3.2 %partials.1 = (bf16[16,4,8,128]{3,2,1,0:T(8,128)(2,1)}, bf16[64,32,128]{2,1,0:T(8,128)(2,1)S(1)}, bf16[64,32,128]{2,1,0:T(8,128)(2,1)S(1)}) custom-call(s32[2]{0:T(128)S(1)} %pad_add_fusion.at_ref, bf16[64,64,128]{2,1,0:T(8,128)(2,1)S(1)} %all-to-all-done.gen_ref.refs_0_, bf16[4,2048,128]{2,1,0:T(8,128)(2,1)S(1)} %pad_maximum_fusion.own_ref, ...), custom_call_target="tpu_custom_call" | custom-call | flops 536870912 | bytes 6291456 | tf_op jit(solution)/shard_map/partials/pallas_call | solution.py:169
  93.9 0.8 copy-done.9
  94.7 0.8 copy-done.10
  95.5 12.3 %all-to-all-start.1 = ((bf16[16,4,8,128]{3,2,1,0:T(8,128)(2,1)}), bf16[16,4,8,128]{3,2,1,0:T(8,128)(2,1)S(1)}, u32[]{:S(2)}, u32[]{:S(2)}) async-start(bf16[16,4,8,128]{3,2,1,0:T(8,128)(2,1)} %get-tuple-element.33), calls=%async_computation.1 | async-start | bytes 262144 | tf_op jit(solution)/shard_map/all_to_all | solution.py:270
  107.8 3.2 %collective-permute-start.6 = (bf16[64,32,128]{2,1,0:T(8,128)(2,1)}, bf16[64,32,128]{2,1,0:T(8,128)(2,1)S(1)}, u32[]{:S(2)}, u32[]{:S(2)}) collective-permute-start(bf16[64,32,128]{2,1,0:T(8,128)(2,1)} %copy-done.10), channel_id=1, source_target_pairs={{0,1},{1,2},{2,3},{3,0},{4,5},{5,6},{6,7},{7,4},{8,9},{9,10},{10,1... | collective-permute-start | bytes 1572872 | tf_op jit(solution)/shard_map/ppermute | solution.py:260
  111.1 3.4 %collective-permute-start.9 = (bf16[64,32,128]{2,1,0:T(8,128)(2,1)}, bf16[64,32,128]{2,1,0:T(8,128)(2,1)S(1)}, u32[]{:S(2)}, u32[]{:S(2)}) collective-permute-start(bf16[64,32,128]{2,1,0:T(8,128)(2,1)} %copy-done.9), channel_id=1, source_target_pairs={{0,3},{1,0},{2,1},{3,2},{4,7},{5,4},{6,5},{7,6},{8,11},{9,8},{10,9... | collective-permute-start | bytes 1572872 | tf_op jit(solution)/shard_map/ppermute | solution.py:260
  114.4 5.5 %all-to-all-done.1 = bf16[16,4,8,128]{3,2,1,0:T(8,128)(2,1)S(1)} async-done(((bf16[16,4,8,128]{3,2,1,0:T(8,128)(2,1)}), bf16[16,4,8,128]{3,2,1,0:T(8,128)(2,1)S(1)}, u32[]{:S(2)}, u32[]{:S(2)}) %all-to-all-start.1) | async-done | bytes 131104 | tf_op jit(solution)/shard_map/all_to_all | solution.py:270
  120.0 0.6 broadcast_in_dim.6
  120.6 4.3 %all-to-all-start.2 = ((f32[16,8,128]{2,1,0:T(8,128)}), f32[16,8,128]{2,1,0:T(8,128)S(1)}, u32[]{:S(2)}, u32[]{:S(2)}) async-start(f32[16,8,128]{2,1,0:T(8,128)} %bitcast.12), calls=%async_computation.2 | async-start | bytes 131072 | tf_op jit(solution)/shard_map/all_to_all | solution.py:270
  124.9 4.5 %collective-permute-start.11 = (bf16[64,32,128]{2,1,0:T(8,128)(2,1)}, bf16[64,32,128]{2,1,0:T(8,128)(2,1)S(1)}, u32[]{:S(2)}, u32[]{:S(2)}) collective-permute-start(bf16[64,32,128]{2,1,0:T(8,128)(2,1)} %copy-done.10), channel_id=1, source_target_pairs={{0,3},{1,0},{2,1},{3,2},{4,7},{5,4},{6,5},{7,6},{8,11},{9,8},{10,9... | collective-permute-start | bytes 1572872 | tf_op jit(solution)/shard_map/ppermute | solution.py:260
  129.4 1.9 %collective-permute-start.7 = (bf16[64,32,128]{2,1,0:T(8,128)(2,1)}, bf16[64,32,128]{2,1,0:T(8,128)(2,1)S(1)}, u32[]{:S(2)}, u32[]{:S(2)}) collective-permute-start(bf16[64,32,128]{2,1,0:T(8,128)(2,1)} %copy-done.9), channel_id=1, source_target_pairs={{0,1},{1,2},{2,3},{3,0},{4,5},{5,6},{6,7},{7,4},{8,9},{9,10},{10,1... | collective-permute-start | bytes 1572872 | tf_op jit(solution)/shard_map/ppermute | solution.py:260
  131.3 0.0 collective-permute-done.6.refs_1_
  131.3 2.2 %collective-permute-start.8 = (bf16[64,32,128]{2,1,0:T(8,128)(2,1)S(1)}, bf16[64,32,128]{2,1,0:T(8,128)(2,1)}, u32[]{:S(2)}, u32[]{:S(2)}) collective-permute-start(bf16[64,32,128]{2,1,0:T(8,128)(2,1)S(1)} %collective-permute-done.6.refs_1_), channel_id=1, source_target_pairs={{0,1},{1,2},{2,3},{3,0},{4,5},{5,6},{6,7},{7,4},{8,9},{9,10},{10,1... | collective-permute-start | bytes 1572872 | tf_op jit(solution)/shard_map/ppermute | solution.py:260
  133.5 0.0 collective-permute-done.9.refs_6_
  133.5 4.3 %collective-permute-start.10 = (bf16[64,32,128]{2,1,0:T(8,128)(2,1)S(1)}, bf16[64,32,128]{2,1,0:T(8,128)(2,1)}, u32[]{:S(2)}, u32[]{:S(2)}) collective-permute-start(bf16[64,32,128]{2,1,0:T(8,128)(2,1)S(1)} %collective-permute-done.9.refs_6_), channel_id=1, source_target_pairs={{0,3},{1,0},{2,1},{3,2},{4,7},{5,4},{6,5},{7,6},{8,11},{9,8},{10,9... | collective-permute-start | bytes 1572872 | tf_op jit(solution)/shard_map/ppermute | solution.py:260
  137.8 0.0 all-to-all-done.2
  137.9 0.7 broadcast_in_dim.7
  138.5 6.5 %all-to-all-start.3 = ((bf16[16,4,8,128]{3,2,1,0:T(8,128)(2,1)}), bf16[16,4,8,128]{3,2,1,0:T(8,128)(2,1)S(1)}, u32[]{:S(2)}, u32[]{:S(2)}) async-start(bf16[16,4,8,128]{3,2,1,0:T(8,128)(2,1)} %broadcast_in_dim.7), calls=%async_computation.3 | async-start | bytes 262144 | tf_op jit(solution)/shard_map/all_to_all | solution.py:270
  145.0 0.0 collective-permute-done.11.refs_5_
  145.1 0.0 collective-permute-done.7.refs_2_
  145.1 11.9 %all-to-all-done.3.refs_7_ = bf16[16,4,8,128]{3,2,1,0:T(8,128)(2,1)S(1)} async-done(((bf16[16,4,8,128]{3,2,1,0:T(8,128)(2,1)}), bf16[16,4,8,128]{3,2,1,0:T(8,128)(2,1)S(1)}, u32[]{:S(2)}, u32[]{:S(2)}) %all-to-all-start.3) | async-done | bytes 131104 | tf_op jit(solution)/shard_map/all_to_all | solution.py:270
  157.0 0.0 collective-permute-done.8.refs_3_
  157.0 0.0 collective-permute-done.10.refs_4_
  157.0 3.9 %theirs.1 = bf16[2,32,64,128]{3,2,1,0:T(8,128)(2,1)S(1)} custom-call(s32[2]{0:T(128)S(1)} %pad_add_fusion.at_ref, bf16[64,64,128]{2,1,0:T(8,128)(2,1)S(1)} %all-to-all-done.gen_ref.refs_0_, bf16[64,32,128]{2,1,0:T(8,128)(2,1)S(1)} %collective-permute-done.6.refs_1_, bf16[64,32,128]{2,1,0:T(8,128)(2,1)S(1)} %collective-permute-done.7.refs_2_, ...), custom_call_target="tpu_custom_call" | custom-call | flops 536870912 | bytes 4194304 | tf_op jit(solution)/shard_map/theirs/pallas_call | solution.py:242
  160.9 6.1 %collective-permute-start.14 = (bf16[2,32,64,128]{3,2,1,0:T(8,128)(2,1)S(1)}, bf16[2,32,64,128]{3,2,1,0:T(8,128)(2,1)S(1)}, u32[]{:S(2)}, u32[]{:S(2)}) collective-permute-start(bf16[2,32,64,128]{3,2,1,0:T(8,128)(2,1)S(1)} %theirs.1), channel_id=1, source_target_pairs={{0,256},{256,0},{1,257},{257,1},{2,258},{258,2},{3,259},{259,3},{4... | collective-permute-start | bytes 3145736 | tf_op jit(solution)/shard_map/ppermute | solution.py:260
  167.0 3.1 %collective-permute-start.12 = (bf16[8,64,128]{2,1,0:T(8,128)(2,1)S(1)}, bf16[8,64,128]{2,1,0:T(8,128)(2,1)S(1)}, u32[]{:S(2)}, u32[]{:S(2)}) collective-permute-start(bf16[8,64,128]{2,1,0:T(8,128)(2,1)S(1)} %get-tuple-element.36), channel_id=1, source_target_pairs={{0,4},{4,8},{8,12},{12,16},{16,20},{20,24},{24,28},{28,32},{32,36}... | collective-permute-start | bytes 393224 | tf_op jit(solution)/shard_map/ppermute | solution.py:266
  170.1 5.8 %collective-permute-start.13 = (bf16[8,64,128]{2,1,0:T(8,128)(2,1)S(1)}, bf16[8,64,128]{2,1,0:T(8,128)(2,1)S(1)}, u32[]{:S(2)}, u32[]{:S(2)}) collective-permute-start(bf16[8,64,128]{2,1,0:T(8,128)(2,1)S(1)} %get-tuple-element.37), channel_id=1, source_target_pairs={{4,0},{8,4},{12,8},{16,12},{20,16},{24,20},{28,24},{32,28},{36,32}... | collective-permute-start | bytes 393224 | tf_op jit(solution)/shard_map/ppermute | solution.py:266
  175.9 0.7 collective-permute-done.12.refs_10_
  176.6 1.2 collective-permute-done.13.refs_11_
  177.8 3.9 %mine.1 = (f32[32,64,128]{2,1,0:T(8,128)S(1)}, f32[32,64,128]{2,1,0:T(8,128)S(1)}) custom-call(s32[2]{0:T(128)S(1)} %pad_add_fusion.at_ref, bf16[64,64,128]{2,1,0:T(8,128)(2,1)S(1)} %all-to-all-done.gen_ref.refs_0_, bf16[64,32,128]{2,1,0:T(8,128)(2,1)S(1)} %collective-permute-done.6.refs_1_, bf16[64,32,128]{2,1,0:T(8,128)(2,1)S(1)} %collective-permute-done.7.refs_2_, ...), custom_call_target="tpu_custom_call" | custom-call | flops 536870912 | bytes 4194304 | tf_op jit(solution)/shard_map/mine/pallas_call | solution.py:242
  181.7 0.0 collective-permute-done.14
  181.7 1.3 fusion
  (17 shorter events, 0.1 us)
Async XLA Ops:
  0.6 1.0 copy-start.6
  1.7 1.0 copy-start.7
  2.7 0.7 copy-start.8
  3.4 21.1 %copy-start = (bf16[2048,128]{1,0:T(8,128)(2,1)S(1)}, bf16[2048,128]{1,0:T(8,128)(2,1)}, u32[]{:S(2)}) copy-start(bf16[2048,128]{1,0:T(8,128)(2,1)} %param.6) | copy-start | bytes 1572868
  3.4 41.1 %copy-start.13 = (s32[32,8]{0,1:T(8,128)S(1)}, s32[32,8]{0,1:T(8,128)}, u32[]{:S(2)}) copy-start(s32[32,8]{0,1:T(8,128)} %param.8) | copy-start | bytes 3076
  5.3 85.4 %all-to-all-start = ((bf16[64,64,128]{2,1,0:T(8,128)(2,1)}), bf16[64,64,128]{2,1,0:T(8,128)(2,1)S(1)}, u32[]{:S(2)}, u32[]{:S(2)}) async-start(bf16[64,64,128]{2,1,0:T(8,128)(2,1)} %pack.1), calls=%async_computation | async-start | bytes 2097152 | tf_op jit(solution)/shard_map/all_to_all | solution.py:270
  24.5 57.3 %collective-permute-start.2 = (bf16[2048,128]{1,0:T(8,128)(2,1)S(1)}, bf16[2048,128]{1,0:T(8,128)(2,1)}, u32[]{:S(2)}, u32[]{:S(2)}) collective-permute-start(bf16[2048,128]{1,0:T(8,128)(2,1)S(1)} %copy-done), channel_id=1, source_target_pairs={{0,3},{1,0},{2,1},{3,2},{4,7},{5,4},{6,5},{7,6},{8,11},{9,8},{10,9... | collective-permute-start | bytes 1572872 | tf_op jit(solution)/shard_map/ppermute | solution.py:260
  29.1 52.7 %collective-permute-start.1 = (bf16[2048,128]{1,0:T(8,128)(2,1)S(1)}, bf16[2048,128]{1,0:T(8,128)(2,1)S(1)}, u32[]{:S(2)}, u32[]{:S(2)}) collective-permute-start(bf16[2048,128]{1,0:T(8,128)(2,1)S(1)} %copy-done), channel_id=1, source_target_pairs={{0,2},{1,3},{2,0},{3,1},{4,6},{5,7},{6,4},{7,5},{8,10},{9,11},{10,... | collective-permute-start | bytes 1572872 | tf_op jit(solution)/shard_map/ppermute | solution.py:260
  31.4 50.4 %collective-permute-start = (bf16[2048,128]{1,0:T(8,128)(2,1)S(1)}, bf16[2048,128]{1,0:T(8,128)(2,1)S(1)}, u32[]{:S(2)}, u32[]{:S(2)}) collective-permute-start(bf16[2048,128]{1,0:T(8,128)(2,1)S(1)} %copy-done), channel_id=1, source_target_pairs={{0,1},{1,2},{2,3},{3,0},{4,5},{5,6},{6,7},{7,4},{8,9},{9,10},{10,1... | collective-permute-start | bytes 1572872 | tf_op jit(solution)/shard_map/ppermute | solution.py:260
  34.0 40.6 %collective-permute-start.3 = (bf16[8,64,128]{2,1,0:T(8,128)(2,1)S(1)}, bf16[8,64,128]{2,1,0:T(8,128)(2,1)S(1)}, u32[]{:S(2)}, u32[]{:S(2)}) collective-permute-start(bf16[8,64,128]{2,1,0:T(8,128)(2,1)S(1)} %bitcast.37), channel_id=1, source_target_pairs={{0,4},{4,8},{8,12},{12,16},{16,20},{20,24},{24,28},{28,32},{32,36}... | collective-permute-start | bytes 393224 | tf_op jit(solution)/shard_map/ppermute | solution.py:266
  36.9 37.7 %collective-permute-start.4 = (bf16[8,64,128]{2,1,0:T(8,128)(2,1)S(1)}, bf16[8,64,128]{2,1,0:T(8,128)(2,1)S(1)}, u32[]{:S(2)}, u32[]{:S(2)}) collective-permute-start(bf16[8,64,128]{2,1,0:T(8,128)(2,1)S(1)} %bitcast.36), channel_id=1, source_target_pairs={{4,0},{8,4},{12,8},{16,12},{20,16},{24,20},{28,24},{32,28},{36,32}... | collective-permute-start | bytes 393224 | tf_op jit(solution)/shard_map/ppermute | solution.py:266
  74.6 1.6 copy-start.1
  79.8 1.0 copy-start.2
  80.8 1.0 copy-start.4
  81.8 0.8 copy-start.11
  81.8 1.0 copy-start.12
  84.5 6.2 %collective-permute-start.5 = (bf16[4,2048,128]{2,1,0:T(8,128)(2,1)S(1)}, bf16[4,2048,128]{2,1,0:T(8,128)(2,1)}, u32[]{:S(2)}, u32[]{:S(2)}) collective-permute-start(bf16[4,2048,128]{2,1,0:T(8,128)(2,1)S(1)} %pad_maximum_fusion.own_ref), channel_id=1, source_target_pairs={{0,256},{256,0},{1,257},{257,1},{2,258},{258,2},{3,259},{259,3},{4... | collective-permute-start | bytes 6291464 | tf_op jit(solution)/shard_map/ppermute | solution.py:260
  93.9 0.8 copy-start.9
  94.7 0.8 copy-start.10
  95.5 24.4 %all-to-all-start.1 = ((bf16[16,4,8,128]{3,2,1,0:T(8,128)(2,1)}), bf16[16,4,8,128]{3,2,1,0:T(8,128)(2,1)S(1)}, u32[]{:S(2)}, u32[]{:S(2)}) async-start(bf16[16,4,8,128]{3,2,1,0:T(8,128)(2,1)} %get-tuple-element.33), calls=%async_computation.1 | async-start | bytes 262144 | tf_op jit(solution)/shard_map/all_to_all | solution.py:270
  107.8 23.5 %collective-permute-start.6 = (bf16[64,32,128]{2,1,0:T(8,128)(2,1)}, bf16[64,32,128]{2,1,0:T(8,128)(2,1)S(1)}, u32[]{:S(2)}, u32[]{:S(2)}) collective-permute-start(bf16[64,32,128]{2,1,0:T(8,128)(2,1)} %copy-done.10), channel_id=1, source_target_pairs={{0,1},{1,2},{2,3},{3,0},{4,5},{5,6},{6,7},{7,4},{8,9},{9,10},{10,1... | collective-permute-start | bytes 1572872 | tf_op jit(solution)/shard_map/ppermute | solution.py:260
  111.1 22.4 %collective-permute-start.9 = (bf16[64,32,128]{2,1,0:T(8,128)(2,1)}, bf16[64,32,128]{2,1,0:T(8,128)(2,1)S(1)}, u32[]{:S(2)}, u32[]{:S(2)}) collective-permute-start(bf16[64,32,128]{2,1,0:T(8,128)(2,1)} %copy-done.9), channel_id=1, source_target_pairs={{0,3},{1,0},{2,1},{3,2},{4,7},{5,4},{6,5},{7,6},{8,11},{9,8},{10,9... | collective-permute-start | bytes 1572872 | tf_op jit(solution)/shard_map/ppermute | solution.py:260
  120.6 17.3 %all-to-all-start.2 = ((f32[16,8,128]{2,1,0:T(8,128)}), f32[16,8,128]{2,1,0:T(8,128)S(1)}, u32[]{:S(2)}, u32[]{:S(2)}) async-start(f32[16,8,128]{2,1,0:T(8,128)} %bitcast.12), calls=%async_computation.2 | async-start | bytes 131072 | tf_op jit(solution)/shard_map/all_to_all | solution.py:270
  124.9 20.1 %collective-permute-start.11 = (bf16[64,32,128]{2,1,0:T(8,128)(2,1)}, bf16[64,32,128]{2,1,0:T(8,128)(2,1)S(1)}, u32[]{:S(2)}, u32[]{:S(2)}) collective-permute-start(bf16[64,32,128]{2,1,0:T(8,128)(2,1)} %copy-done.10), channel_id=1, source_target_pairs={{0,3},{1,0},{2,1},{3,2},{4,7},{5,4},{6,5},{7,6},{8,11},{9,8},{10,9... | collective-permute-start | bytes 1572872 | tf_op jit(solution)/shard_map/ppermute | solution.py:260
  129.4 15.7 %collective-permute-start.7 = (bf16[64,32,128]{2,1,0:T(8,128)(2,1)}, bf16[64,32,128]{2,1,0:T(8,128)(2,1)S(1)}, u32[]{:S(2)}, u32[]{:S(2)}) collective-permute-start(bf16[64,32,128]{2,1,0:T(8,128)(2,1)} %copy-done.9), channel_id=1, source_target_pairs={{0,1},{1,2},{2,3},{3,0},{4,5},{5,6},{6,7},{7,4},{8,9},{9,10},{10,1... | collective-permute-start | bytes 1572872 | tf_op jit(solution)/shard_map/ppermute | solution.py:260
  131.3 25.7 %collective-permute-start.8 = (bf16[64,32,128]{2,1,0:T(8,128)(2,1)S(1)}, bf16[64,32,128]{2,1,0:T(8,128)(2,1)}, u32[]{:S(2)}, u32[]{:S(2)}) collective-permute-start(bf16[64,32,128]{2,1,0:T(8,128)(2,1)S(1)} %collective-permute-done.6.refs_1_), channel_id=1, source_target_pairs={{0,1},{1,2},{2,3},{3,0},{4,5},{5,6},{6,7},{7,4},{8,9},{9,10},{10,1... | collective-permute-start | bytes 1572872 | tf_op jit(solution)/shard_map/ppermute | solution.py:260
  133.5 23.5 %collective-permute-start.10 = (bf16[64,32,128]{2,1,0:T(8,128)(2,1)S(1)}, bf16[64,32,128]{2,1,0:T(8,128)(2,1)}, u32[]{:S(2)}, u32[]{:S(2)}) collective-permute-start(bf16[64,32,128]{2,1,0:T(8,128)(2,1)S(1)} %collective-permute-done.9.refs_6_), channel_id=1, source_target_pairs={{0,3},{1,0},{2,1},{3,2},{4,7},{5,4},{6,5},{7,6},{8,11},{9,8},{10,9... | collective-permute-start | bytes 1572872 | tf_op jit(solution)/shard_map/ppermute | solution.py:260
  138.5 18.5 %all-to-all-start.3 = ((bf16[16,4,8,128]{3,2,1,0:T(8,128)(2,1)}), bf16[16,4,8,128]{3,2,1,0:T(8,128)(2,1)S(1)}, u32[]{:S(2)}, u32[]{:S(2)}) async-start(bf16[16,4,8,128]{3,2,1,0:T(8,128)(2,1)} %broadcast_in_dim.7), calls=%async_computation.3 | async-start | bytes 262144 | tf_op jit(solution)/shard_map/all_to_all | solution.py:270
  157.0 20.8 %copy-start.3 = (f32[32,64,128]{2,1,0:T(8,128)S(1)}, f32[32,64,128]{2,1,0:T(8,128)}, u32[]{:S(2)}) copy-start(f32[32,64,128]{2,1,0:T(8,128)} %copy-done.2) | copy-start | bytes 3145732
  157.0 20.8 %copy-start.5 = (f32[32,64,128]{2,1,0:T(8,128)S(1)}, f32[32,64,128]{2,1,0:T(8,128)}, u32[]{:S(2)}) copy-start(f32[32,64,128]{2,1,0:T(8,128)} %copy-done.4) | copy-start | bytes 3145732
  160.9 20.8 %collective-permute-start.14 = (bf16[2,32,64,128]{3,2,1,0:T(8,128)(2,1)S(1)}, bf16[2,32,64,128]{3,2,1,0:T(8,128)(2,1)S(1)}, u32[]{:S(2)}, u32[]{:S(2)}) collective-permute-start(bf16[2,32,64,128]{3,2,1,0:T(8,128)(2,1)S(1)} %theirs.1), channel_id=1, source_target_pairs={{0,256},{256,0},{1,257},{257,1},{2,258},{258,2},{3,259},{259,3},{4... | collective-permute-start | bytes 3145736 | tf_op jit(solution)/shard_map/ppermute | solution.py:260
  167.0 9.6 %collective-permute-start.12 = (bf16[8,64,128]{2,1,0:T(8,128)(2,1)S(1)}, bf16[8,64,128]{2,1,0:T(8,128)(2,1)S(1)}, u32[]{:S(2)}, u32[]{:S(2)}) collective-permute-start(bf16[8,64,128]{2,1,0:T(8,128)(2,1)S(1)} %get-tuple-element.36), channel_id=1, source_target_pairs={{0,4},{4,8},{8,12},{12,16},{16,20},{20,24},{24,28},{28,32},{32,36}... | collective-permute-start | bytes 393224 | tf_op jit(solution)/shard_map/ppermute | solution.py:266
  170.1 7.7 %collective-permute-start.13 = (bf16[8,64,128]{2,1,0:T(8,128)(2,1)S(1)}, bf16[8,64,128]{2,1,0:T(8,128)(2,1)S(1)}, u32[]{:S(2)}, u32[]{:S(2)}) collective-permute-start(bf16[8,64,128]{2,1,0:T(8,128)(2,1)S(1)} %get-tuple-element.37), channel_id=1, source_target_pairs={{4,0},{8,4},{12,8},{16,12},{20,16},{24,20},{28,24},{32,28},{36,32}... | collective-permute-start | bytes 393224 | tf_op jit(solution)/shard_map/ppermute | solution.py:266

commit v5 on v4

--- a/solution.py
+++ b/solution.py
@@ -61,7 +61,6 @@
         out_shape=(out,) * CHUNKS,
         in_specs=[whole(SMEM), whole(VMEM), whole(VMEM)],
         out_specs=(whole(VMEM),) * CHUNKS,
-        compiler_params=grant(6),
         cost_estimate=cost(0, 8 * ranks * width),
         name="pack",
     )(order_map, left, right)
@@ -136,14 +135,12 @@
     )(local_cols, couplings, blocks, low, high)
 
 
-def reduce_kernel(at_ref, gen_ref, own_ref, other_ref, out_ref, first_ref, second_ref, lhs):
+def reduce_kernel(at_ref, gen_ref, own_ref, other_ref, out_ref, lhs):
     half, me = at_ref[0], at_ref[1]
     blocks, ranks, _ = gen_ref.shape
     count = blocks // 2
     parts = own_ref.shape[0]
     low = low_lanes((ranks, LANES))
-    first_ref[...] = gen_ref[:, : ranks // 2]
-    second_ref[...] = gen_ref[:, ranks // 2 :]
     for side, first in ((0, half * count), (1, (1 - half) * count)):
         for k in range(count // 2):
             one, two = gen_ref[first + 2 * k], gen_ref[first + 2 * k + 1]
@@ -162,15 +159,14 @@
 
 
 def reduced(at, gens, own, other, splits):
-    blocks, ranks, _ = gens.shape
+    _, ranks, _ = gens.shape
     parts, rows, _ = own.shape
-    half_ranks = jax.ShapeDtypeStruct((blocks, ranks // 2, LANES), BF16)
     out = jax.ShapeDtypeStruct((splits, parts, 2 * ranks // splits, LANES), BF16)
     return pl.pallas_call(
         reduce_kernel,
-        out_shape=(out, half_ranks, half_ranks),
+        out_shape=out,
         in_specs=[whole(SMEM)] + [whole(VMEM)] * 3,
-        out_specs=(whole(VMEM),) * 3,
+        out_specs=whole(VMEM),
         scratch_shapes=[pltpu.VMEM((2, 2 * ranks, rows), BF16)],
         compiler_params=grant(14),
         cost_estimate=cost(8 * ranks * rows * parts * LANES, 6 << 20),
@@ -278,29 +274,31 @@
     n_z, n_x, n_col = (lax.axis_size(a) for a in ("z", "x", "col"))
     blocks = samples.reshape(count, BS, width)
 
+    (packed,) = pack(child_map[0, 0], gen_left[0], gen_right[0])
+    gens = spread_out(packed, ("z", "x"))
+
+    shifted = [around(samples, "col", k) for k in range(1, n_col)]
+    panels = jnp.stack([samples, *shifted])
+    others = around(panels, "half", 1)
     low = along_front(blocks[count - HB :], 1)
     high = along_front(blocks[:HB], -1)
-    (packed,) = pack(child_map[0, 0], gen_left[0], gen_right[0])
-    gens = spread_out(packed, ("z", "x"))
-
-    shifted = [around(samples, "col", k) for k in range(1, n_col)]
+
     local_cols = coupling_cols - lax.axis_index(FRONT) * count + HB
-    sparse_range, sparse_rows, up, down = sparse(local_cols, couplings, blocks, low, high)
-    shifted, up, down = lax.optimization_barrier((shifted, up, down))
-    panels = jnp.stack([samples, *shifted])
-    others = around(panels, "half", 1)
-    below, above = along_front(up, 1), along_front(down, -1)
-
-    gens, panels, others, sparse_range, sparse_rows = lax.optimization_barrier(
-        (gens, panels, others, sparse_range, sparse_rows)
-    )
-    added = (sparse_range, sparse_rows, below, above)
-    partial, first, second = reduced(at, gens, panels, others, n_z)
+    gens, panels, others, local_cols = lax.optimization_barrier((gens, panels, others, local_cols))
+    partial = reduced(at, gens, panels, others, n_z)
+
+    middle = gens.shape[1] // 2
+    first, second = gens[:, :middle], gens[:, middle:]
     up_a, down_b = around(first, "col", 1), around(second, "col", -1)
     up_b, down_a = around(second, "col", 1), around(first, "col", -1)
     far_a, far_b = around(up_a, "col", 1), around(down_b, "col", -1)
-
+    sparse_range, sparse_rows, up, down = sparse(local_cols, couplings, blocks, low, high)
     by_z = spread_out(partial, "z")
+    by_z, up, down = lax.optimization_barrier((by_z, up, down))
+    below, above = along_front(up, 1), along_front(down, -1)
+    at_last, below, above = lax.optimization_barrier((at, below, above))
+    added = (sparse_range, sparse_rows, below, above)
+
     by_z = jnp.sum(by_z.astype(F32), axis=0)
     copies = jnp.broadcast_to(by_z, (n_x, *by_z.shape)).reshape(n_x * n_col, *by_z.shape[1:])
     arrived = spread_out(copies, ("x", "col"))
@@ -309,10 +307,10 @@
     w = spread_out(copies, "z")
 
     everyone = (gens, up_a, up_b, far_a, far_b, down_a, down_b)
-    received = around(low_rank(at, everyone, w), "half", 1)
+    received = around(low_rank(at_last, everyone, w), "half", 1)
     range_out, rows_out = (
         (ours + theirs.astype(F32)).astype(BF16)
-        for ours, theirs in zip(low_rank(at, everyone, w, added), received)
+        for ours, theirs in zip(low_rank(at_last, everyone, w, added), received)
     )
     return range_out.reshape(samples.shape), rows_out.reshape(samples.shape)
 

time: 184 us -> 174 us (0.946)
  starting transfers between devices: 98.5 us -> 90.4 us
  local copies, waits for them, and re-layouts: 10.2 us -> 4.42 us
  waiting for transfers between devices: 53.6 us -> 57 us
    ppermute x11, waiting for transfers between devices: 4.2 us -> 27.3 us  [around(): return lax.ppermute(x, axis, [(i, (i + by) % count) for i in range(count)])]
    ppermute x4, waiting for transfers between devices: 32 us -> 18.8 us  [along_front(): return lax.ppermute(x, FRONT, pairs)]
    unnamed x29 -> x19, local copies, waits for them, and re-layouts: 8.89 us -> 2.05 us
    all_to_all x4, waiting for transfers between devices: 17.5 us -> 10.9 us  [spread_out(): return lax.all_to_all(x, axis, split_axis=0, concat_axis=0, tiled=True)]
    ppermute x11, starting transfers between devices: 36.9 us -> 32.1 us  [around(): return lax.ppermute(x, axis, [(i, (i + by) % count) for i in range(count)])]
  transfers between devices with their start and end apart: 19 -> 19, of which waited for: 6 -> 9; matrix products, arithmetic and copies ran while one was open for 2% -> 2% of each run, Pallas kernels for 4% -> 4%
where the time goes in v5:
time: 174 us; the launch traced here: 173 us
  starting transfers between devices  90.4 us (52%)
  waiting for transfers between devices  57 us (33%)
  Pallas kernels  17.3 us (10%)
  local copies, waits for them, and re-layouts  4.42 us (3%)
  other arithmetic  2.72 us (2%)
    all_to_all x4, starting transfers between devices, spread_out(): return lax.all_to_all(x, axis, split_axis=0, concat_axis=0, tiled=True)  40.8 us
    ppermute x11, starting transfers between devices, around(): return lax.ppermute(x, axis, [(i, (i + by) % count) for i in range(count)])  32.1 us
    ppermute x11, waiting for transfers between devices, around(): return lax.ppermute(x, axis, [(i, (i + by) % count) for i in range(count)])  27.3 us
    ppermute x4, waiting for transfers between devices, along_front(): return lax.ppermute(x, FRONT, pairs)  18.8 us
    ppermute x4, starting transfers between devices, along_front(): return lax.ppermute(x, FRONT, pairs)  17.5 us
    all_to_all x4, waiting for transfers between devices, spread_out(): return lax.all_to_all(x, axis, split_axis=0, concat_axis=0, tiled=True)  10.9 us
    pallas_call x2, Pallas kernels, low_rank(): pl.pallas_call(functools.partial(low_rank_kernel, mine, len(gens)), grid_...  7.78 us
    pallas_call x1, Pallas kernels, sparse(): pl.pallas_call(sparse_kernel, grid=(count // per,), out_shape=(jax.ShapeD...  3.66 us
  transfers between devices with their start and end apart: 19, of which 9 were waited for; matrix products, arithmetic and copies ran while one was open for 2% of the time, Pallas kernels for 4%

profile of v5, /device:TPU:1, one launch (start us, length us, event | category | flops | bytes accessed | tf_op | source)
XLA Modules:
  0.0 172.9 jit_solution(17193560747403979964)
XLA Ops:
  0.6 0.0 copy-start
  0.6 2.7 %pack.1 = bf16[64,64,128]{2,1,0:T(8,128)(2,1)} custom-call(s32[64]{0:T(128)} %bitcast.38, bf16[64,4096]{1,0:T(8,128)(2,1)} %bitcast.28, bf16[64,4096]{1,0:T(8,128)(2,1)} %bitcast.29), custom_call_target="tpu_custom_call" | custom-call | bytes 2097152 | tf_op jit(solution)/shard_map/pack/pallas_call | solution.py:59
  3.3 19.1 %all-to-all-start = ((bf16[64,64,128]{2,1,0:T(8,128)(2,1)}), bf16[64,64,128]{2,1,0:T(8,128)(2,1)S(1)}, u32[]{:S(2)}, u32[]{:S(2)}) async-start(bf16[64,64,128]{2,1,0:T(8,128)(2,1)} %pack.1), calls=%async_computation | async-start | bytes 2097152 | tf_op jit(solution)/shard_map/all_to_all | solution.py:266
  22.4 0.0 copy-done
  22.4 4.6 %collective-permute-start.2 = (bf16[2048,128]{1,0:T(8,128)(2,1)S(1)}, bf16[2048,128]{1,0:T(8,128)(2,1)S(1)}, u32[]{:S(2)}, u32[]{:S(2)}) collective-permute-start(bf16[2048,128]{1,0:T(8,128)(2,1)S(1)} %copy-done), channel_id=1, source_target_pairs={{0,3},{1,0},{2,1},{3,2},{4,7},{5,4},{6,5},{7,6},{8,11},{9,8},{10,9... | collective-permute-start | bytes 1572872 | tf_op jit(solution)/shard_map/ppermute | solution.py:256
  27.1 2.3 %collective-permute-start.1 = (bf16[2048,128]{1,0:T(8,128)(2,1)S(1)}, bf16[2048,128]{1,0:T(8,128)(2,1)S(1)}, u32[]{:S(2)}, u32[]{:S(2)}) collective-permute-start(bf16[2048,128]{1,0:T(8,128)(2,1)S(1)} %copy-done), channel_id=1, source_target_pairs={{0,2},{1,3},{2,0},{3,1},{4,6},{5,7},{6,4},{7,5},{8,10},{9,11},{10,... | collective-permute-start | bytes 1572872 | tf_op jit(solution)/shard_map/ppermute | solution.py:256
  29.3 2.6 %collective-permute-start = (bf16[2048,128]{1,0:T(8,128)(2,1)S(1)}, bf16[2048,128]{1,0:T(8,128)(2,1)S(1)}, u32[]{:S(2)}, u32[]{:S(2)}) collective-permute-start(bf16[2048,128]{1,0:T(8,128)(2,1)S(1)} %copy-done), channel_id=1, source_target_pairs={{0,1},{1,2},{2,3},{3,0},{4,5},{5,6},{6,7},{7,4},{8,9},{9,10},{10,1... | collective-permute-start | bytes 1572872 | tf_op jit(solution)/shard_map/ppermute | solution.py:256
  31.9 6.5 %collective-permute-done.2 = bf16[2048,128]{1,0:T(8,128)(2,1)S(1)} collective-permute-done((bf16[2048,128]{1,0:T(8,128)(2,1)S(1)}, bf16[2048,128]{1,0:T(8,128)(2,1)S(1)}, u32[]{:S(2)}, u32[]{:S(2)}) %collective-permute-start.2) | collective-permute-done | bytes 524320 | tf_op jit(solution)/shard_map/ppermute | solution.py:256
  38.4 4.3 %collective-permute-done.1 = bf16[2048,128]{1,0:T(8,128)(2,1)S(1)} collective-permute-done((bf16[2048,128]{1,0:T(8,128)(2,1)S(1)}, bf16[2048,128]{1,0:T(8,128)(2,1)S(1)}, u32[]{:S(2)}, u32[]{:S(2)}) %collective-permute-start.1) | collective-permute-done | bytes 524320 | tf_op jit(solution)/shard_map/ppermute | solution.py:256
  42.7 12.8 %collective-permute-done = bf16[2048,128]{1,0:T(8,128)(2,1)S(1)} collective-permute-done((bf16[2048,128]{1,0:T(8,128)(2,1)S(1)}, bf16[2048,128]{1,0:T(8,128)(2,1)S(1)}, u32[]{:S(2)}, u32[]{:S(2)}) %collective-permute-start) | collective-permute-done | bytes 524320 | tf_op jit(solution)/shard_map/ppermute | solution.py:256
  55.5 1.3 pad_maximum_fusion.own_ref
  56.9 2.4 %collective-permute-start.3 = (bf16[4,2048,128]{2,1,0:T(8,128)(2,1)S(1)}, bf16[4,2048,128]{2,1,0:T(8,128)(2,1)}, u32[]{:S(2)}, u32[]{:S(2)}) collective-permute-start(bf16[4,2048,128]{2,1,0:T(8,128)(2,1)S(1)} %pad_maximum_fusion.own_ref), channel_id=1, source_target_pairs={{0,256},{256,0},{1,257},{257,1},{2,258},{258,2},{3,259},{259,3},{4... | collective-permute-start | bytes 6291464 | tf_op jit(solution)/shard_map/ppermute | solution.py:256
  59.3 0.0 copy-done.8
  59.3 0.1 copy.9
  59.4 0.1 pad_add_fusion.at_ref
  59.4 3.7 %collective-permute-done.3.other_ref = bf16[4,2048,128]{2,1,0:T(8,128)(2,1)} collective-permute-done((bf16[4,2048,128]{2,1,0:T(8,128)(2,1)S(1)}, bf16[4,2048,128]{2,1,0:T(8,128)(2,1)}, u32[]{:S(2)}, u32[]{:S(2)}) %collective-permute-start.3) | collective-permute-done | bytes 2097184 | tf_op jit(solution)/shard_map/ppermute | solution.py:256
  63.2 10.9 %all-to-all-done.gen_ref.refs_0_ = bf16[64,64,128]{2,1,0:T(8,128)(2,1)S(1)} async-done(((bf16[64,64,128]{2,1,0:T(8,128)(2,1)}), bf16[64,64,128]{2,1,0:T(8,128)(2,1)S(1)}, u32[]{:S(2)}, u32[]{:S(2)}) %all-to-all-start) | async-done | bytes 1048608 | tf_op jit(solution)/shard_map/all_to_all | solution.py:266
  74.0 3.2 %partials.1 = bf16[16,4,8,128]{3,2,1,0:T(8,128)(2,1)} custom-call(s32[2]{0:T(128)S(1)} %pad_add_fusion.at_ref, bf16[64,64,128]{2,1,0:T(8,128)(2,1)S(1)} %all-to-all-done.gen_ref.refs_0_, bf16[4,2048,128]{2,1,0:T(8,128)(2,1)S(1)} %pad_maximum_fusion.own_ref, bf16[4,2048,128]{2,1,0:T(8,128)(2,1)} %collective-permute-done.3.other_ref), custom_call_target="tpu_custom_call" | custom-call | flops 536870912 | bytes 6291456 | tf_op jit(solution)/shard_map/partials/pallas_call | solution.py:165
  77.2 6.0 %all-to-all-start.1 = ((bf16[16,4,8,128]{3,2,1,0:T(8,128)(2,1)}), bf16[16,4,8,128]{3,2,1,0:T(8,128)(2,1)S(1)}, u32[]{:S(2)}, u32[]{:S(2)}) async-start(bf16[16,4,8,128]{3,2,1,0:T(8,128)(2,1)} %partials.1), calls=%async_computation.1 | async-start | bytes 262144 | tf_op jit(solution)/shard_map/all_to_all | solution.py:266
  83.2 0.0 copy-start.2
  83.2 1.0 fusion.2
  84.2 4.6 %collective-permute-start.11 = (bf16[64,32,128]{2,1,0:T(8,128)(2,1)}, bf16[64,32,128]{2,1,0:T(8,128)(2,1)S(1)}, u32[]{:S(2)}, u32[]{:S(2)}) collective-permute-start(bf16[64,32,128]{2,1,0:T(8,128)(2,1)} %get-tuple-element.36), channel_id=1, source_target_pairs={{0,3},{1,0},{2,1},{3,2},{4,7},{5,4},{6,5},{7,6},{8,11},{9,8},{10,9... | collective-permute-start | bytes 1572872 | tf_op jit(solution)/shard_map/ppermute | solution.py:256
  88.9 1.9 %collective-permute-start.8 = (bf16[64,32,128]{2,1,0:T(8,128)(2,1)}, bf16[64,32,128]{2,1,0:T(8,128)(2,1)S(1)}, u32[]{:S(2)}, u32[]{:S(2)}) collective-permute-start(bf16[64,32,128]{2,1,0:T(8,128)(2,1)} %get-tuple-element.37), channel_id=1, source_target_pairs={{0,1},{1,2},{2,3},{3,0},{4,5},{5,6},{6,7},{7,4},{8,9},{9,10},{10,1... | collective-permute-start | bytes 1572872 | tf_op jit(solution)/shard_map/ppermute | solution.py:256
  90.8 0.0 copy-done.1
  90.8 2.9 %collective-permute-start.4 = (bf16[8,64,128]{2,1,0:T(8,128)(2,1)S(1)}, bf16[8,64,128]{2,1,0:T(8,128)(2,1)S(1)}, u32[]{:S(2)}, u32[]{:S(2)}) collective-permute-start(bf16[8,64,128]{2,1,0:T(8,128)(2,1)S(1)} %bitcast.37), channel_id=1, source_target_pairs={{0,4},{4,8},{8,12},{12,16},{16,20},{20,24},{24,28},{28,32},{32,36}... | collective-permute-start | bytes 393224 | tf_op jit(solution)/shard_map/ppermute | solution.py:262
  93.8 8.3 %collective-permute-start.5 = (bf16[8,64,128]{2,1,0:T(8,128)(2,1)S(1)}, bf16[8,64,128]{2,1,0:T(8,128)(2,1)S(1)}, u32[]{:S(2)}, u32[]{:S(2)}) collective-permute-start(bf16[8,64,128]{2,1,0:T(8,128)(2,1)S(1)} %bitcast.36), channel_id=1, source_target_pairs={{4,0},{8,4},{12,8},{16,12},{20,16},{24,20},{28,24},{32,28},{36,32}... | collective-permute-start | bytes 393224 | tf_op jit(solution)/shard_map/ppermute | solution.py:262
  102.1 0.7 collective-permute-done.4.low_ref
  102.8 1.2 collective-permute-done.5.high_ref
  104.0 0.0 copy-done.2
  104.0 3.7 %sparse.1 = (f32[32,64,128]{2,1,0:T(8,128)S(1)}, f32[32,64,128]{2,1,0:T(8,128)S(1)}, bf16[8,64,128]{2,1,0:T(8,128)(2,1)S(1)}, bf16[8,64,128]{2,1,0:T(8,128)(2,1)S(1)}) custom-call(s32[32,8]{1,0:T(8,128)S(1)} %subtract_add_fusion.cols_ref, bf16[32,64,512]{2,1,0:T(8,128)(2,1)S(1)} %copy-done.2, bf16[32,64,128]{2,1,0:T(8,128)(2,1)S(1)} %bitcast.27, ...), custom_call_target="tpu_custom_call" | custom-call | flops 536870912 | bytes 6291456 | tf_op jit(solution)/shard_map/sparse/pallas_call | solution.py:106
  107.7 0.0 copy-start.3
  107.7 1.0 copy-done.3
  108.7 1.0 copy-done.5
  109.6 0.0 all-to-all-done.1
  109.7 0.7 broadcast_in_dim.6
  110.3 4.3 %all-to-all-start.2 = ((f32[16,8,128]{2,1,0:T(8,128)}), f32[16,8,128]{2,1,0:T(8,128)S(1)}, u32[]{:S(2)}, u32[]{:S(2)}) async-start(f32[16,8,128]{2,1,0:T(8,128)} %bitcast.12), calls=%async_computation.2 | async-start | bytes 131072 | tf_op jit(solution)/shard_map/all_to_all | solution.py:266
  114.6 0.0 copy-done.7
  114.7 3.3 %collective-permute-start.9 = (bf16[64,32,128]{2,1,0:T(8,128)(2,1)}, bf16[64,32,128]{2,1,0:T(8,128)(2,1)S(1)}, u32[]{:S(2)}, u32[]{:S(2)}) collective-permute-start(bf16[64,32,128]{2,1,0:T(8,128)(2,1)} %get-tuple-element.36), channel_id=1, source_target_pairs={{0,1},{1,2},{2,3},{3,0},{4,5},{5,6},{6,7},{7,4},{8,9},{9,10},{10,1... | collective-permute-start | bytes 1572872 | tf_op jit(solution)/shard_map/ppermute | solution.py:256
  117.9 3.2 %collective-permute-start.13 = (bf16[64,32,128]{2,1,0:T(8,128)(2,1)}, bf16[64,32,128]{2,1,0:T(8,128)(2,1)S(1)}, u32[]{:S(2)}, u32[]{:S(2)}) collective-permute-start(bf16[64,32,128]{2,1,0:T(8,128)(2,1)} %get-tuple-element.37), channel_id=1, source_target_pairs={{0,3},{1,0},{2,1},{3,2},{4,7},{5,4},{6,5},{7,6},{8,11},{9,8},{10,9... | collective-permute-start | bytes 1572872 | tf_op jit(solution)/shard_map/ppermute | solution.py:256
  121.2 0.0 collective-permute-done.11.refs_6_
  121.2 3.3 %collective-permute-start.12 = (bf16[64,32,128]{2,1,0:T(8,128)(2,1)S(1)}, bf16[64,32,128]{2,1,0:T(8,128)(2,1)}, u32[]{:S(2)}, u32[]{:S(2)}) collective-permute-start(bf16[64,32,128]{2,1,0:T(8,128)(2,1)S(1)} %collective-permute-done.11.refs_6_), channel_id=1, source_target_pairs={{0,3},{1,0},{2,1},{3,2},{4,7},{5,4},{6,5},{7,6},{8,11},{9,8},{10,9... | collective-permute-start | bytes 1572872 | tf_op jit(solution)/shard_map/ppermute | solution.py:256
  124.5 0.0 collective-permute-done.8.refs_1_
  124.5 2.0 %collective-permute-start.10 = (bf16[64,32,128]{2,1,0:T(8,128)(2,1)S(1)}, bf16[64,32,128]{2,1,0:T(8,128)(2,1)}, u32[]{:S(2)}, u32[]{:S(2)}) collective-permute-start(bf16[64,32,128]{2,1,0:T(8,128)(2,1)S(1)} %collective-permute-done.8.refs_1_), channel_id=1, source_target_pairs={{0,1},{1,2},{2,3},{3,0},{4,5},{5,6},{6,7},{7,4},{8,9},{9,10},{10,1... | collective-permute-start | bytes 1572872 | tf_op jit(solution)/shard_map/ppermute | solution.py:256
  126.5 0.0 all-to-all-done.2
  126.5 0.7 broadcast_in_dim.7
  127.2 11.4 %all-to-all-start.3 = ((bf16[16,4,8,128]{3,2,1,0:T(8,128)(2,1)}), bf16[16,4,8,128]{3,2,1,0:T(8,128)(2,1)S(1)}, u32[]{:S(2)}, u32[]{:S(2)}) async-start(bf16[16,4,8,128]{3,2,1,0:T(8,128)(2,1)} %broadcast_in_dim.7), calls=%async_computation.3 | async-start | bytes 262144 | tf_op jit(solution)/shard_map/all_to_all | solution.py:266
  138.5 3.3 %collective-permute-start.6 = (bf16[8,64,128]{2,1,0:T(8,128)(2,1)S(1)}, bf16[8,64,128]{2,1,0:T(8,128)(2,1)S(1)}, u32[]{:S(2)}, u32[]{:S(2)}) collective-permute-start(bf16[8,64,128]{2,1,0:T(8,128)(2,1)S(1)} %get-tuple-element.24), channel_id=1, source_target_pairs={{0,4},{4,8},{8,12},{12,16},{16,20},{20,24},{24,28},{28,32},{32,36}... | collective-permute-start | bytes 393224 | tf_op jit(solution)/shard_map/ppermute | solution.py:262
  141.8 14.0 %collective-permute-done.6.refs_10_ = bf16[8,64,128]{2,1,0:T(8,128)(2,1)S(1)} collective-permute-done((bf16[8,64,128]{2,1,0:T(8,128)(2,1)S(1)}, bf16[8,64,128]{2,1,0:T(8,128)(2,1)S(1)}, u32[]{:S(2)}, u32[]{:S(2)}) %collective-permute-start.6) | collective-permute-done | bytes 131104 | tf_op jit(solution)/shard_map/ppermute | solution.py:262
  155.8 3.0 %collective-permute-start.7 = (bf16[8,64,128]{2,1,0:T(8,128)(2,1)}, bf16[8,64,128]{2,1,0:T(8,128)(2,1)S(1)}, u32[]{:S(2)}, u32[]{:S(2)}) collective-permute-start(bf16[8,64,128]{2,1,0:T(8,128)(2,1)} %copy-done.7), channel_id=1, source_target_pairs={{4,0},{8,4},{12,8},{16,12},{20,16},{24,20},{28,24},{32,28},{36,32}... | collective-permute-start | bytes 393224 | tf_op jit(solution)/shard_map/ppermute | solution.py:262
  158.9 2.9 %collective-permute-done.7.refs_11_ = bf16[8,64,128]{2,1,0:T(8,128)(2,1)S(1)} collective-permute-done((bf16[8,64,128]{2,1,0:T(8,128)(2,1)}, bf16[8,64,128]{2,1,0:T(8,128)(2,1)S(1)}, u32[]{:S(2)}, u32[]{:S(2)}) %collective-permute-start.7) | collective-permute-done | bytes 131104 | tf_op jit(solution)/shard_map/ppermute | solution.py:262
  161.8 0.0 collective-permute-done.9.refs_2_
  161.8 0.0 collective-permute-done.13.refs_5_
  161.8 0.0 all-to-all-done.3.refs_7_
  161.8 0.0 copy-start.4
  161.8 0.0 copy-start.6
  161.8 0.0 collective-permute-done.12.refs_4_
  161.8 0.0 collective-permute-done.10.refs_3_
  161.8 3.9 %theirs.1 = bf16[2,32,64,128]{3,2,1,0:T(8,128)(2,1)S(1)} custom-call(s32[2]{0:T(128)S(1)} %pad_add_fusion.at_ref, bf16[64,64,128]{2,1,0:T(8,128)(2,1)S(1)} %all-to-all-done.gen_ref.refs_0_, bf16[64,32,128]{2,1,0:T(8,128)(2,1)S(1)} %collective-permute-done.8.refs_1_, bf16[64,32,128]{2,1,0:T(8,128)(2,1)S(1)} %collective-permute-done.9.refs_2_, ...), custom_call_target="tpu_custom_call" | custom-call | flops 536870912 | bytes 4194304 | tf_op jit(solution)/shard_map/theirs/pallas_call | solution.py:238
  165.7 1.9 %collective-permute-start.14 = (bf16[2,32,64,128]{3,2,1,0:T(8,128)(2,1)S(1)}, bf16[2,32,64,128]{3,2,1,0:T(8,128)(2,1)S(1)}, u32[]{:S(2)}, u32[]{:S(2)}) collective-permute-start(bf16[2,32,64,128]{3,2,1,0:T(8,128)(2,1)S(1)} %theirs.1), channel_id=1, source_target_pairs={{0,256},{256,0},{1,257},{257,1},{2,258},{258,2},{3,259},{259,3},{4... | collective-permute-start | bytes 3145736 | tf_op jit(solution)/shard_map/ppermute | solution.py:256
  167.6 0.0 copy-done.4
  167.6 0.0 copy-done.6
  167.6 3.9 %mine.1 = (f32[32,64,128]{2,1,0:T(8,128)S(1)}, f32[32,64,128]{2,1,0:T(8,128)S(1)}) custom-call(s32[2]{0:T(128)S(1)} %pad_add_fusion.at_ref, bf16[64,64,128]{2,1,0:T(8,128)(2,1)S(1)} %all-to-all-done.gen_ref.refs_0_, bf16[64,32,128]{2,1,0:T(8,128)(2,1)S(1)} %collective-permute-done.8.refs_1_, bf16[64,32,128]{2,1,0:T(8,128)(2,1)S(1)} %collective-permute-done.9.refs_2_, ...), custom_call_target="tpu_custom_call" | custom-call | flops 536870912 | bytes 4194304 | tf_op jit(solution)/shard_map/mine/pallas_call | solution.py:238
  171.6 0.0 collective-permute-done.14
  171.6 1.3 fusion
  (8 shorter events, 0.1 us)
Async XLA Ops:
  0.6 21.8 %copy-start = (bf16[2048,128]{1,0:T(8,128)(2,1)S(1)}, bf16[2048,128]{1,0:T(8,128)(2,1)}, u32[]{:S(2)}) copy-start(bf16[2048,128]{1,0:T(8,128)(2,1)} %param.6) | copy-start | bytes 1572868
  3.3 70.7 %all-to-all-start = ((bf16[64,64,128]{2,1,0:T(8,128)(2,1)}), bf16[64,64,128]{2,1,0:T(8,128)(2,1)S(1)}, u32[]{:S(2)}, u32[]{:S(2)}) async-start(bf16[64,64,128]{2,1,0:T(8,128)(2,1)} %pack.1), calls=%async_computation | async-start | bytes 2097152 | tf_op jit(solution)/shard_map/all_to_all | solution.py:266
  22.4 16.0 %collective-permute-start.2 = (bf16[2048,128]{1,0:T(8,128)(2,1)S(1)}, bf16[2048,128]{1,0:T(8,128)(2,1)S(1)}, u32[]{:S(2)}, u32[]{:S(2)}) collective-permute-start(bf16[2048,128]{1,0:T(8,128)(2,1)S(1)} %copy-done), channel_id=1, source_target_pairs={{0,3},{1,0},{2,1},{3,2},{4,7},{5,4},{6,5},{7,6},{8,11},{9,8},{10,9... | collective-permute-start | bytes 1572872 | tf_op jit(solution)/shard_map/ppermute | solution.py:256
  27.1 15.7 %collective-permute-start.1 = (bf16[2048,128]{1,0:T(8,128)(2,1)S(1)}, bf16[2048,128]{1,0:T(8,128)(2,1)S(1)}, u32[]{:S(2)}, u32[]{:S(2)}) collective-permute-start(bf16[2048,128]{1,0:T(8,128)(2,1)S(1)} %copy-done), channel_id=1, source_target_pairs={{0,2},{1,3},{2,0},{3,1},{4,6},{5,7},{6,4},{7,5},{8,10},{9,11},{10,... | collective-permute-start | bytes 1572872 | tf_op jit(solution)/shard_map/ppermute | solution.py:256
  29.3 26.2 %collective-permute-start = (bf16[2048,128]{1,0:T(8,128)(2,1)S(1)}, bf16[2048,128]{1,0:T(8,128)(2,1)S(1)}, u32[]{:S(2)}, u32[]{:S(2)}) collective-permute-start(bf16[2048,128]{1,0:T(8,128)(2,1)S(1)} %copy-done), channel_id=1, source_target_pairs={{0,1},{1,2},{2,3},{3,0},{4,5},{5,6},{6,7},{7,4},{8,9},{9,10},{10,1... | collective-permute-start | bytes 1572872 | tf_op jit(solution)/shard_map/ppermute | solution.py:256
  55.5 3.7 %copy-start.8 = (s32[32,8]{0,1:T(8,128)S(1)}, s32[32,8]{0,1:T(8,128)}, u32[]{:S(2)}) copy-start(s32[32,8]{0,1:T(8,128)} %param.8) | copy-start | bytes 3076
  56.9 6.3 %collective-permute-start.3 = (bf16[4,2048,128]{2,1,0:T(8,128)(2,1)S(1)}, bf16[4,2048,128]{2,1,0:T(8,128)(2,1)}, u32[]{:S(2)}, u32[]{:S(2)}) collective-permute-start(bf16[4,2048,128]{2,1,0:T(8,128)(2,1)S(1)} %pad_maximum_fusion.own_ref), channel_id=1, source_target_pairs={{0,256},{256,0},{1,257},{257,1},{2,258},{258,2},{3,259},{259,3},{4... | collective-permute-start | bytes 6291464 | tf_op jit(solution)/shard_map/ppermute | solution.py:256
  77.2 13.6 %copy-start.1 = (bf16[2048,128]{1,0:T(8,128)(2,1)S(1)}, bf16[2048,128]{1,0:T(8,128)(2,1)}, u32[]{:S(2)}) copy-start(bf16[2048,128]{1,0:T(8,128)(2,1)} %param.6) | copy-start | bytes 1572868
  77.2 32.4 %all-to-all-start.1 = ((bf16[16,4,8,128]{3,2,1,0:T(8,128)(2,1)}), bf16[16,4,8,128]{3,2,1,0:T(8,128)(2,1)S(1)}, u32[]{:S(2)}, u32[]{:S(2)}) async-start(bf16[16,4,8,128]{3,2,1,0:T(8,128)(2,1)} %partials.1), calls=%async_computation.1 | async-start | bytes 262144 | tf_op jit(solution)/shard_map/all_to_all | solution.py:266
  83.2 20.8 %copy-start.2 = (bf16[32,64,512]{2,1,0:T(8,128)(2,1)S(1)}, bf16[32,64,512]{2,1,0:T(8,128)(2,1)}, u32[]{:S(2)}) copy-start(bf16[32,64,512]{2,1,0:T(8,128)(2,1)} %a_ref.1) | copy-start | bytes 6291460
  84.2 36.9 %collective-permute-start.11 = (bf16[64,32,128]{2,1,0:T(8,128)(2,1)}, bf16[64,32,128]{2,1,0:T(8,128)(2,1)S(1)}, u32[]{:S(2)}, u32[]{:S(2)}) collective-permute-start(bf16[64,32,128]{2,1,0:T(8,128)(2,1)} %get-tuple-element.36), channel_id=1, source_target_pairs={{0,3},{1,0},{2,1},{3,2},{4,7},{5,4},{6,5},{7,6},{8,11},{9,8},{10,9... | collective-permute-start | bytes 1572872 | tf_op jit(solution)/shard_map/ppermute | solution.py:256
  88.9 35.6 %collective-permute-start.8 = (bf16[64,32,128]{2,1,0:T(8,128)(2,1)}, bf16[64,32,128]{2,1,0:T(8,128)(2,1)S(1)}, u32[]{:S(2)}, u32[]{:S(2)}) collective-permute-start(bf16[64,32,128]{2,1,0:T(8,128)(2,1)} %get-tuple-element.37), channel_id=1, source_target_pairs={{0,1},{1,2},{2,3},{3,0},{4,5},{5,6},{6,7},{7,4},{8,9},{9,10},{10,1... | collective-permute-start | bytes 1572872 | tf_op jit(solution)/shard_map/ppermute | solution.py:256
  90.8 11.9 %collective-permute-start.4 = (bf16[8,64,128]{2,1,0:T(8,128)(2,1)S(1)}, bf16[8,64,128]{2,1,0:T(8,128)(2,1)S(1)}, u32[]{:S(2)}, u32[]{:S(2)}) collective-permute-start(bf16[8,64,128]{2,1,0:T(8,128)(2,1)S(1)} %bitcast.37), channel_id=1, source_target_pairs={{0,4},{4,8},{8,12},{12,16},{16,20},{20,24},{24,28},{28,32},{32,36}... | collective-permute-start | bytes 393224 | tf_op jit(solution)/shard_map/ppermute | solution.py:262
  93.8 10.2 %collective-permute-start.5 = (bf16[8,64,128]{2,1,0:T(8,128)(2,1)S(1)}, bf16[8,64,128]{2,1,0:T(8,128)(2,1)S(1)}, u32[]{:S(2)}, u32[]{:S(2)}) collective-permute-start(bf16[8,64,128]{2,1,0:T(8,128)(2,1)S(1)} %bitcast.36), channel_id=1, source_target_pairs={{4,0},{8,4},{12,8},{16,12},{20,16},{24,20},{28,24},{32,28},{36,32}... | collective-permute-start | bytes 393224 | tf_op jit(solution)/shard_map/ppermute | solution.py:262
  107.7 1.0 copy-start.3
  108.7 1.0 copy-start.5
  109.6 5.0 %copy-start.7 = (bf16[8,64,128]{2,1,0:T(8,128)(2,1)}, bf16[8,64,128]{2,1,0:T(8,128)(2,1)S(1)}, u32[]{:S(2)}) copy-start(bf16[8,64,128]{2,1,0:T(8,128)(2,1)S(1)} %get-tuple-element.25) | copy-start | bytes 393220
  110.3 16.2 %all-to-all-start.2 = ((f32[16,8,128]{2,1,0:T(8,128)}), f32[16,8,128]{2,1,0:T(8,128)S(1)}, u32[]{:S(2)}, u32[]{:S(2)}) async-start(f32[16,8,128]{2,1,0:T(8,128)} %bitcast.12), calls=%async_computation.2 | async-start | bytes 131072 | tf_op jit(solution)/shard_map/all_to_all | solution.py:266
  114.7 47.1 %collective-permute-start.9 = (bf16[64,32,128]{2,1,0:T(8,128)(2,1)}, bf16[64,32,128]{2,1,0:T(8,128)(2,1)S(1)}, u32[]{:S(2)}, u32[]{:S(2)}) collective-permute-start(bf16[64,32,128]{2,1,0:T(8,128)(2,1)} %get-tuple-element.36), channel_id=1, source_target_pairs={{0,1},{1,2},{2,3},{3,0},{4,5},{5,6},{6,7},{7,4},{8,9},{9,10},{10,1... | collective-permute-start | bytes 1572872 | tf_op jit(solution)/shard_map/ppermute | solution.py:256
  117.9 43.8 %collective-permute-start.13 = (bf16[64,32,128]{2,1,0:T(8,128)(2,1)}, bf16[64,32,128]{2,1,0:T(8,128)(2,1)S(1)}, u32[]{:S(2)}, u32[]{:S(2)}) collective-permute-start(bf16[64,32,128]{2,1,0:T(8,128)(2,1)} %get-tuple-element.37), channel_id=1, source_target_pairs={{0,3},{1,0},{2,1},{3,2},{4,7},{5,4},{6,5},{7,6},{8,11},{9,8},{10,9... | collective-permute-start | bytes 1572872 | tf_op jit(solution)/shard_map/ppermute | solution.py:256
  121.2 40.6 %collective-permute-start.12 = (bf16[64,32,128]{2,1,0:T(8,128)(2,1)S(1)}, bf16[64,32,128]{2,1,0:T(8,128)(2,1)}, u32[]{:S(2)}, u32[]{:S(2)}) collective-permute-start(bf16[64,32,128]{2,1,0:T(8,128)(2,1)S(1)} %collective-permute-done.11.refs_6_), channel_id=1, source_target_pairs={{0,3},{1,0},{2,1},{3,2},{4,7},{5,4},{6,5},{7,6},{8,11},{9,8},{10,9... | collective-permute-start | bytes 1572872 | tf_op jit(solution)/shard_map/ppermute | solution.py:256
  124.5 37.3 %collective-permute-start.10 = (bf16[64,32,128]{2,1,0:T(8,128)(2,1)S(1)}, bf16[64,32,128]{2,1,0:T(8,128)(2,1)}, u32[]{:S(2)}, u32[]{:S(2)}) collective-permute-start(bf16[64,32,128]{2,1,0:T(8,128)(2,1)S(1)} %collective-permute-done.8.refs_1_), channel_id=1, source_target_pairs={{0,1},{1,2},{2,3},{3,0},{4,5},{5,6},{6,7},{7,4},{8,9},{9,10},{10,1... | collective-permute-start | bytes 1572872 | tf_op jit(solution)/shard_map/ppermute | solution.py:256
  127.2 34.6 %all-to-all-start.3 = ((bf16[16,4,8,128]{3,2,1,0:T(8,128)(2,1)}), bf16[16,4,8,128]{3,2,1,0:T(8,128)(2,1)S(1)}, u32[]{:S(2)}, u32[]{:S(2)}) async-start(bf16[16,4,8,128]{3,2,1,0:T(8,128)(2,1)} %broadcast_in_dim.7), calls=%async_computation.3 | async-start | bytes 262144 | tf_op jit(solution)/shard_map/all_to_all | solution.py:266
  138.5 17.3 %collective-permute-start.6 = (bf16[8,64,128]{2,1,0:T(8,128)(2,1)S(1)}, bf16[8,64,128]{2,1,0:T(8,128)(2,1)S(1)}, u32[]{:S(2)}, u32[]{:S(2)}) collective-permute-start(bf16[8,64,128]{2,1,0:T(8,128)(2,1)S(1)} %get-tuple-element.24), channel_id=1, source_target_pairs={{0,4},{4,8},{8,12},{12,16},{16,20},{20,24},{24,28},{28,32},{32,36}... | collective-permute-start | bytes 393224 | tf_op jit(solution)/shard_map/ppermute | solution.py:262
  155.8 5.9 %collective-permute-start.7 = (bf16[8,64,128]{2,1,0:T(8,128)(2,1)}, bf16[8,64,128]{2,1,0:T(8,128)(2,1)S(1)}, u32[]{:S(2)}, u32[]{:S(2)}) collective-permute-start(bf16[8,64,128]{2,1,0:T(8,128)(2,1)} %copy-done.7), channel_id=1, source_target_pairs={{4,0},{8,4},{12,8},{16,12},{20,16},{24,20},{28,24},{32,28},{36,32}... | collective-permute-start | bytes 393224 | tf_op jit(solution)/shard_map/ppermute | solution.py:262
  161.8 5.8 %copy-start.4 = (f32[32,64,128]{2,1,0:T(8,128)S(1)}, f32[32,64,128]{2,1,0:T(8,128)}, u32[]{:S(2)}) copy-start(f32[32,64,128]{2,1,0:T(8,128)} %copy-done.3) | copy-start | bytes 3145732
  161.8 5.8 %copy-start.6 = (f32[32,64,128]{2,1,0:T(8,128)S(1)}, f32[32,64,128]{2,1,0:T(8,128)}, u32[]{:S(2)}) copy-start(f32[32,64,128]{2,1,0:T(8,128)} %copy-done.5) | copy-start | bytes 3145732
  165.7 5.9 %collective-permute-start.14 = (bf16[2,32,64,128]{3,2,1,0:T(8,128)(2,1)S(1)}, bf16[2,32,64,128]{3,2,1,0:T(8,128)(2,1)S(1)}, u32[]{:S(2)}, u32[]{:S(2)}) collective-permute-start(bf16[2,32,64,128]{3,2,1,0:T(8,128)(2,1)S(1)} %theirs.1), channel_id=1, source_target_pairs={{0,256},{256,0},{1,257},{257,1},{2,258},{258,2},{3,259},{259,3},{4... | collective-permute-start | bytes 3145736 | tf_op jit(solution)/shard_map/ppermute | solution.py:256

commit v6 on v5

--- a/solution.py
+++ b/solution.py
@@ -12,7 +12,7 @@
 NB = 8
 HB = 8
 LANES = 128
-CHUNKS = 1
+CHUNKS = 2
 FRONT = ("half", "z", "x")
 F32 = jnp.float32
 BF16 = jnp.bfloat16
@@ -135,18 +135,22 @@
     )(local_cols, couplings, blocks, low, high)
 
 
-def reduce_kernel(at_ref, gen_ref, own_ref, other_ref, out_ref, lhs):
+def reduce_kernel(at_ref, *refs):
+    gen_refs, (own_ref, other_ref, out_ref, lhs) = refs[:CHUNKS], refs[CHUNKS:]
     half, me = at_ref[0], at_ref[1]
-    blocks, ranks, _ = gen_ref.shape
+    blocks, ranks, _ = gen_refs[0].shape
     count = blocks // 2
     parts = own_ref.shape[0]
     low = low_lanes((ranks, LANES))
     for side, first in ((0, half * count), (1, (1 - half) * count)):
-        for k in range(count // 2):
-            one, two = gen_ref[first + 2 * k], gen_ref[first + 2 * k + 1]
-            lanes = slice(k * LANES, (k + 1) * LANES)
-            lhs[side, :ranks, lanes] = jnp.where(low, one, swapped_halves(two))
-            lhs[side, ranks:, lanes] = jnp.where(low, swapped_halves(one), two)
+        for part, gen_ref in enumerate(gen_refs):
+            left = slice(part * ranks, (part + 1) * ranks)
+            right = slice((CHUNKS + part) * ranks, (CHUNKS + part + 1) * ranks)
+            for k in range(count // 2):
+                one, two = gen_ref[first + 2 * k], gen_ref[first + 2 * k + 1]
+                lanes = slice(k * LANES, (k + 1) * LANES)
+                lhs[side, left, lanes] = jnp.where(low, one, swapped_halves(two))
+                lhs[side, right, lanes] = jnp.where(low, swapped_halves(one), two)
     for pair in range(0, parts, 2):
         total = 0.0
         for side, ref in ((0, own_ref), (1, other_ref)):
@@ -159,27 +163,28 @@
 
 
 def reduced(at, gens, own, other, splits):
-    _, ranks, _ = gens.shape
+    ranks = CHUNKS * gens[0].shape[1]
     parts, rows, _ = own.shape
     out = jax.ShapeDtypeStruct((splits, parts, 2 * ranks // splits, LANES), BF16)
     return pl.pallas_call(
         reduce_kernel,
         out_shape=out,
-        in_specs=[whole(SMEM)] + [whole(VMEM)] * 3,
+        in_specs=[whole(SMEM)] + [whole(VMEM)] * (CHUNKS + 2),
         out_specs=whole(VMEM),
         scratch_shapes=[pltpu.VMEM((2, 2 * ranks, rows), BF16)],
         compiler_params=grant(14),
         cost_estimate=cost(8 * ranks * rows * parts * LANES, 6 << 20),
         name="partials",
-    )(at, gens, own, other)
+    )(at, *gens, own, other)
 
 
 def low_rank_kernel(mine, pieces, at_ref, *refs):
     gens, w_ref, refs = refs[:pieces], refs[pieces], refs[pieces + 1 :]
     me, step, steps = at_ref[1], pl.program_id(0), pl.num_programs(0)
-    per, ranks, _ = gens[0].shape
+    per = gens[0].shape[0]
     lhs = refs[-1]
-    parts = lhs.shape[1] // ranks
+    parts = w_ref.shape[1]
+    ranks = lhs.shape[1] // parts
     low = low_lanes((LANES, LANES))
 
     @pl.when(step == 0)
@@ -214,7 +219,7 @@
 
 
 def low_rank(at, gens, w, added=()):
-    blocks, _, _ = gens[0].shape
+    blocks = gens[0].shape[0]
     count, per = blocks // 2, HB
     steps = count // per
     mine = bool(added)
@@ -274,31 +279,30 @@
     n_z, n_x, n_col = (lax.axis_size(a) for a in ("z", "x", "col"))
     blocks = samples.reshape(count, BS, width)
 
-    (packed,) = pack(child_map[0, 0], gen_left[0], gen_right[0])
-    gens = spread_out(packed, ("z", "x"))
+    packed_a, packed_b = pack(child_map[0, 0], gen_left[0], gen_right[0])
+    gens_a = spread_out(packed_a, ("z", "x"))
+    gens_b = spread_out(packed_b, ("z", "x"))
 
     shifted = [around(samples, "col", k) for k in range(1, n_col)]
+    low = along_front(blocks[count - HB :], 1)
+    high = along_front(blocks[:HB], -1)
+    local_cols = coupling_cols - lax.axis_index(FRONT) * count + HB
+
+    up_a, down_a = around(gens_a, "col", 1), around(gens_a, "col", -1)
+    shifted, _ = lax.optimization_barrier((shifted, gens_a))
     panels = jnp.stack([samples, *shifted])
     others = around(panels, "half", 1)
-    low = along_front(blocks[count - HB :], 1)
-    high = along_front(blocks[:HB], -1)
-
-    local_cols = coupling_cols - lax.axis_index(FRONT) * count + HB
-    gens, panels, others, local_cols = lax.optimization_barrier((gens, panels, others, local_cols))
-    partial = reduced(at, gens, panels, others, n_z)
-
-    middle = gens.shape[1] // 2
-    first, second = gens[:, :middle], gens[:, middle:]
-    up_a, down_b = around(first, "col", 1), around(second, "col", -1)
-    up_b, down_a = around(second, "col", 1), around(first, "col", -1)
-    far_a, far_b = around(up_a, "col", 1), around(down_b, "col", -1)
+    far_a = around(up_a, "col", 1)
     sparse_range, sparse_rows, up, down = sparse(local_cols, couplings, blocks, low, high)
+    below, above = along_front(up, 1), along_front(down, -1)
+    added = (sparse_range, sparse_rows, below, above)
+
+    gens_b, panels, others, up, down = lax.optimization_barrier((gens_b, panels, others, up, down))
+    partial = reduced(at, (gens_a, gens_b), panels, others, n_z)
+    up_b, down_b = around(gens_b, "col", 1), around(gens_b, "col", -1)
+    far_b = around(down_b, "col", -1)
+
     by_z = spread_out(partial, "z")
-    by_z, up, down = lax.optimization_barrier((by_z, up, down))
-    below, above = along_front(up, 1), along_front(down, -1)
-    at_last, below, above = lax.optimization_barrier((at, below, above))
-    added = (sparse_range, sparse_rows, below, above)
-
     by_z = jnp.sum(by_z.astype(F32), axis=0)
     copies = jnp.broadcast_to(by_z, (n_x, *by_z.shape)).reshape(n_x * n_col, *by_z.shape[1:])
     arrived = spread_out(copies, ("x", "col"))
@@ -306,11 +310,11 @@
     copies = jnp.broadcast_to(slice_sum, (n_z, *slice_sum.shape))
     w = spread_out(copies, "z")
 
-    everyone = (gens, up_a, up_b, far_a, far_b, down_a, down_b)
-    received = around(low_rank(at_last, everyone, w), "half", 1)
+    everyone = (gens_a, gens_b, up_a, up_b, far_a, far_b, down_a, down_b)
+    received = around(low_rank(at, everyone, w), "half", 1)
     range_out, rows_out = (
         (ours + theirs.astype(F32)).astype(BF16)
-        for ours, theirs in zip(low_rank(at_last, everyone, w, added), received)
+        for ours, theirs in zip(low_rank(at, everyone, w, added), received)
     )
     return range_out.reshape(samples.shape), rows_out.reshape(samples.shape)
 

time: 174 us -> 204 us (1.17)
  starting transfers between devices: 90.4 us -> 110 us
  local copies, waits for them, and re-layouts: 4.42 us -> 9.78 us
  waiting for transfers between devices: 57 us -> 60.5 us
    all_to_all x4 -> x5, starting transfers between devices: 40.8 us -> 54.9 us  [spread_out(): return lax.all_to_all(x, axis, split_axis=0, concat_axis=0, tiled=True)]
    ppermute x11, starting transfers between devices: 32.1 us -> 37.6 us  [around(): return lax.ppermute(x, axis, [(i, (i + by) % count) for i in range(count)])]
    unnamed x19 -> x31, local copies, waits for them, and re-layouts: 2.05 us -> 6.79 us
    ppermute x11, waiting for transfers between devices: 27.3 us -> 32.1 us  [around(): return lax.ppermute(x, axis, [(i, (i + by) % count) for i in range(count)])]
    all_to_all x4 -> x5, waiting for transfers between devices: 10.9 us -> 8.95 us  [spread_out(): return lax.all_to_all(x, axis, split_axis=0, concat_axis=0, tiled=True)]
  transfers between devices with their start and end apart: 19 -> 20, of which waited for: 9 -> 9; matrix products, arithmetic and copies ran while one was open for 2% -> 2% of each run, Pallas kernels for 4% -> 4%
where the time goes in v6:
time: 204 us; the launch traced here: 202 us
  starting transfers between devices  110 us (54%)
  waiting for transfers between devices  60.5 us (30%)
  Pallas kernels  17.2 us (8%)
  local copies, waits for them, and re-layouts  9.78 us (5%)
  other arithmetic  3.04 us (1%)
    all_to_all x5, starting transfers between devices, spread_out(): return lax.all_to_all(x, axis, split_axis=0, concat_axis=0, tiled=True)  54.9 us
    ppermute x11, starting transfers between devices, around(): return lax.ppermute(x, axis, [(i, (i + by) % count) for i in range(count)])  37.6 us
    ppermute x11, waiting for transfers between devices, around(): return lax.ppermute(x, axis, [(i, (i + by) % count) for i in range(count)])  32.1 us
    ppermute x4, waiting for transfers between devices, along_front(): return lax.ppermute(x, FRONT, pairs)  19.4 us
    ppermute x4, starting transfers between devices, along_front(): return lax.ppermute(x, FRONT, pairs)  17.8 us
    all_to_all x5, waiting for transfers between devices, spread_out(): return lax.all_to_all(x, axis, split_axis=0, concat_axis=0, tiled=True)  8.95 us
    pallas_call x2, Pallas kernels, low_rank(): pl.pallas_call(functools.partial(low_rank_kernel, mine, len(gens)), grid_...  7.8 us
    unnamed x31, local copies, waits for them, and re-layouts  6.79 us
  transfers between devices with their start and end apart: 20, of which 9 were waited for; matrix products, arithmetic and copies ran while one was open for 2% of the time, Pallas kernels for 4%

profile of v6, /device:TPU:1, one launch (start us, length us, event | category | flops | bytes accessed | tf_op | source)
XLA Modules:
  0.0 201.7 jit_solution(11538678970222349630)
XLA Ops:
  0.6 0.0 copy-start
  0.6 2.6 %pack.1 = (bf16[64,32,128]{2,1,0:T(8,128)(2,1)}, bf16[64,32,128]{2,1,0:T(8,128)(2,1)}) custom-call(s32[64]{0:T(128)} %bitcast.36, bf16[64,4096]{1,0:T(8,128)(2,1)} %bitcast.28, bf16[64,4096]{1,0:T(8,128)(2,1)} %bitcast.29), custom_call_target="tpu_custom_call" | custom-call | bytes 2097152 | tf_op jit(solution)/shard_map/pack/pallas_call | solution.py:59
  3.3 19.1 %all-to-all-start = ((bf16[64,32,128]{2,1,0:T(8,128)(2,1)}), bf16[64,32,128]{2,1,0:T(8,128)(2,1)S(1)}, u32[]{:S(2)}, u32[]{:S(2)}) async-start(bf16[64,32,128]{2,1,0:T(8,128)(2,1)} %get-tuple-element.16), calls=%async_computation | async-start | bytes 1048576 | tf_op jit(solution)/shard_map/all_to_all | solution.py:271
  22.4 0.0 copy-done
  22.4 4.6 %collective-permute-start.2 = (bf16[2048,128]{1,0:T(8,128)(2,1)S(1)}, bf16[2048,128]{1,0:T(8,128)(2,1)S(1)}, u32[]{:S(2)}, u32[]{:S(2)}) collective-permute-start(bf16[2048,128]{1,0:T(8,128)(2,1)S(1)} %copy-done), channel_id=1, source_target_pairs={{0,3},{1,0},{2,1},{3,2},{4,7},{5,4},{6,5},{7,6},{8,11},{9,8},{10,9... | collective-permute-start | bytes 1572872 | tf_op jit(solution)/shard_map/ppermute | solution.py:261
  27.0 2.3 %collective-permute-start.1 = (bf16[2048,128]{1,0:T(8,128)(2,1)S(1)}, bf16[2048,128]{1,0:T(8,128)(2,1)S(1)}, u32[]{:S(2)}, u32[]{:S(2)}) collective-permute-start(bf16[2048,128]{1,0:T(8,128)(2,1)S(1)} %copy-done), channel_id=1, source_target_pairs={{0,2},{1,3},{2,0},{3,1},{4,6},{5,7},{6,4},{7,5},{8,10},{9,11},{10,... | collective-permute-start | bytes 1572872 | tf_op jit(solution)/shard_map/ppermute | solution.py:261
  29.3 2.6 %collective-permute-start = (bf16[2048,128]{1,0:T(8,128)(2,1)S(1)}, bf16[2048,128]{1,0:T(8,128)(2,1)S(1)}, u32[]{:S(2)}, u32[]{:S(2)}) collective-permute-start(bf16[2048,128]{1,0:T(8,128)(2,1)S(1)} %copy-done), channel_id=1, source_target_pairs={{0,1},{1,2},{2,3},{3,0},{4,5},{5,6},{6,7},{7,4},{8,9},{9,10},{10,1... | collective-permute-start | bytes 1572872 | tf_op jit(solution)/shard_map/ppermute | solution.py:261
  31.9 6.5 %collective-permute-done.2 = bf16[2048,128]{1,0:T(8,128)(2,1)S(1)} collective-permute-done((bf16[2048,128]{1,0:T(8,128)(2,1)S(1)}, bf16[2048,128]{1,0:T(8,128)(2,1)S(1)}, u32[]{:S(2)}, u32[]{:S(2)}) %collective-permute-start.2) | collective-permute-done | bytes 524320 | tf_op jit(solution)/shard_map/ppermute | solution.py:261
  38.4 4.3 %collective-permute-done.1 = bf16[2048,128]{1,0:T(8,128)(2,1)S(1)} collective-permute-done((bf16[2048,128]{1,0:T(8,128)(2,1)S(1)}, bf16[2048,128]{1,0:T(8,128)(2,1)S(1)}, u32[]{:S(2)}, u32[]{:S(2)}) %collective-permute-start.1) | collective-permute-done | bytes 524320 | tf_op jit(solution)/shard_map/ppermute | solution.py:261
  42.7 12.8 %collective-permute-done = bf16[2048,128]{1,0:T(8,128)(2,1)S(1)} collective-permute-done((bf16[2048,128]{1,0:T(8,128)(2,1)S(1)}, bf16[2048,128]{1,0:T(8,128)(2,1)S(1)}, u32[]{:S(2)}, u32[]{:S(2)}) %collective-permute-start) | collective-permute-done | bytes 524320 | tf_op jit(solution)/shard_map/ppermute | solution.py:261
  55.5 0.0 all-to-all-done.refs_0_
  55.5 0.0 copy-done.11
  55.5 0.0 copy-done.12
  55.5 0.8 copy-done.13
  56.3 1.6 pad_maximum_fusion.refs_2_
  57.9 2.4 %collective-permute-start.3 = (bf16[4,2048,128]{2,1,0:T(8,128)(2,1)S(1)}, bf16[4,2048,128]{2,1,0:T(8,128)(2,1)}, u32[]{:S(2)}, u32[]{:S(2)}) collective-permute-start(bf16[4,2048,128]{2,1,0:T(8,128)(2,1)S(1)} %pad_maximum_fusion.refs_2_), channel_id=1, source_target_pairs={{0,256},{256,0},{1,257},{257,1},{2,258},{258,2},{3,259},{259,3},{4... | collective-permute-start | bytes 6291464 | tf_op jit(solution)/shard_map/ppermute | solution.py:261
  60.3 14.5 %all-to-all-start.1 = ((bf16[64,32,128]{2,1,0:T(8,128)(2,1)}), bf16[64,32,128]{2,1,0:T(8,128)(2,1)S(1)}, u32[]{:S(2)}, u32[]{:S(2)}) async-start(bf16[64,32,128]{2,1,0:T(8,128)(2,1)} %get-tuple-element.17), calls=%async_computation.1 | async-start | bytes 1048576 | tf_op jit(solution)/shard_map/all_to_all | solution.py:271
  74.9 1.7 fusion.2
  76.6 2.9 %collective-permute-start.4 = (bf16[8,64,128]{2,1,0:T(8,128)(2,1)}, bf16[8,64,128]{2,1,0:T(8,128)(2,1)S(1)}, u32[]{:S(2)}, u32[]{:S(2)}) collective-permute-start(bf16[8,64,128]{2,1,0:T(8,128)(2,1)} %bitcast.10), channel_id=1, source_target_pairs={{0,4},{4,8},{8,12},{12,16},{16,20},{20,24},{24,28},{28,32},{32,36}... | collective-permute-start | bytes 393224 | tf_op jit(solution)/shard_map/ppermute | solution.py:267
  79.5 6.0 %collective-permute-start.5 = (bf16[8,64,128]{2,1,0:T(8,128)(2,1)}, bf16[8,64,128]{2,1,0:T(8,128)(2,1)S(1)}, u32[]{:S(2)}, u32[]{:S(2)}) collective-permute-start(bf16[8,64,128]{2,1,0:T(8,128)(2,1)} %bitcast.11), channel_id=1, source_target_pairs={{4,0},{8,4},{12,8},{16,12},{20,16},{24,20},{28,24},{32,28},{36,32}... | collective-permute-start | bytes 393224 | tf_op jit(solution)/shard_map/ppermute | solution.py:267
  85.5 0.1 copy.10
  85.6 0.1 pad_add_fusion.at_ref
  85.7 17.5 %collective-permute-done.4.low_ref = bf16[8,64,128]{2,1,0:T(8,128)(2,1)S(1)} collective-permute-done((bf16[8,64,128]{2,1,0:T(8,128)(2,1)}, bf16[8,64,128]{2,1,0:T(8,128)(2,1)S(1)}, u32[]{:S(2)}, u32[]{:S(2)}) %collective-permute-start.4) | collective-permute-done | bytes 131104 | tf_op jit(solution)/shard_map/ppermute | solution.py:267
  103.2 0.0 collective-permute-done.5.high_ref
  103.2 1.0 copy-done.1
  104.3 1.6 copy-done.2
  105.8 3.6 %sparse.1 = (f32[32,64,128]{2,1,0:T(8,128)S(1)}, f32[32,64,128]{2,1,0:T(8,128)S(1)}, bf16[8,64,128]{2,1,0:T(8,128)(2,1)S(1)}, bf16[8,64,128]{2,1,0:T(8,128)(2,1)S(1)}) custom-call(s32[32,8]{1,0:T(8,128)S(1)} %subtract_add_fusion.cols_ref, bf16[32,64,512]{2,1,0:T(8,128)(2,1)S(1)} %copy-done.2, bf16[32,64,128]{2,1,0:T(8,128)(2,1)S(1)} %bitcast.27, ...), custom_call_target="tpu_custom_call" | custom-call | flops 536870912 | bytes 6291456 | tf_op jit(solution)/shard_map/sparse/pallas_call | solution.py:106
  109.5 1.0 copy-done.3
  110.5 1.0 copy-done.5
  111.5 0.6 copy-done.7
  112.1 0.6 copy-done.9
  112.8 0.0 all-to-all-done.1.refs_1_
  112.8 0.0 collective-permute-done.3.refs_3_
  112.8 3.2 %partials.1 = bf16[16,4,8,128]{3,2,1,0:T(8,128)(2,1)} custom-call(s32[2]{0:T(128)S(1)} %pad_add_fusion.at_ref, bf16[64,32,128]{2,1,0:T(8,128)(2,1)S(1)} %all-to-all-done.refs_0_, bf16[64,32,128]{2,1,0:T(8,128)(2,1)S(1)} %all-to-all-done.1.refs_1_, bf16[4,2048,128]{2,1,0:T(8,128)(2,1)S(1)} %pad_maximum_fusion.refs_2_, ...), custom_call_target="tpu_custom_call" | custom-call | flops 536870912 | bytes 6291456 | tf_op jit(solution)/shard_map/partials/pallas_call | solution.py:169
  115.9 11.4 %all-to-all-start.2 = ((bf16[16,4,8,128]{3,2,1,0:T(8,128)(2,1)}), bf16[16,4,8,128]{3,2,1,0:T(8,128)(2,1)S(1)}, u32[]{:S(2)}, u32[]{:S(2)}) async-start(bf16[16,4,8,128]{3,2,1,0:T(8,128)(2,1)} %partials.1), calls=%async_computation.2 | async-start | bytes 262144 | tf_op jit(solution)/shard_map/all_to_all | solution.py:271
  127.4 1.9 collective-permute-start.6
  129.3 4.6 %collective-permute-start.9 = (bf16[64,32,128]{2,1,0:T(8,128)(2,1)S(1)}, bf16[64,32,128]{2,1,0:T(8,128)(2,1)S(1)}, u32[]{:S(2)}, u32[]{:S(2)}) collective-permute-start(bf16[64,32,128]{2,1,0:T(8,128)(2,1)S(1)} %all-to-all-done.1.refs_1_), channel_id=1, source_target_pairs={{0,3},{1,0},{2,1},{3,2},{4,7},{5,4},{6,5},{7,6},{8,11},{9,8},{10,9... | collective-permute-start | bytes 1572872 | tf_op jit(solution)/shard_map/ppermute | solution.py:261
  133.9 5.5 %all-to-all-done.2 = bf16[16,4,8,128]{3,2,1,0:T(8,128)(2,1)S(1)} async-done(((bf16[16,4,8,128]{3,2,1,0:T(8,128)(2,1)}), bf16[16,4,8,128]{3,2,1,0:T(8,128)(2,1)S(1)}, u32[]{:S(2)}, u32[]{:S(2)}) %all-to-all-start.2) | async-done | bytes 131104 | tf_op jit(solution)/shard_map/all_to_all | solution.py:271
  139.4 0.6 broadcast_in_dim.6
  140.0 3.5 %all-to-all-start.3 = ((f32[16,8,128]{2,1,0:T(8,128)}), f32[16,8,128]{2,1,0:T(8,128)S(1)}, u32[]{:S(2)}, u32[]{:S(2)}) async-start(f32[16,8,128]{2,1,0:T(8,128)} %bitcast.12), calls=%async_computation.3 | async-start | bytes 131072 | tf_op jit(solution)/shard_map/all_to_all | solution.py:271
  143.5 4.4 %collective-permute-start.11 = (bf16[64,32,128]{2,1,0:T(8,128)(2,1)S(1)}, bf16[64,32,128]{2,1,0:T(8,128)(2,1)S(1)}, u32[]{:S(2)}, u32[]{:S(2)}) collective-permute-start(bf16[64,32,128]{2,1,0:T(8,128)(2,1)S(1)} %all-to-all-done.refs_0_), channel_id=1, source_target_pairs={{0,3},{1,0},{2,1},{3,2},{4,7},{5,4},{6,5},{7,6},{8,11},{9,8},{10,9... | collective-permute-start | bytes 1572872 | tf_op jit(solution)/shard_map/ppermute | solution.py:261
  147.9 0.0 collective-permute-done.6.refs_2_
  147.9 1.9 collective-permute-start.8
  149.8 2.1 %collective-permute-start.7 = (bf16[64,32,128]{2,1,0:T(8,128)(2,1)S(1)}, bf16[64,32,128]{2,1,0:T(8,128)(2,1)}, u32[]{:S(2)}, u32[]{:S(2)}) collective-permute-start(bf16[64,32,128]{2,1,0:T(8,128)(2,1)S(1)} %all-to-all-done.1.refs_1_), channel_id=1, source_target_pairs={{0,1},{1,2},{2,3},{3,0},{4,5},{5,6},{6,7},{7,4},{8,9},{9,10},{10,1... | collective-permute-start | bytes 1572872 | tf_op jit(solution)/shard_map/ppermute | solution.py:261
  152.0 0.0 collective-permute-done.9.refs_7_
  152.0 4.4 %collective-permute-start.10 = (bf16[64,32,128]{2,1,0:T(8,128)(2,1)S(1)}, bf16[64,32,128]{2,1,0:T(8,128)(2,1)}, u32[]{:S(2)}, u32[]{:S(2)}) collective-permute-start(bf16[64,32,128]{2,1,0:T(8,128)(2,1)S(1)} %collective-permute-done.9.refs_7_), channel_id=1, source_target_pairs={{0,3},{1,0},{2,1},{3,2},{4,7},{5,4},{6,5},{7,6},{8,11},{9,8},{10,9... | collective-permute-start | bytes 1572872 | tf_op jit(solution)/shard_map/ppermute | solution.py:261
  156.4 0.0 all-to-all-done.3
  156.4 0.7 broadcast_in_dim.7
  157.1 6.3 %all-to-all-start.4 = ((bf16[16,4,8,128]{3,2,1,0:T(8,128)(2,1)}), bf16[16,4,8,128]{3,2,1,0:T(8,128)(2,1)S(1)}, u32[]{:S(2)}, u32[]{:S(2)}) async-start(bf16[16,4,8,128]{3,2,1,0:T(8,128)(2,1)} %broadcast_in_dim.7), calls=%async_computation.4 | async-start | bytes 262144 | tf_op jit(solution)/shard_map/all_to_all | solution.py:271
  163.4 0.0 collective-permute-done.11.refs_6_
  163.4 0.0 collective-permute-done.8.refs_4_
  163.4 8.4 %collective-permute-done.7.refs_3_ = bf16[64,32,128]{2,1,0:T(8,128)(2,1)} collective-permute-done((bf16[64,32,128]{2,1,0:T(8,128)(2,1)S(1)}, bf16[64,32,128]{2,1,0:T(8,128)(2,1)}, u32[]{:S(2)}, u32[]{:S(2)}) %collective-permute-start.7) | collective-permute-done | bytes 524320 | tf_op jit(solution)/shard_map/ppermute | solution.py:261
  171.9 3.5 %all-to-all-done.4.refs_8_ = bf16[16,4,8,128]{3,2,1,0:T(8,128)(2,1)S(1)} async-done(((bf16[16,4,8,128]{3,2,1,0:T(8,128)(2,1)}), bf16[16,4,8,128]{3,2,1,0:T(8,128)(2,1)S(1)}, u32[]{:S(2)}, u32[]{:S(2)}) %all-to-all-start.4) | async-done | bytes 131104 | tf_op jit(solution)/shard_map/all_to_all | solution.py:271
  175.4 0.0 collective-permute-done.10.refs_5_
  175.4 3.9 %theirs.1 = bf16[2,32,64,128]{3,2,1,0:T(8,128)(2,1)S(1)} custom-call(s32[2]{0:T(128)S(1)} %pad_add_fusion.at_ref, bf16[64,32,128]{2,1,0:T(8,128)(2,1)S(1)} %all-to-all-done.refs_0_, bf16[64,32,128]{2,1,0:T(8,128)(2,1)S(1)} %all-to-all-done.1.refs_1_, bf16[64,32,128]{2,1,0:T(8,128)(2,1)S(1)} %collective-permute-done.6.refs_2_, ...), custom_call_target="tpu_custom_call" | custom-call | flops 536870912 | bytes 4194304 | tf_op jit(solution)/shard_map/theirs/pallas_call | solution.py:243
  179.3 6.4 %collective-permute-start.14 = (bf16[2,32,64,128]{3,2,1,0:T(8,128)(2,1)S(1)}, bf16[2,32,64,128]{3,2,1,0:T(8,128)(2,1)S(1)}, u32[]{:S(2)}, u32[]{:S(2)}) collective-permute-start(bf16[2,32,64,128]{3,2,1,0:T(8,128)(2,1)S(1)} %theirs.1), channel_id=1, source_target_pairs={{0,256},{256,0},{1,257},{257,1},{2,258},{258,2},{3,259},{259,3},{4... | collective-permute-start | bytes 3145736 | tf_op jit(solution)/shard_map/ppermute | solution.py:261
  185.7 2.8 %collective-permute-start.12 = (bf16[8,64,128]{2,1,0:T(8,128)(2,1)S(1)}, bf16[8,64,128]{2,1,0:T(8,128)(2,1)S(1)}, u32[]{:S(2)}, u32[]{:S(2)}) collective-permute-start(bf16[8,64,128]{2,1,0:T(8,128)(2,1)S(1)} %copy-done.10), channel_id=1, source_target_pairs={{0,4},{4,8},{8,12},{12,16},{16,20},{20,24},{24,28},{28,32},{32,36}... | collective-permute-start | bytes 393224 | tf_op jit(solution)/shard_map/ppermute | solution.py:267
  188.5 6.1 %collective-permute-start.13 = (bf16[8,64,128]{2,1,0:T(8,128)(2,1)S(1)}, bf16[8,64,128]{2,1,0:T(8,128)(2,1)S(1)}, u32[]{:S(2)}, u32[]{:S(2)}) collective-permute-start(bf16[8,64,128]{2,1,0:T(8,128)(2,1)S(1)} %copy-done.8), channel_id=1, source_target_pairs={{4,0},{8,4},{12,8},{16,12},{20,16},{24,20},{28,24},{32,28},{36,32}... | collective-permute-start | bytes 393224 | tf_op jit(solution)/shard_map/ppermute | solution.py:267
  194.6 0.7 collective-permute-done.12.refs_11_
  195.3 1.2 collective-permute-done.13.refs_12_
  196.5 0.0 copy-done.6
  196.5 3.9 %mine.1 = (f32[32,64,128]{2,1,0:T(8,128)S(1)}, f32[32,64,128]{2,1,0:T(8,128)S(1)}) custom-call(s32[2]{0:T(128)S(1)} %pad_add_fusion.at_ref, bf16[64,32,128]{2,1,0:T(8,128)(2,1)S(1)} %all-to-all-done.refs_0_, bf16[64,32,128]{2,1,0:T(8,128)(2,1)S(1)} %all-to-all-done.1.refs_1_, bf16[64,32,128]{2,1,0:T(8,128)(2,1)S(1)} %collective-permute-done.6.refs_2_, ...), custom_call_target="tpu_custom_call" | custom-call | flops 536870912 | bytes 4194304 | tf_op jit(solution)/shard_map/mine/pallas_call | solution.py:243
  200.4 0.0 collective-permute-done.14
  200.4 1.3 fusion
  (21 shorter events, 0.1 us)
Async XLA Ops:
  0.6 21.7 %copy-start = (bf16[2048,128]{1,0:T(8,128)(2,1)S(1)}, bf16[2048,128]{1,0:T(8,128)(2,1)}, u32[]{:S(2)}) copy-start(bf16[2048,128]{1,0:T(8,128)(2,1)} %param.6) | copy-start | bytes 1572868
  3.3 52.2 %all-to-all-start = ((bf16[64,32,128]{2,1,0:T(8,128)(2,1)}), bf16[64,32,128]{2,1,0:T(8,128)(2,1)S(1)}, u32[]{:S(2)}, u32[]{:S(2)}) async-start(bf16[64,32,128]{2,1,0:T(8,128)(2,1)} %get-tuple-element.16), calls=%async_computation | async-start | bytes 1048576 | tf_op jit(solution)/shard_map/all_to_all | solution.py:271
  22.4 16.0 %collective-permute-start.2 = (bf16[2048,128]{1,0:T(8,128)(2,1)S(1)}, bf16[2048,128]{1,0:T(8,128)(2,1)S(1)}, u32[]{:S(2)}, u32[]{:S(2)}) collective-permute-start(bf16[2048,128]{1,0:T(8,128)(2,1)S(1)} %copy-done), channel_id=1, source_target_pairs={{0,3},{1,0},{2,1},{3,2},{4,7},{5,4},{6,5},{7,6},{8,11},{9,8},{10,9... | collective-permute-start | bytes 1572872 | tf_op jit(solution)/shard_map/ppermute | solution.py:261
  27.0 15.7 %collective-permute-start.1 = (bf16[2048,128]{1,0:T(8,128)(2,1)S(1)}, bf16[2048,128]{1,0:T(8,128)(2,1)S(1)}, u32[]{:S(2)}, u32[]{:S(2)}) collective-permute-start(bf16[2048,128]{1,0:T(8,128)(2,1)S(1)} %copy-done), channel_id=1, source_target_pairs={{0,2},{1,3},{2,0},{3,1},{4,6},{5,7},{6,4},{7,5},{8,10},{9,11},{10,... | collective-permute-start | bytes 1572872 | tf_op jit(solution)/shard_map/ppermute | solution.py:261
  29.3 26.2 %collective-permute-start = (bf16[2048,128]{1,0:T(8,128)(2,1)S(1)}, bf16[2048,128]{1,0:T(8,128)(2,1)S(1)}, u32[]{:S(2)}, u32[]{:S(2)}) collective-permute-start(bf16[2048,128]{1,0:T(8,128)(2,1)S(1)} %copy-done), channel_id=1, source_target_pairs={{0,1},{1,2},{2,3},{3,0},{4,5},{5,6},{6,7},{7,4},{8,9},{9,10},{10,1... | collective-permute-start | bytes 1572872 | tf_op jit(solution)/shard_map/ppermute | solution.py:261
  38.4 17.1 %copy-start.11 = (bf16[2048,128]{1,0:T(8,128)(2,1)}, bf16[2048,128]{1,0:T(8,128)(2,1)S(1)}, u32[]{:S(2)}) copy-start(bf16[2048,128]{1,0:T(8,128)(2,1)S(1)} %collective-permute-done.2) | copy-start | bytes 1572868
  42.7 12.8 %copy-start.12 = (bf16[2048,128]{1,0:T(8,128)(2,1)}, bf16[2048,128]{1,0:T(8,128)(2,1)S(1)}, u32[]{:S(2)}) copy-start(bf16[2048,128]{1,0:T(8,128)(2,1)S(1)} %collective-permute-done.1) | copy-start | bytes 1572868
  55.5 0.8 copy-start.13
  56.3 29.2 %copy-start.14 = (s32[32,8]{0,1:T(8,128)S(1)}, s32[32,8]{0,1:T(8,128)}, u32[]{:S(2)}) copy-start(s32[32,8]{0,1:T(8,128)} %param.8) | copy-start | bytes 3076
  57.9 54.8 %collective-permute-start.3 = (bf16[4,2048,128]{2,1,0:T(8,128)(2,1)S(1)}, bf16[4,2048,128]{2,1,0:T(8,128)(2,1)}, u32[]{:S(2)}, u32[]{:S(2)}) collective-permute-start(bf16[4,2048,128]{2,1,0:T(8,128)(2,1)S(1)} %pad_maximum_fusion.refs_2_), channel_id=1, source_target_pairs={{0,256},{256,0},{1,257},{257,1},{2,258},{258,2},{3,259},{259,3},{4... | collective-permute-start | bytes 6291464 | tf_op jit(solution)/shard_map/ppermute | solution.py:261
  60.3 52.4 %all-to-all-start.1 = ((bf16[64,32,128]{2,1,0:T(8,128)(2,1)}), bf16[64,32,128]{2,1,0:T(8,128)(2,1)S(1)}, u32[]{:S(2)}, u32[]{:S(2)}) async-start(bf16[64,32,128]{2,1,0:T(8,128)(2,1)} %get-tuple-element.17), calls=%async_computation.1 | async-start | bytes 1048576 | tf_op jit(solution)/shard_map/all_to_all | solution.py:271
  76.6 26.6 %collective-permute-start.4 = (bf16[8,64,128]{2,1,0:T(8,128)(2,1)}, bf16[8,64,128]{2,1,0:T(8,128)(2,1)S(1)}, u32[]{:S(2)}, u32[]{:S(2)}) collective-permute-start(bf16[8,64,128]{2,1,0:T(8,128)(2,1)} %bitcast.10), channel_id=1, source_target_pairs={{0,4},{4,8},{8,12},{12,16},{16,20},{20,24},{24,28},{28,32},{32,36}... | collective-permute-start | bytes 393224 | tf_op jit(solution)/shard_map/ppermute | solution.py:267
  79.5 23.7 %collective-permute-start.5 = (bf16[8,64,128]{2,1,0:T(8,128)(2,1)}, bf16[8,64,128]{2,1,0:T(8,128)(2,1)S(1)}, u32[]{:S(2)}, u32[]{:S(2)}) collective-permute-start(bf16[8,64,128]{2,1,0:T(8,128)(2,1)} %bitcast.11), channel_id=1, source_target_pairs={{4,0},{8,4},{12,8},{16,12},{20,16},{24,20},{28,24},{32,28},{36,32}... | collective-permute-start | bytes 393224 | tf_op jit(solution)/shard_map/ppermute | solution.py:267
  103.2 1.0 copy-start.1
  104.2 1.6 copy-start.2
  109.5 1.0 copy-start.3
  110.5 1.0 copy-start.5
  111.5 0.7 copy-start.7
  112.1 0.7 copy-start.9
  115.9 23.4 %all-to-all-start.2 = ((bf16[16,4,8,128]{3,2,1,0:T(8,128)(2,1)}), bf16[16,4,8,128]{3,2,1,0:T(8,128)(2,1)S(1)}, u32[]{:S(2)}, u32[]{:S(2)}) async-start(bf16[16,4,8,128]{3,2,1,0:T(8,128)(2,1)} %partials.1), calls=%async_computation.2 | async-start | bytes 262144 | tf_op jit(solution)/shard_map/all_to_all | solution.py:271
  127.4 20.5 %collective-permute-start.6 = (bf16[64,32,128]{2,1,0:T(8,128)(2,1)S(1)}, bf16[64,32,128]{2,1,0:T(8,128)(2,1)S(1)}, u32[]{:S(2)}, u32[]{:S(2)}) collective-permute-start(bf16[64,32,128]{2,1,0:T(8,128)(2,1)S(1)} %all-to-all-done.refs_0_), channel_id=1, source_target_pairs={{0,1},{1,2},{2,3},{3,0},{4,5},{5,6},{6,7},{7,4},{8,9},{9,10},{10,1... | collective-permute-start | bytes 1572872 | tf_op jit(solution)/shard_map/ppermute | solution.py:261
  129.3 22.7 %collective-permute-start.9 = (bf16[64,32,128]{2,1,0:T(8,128)(2,1)S(1)}, bf16[64,32,128]{2,1,0:T(8,128)(2,1)S(1)}, u32[]{:S(2)}, u32[]{:S(2)}) collective-permute-start(bf16[64,32,128]{2,1,0:T(8,128)(2,1)S(1)} %all-to-all-done.1.refs_1_), channel_id=1, source_target_pairs={{0,3},{1,0},{2,1},{3,2},{4,7},{5,4},{6,5},{7,6},{8,11},{9,8},{10,9... | collective-permute-start | bytes 1572872 | tf_op jit(solution)/shard_map/ppermute | solution.py:261
  140.0 16.3 %all-to-all-start.3 = ((f32[16,8,128]{2,1,0:T(8,128)}), f32[16,8,128]{2,1,0:T(8,128)S(1)}, u32[]{:S(2)}, u32[]{:S(2)}) async-start(f32[16,8,128]{2,1,0:T(8,128)} %bitcast.12), calls=%async_computation.3 | async-start | bytes 131072 | tf_op jit(solution)/shard_map/all_to_all | solution.py:271
  143.5 19.9 %collective-permute-start.11 = (bf16[64,32,128]{2,1,0:T(8,128)(2,1)S(1)}, bf16[64,32,128]{2,1,0:T(8,128)(2,1)S(1)}, u32[]{:S(2)}, u32[]{:S(2)}) collective-permute-start(bf16[64,32,128]{2,1,0:T(8,128)(2,1)S(1)} %all-to-all-done.refs_0_), channel_id=1, source_target_pairs={{0,3},{1,0},{2,1},{3,2},{4,7},{5,4},{6,5},{7,6},{8,11},{9,8},{10,9... | collective-permute-start | bytes 1572872 | tf_op jit(solution)/shard_map/ppermute | solution.py:261
  147.9 15.5 %collective-permute-start.8 = (bf16[64,32,128]{2,1,0:T(8,128)(2,1)S(1)}, bf16[64,32,128]{2,1,0:T(8,128)(2,1)S(1)}, u32[]{:S(2)}, u32[]{:S(2)}) collective-permute-start(bf16[64,32,128]{2,1,0:T(8,128)(2,1)S(1)} %collective-permute-done.6.refs_2_), channel_id=1, source_target_pairs={{0,1},{1,2},{2,3},{3,0},{4,5},{5,6},{6,7},{7,4},{8,9},{9,10},{10,1... | collective-permute-start | bytes 1572872 | tf_op jit(solution)/shard_map/ppermute | solution.py:261
  149.8 22.1 %collective-permute-start.7 = (bf16[64,32,128]{2,1,0:T(8,128)(2,1)S(1)}, bf16[64,32,128]{2,1,0:T(8,128)(2,1)}, u32[]{:S(2)}, u32[]{:S(2)}) collective-permute-start(bf16[64,32,128]{2,1,0:T(8,128)(2,1)S(1)} %all-to-all-done.1.refs_1_), channel_id=1, source_target_pairs={{0,1},{1,2},{2,3},{3,0},{4,5},{5,6},{6,7},{7,4},{8,9},{9,10},{10,1... | collective-permute-start | bytes 1572872 | tf_op jit(solution)/shard_map/ppermute | solution.py:261
  152.0 23.4 %collective-permute-start.10 = (bf16[64,32,128]{2,1,0:T(8,128)(2,1)S(1)}, bf16[64,32,128]{2,1,0:T(8,128)(2,1)}, u32[]{:S(2)}, u32[]{:S(2)}) collective-permute-start(bf16[64,32,128]{2,1,0:T(8,128)(2,1)S(1)} %collective-permute-done.9.refs_7_), channel_id=1, source_target_pairs={{0,3},{1,0},{2,1},{3,2},{4,7},{5,4},{6,5},{7,6},{8,11},{9,8},{10,9... | collective-permute-start | bytes 1572872 | tf_op jit(solution)/shard_map/ppermute | solution.py:261
  157.1 18.3 %all-to-all-start.4 = ((bf16[16,4,8,128]{3,2,1,0:T(8,128)(2,1)}), bf16[16,4,8,128]{3,2,1,0:T(8,128)(2,1)S(1)}, u32[]{:S(2)}, u32[]{:S(2)}) async-start(bf16[16,4,8,128]{3,2,1,0:T(8,128)(2,1)} %broadcast_in_dim.7), calls=%async_computation.4 | async-start | bytes 262144 | tf_op jit(solution)/shard_map/all_to_all | solution.py:271
  163.4 22.3 %copy-start.10 = (bf16[8,64,128]{2,1,0:T(8,128)(2,1)S(1)}, bf16[8,64,128]{2,1,0:T(8,128)(2,1)}, u32[]{:S(2)}) copy-start(bf16[8,64,128]{2,1,0:T(8,128)(2,1)} %copy-done.9) | copy-start | bytes 393220
  163.4 25.1 %copy-start.8 = (bf16[8,64,128]{2,1,0:T(8,128)(2,1)S(1)}, bf16[8,64,128]{2,1,0:T(8,128)(2,1)}, u32[]{:S(2)}) copy-start(bf16[8,64,128]{2,1,0:T(8,128)(2,1)} %copy-done.7) | copy-start | bytes 393220
  175.3 21.2 %copy-start.4 = (f32[32,64,128]{2,1,0:T(8,128)S(1)}, f32[32,64,128]{2,1,0:T(8,128)}, u32[]{:S(2)}) copy-start(f32[32,64,128]{2,1,0:T(8,128)} %copy-done.3) | copy-start | bytes 3145732
  175.4 21.2 %copy-start.6 = (f32[32,64,128]{2,1,0:T(8,128)S(1)}, f32[32,64,128]{2,1,0:T(8,128)}, u32[]{:S(2)}) copy-start(f32[32,64,128]{2,1,0:T(8,128)} %copy-done.5) | copy-start | bytes 3145732
  179.3 21.2 %collective-permute-start.14 = (bf16[2,32,64,128]{3,2,1,0:T(8,128)(2,1)S(1)}, bf16[2,32,64,128]{3,2,1,0:T(8,128)(2,1)S(1)}, u32[]{:S(2)}, u32[]{:S(2)}) collective-permute-start(bf16[2,32,64,128]{3,2,1,0:T(8,128)(2,1)S(1)} %theirs.1), channel_id=1, source_target_pairs={{0,256},{256,0},{1,257},{257,1},{2,258},{258,2},{3,259},{259,3},{4... | collective-permute-start | bytes 3145736 | tf_op jit(solution)/shard_map/ppermute | solution.py:261
  185.7 9.6 %collective-permute-start.12 = (bf16[8,64,128]{2,1,0:T(8,128)(2,1)S(1)}, bf16[8,64,128]{2,1,0:T(8,128)(2,1)S(1)}, u32[]{:S(2)}, u32[]{:S(2)}) collective-permute-start(bf16[8,64,128]{2,1,0:T(8,128)(2,1)S(1)} %copy-done.10), channel_id=1, source_target_pairs={{0,4},{4,8},{8,12},{12,16},{16,20},{20,24},{24,28},{28,32},{32,36}... | collective-permute-start | bytes 393224 | tf_op jit(solution)/shard_map/ppermute | solution.py:267
  188.5 8.0 %collective-permute-start.13 = (bf16[8,64,128]{2,1,0:T(8,128)(2,1)S(1)}, bf16[8,64,128]{2,1,0:T(8,128)(2,1)S(1)}, u32[]{:S(2)}, u32[]{:S(2)}) collective-permute-start(bf16[8,64,128]{2,1,0:T(8,128)(2,1)S(1)} %copy-done.8), channel_id=1, source_target_pairs={{4,0},{8,4},{12,8},{16,12},{20,16},{24,20},{28,24},{32,28},{36,32}... | collective-permute-start | bytes 393224 | tf_op jit(solution)/shard_map/ppermute | solution.py:267

commit v7 on v5

--- a/solution.py
+++ b/solution.py
@@ -290,13 +290,13 @@
     middle = gens.shape[1] // 2
     first, second = gens[:, :middle], gens[:, middle:]
     up_a, down_b = around(first, "col", 1), around(second, "col", -1)
-    up_b, down_a = around(second, "col", 1), around(first, "col", -1)
+    up_b = around(second, "col", 1)
+    down_a = around(first, "col", -1)
     far_a, far_b = around(up_a, "col", 1), around(down_b, "col", -1)
     sparse_range, sparse_rows, up, down = sparse(local_cols, couplings, blocks, low, high)
     by_z = spread_out(partial, "z")
-    by_z, up, down = lax.optimization_barrier((by_z, up, down))
+    at_last, up, down = lax.optimization_barrier((at, up, down))
     below, above = along_front(up, 1), along_front(down, -1)
-    at_last, below, above = lax.optimization_barrier((at, below, above))
     added = (sparse_range, sparse_rows, below, above)
 
     by_z = jnp.sum(by_z.astype(F32), axis=0)
@@ -307,10 +307,11 @@
     w = spread_out(copies, "z")
 
     everyone = (gens, up_a, up_b, far_a, far_b, down_a, down_b)
-    received = around(low_rank(at_last, everyone, w), "half", 1)
+    theirs = low_rank(at_last, everyone, w)
+    received = around(theirs, "half", 1)
     range_out, rows_out = (
-        (ours + theirs.astype(F32)).astype(BF16)
-        for ours, theirs in zip(low_rank(at_last, everyone, w, added), received)
+        (mine + given.astype(F32)).astype(BF16)
+        for mine, given in zip(low_rank(at_last, everyone, w, added), received)
     )
     return range_out.reshape(samples.shape), rows_out.reshape(samples.shape)
 

time: 174 us -> 177 us (1.017)
  the two profiles are of different devices: /device:TPU:1 before, /device:TPU:126 now
where the time goes in v7:
time: 177 us; the launch traced here: 176 us
  starting transfers between devices  85.6 us (48%)
  waiting for transfers between devices  62.7 us (35%)
  Pallas kernels  17.4 us (10%)
  local copies, waits for them, and re-layouts  6.67 us (4%)
  other arithmetic  2.74 us (2%)
    all_to_all x4, starting transfers between devices, spread_out(): return lax.all_to_all(x, axis, split_axis=0, concat_axis=0, tiled=True)  39.5 us
    ppermute x11, starting transfers between devices, around(): return lax.ppermute(x, axis, [(i, (i + by) % count) for i in range(count)])  33.4 us
    ppermute x11, waiting for transfers between devices, around(): return lax.ppermute(x, axis, [(i, (i + by) % count) for i in range(count)])  24.5 us
    ppermute x4, waiting for transfers between devices, along_front(): return lax.ppermute(x, FRONT, pairs)  19.7 us
    all_to_all x4, waiting for transfers between devices, spread_out(): return lax.all_to_all(x, axis, split_axis=0, concat_axis=0, tiled=True)  18.5 us
    ppermute x4, starting transfers between devices, along_front(): return lax.ppermute(x, FRONT, pairs)  12.8 us
    pallas_call x2, Pallas kernels, low_rank(): pl.pallas_call(functools.partial(low_rank_kernel, mine, len(gens)), grid_...  7.94 us
    unnamed x21, local copies, waits for them, and re-layouts  4.29 us
  transfers between devices with their start and end apart: 19, of which 9 were waited for; matrix products, arithmetic and copies ran while one was open for 2% of the time, Pallas kernels for 4%

profile of v7, /device:TPU:126, one launch (start us, length us, event | category | flops | bytes accessed | tf_op | source)
XLA Modules:
  0.0 176.0 jit_solution(5350985245444752469)
XLA Ops:
  0.6 0.0 copy-start
  0.6 2.6 %pack.1 = bf16[64,64,128]{2,1,0:T(8,128)(2,1)} custom-call(s32[64]{0:T(128)} %bitcast.38, bf16[64,4096]{1,0:T(8,128)(2,1)} %bitcast.28, bf16[64,4096]{1,0:T(8,128)(2,1)} %bitcast.29), custom_call_target="tpu_custom_call" | custom-call | bytes 2097152 | tf_op jit(solution)/shard_map/pack/pallas_call | solution.py:59
  3.3 17.2 %all-to-all-start = ((bf16[64,64,128]{2,1,0:T(8,128)(2,1)}), bf16[64,64,128]{2,1,0:T(8,128)(2,1)S(1)}, u32[]{:S(2)}, u32[]{:S(2)}) async-start(bf16[64,64,128]{2,1,0:T(8,128)(2,1)} %pack.1), calls=%async_computation | async-start | bytes 2097152 | tf_op jit(solution)/shard_map/all_to_all | solution.py:266
  20.5 0.0 copy-done
  20.5 2.7 %collective-permute-start.2 = (bf16[2048,128]{1,0:T(8,128)(2,1)S(1)}, bf16[2048,128]{1,0:T(8,128)(2,1)S(1)}, u32[]{:S(2)}, u32[]{:S(2)}) collective-permute-start(bf16[2048,128]{1,0:T(8,128)(2,1)S(1)} %copy-done), channel_id=1, source_target_pairs={{0,3},{1,0},{2,1},{3,2},{4,7},{5,4},{6,5},{7,6},{8,11},{9,8},{10,9... | collective-permute-start | bytes 1572872 | tf_op jit(solution)/shard_map/ppermute | solution.py:256
  23.2 2.8 %collective-permute-start.1 = (bf16[2048,128]{1,0:T(8,128)(2,1)S(1)}, bf16[2048,128]{1,0:T(8,128)(2,1)S(1)}, u32[]{:S(2)}, u32[]{:S(2)}) collective-permute-start(bf16[2048,128]{1,0:T(8,128)(2,1)S(1)} %copy-done), channel_id=1, source_target_pairs={{0,2},{1,3},{2,0},{3,1},{4,6},{5,7},{6,4},{7,5},{8,10},{9,11},{10,... | collective-permute-start | bytes 1572872 | tf_op jit(solution)/shard_map/ppermute | solution.py:256
  26.0 4.1 %collective-permute-start = (bf16[2048,128]{1,0:T(8,128)(2,1)S(1)}, bf16[2048,128]{1,0:T(8,128)(2,1)S(1)}, u32[]{:S(2)}, u32[]{:S(2)}) collective-permute-start(bf16[2048,128]{1,0:T(8,128)(2,1)S(1)} %copy-done), channel_id=1, source_target_pairs={{0,1},{1,2},{2,3},{3,0},{4,5},{5,6},{6,7},{7,4},{8,9},{9,10},{10,1... | collective-permute-start | bytes 1572872 | tf_op jit(solution)/shard_map/ppermute | solution.py:256
  30.1 17.8 %collective-permute-done.2 = bf16[2048,128]{1,0:T(8,128)(2,1)S(1)} collective-permute-done((bf16[2048,128]{1,0:T(8,128)(2,1)S(1)}, bf16[2048,128]{1,0:T(8,128)(2,1)S(1)}, u32[]{:S(2)}, u32[]{:S(2)}) %collective-permute-start.2) | collective-permute-done | bytes 524320 | tf_op jit(solution)/shard_map/ppermute | solution.py:256
  48.0 0.0 collective-permute-done.1
  48.0 2.5 %collective-permute-done = bf16[2048,128]{1,0:T(8,128)(2,1)S(1)} collective-permute-done((bf16[2048,128]{1,0:T(8,128)(2,1)S(1)}, bf16[2048,128]{1,0:T(8,128)(2,1)S(1)}, u32[]{:S(2)}, u32[]{:S(2)}) %collective-permute-start) | collective-permute-done | bytes 524320 | tf_op jit(solution)/shard_map/ppermute | solution.py:256
  50.5 1.3 pad_maximum_fusion.own_ref
  51.8 1.9 %collective-permute-start.3 = (bf16[4,2048,128]{2,1,0:T(8,128)(2,1)S(1)}, bf16[4,2048,128]{2,1,0:T(8,128)(2,1)}, u32[]{:S(2)}, u32[]{:S(2)}) collective-permute-start(bf16[4,2048,128]{2,1,0:T(8,128)(2,1)S(1)} %pad_maximum_fusion.own_ref), channel_id=1, source_target_pairs={{0,256},{256,0},{1,257},{257,1},{2,258},{258,2},{3,259},{259,3},{4... | collective-permute-start | bytes 6291464 | tf_op jit(solution)/shard_map/ppermute | solution.py:256
  53.8 0.0 copy-done.9
  53.8 0.1 copy.9
  53.9 0.1 pad_add_fusion.at_ref
  53.9 4.1 %collective-permute-done.3.other_ref = bf16[4,2048,128]{2,1,0:T(8,128)(2,1)} collective-permute-done((bf16[4,2048,128]{2,1,0:T(8,128)(2,1)S(1)}, bf16[4,2048,128]{2,1,0:T(8,128)(2,1)}, u32[]{:S(2)}, u32[]{:S(2)}) %collective-permute-start.3) | collective-permute-done | bytes 2097184 | tf_op jit(solution)/shard_map/ppermute | solution.py:256
  58.0 15.1 %all-to-all-done.gen_ref.refs_0_ = bf16[64,64,128]{2,1,0:T(8,128)(2,1)S(1)} async-done(((bf16[64,64,128]{2,1,0:T(8,128)(2,1)}), bf16[64,64,128]{2,1,0:T(8,128)(2,1)S(1)}, u32[]{:S(2)}, u32[]{:S(2)}) %all-to-all-start) | async-done | bytes 1048608 | tf_op jit(solution)/shard_map/all_to_all | solution.py:266
  73.1 3.1 %partials.1 = bf16[16,4,8,128]{3,2,1,0:T(8,128)(2,1)} custom-call(s32[2]{0:T(128)S(1)} %pad_add_fusion.at_ref, bf16[64,64,128]{2,1,0:T(8,128)(2,1)S(1)} %all-to-all-done.gen_ref.refs_0_, bf16[4,2048,128]{2,1,0:T(8,128)(2,1)S(1)} %pad_maximum_fusion.own_ref, bf16[4,2048,128]{2,1,0:T(8,128)(2,1)} %collective-permute-done.3.other_ref), custom_call_target="tpu_custom_call" | custom-call | flops 536870912 | bytes 6291456 | tf_op jit(solution)/shard_map/partials/pallas_call | solution.py:165
  76.2 6.6 %all-to-all-start.1 = ((bf16[16,4,8,128]{3,2,1,0:T(8,128)(2,1)}), bf16[16,4,8,128]{3,2,1,0:T(8,128)(2,1)S(1)}, u32[]{:S(2)}, u32[]{:S(2)}) async-start(bf16[16,4,8,128]{3,2,1,0:T(8,128)(2,1)} %partials.1), calls=%async_computation.1 | async-start | bytes 262144 | tf_op jit(solution)/shard_map/all_to_all | solution.py:266
  82.9 1.0 fusion.2
  83.9 2.6 %collective-permute-start.9 = (bf16[64,32,128]{2,1,0:T(8,128)(2,1)}, bf16[64,32,128]{2,1,0:T(8,128)(2,1)S(1)}, u32[]{:S(2)}, u32[]{:S(2)}) collective-permute-start(bf16[64,32,128]{2,1,0:T(8,128)(2,1)} %get-tuple-element.30), channel_id=1, source_target_pairs={{0,3},{1,0},{2,1},{3,2},{4,7},{5,4},{6,5},{7,6},{8,11},{9,8},{10,9... | collective-permute-start | bytes 1572872 | tf_op jit(solution)/shard_map/ppermute | solution.py:256
  86.6 4.4 %collective-permute-start.6 = (bf16[64,32,128]{2,1,0:T(8,128)(2,1)}, bf16[64,32,128]{2,1,0:T(8,128)(2,1)S(1)}, u32[]{:S(2)}, u32[]{:S(2)}) collective-permute-start(bf16[64,32,128]{2,1,0:T(8,128)(2,1)} %get-tuple-element.31), channel_id=1, source_target_pairs={{0,1},{1,2},{2,3},{3,0},{4,5},{5,6},{6,7},{7,4},{8,9},{9,10},{10,1... | collective-permute-start | bytes 1572872 | tf_op jit(solution)/shard_map/ppermute | solution.py:256
  91.0 3.4 %all-to-all-done.1 = bf16[16,4,8,128]{3,2,1,0:T(8,128)(2,1)S(1)} async-done(((bf16[16,4,8,128]{3,2,1,0:T(8,128)(2,1)}), bf16[16,4,8,128]{3,2,1,0:T(8,128)(2,1)S(1)}, u32[]{:S(2)}, u32[]{:S(2)}) %all-to-all-start.1) | async-done | bytes 131104 | tf_op jit(solution)/shard_map/all_to_all | solution.py:266
  94.4 0.6 broadcast_in_dim.6
  95.0 7.2 %all-to-all-start.2 = ((f32[16,8,128]{2,1,0:T(8,128)}), f32[16,8,128]{2,1,0:T(8,128)S(1)}, u32[]{:S(2)}, u32[]{:S(2)}) async-start(f32[16,8,128]{2,1,0:T(8,128)} %bitcast.12), calls=%async_computation.2 | async-start | bytes 131072 | tf_op jit(solution)/shard_map/all_to_all | solution.py:266
  102.3 2.5 %collective-permute-start.7 = (bf16[64,32,128]{2,1,0:T(8,128)(2,1)}, bf16[64,32,128]{2,1,0:T(8,128)(2,1)S(1)}, u32[]{:S(2)}, u32[]{:S(2)}) collective-permute-start(bf16[64,32,128]{2,1,0:T(8,128)(2,1)} %get-tuple-element.30), channel_id=1, source_target_pairs={{0,1},{1,2},{2,3},{3,0},{4,5},{5,6},{6,7},{7,4},{8,9},{9,10},{10,1... | collective-permute-start | bytes 1572872 | tf_op jit(solution)/shard_map/ppermute | solution.py:256
  104.7 3.4 %collective-permute-start.11 = (bf16[64,32,128]{2,1,0:T(8,128)(2,1)}, bf16[64,32,128]{2,1,0:T(8,128)(2,1)}, u32[]{:S(2)}, u32[]{:S(2)}) collective-permute-start(bf16[64,32,128]{2,1,0:T(8,128)(2,1)} %get-tuple-element.31), channel_id=1, source_target_pairs={{0,3},{1,0},{2,1},{3,2},{4,7},{5,4},{6,5},{7,6},{8,11},{9,8},{10,9... | collective-permute-start | bytes 1572872 | tf_op jit(solution)/shard_map/ppermute | solution.py:256
  108.1 0.0 collective-permute-done.9.refs_6_
  108.1 2.8 %collective-permute-start.10 = (bf16[64,32,128]{2,1,0:T(8,128)(2,1)S(1)}, bf16[64,32,128]{2,1,0:T(8,128)(2,1)}, u32[]{:S(2)}, u32[]{:S(2)}) collective-permute-start(bf16[64,32,128]{2,1,0:T(8,128)(2,1)S(1)} %collective-permute-done.9.refs_6_), channel_id=1, source_target_pairs={{0,3},{1,0},{2,1},{3,2},{4,7},{5,4},{6,5},{7,6},{8,11},{9,8},{10,9... | collective-permute-start | bytes 1572872 | tf_op jit(solution)/shard_map/ppermute | solution.py:256
  110.9 0.0 collective-permute-done.6.refs_1_
  110.9 4.3 %collective-permute-start.8 = (bf16[64,32,128]{2,1,0:T(8,128)(2,1)S(1)}, bf16[64,32,128]{2,1,0:T(8,128)(2,1)}, u32[]{:S(2)}, u32[]{:S(2)}) collective-permute-start(bf16[64,32,128]{2,1,0:T(8,128)(2,1)S(1)} %collective-permute-done.6.refs_1_), channel_id=1, source_target_pairs={{0,1},{1,2},{2,3},{3,0},{4,5},{5,6},{6,7},{7,4},{8,9},{9,10},{10,1... | collective-permute-start | bytes 1572872 | tf_op jit(solution)/shard_map/ppermute | solution.py:256
  115.2 0.0 all-to-all-done.2
  115.2 0.7 broadcast_in_dim.7
  115.9 8.4 %all-to-all-start.3 = ((bf16[16,4,8,128]{3,2,1,0:T(8,128)(2,1)}), bf16[16,4,8,128]{3,2,1,0:T(8,128)(2,1)S(1)}, u32[]{:S(2)}, u32[]{:S(2)}) async-start(bf16[16,4,8,128]{3,2,1,0:T(8,128)(2,1)} %broadcast_in_dim.7), calls=%async_computation.3 | async-start | bytes 262144 | tf_op jit(solution)/shard_map/all_to_all | solution.py:266
  124.3 0.0 copy-done.1
  124.3 4.6 %collective-permute-start.4 = (bf16[8,64,128]{2,1,0:T(8,128)(2,1)S(1)}, bf16[8,64,128]{2,1,0:T(8,128)(2,1)S(1)}, u32[]{:S(2)}, u32[]{:S(2)}) collective-permute-start(bf16[8,64,128]{2,1,0:T(8,128)(2,1)S(1)} %bitcast.37), channel_id=1, source_target_pairs={{0,4},{4,8},{8,12},{12,16},{16,20},{20,24},{24,28},{28,32},{32,36}... | collective-permute-start | bytes 393224 | tf_op jit(solution)/shard_map/ppermute | solution.py:262
  128.9 2.6 %collective-permute-done.4.low_ref = bf16[8,64,128]{2,1,0:T(8,128)(2,1)S(1)} collective-permute-done((bf16[8,64,128]{2,1,0:T(8,128)(2,1)S(1)}, bf16[8,64,128]{2,1,0:T(8,128)(2,1)S(1)}, u32[]{:S(2)}, u32[]{:S(2)}) %collective-permute-start.4) | collective-permute-done | bytes 131104 | tf_op jit(solution)/shard_map/ppermute | solution.py:262
  131.5 2.4 %collective-permute-start.5 = (bf16[8,64,128]{2,1,0:T(8,128)(2,1)S(1)}, bf16[8,64,128]{2,1,0:T(8,128)(2,1)S(1)}, u32[]{:S(2)}, u32[]{:S(2)}) collective-permute-start(bf16[8,64,128]{2,1,0:T(8,128)(2,1)S(1)} %bitcast.36), channel_id=1, source_target_pairs={{4,0},{8,4},{12,8},{16,12},{20,16},{24,20},{28,24},{32,28},{36,32}... | collective-permute-start | bytes 393224 | tf_op jit(solution)/shard_map/ppermute | solution.py:262
  133.9 8.2 %collective-permute-done.5.high_ref = bf16[8,64,128]{2,1,0:T(8,128)(2,1)S(1)} collective-permute-done((bf16[8,64,128]{2,1,0:T(8,128)(2,1)S(1)}, bf16[8,64,128]{2,1,0:T(8,128)(2,1)S(1)}, u32[]{:S(2)}, u32[]{:S(2)}) %collective-permute-start.5) | collective-permute-done | bytes 131104 | tf_op jit(solution)/shard_map/ppermute | solution.py:262
  142.1 1.6 copy-done.2
  143.7 3.6 %sparse.1 = (f32[32,64,128]{2,1,0:T(8,128)S(1)}, f32[32,64,128]{2,1,0:T(8,128)S(1)}, bf16[8,64,128]{2,1,0:T(8,128)(2,1)S(1)}, bf16[8,64,128]{2,1,0:T(8,128)(2,1)S(1)}) custom-call(s32[32,8]{1,0:T(8,128)S(1)} %subtract_add_fusion.cols_ref, bf16[32,64,512]{2,1,0:T(8,128)(2,1)S(1)} %copy-done.2, bf16[32,64,128]{2,1,0:T(8,128)(2,1)S(1)} %bitcast.27, ...), custom_call_target="tpu_custom_call" | custom-call | flops 536870912 | bytes 6291456 | tf_op jit(solution)/shard_map/sparse/pallas_call | solution.py:106
  147.4 0.0 copy-start.3
  147.4 1.0 copy-done.3
  148.4 1.0 copy-done.5
  149.3 0.6 copy-done.7
  150.0 0.0 collective-permute-done.7.refs_2_
  150.0 0.0 collective-permute-done.11.refs_5_
  150.0 0.0 all-to-all-done.3.refs_7_
  150.0 0.0 copy-start.4
  150.0 0.0 copy-start.6
  150.0 0.0 collective-permute-done.10.refs_4_
  150.0 0.0 collective-permute-done.8.refs_3_
  150.0 4.0 %theirs.1 = bf16[2,32,64,128]{3,2,1,0:T(8,128)(2,1)S(1)} custom-call(s32[2]{0:T(128)S(1)} %pad_add_fusion.at_ref, bf16[64,64,128]{2,1,0:T(8,128)(2,1)S(1)} %all-to-all-done.gen_ref.refs_0_, bf16[64,32,128]{2,1,0:T(8,128)(2,1)S(1)} %collective-permute-done.6.refs_1_, bf16[64,32,128]{2,1,0:T(8,128)(2,1)S(1)} %collective-permute-done.7.refs_2_, ...), custom_call_target="tpu_custom_call" | custom-call | flops 536870912 | bytes 4194304 | tf_op jit(solution)/shard_map/theirs/pallas_call | solution.py:238
  154.0 1.9 %collective-permute-start.14 = (bf16[2,32,64,128]{3,2,1,0:T(8,128)(2,1)S(1)}, bf16[2,32,64,128]{3,2,1,0:T(8,128)(2,1)S(1)}, u32[]{:S(2)}, u32[]{:S(2)}) collective-permute-start(bf16[2,32,64,128]{3,2,1,0:T(8,128)(2,1)S(1)} %theirs.1), channel_id=1, source_target_pairs={{0,256},{256,0},{1,257},{257,1},{2,258},{258,2},{3,259},{259,3},{4... | collective-permute-start | bytes 3145736 | tf_op jit(solution)/shard_map/ppermute | solution.py:256
  155.9 0.0 copy-done.8
  156.0 3.9 %collective-permute-start.12 = (bf16[8,64,128]{2,1,0:T(8,128)(2,1)S(1)}, bf16[8,64,128]{2,1,0:T(8,128)(2,1)S(1)}, u32[]{:S(2)}, u32[]{:S(2)}) collective-permute-start(bf16[8,64,128]{2,1,0:T(8,128)(2,1)S(1)} %copy-done.8), channel_id=1, source_target_pairs={{0,4},{4,8},{8,12},{12,16},{16,20},{20,24},{24,28},{28,32},{32,36}... | collective-permute-start | bytes 393224 | tf_op jit(solution)/shard_map/ppermute | solution.py:262
  159.9 1.9 %collective-permute-start.13 = (bf16[8,64,128]{2,1,0:T(8,128)(2,1)S(1)}, bf16[8,64,128]{2,1,0:T(8,128)(2,1)S(1)}, u32[]{:S(2)}, u32[]{:S(2)}) collective-permute-start(bf16[8,64,128]{2,1,0:T(8,128)(2,1)S(1)} %get-tuple-element.25), channel_id=1, source_target_pairs={{4,0},{8,4},{12,8},{16,12},{20,16},{24,20},{28,24},{32,28},{36,32}... | collective-permute-start | bytes 393224 | tf_op jit(solution)/shard_map/ppermute | solution.py:262
  161.8 1.9 %collective-permute-done.12.refs_10_ = bf16[8,64,128]{2,1,0:T(8,128)(2,1)S(1)} collective-permute-done((bf16[8,64,128]{2,1,0:T(8,128)(2,1)S(1)}, bf16[8,64,128]{2,1,0:T(8,128)(2,1)S(1)}, u32[]{:S(2)}, u32[]{:S(2)}) %collective-permute-start.12) | collective-permute-done | bytes 131104 | tf_op jit(solution)/shard_map/ppermute | solution.py:262
  163.8 7.0 %collective-permute-done.13.refs_11_ = bf16[8,64,128]{2,1,0:T(8,128)(2,1)S(1)} collective-permute-done((bf16[8,64,128]{2,1,0:T(8,128)(2,1)S(1)}, bf16[8,64,128]{2,1,0:T(8,128)(2,1)S(1)}, u32[]{:S(2)}, u32[]{:S(2)}) %collective-permute-start.13) | collective-permute-done | bytes 131104 | tf_op jit(solution)/shard_map/ppermute | solution.py:262
  170.7 0.0 copy-done.4
  170.7 0.0 copy-done.6
  170.7 4.0 %mine.1 = (f32[32,64,128]{2,1,0:T(8,128)S(1)}, f32[32,64,128]{2,1,0:T(8,128)S(1)}) custom-call(s32[2]{0:T(128)S(1)} %pad_add_fusion.at_ref, bf16[64,64,128]{2,1,0:T(8,128)(2,1)S(1)} %all-to-all-done.gen_ref.refs_0_, bf16[64,32,128]{2,1,0:T(8,128)(2,1)S(1)} %collective-permute-done.6.refs_1_, bf16[64,32,128]{2,1,0:T(8,128)(2,1)S(1)} %collective-permute-done.7.refs_2_, ...), custom_call_target="tpu_custom_call" | custom-call | flops 536870912 | bytes 4194304 | tf_op jit(solution)/shard_map/mine/pallas_call | solution.py:238
  174.7 0.0 collective-permute-done.14
  174.7 1.3 fusion
  (10 shorter events, 0.1 us)
Async XLA Ops:
  0.6 19.9 %copy-start = (bf16[2048,128]{1,0:T(8,128)(2,1)S(1)}, bf16[2048,128]{1,0:T(8,128)(2,1)}, u32[]{:S(2)}) copy-start(bf16[2048,128]{1,0:T(8,128)(2,1)} %param.6) | copy-start | bytes 1572868
  3.3 69.8 %all-to-all-start = ((bf16[64,64,128]{2,1,0:T(8,128)(2,1)}), bf16[64,64,128]{2,1,0:T(8,128)(2,1)S(1)}, u32[]{:S(2)}, u32[]{:S(2)}) async-start(bf16[64,64,128]{2,1,0:T(8,128)(2,1)} %pack.1), calls=%async_computation | async-start | bytes 2097152 | tf_op jit(solution)/shard_map/all_to_all | solution.py:266
  20.5 27.4 %collective-permute-start.2 = (bf16[2048,128]{1,0:T(8,128)(2,1)S(1)}, bf16[2048,128]{1,0:T(8,128)(2,1)S(1)}, u32[]{:S(2)}, u32[]{:S(2)}) collective-permute-start(bf16[2048,128]{1,0:T(8,128)(2,1)S(1)} %copy-done), channel_id=1, source_target_pairs={{0,3},{1,0},{2,1},{3,2},{4,7},{5,4},{6,5},{7,6},{8,11},{9,8},{10,9... | collective-permute-start | bytes 1572872 | tf_op jit(solution)/shard_map/ppermute | solution.py:256
  23.2 24.8 %collective-permute-start.1 = (bf16[2048,128]{1,0:T(8,128)(2,1)S(1)}, bf16[2048,128]{1,0:T(8,128)(2,1)S(1)}, u32[]{:S(2)}, u32[]{:S(2)}) collective-permute-start(bf16[2048,128]{1,0:T(8,128)(2,1)S(1)} %copy-done), channel_id=1, source_target_pairs={{0,2},{1,3},{2,0},{3,1},{4,6},{5,7},{6,4},{7,5},{8,10},{9,11},{10,... | collective-permute-start | bytes 1572872 | tf_op jit(solution)/shard_map/ppermute | solution.py:256
  26.0 24.5 %collective-permute-start = (bf16[2048,128]{1,0:T(8,128)(2,1)S(1)}, bf16[2048,128]{1,0:T(8,128)(2,1)S(1)}, u32[]{:S(2)}, u32[]{:S(2)}) collective-permute-start(bf16[2048,128]{1,0:T(8,128)(2,1)S(1)} %copy-done), channel_id=1, source_target_pairs={{0,1},{1,2},{2,3},{3,0},{4,5},{5,6},{6,7},{7,4},{8,9},{9,10},{10,1... | collective-permute-start | bytes 1572872 | tf_op jit(solution)/shard_map/ppermute | solution.py:256
  50.5 3.3 %copy-start.9 = (s32[32,8]{0,1:T(8,128)S(1)}, s32[32,8]{0,1:T(8,128)}, u32[]{:S(2)}) copy-start(s32[32,8]{0,1:T(8,128)} %param.8) | copy-start | bytes 3076
  51.8 6.2 %collective-permute-start.3 = (bf16[4,2048,128]{2,1,0:T(8,128)(2,1)S(1)}, bf16[4,2048,128]{2,1,0:T(8,128)(2,1)}, u32[]{:S(2)}, u32[]{:S(2)}) collective-permute-start(bf16[4,2048,128]{2,1,0:T(8,128)(2,1)S(1)} %pad_maximum_fusion.own_ref), channel_id=1, source_target_pairs={{0,256},{256,0},{1,257},{257,1},{2,258},{258,2},{3,259},{259,3},{4... | collective-permute-start | bytes 6291464 | tf_op jit(solution)/shard_map/ppermute | solution.py:256
  76.2 48.0 %copy-start.1 = (bf16[2048,128]{1,0:T(8,128)(2,1)S(1)}, bf16[2048,128]{1,0:T(8,128)(2,1)}, u32[]{:S(2)}) copy-start(bf16[2048,128]{1,0:T(8,128)(2,1)} %param.6) | copy-start | bytes 1572868
  76.2 18.1 %all-to-all-start.1 = ((bf16[16,4,8,128]{3,2,1,0:T(8,128)(2,1)}), bf16[16,4,8,128]{3,2,1,0:T(8,128)(2,1)S(1)}, u32[]{:S(2)}, u32[]{:S(2)}) async-start(bf16[16,4,8,128]{3,2,1,0:T(8,128)(2,1)} %partials.1), calls=%async_computation.1 | async-start | bytes 262144 | tf_op jit(solution)/shard_map/all_to_all | solution.py:266
  83.9 24.2 %collective-permute-start.9 = (bf16[64,32,128]{2,1,0:T(8,128)(2,1)}, bf16[64,32,128]{2,1,0:T(8,128)(2,1)S(1)}, u32[]{:S(2)}, u32[]{:S(2)}) collective-permute-start(bf16[64,32,128]{2,1,0:T(8,128)(2,1)} %get-tuple-element.30), channel_id=1, source_target_pairs={{0,3},{1,0},{2,1},{3,2},{4,7},{5,4},{6,5},{7,6},{8,11},{9,8},{10,9... | collective-permute-start | bytes 1572872 | tf_op jit(solution)/shard_map/ppermute | solution.py:256
  86.6 24.3 %collective-permute-start.6 = (bf16[64,32,128]{2,1,0:T(8,128)(2,1)}, bf16[64,32,128]{2,1,0:T(8,128)(2,1)S(1)}, u32[]{:S(2)}, u32[]{:S(2)}) collective-permute-start(bf16[64,32,128]{2,1,0:T(8,128)(2,1)} %get-tuple-element.31), channel_id=1, source_target_pairs={{0,1},{1,2},{2,3},{3,0},{4,5},{5,6},{6,7},{7,4},{8,9},{9,10},{10,1... | collective-permute-start | bytes 1572872 | tf_op jit(solution)/shard_map/ppermute | solution.py:256
  95.0 20.2 %all-to-all-start.2 = ((f32[16,8,128]{2,1,0:T(8,128)}), f32[16,8,128]{2,1,0:T(8,128)S(1)}, u32[]{:S(2)}, u32[]{:S(2)}) async-start(f32[16,8,128]{2,1,0:T(8,128)} %bitcast.12), calls=%async_computation.2 | async-start | bytes 131072 | tf_op jit(solution)/shard_map/all_to_all | solution.py:266
  102.3 47.7 %collective-permute-start.7 = (bf16[64,32,128]{2,1,0:T(8,128)(2,1)}, bf16[64,32,128]{2,1,0:T(8,128)(2,1)S(1)}, u32[]{:S(2)}, u32[]{:S(2)}) collective-permute-start(bf16[64,32,128]{2,1,0:T(8,128)(2,1)} %get-tuple-element.30), channel_id=1, source_target_pairs={{0,1},{1,2},{2,3},{3,0},{4,5},{5,6},{6,7},{7,4},{8,9},{9,10},{10,1... | collective-permute-start | bytes 1572872 | tf_op jit(solution)/shard_map/ppermute | solution.py:256
  104.7 45.3 %collective-permute-start.11 = (bf16[64,32,128]{2,1,0:T(8,128)(2,1)}, bf16[64,32,128]{2,1,0:T(8,128)(2,1)}, u32[]{:S(2)}, u32[]{:S(2)}) collective-permute-start(bf16[64,32,128]{2,1,0:T(8,128)(2,1)} %get-tuple-element.31), channel_id=1, source_target_pairs={{0,3},{1,0},{2,1},{3,2},{4,7},{5,4},{6,5},{7,6},{8,11},{9,8},{10,9... | collective-permute-start | bytes 1572872 | tf_op jit(solution)/shard_map/ppermute | solution.py:256
  108.1 41.9 %collective-permute-start.10 = (bf16[64,32,128]{2,1,0:T(8,128)(2,1)S(1)}, bf16[64,32,128]{2,1,0:T(8,128)(2,1)}, u32[]{:S(2)}, u32[]{:S(2)}) collective-permute-start(bf16[64,32,128]{2,1,0:T(8,128)(2,1)S(1)} %collective-permute-done.9.refs_6_), channel_id=1, source_target_pairs={{0,3},{1,0},{2,1},{3,2},{4,7},{5,4},{6,5},{7,6},{8,11},{9,8},{10,9... | collective-permute-start | bytes 1572872 | tf_op jit(solution)/shard_map/ppermute | solution.py:256
  110.9 39.1 %collective-permute-start.8 = (bf16[64,32,128]{2,1,0:T(8,128)(2,1)S(1)}, bf16[64,32,128]{2,1,0:T(8,128)(2,1)}, u32[]{:S(2)}, u32[]{:S(2)}) collective-permute-start(bf16[64,32,128]{2,1,0:T(8,128)(2,1)S(1)} %collective-permute-done.6.refs_1_), channel_id=1, source_target_pairs={{0,1},{1,2},{2,3},{3,0},{4,5},{5,6},{6,7},{7,4},{8,9},{9,10},{10,1... | collective-permute-start | bytes 1572872 | tf_op jit(solution)/shard_map/ppermute | solution.py:256
  115.9 34.1 %all-to-all-start.3 = ((bf16[16,4,8,128]{3,2,1,0:T(8,128)(2,1)}), bf16[16,4,8,128]{3,2,1,0:T(8,128)(2,1)S(1)}, u32[]{:S(2)}, u32[]{:S(2)}) async-start(bf16[16,4,8,128]{3,2,1,0:T(8,128)(2,1)} %broadcast_in_dim.7), calls=%async_computation.3 | async-start | bytes 262144 | tf_op jit(solution)/shard_map/all_to_all | solution.py:266
  124.3 7.2 %collective-permute-start.4 = (bf16[8,64,128]{2,1,0:T(8,128)(2,1)S(1)}, bf16[8,64,128]{2,1,0:T(8,128)(2,1)S(1)}, u32[]{:S(2)}, u32[]{:S(2)}) collective-permute-start(bf16[8,64,128]{2,1,0:T(8,128)(2,1)S(1)} %bitcast.37), channel_id=1, source_target_pairs={{0,4},{4,8},{8,12},{12,16},{16,20},{20,24},{24,28},{28,32},{32,36}... | collective-permute-start | bytes 393224 | tf_op jit(solution)/shard_map/ppermute | solution.py:262
  131.5 10.6 %collective-permute-start.5 = (bf16[8,64,128]{2,1,0:T(8,128)(2,1)S(1)}, bf16[8,64,128]{2,1,0:T(8,128)(2,1)S(1)}, u32[]{:S(2)}, u32[]{:S(2)}) collective-permute-start(bf16[8,64,128]{2,1,0:T(8,128)(2,1)S(1)} %bitcast.36), channel_id=1, source_target_pairs={{4,0},{8,4},{12,8},{16,12},{20,16},{24,20},{28,24},{32,28},{36,32}... | collective-permute-start | bytes 393224 | tf_op jit(solution)/shard_map/ppermute | solution.py:262
  142.1 1.6 copy-start.2
  147.4 1.0 copy-start.3
  148.4 1.0 copy-start.5
  149.3 0.6 copy-start.7
  150.0 6.0 %copy-start.8 = (bf16[8,64,128]{2,1,0:T(8,128)(2,1)S(1)}, bf16[8,64,128]{2,1,0:T(8,128)(2,1)}, u32[]{:S(2)}) copy-start(bf16[8,64,128]{2,1,0:T(8,128)(2,1)} %copy-done.7) | copy-start | bytes 393220
  150.0 20.7 %copy-start.4 = (f32[32,64,128]{2,1,0:T(8,128)S(1)}, f32[32,64,128]{2,1,0:T(8,128)}, u32[]{:S(2)}) copy-start(f32[32,64,128]{2,1,0:T(8,128)} %copy-done.3) | copy-start | bytes 3145732
  150.0 20.7 %copy-start.6 = (f32[32,64,128]{2,1,0:T(8,128)S(1)}, f32[32,64,128]{2,1,0:T(8,128)}, u32[]{:S(2)}) copy-start(f32[32,64,128]{2,1,0:T(8,128)} %copy-done.5) | copy-start | bytes 3145732
  154.0 20.7 %collective-permute-start.14 = (bf16[2,32,64,128]{3,2,1,0:T(8,128)(2,1)S(1)}, bf16[2,32,64,128]{3,2,1,0:T(8,128)(2,1)S(1)}, u32[]{:S(2)}, u32[]{:S(2)}) collective-permute-start(bf16[2,32,64,128]{3,2,1,0:T(8,128)(2,1)S(1)} %theirs.1), channel_id=1, source_target_pairs={{0,256},{256,0},{1,257},{257,1},{2,258},{258,2},{3,259},{259,3},{4... | collective-permute-start | bytes 3145736 | tf_op jit(solution)/shard_map/ppermute | solution.py:256
  156.0 7.8 %collective-permute-start.12 = (bf16[8,64,128]{2,1,0:T(8,128)(2,1)S(1)}, bf16[8,64,128]{2,1,0:T(8,128)(2,1)S(1)}, u32[]{:S(2)}, u32[]{:S(2)}) collective-permute-start(bf16[8,64,128]{2,1,0:T(8,128)(2,1)S(1)} %copy-done.8), channel_id=1, source_target_pairs={{0,4},{4,8},{8,12},{12,16},{16,20},{20,24},{24,28},{28,32},{32,36}... | collective-permute-start | bytes 393224 | tf_op jit(solution)/shard_map/ppermute | solution.py:262
  159.9 10.8 %collective-permute-start.13 = (bf16[8,64,128]{2,1,0:T(8,128)(2,1)S(1)}, bf16[8,64,128]{2,1,0:T(8,128)(2,1)S(1)}, u32[]{:S(2)}, u32[]{:S(2)}) collective-permute-start(bf16[8,64,128]{2,1,0:T(8,128)(2,1)S(1)} %get-tuple-element.25), channel_id=1, source_target_pairs={{4,0},{8,4},{12,8},{16,12},{20,16},{24,20},{28,24},{32,28},{36,32}... | collective-permute-start | bytes 393224 | tf_op jit(solution)/shard_map/ppermute | solution.py:262

commit v8 on v4

--- a/solution.py
+++ b/solution.py
@@ -40,7 +40,9 @@
     return lax.broadcasted_iota(jnp.int32, shape, 1) < BS
 
 
-def pack_kernel(map_ref, left_ref, right_ref, *out_refs):
+def pack_kernel(map_ref, left_ref, right_ref, own_ref, head_ref, tail_ref, *out_refs):
+    head_ref[...] = own_ref[:HB]
+    tail_ref[...] = own_ref[own_ref.shape[0] - HB :]
     ranks = left_ref.shape[0] // len(out_refs)
     low = low_lanes((ranks, LANES))
     for k in range(left_ref.shape[1] // LANES):
@@ -53,18 +55,18 @@
             out_ref[two] = jnp.where(low, swapped_halves(left), right)
 
 
-def pack(order_map, left, right):
+def pack(order_map, left, right, blocks):
     ranks, width = left.shape
     out = jax.ShapeDtypeStruct((width // BS, ranks // CHUNKS, LANES), BF16)
+    edge = jax.ShapeDtypeStruct((HB, *blocks.shape[1:]), BF16)
     return pl.pallas_call(
         pack_kernel,
-        out_shape=(out,) * CHUNKS,
-        in_specs=[whole(SMEM), whole(VMEM), whole(VMEM)],
-        out_specs=(whole(VMEM),) * CHUNKS,
-        compiler_params=grant(6),
+        out_shape=(edge, edge, *(out,) * CHUNKS),
+        in_specs=[whole(SMEM)] + [whole(VMEM)] * 3,
+        out_specs=(whole(VMEM),) * (2 + CHUNKS),
         cost_estimate=cost(0, 8 * ranks * width),
         name="pack",
-    )(order_map, left, right)
+    )(order_map, left, right, blocks)
 
 
 def sparse_kernel(
@@ -136,14 +138,12 @@
     )(local_cols, couplings, blocks, low, high)
 
 
-def reduce_kernel(at_ref, gen_ref, own_ref, other_ref, out_ref, first_ref, second_ref, lhs):
+def reduce_kernel(at_ref, gen_ref, own_ref, other_ref, out_ref, lhs):
     half, me = at_ref[0], at_ref[1]
     blocks, ranks, _ = gen_ref.shape
     count = blocks // 2
     parts = own_ref.shape[0]
     low = low_lanes((ranks, LANES))
-    first_ref[...] = gen_ref[:, : ranks // 2]
-    second_ref[...] = gen_ref[:, ranks // 2 :]
     for side, first in ((0, half * count), (1, (1 - half) * count)):
         for k in range(count // 2):
             one, two = gen_ref[first + 2 * k], gen_ref[first + 2 * k + 1]
@@ -162,15 +162,14 @@
 
 
 def reduced(at, gens, own, other, splits):
-    blocks, ranks, _ = gens.shape
+    _, ranks, _ = gens.shape
     parts, rows, _ = own.shape
-    half_ranks = jax.ShapeDtypeStruct((blocks, ranks // 2, LANES), BF16)
     out = jax.ShapeDtypeStruct((splits, parts, 2 * ranks // splits, LANES), BF16)
     return pl.pallas_call(
         reduce_kernel,
-        out_shape=(out, half_ranks, half_ranks),
+        out_shape=out,
         in_specs=[whole(SMEM)] + [whole(VMEM)] * 3,
-        out_specs=(whole(VMEM),) * 3,
+        out_specs=whole(VMEM),
         scratch_shapes=[pltpu.VMEM((2, 2 * ranks, rows), BF16)],
         compiler_params=grant(14),
         cost_estimate=cost(8 * ranks * rows * parts * LANES, 6 << 20),
@@ -278,9 +277,8 @@
     n_z, n_x, n_col = (lax.axis_size(a) for a in ("z", "x", "col"))
     blocks = samples.reshape(count, BS, width)
 
-    low = along_front(blocks[count - HB :], 1)
-    high = along_front(blocks[:HB], -1)
-    (packed,) = pack(child_map[0, 0], gen_left[0], gen_right[0])
+    head, tail, packed = pack(child_map[0, 0], gen_left[0], gen_right[0], blocks)
+    low, high = along_front(tail, 1), along_front(head, -1)
     gens = spread_out(packed, ("z", "x"))
 
     shifted = [around(samples, "col", k) for k in range(1, n_col)]
@@ -295,7 +293,9 @@
         (gens, panels, others, sparse_range, sparse_rows)
     )
     added = (sparse_range, sparse_rows, below, above)
-    partial, first, second = reduced(at, gens, panels, others, n_z)
+    partial = reduced(at, gens, panels, others, n_z)
+    middle = gens.shape[1] // 2
+    first, second = gens[:, :middle], gens[:, middle:]
     up_a, down_b = around(first, "col", 1), around(second, "col", -1)
     up_b, down_a = around(second, "col", 1), around(first, "col", -1)
     far_a, far_b = around(up_a, "col", 1), around(down_b, "col", -1)

time: 184 us -> 181 us (0.984)
  local copies, waits for them, and re-layouts: 10.2 us -> 6.91 us
    unnamed x29 -> x23, local copies, waits for them, and re-layouts: 8.89 us -> 4.58 us
where the time goes in v8:
time: 181 us; the launch traced here: 180 us
  starting transfers between devices  99 us (55%)
  waiting for transfers between devices  52 us (29%)
  Pallas kernels  17.5 us (10%)
  local copies, waits for them, and re-layouts  6.91 us (4%)
  other arithmetic  3.19 us (2%)
    all_to_all x4, starting transfers between devices, spread_out(): return lax.all_to_all(x, axis, split_axis=0, concat_axis=0, tiled=True)  42.6 us
    ppermute x11, starting transfers between devices, around(): return lax.ppermute(x, axis, [(i, (i + by) % count) for i in range(count)])  37.1 us
    ppermute x4, waiting for transfers between devices, along_front(): return lax.ppermute(x, FRONT, pairs)  31.4 us
    ppermute x4, starting transfers between devices, along_front(): return lax.ppermute(x, FRONT, pairs)  19.3 us
    all_to_all x4, waiting for transfers between devices, spread_out(): return lax.all_to_all(x, axis, split_axis=0, concat_axis=0, tiled=True)  16.4 us
    pallas_call x2, Pallas kernels, low_rank(): pl.pallas_call(functools.partial(low_rank_kernel, mine, len(gens)), grid_...  7.79 us
    unnamed x23, local copies, waits for them, and re-layouts  4.58 us
    ppermute x11, waiting for transfers between devices, around(): return lax.ppermute(x, axis, [(i, (i + by) % count) for i in range(count)])  4.2 us
  transfers between devices with their start and end apart: 19, of which 6 were waited for; matrix products, arithmetic and copies ran while one was open for 2% of the time, Pallas kernels for 4%

profile of v8, /device:TPU:1, one launch (start us, length us, event | category | flops | bytes accessed | tf_op | source)
XLA Modules:
  0.0 179.5 jit_solution(9714968397060515472)
XLA Ops:
  0.6 0.0 copy-start
  0.6 0.0 copy-start.8
  0.7 2.9 %pack.1 = (bf16[8,64,128]{2,1,0:T(8,128)(2,1)}, bf16[8,64,128]{2,1,0:T(8,128)(2,1)}, bf16[64,64,128]{2,1,0:T(8,128)(2,1)}) custom-call(s32[64]{0:T(128)} %bitcast.34, bf16[64,4096]{1,0:T(8,128)(2,1)} %bitcast.27, bf16[64,4096]{1,0:T(8,128)(2,1)} %bitcast.28, bf16[32,64,128]{2,1,0:T(8,128)(2,1)} %bitcast.24), custom_call_target="tpu_custom_call" | custom-call | bytes 2097152 | tf_op jit(solution)/shard_map/pack/pallas_call | solution.py:62
  3.5 19.2 %all-to-all-start = ((bf16[64,64,128]{2,1,0:T(8,128)(2,1)}), bf16[64,64,128]{2,1,0:T(8,128)(2,1)S(1)}, u32[]{:S(2)}, u32[]{:S(2)}) async-start(bf16[64,64,128]{2,1,0:T(8,128)(2,1)} %get-tuple-element.21), calls=%async_computation | async-start | bytes 2097152 | tf_op jit(solution)/shard_map/all_to_all | solution.py:269
  22.8 0.0 copy-done
  22.8 3.2 %collective-permute-start = (bf16[2048,128]{1,0:T(8,128)(2,1)S(1)}, bf16[2048,128]{1,0:T(8,128)(2,1)S(1)}, u32[]{:S(2)}, u32[]{:S(2)}) collective-permute-start(bf16[2048,128]{1,0:T(8,128)(2,1)S(1)} %copy-done), channel_id=1, source_target_pairs={{0,1},{1,2},{2,3},{3,0},{4,5},{5,6},{6,7},{7,4},{8,9},{9,10},{10,1... | collective-permute-start | bytes 1572872 | tf_op jit(solution)/shard_map/ppermute | solution.py:259
  26.0 3.4 %collective-permute-start.2 = (bf16[2048,128]{1,0:T(8,128)(2,1)S(1)}, bf16[2048,128]{1,0:T(8,128)(2,1)S(1)}, u32[]{:S(2)}, u32[]{:S(2)}) collective-permute-start(bf16[2048,128]{1,0:T(8,128)(2,1)S(1)} %copy-done), channel_id=1, source_target_pairs={{0,3},{1,0},{2,1},{3,2},{4,7},{5,4},{6,5},{7,6},{8,11},{9,8},{10,9... | collective-permute-start | bytes 1572872 | tf_op jit(solution)/shard_map/ppermute | solution.py:259
  29.4 3.5 %collective-permute-start.1 = (bf16[2048,128]{1,0:T(8,128)(2,1)S(1)}, bf16[2048,128]{1,0:T(8,128)(2,1)}, u32[]{:S(2)}, u32[]{:S(2)}) collective-permute-start(bf16[2048,128]{1,0:T(8,128)(2,1)S(1)} %copy-done), channel_id=1, source_target_pairs={{0,2},{1,3},{2,0},{3,1},{4,6},{5,7},{6,4},{7,5},{8,10},{9,11},{10,... | collective-permute-start | bytes 1572872 | tf_op jit(solution)/shard_map/ppermute | solution.py:259
  32.9 0.0 copy-done.10
  32.9 2.9 %collective-permute-start.3 = (bf16[8,64,128]{2,1,0:T(8,128)(2,1)S(1)}, bf16[8,64,128]{2,1,0:T(8,128)(2,1)S(1)}, u32[]{:S(2)}, u32[]{:S(2)}) collective-permute-start(bf16[8,64,128]{2,1,0:T(8,128)(2,1)S(1)} %copy-done.10), channel_id=1, source_target_pairs={{0,4},{4,8},{8,12},{12,16},{16,20},{20,24},{24,28},{28,32},{32,36}... | collective-permute-start | bytes 393224 | tf_op jit(solution)/shard_map/ppermute | solution.py:265
  35.8 0.0 copy-done.9
  35.9 7.5 %collective-permute-start.4 = (bf16[8,64,128]{2,1,0:T(8,128)(2,1)S(1)}, bf16[8,64,128]{2,1,0:T(8,128)(2,1)S(1)}, u32[]{:S(2)}, u32[]{:S(2)}) collective-permute-start(bf16[8,64,128]{2,1,0:T(8,128)(2,1)S(1)} %copy-done.9), channel_id=1, source_target_pairs={{4,0},{8,4},{12,8},{16,12},{20,16},{24,20},{28,24},{32,28},{36,32}... | collective-permute-start | bytes 393224 | tf_op jit(solution)/shard_map/ppermute | solution.py:265
  43.4 0.0 copy-done.8
  43.4 0.1 copy.10
  43.5 29.4 %collective-permute-done.3.low_ref = bf16[8,64,128]{2,1,0:T(8,128)(2,1)S(1)} collective-permute-done((bf16[8,64,128]{2,1,0:T(8,128)(2,1)S(1)}, bf16[8,64,128]{2,1,0:T(8,128)(2,1)S(1)}, u32[]{:S(2)}, u32[]{:S(2)}) %collective-permute-start.3) | collective-permute-done | bytes 131104 | tf_op jit(solution)/shard_map/ppermute | solution.py:265
  72.9 0.0 collective-permute-done.4.high_ref
  72.9 1.6 copy-done.1
  74.5 3.6 %sparse.1 = (f32[32,64,128]{2,1,0:T(8,128)S(1)}, f32[32,64,128]{2,1,0:T(8,128)S(1)}, bf16[8,64,128]{2,1,0:T(8,128)(2,1)S(1)}, bf16[8,64,128]{2,1,0:T(8,128)(2,1)S(1)}) custom-call(s32[32,8]{1,0:T(8,128)S(1)} %subtract_add_fusion.cols_ref, bf16[32,64,512]{2,1,0:T(8,128)(2,1)S(1)} %copy-done.1, bf16[32,64,128]{2,1,0:T(8,128)(2,1)S(1)} %bitcast.26, ...), custom_call_target="tpu_custom_call" | custom-call | flops 536870912 | bytes 6291456 | tf_op jit(solution)/shard_map/sparse/pallas_call | solution.py:109
  78.1 0.0 copy-start.2
  78.1 1.0 copy-done.2
  79.1 1.0 copy-done.4
  80.1 0.0 collective-permute-done
  80.1 0.0 collective-permute-done.2
  80.1 0.0 copy-start.7
  80.1 0.0 collective-permute-done.1
  80.1 0.8 copy-done.6
  80.9 0.2 copy-done.7
  81.1 1.8 pad_maximum_fusion.own_ref
  82.8 1.9 %collective-permute-start.5 = (bf16[4,2048,128]{2,1,0:T(8,128)(2,1)S(1)}, bf16[4,2048,128]{2,1,0:T(8,128)(2,1)}, u32[]{:S(2)}, u32[]{:S(2)}) collective-permute-start(bf16[4,2048,128]{2,1,0:T(8,128)(2,1)S(1)} %pad_maximum_fusion.own_ref), channel_id=1, source_target_pairs={{0,256},{256,0},{1,257},{257,1},{2,258},{258,2},{3,259},{259,3},{4... | collective-permute-start | bytes 6291464 | tf_op jit(solution)/shard_map/ppermute | solution.py:259
  84.8 0.1 pad_add_fusion.at_ref
  84.8 4.2 %collective-permute-done.5.other_ref = bf16[4,2048,128]{2,1,0:T(8,128)(2,1)} collective-permute-done((bf16[4,2048,128]{2,1,0:T(8,128)(2,1)S(1)}, bf16[4,2048,128]{2,1,0:T(8,128)(2,1)}, u32[]{:S(2)}, u32[]{:S(2)}) %collective-permute-start.5) | collective-permute-done | bytes 2097184 | tf_op jit(solution)/shard_map/ppermute | solution.py:259
  89.0 0.0 all-to-all-done.gen_ref.refs_0_
  89.0 3.2 %partials.1 = bf16[16,4,8,128]{3,2,1,0:T(8,128)(2,1)} custom-call(s32[2]{0:T(128)S(1)} %pad_add_fusion.at_ref, bf16[64,64,128]{2,1,0:T(8,128)(2,1)S(1)} %all-to-all-done.gen_ref.refs_0_, bf16[4,2048,128]{2,1,0:T(8,128)(2,1)S(1)} %pad_maximum_fusion.own_ref, bf16[4,2048,128]{2,1,0:T(8,128)(2,1)} %collective-permute-done.5.other_ref), custom_call_target="tpu_custom_call" | custom-call | flops 536870912 | bytes 6291456 | tf_op jit(solution)/shard_map/partials/pallas_call | solution.py:168
  92.2 12.3 %all-to-all-start.1 = ((bf16[16,4,8,128]{3,2,1,0:T(8,128)(2,1)}), bf16[16,4,8,128]{3,2,1,0:T(8,128)(2,1)S(1)}, u32[]{:S(2)}, u32[]{:S(2)}) async-start(bf16[16,4,8,128]{3,2,1,0:T(8,128)(2,1)} %partials.1), calls=%async_computation.1 | async-start | bytes 262144 | tf_op jit(solution)/shard_map/all_to_all | solution.py:269
  104.5 1.0 fusion.2
  105.6 4.6 %collective-permute-start.9 = (bf16[64,32,128]{2,1,0:T(8,128)(2,1)}, bf16[64,32,128]{2,1,0:T(8,128)(2,1)S(1)}, u32[]{:S(2)}, u32[]{:S(2)}) collective-permute-start(bf16[64,32,128]{2,1,0:T(8,128)(2,1)} %get-tuple-element.42), channel_id=1, source_target_pairs={{0,3},{1,0},{2,1},{3,2},{4,7},{5,4},{6,5},{7,6},{8,11},{9,8},{10,9... | collective-permute-start | bytes 1572872 | tf_op jit(solution)/shard_map/ppermute | solution.py:259
  110.2 1.9 %collective-permute-start.6 = (bf16[64,32,128]{2,1,0:T(8,128)(2,1)}, bf16[64,32,128]{2,1,0:T(8,128)(2,1)S(1)}, u32[]{:S(2)}, u32[]{:S(2)}) collective-permute-start(bf16[64,32,128]{2,1,0:T(8,128)(2,1)} %get-tuple-element.43), channel_id=1, source_target_pairs={{0,1},{1,2},{2,3},{3,0},{4,5},{5,6},{6,7},{7,4},{8,9},{9,10},{10,1... | collective-permute-start | bytes 1572872 | tf_op jit(solution)/shard_map/ppermute | solution.py:259
  112.2 4.5 %all-to-all-done.1 = bf16[16,4,8,128]{3,2,1,0:T(8,128)(2,1)S(1)} async-done(((bf16[16,4,8,128]{3,2,1,0:T(8,128)(2,1)}), bf16[16,4,8,128]{3,2,1,0:T(8,128)(2,1)S(1)}, u32[]{:S(2)}, u32[]{:S(2)}) %all-to-all-start.1) | async-done | bytes 131104 | tf_op jit(solution)/shard_map/all_to_all | solution.py:269
  116.7 0.6 broadcast_in_dim.6
  117.3 4.3 %all-to-all-start.2 = ((f32[16,8,128]{2,1,0:T(8,128)}), f32[16,8,128]{2,1,0:T(8,128)S(1)}, u32[]{:S(2)}, u32[]{:S(2)}) async-start(f32[16,8,128]{2,1,0:T(8,128)} %bitcast.10), calls=%async_computation.2 | async-start | bytes 131072 | tf_op jit(solution)/shard_map/all_to_all | solution.py:269
  121.6 3.3 %collective-permute-start.7 = (bf16[64,32,128]{2,1,0:T(8,128)(2,1)}, bf16[64,32,128]{2,1,0:T(8,128)(2,1)S(1)}, u32[]{:S(2)}, u32[]{:S(2)}) collective-permute-start(bf16[64,32,128]{2,1,0:T(8,128)(2,1)} %get-tuple-element.42), channel_id=1, source_target_pairs={{0,1},{1,2},{2,3},{3,0},{4,5},{5,6},{6,7},{7,4},{8,9},{9,10},{10,1... | collective-permute-start | bytes 1572872 | tf_op jit(solution)/shard_map/ppermute | solution.py:259
  124.9 3.2 %collective-permute-start.11 = (bf16[64,32,128]{2,1,0:T(8,128)(2,1)}, bf16[64,32,128]{2,1,0:T(8,128)(2,1)S(1)}, u32[]{:S(2)}, u32[]{:S(2)}) collective-permute-start(bf16[64,32,128]{2,1,0:T(8,128)(2,1)} %get-tuple-element.43), channel_id=1, source_target_pairs={{0,3},{1,0},{2,1},{3,2},{4,7},{5,4},{6,5},{7,6},{8,11},{9,8},{10,9... | collective-permute-start | bytes 1572872 | tf_op jit(solution)/shard_map/ppermute | solution.py:259
  128.1 0.0 collective-permute-done.9.refs_6_
  128.1 3.3 %collective-permute-start.10 = (bf16[64,32,128]{2,1,0:T(8,128)(2,1)S(1)}, bf16[64,32,128]{2,1,0:T(8,128)(2,1)}, u32[]{:S(2)}, u32[]{:S(2)}) collective-permute-start(bf16[64,32,128]{2,1,0:T(8,128)(2,1)S(1)} %collective-permute-done.9.refs_6_), channel_id=1, source_target_pairs={{0,3},{1,0},{2,1},{3,2},{4,7},{5,4},{6,5},{7,6},{8,11},{9,8},{10,9... | collective-permute-start | bytes 1572872 | tf_op jit(solution)/shard_map/ppermute | solution.py:259
  131.4 0.0 collective-permute-done.6.refs_1_
  131.4 2.0 %collective-permute-start.8 = (bf16[64,32,128]{2,1,0:T(8,128)(2,1)S(1)}, bf16[64,32,128]{2,1,0:T(8,128)(2,1)}, u32[]{:S(2)}, u32[]{:S(2)}) collective-permute-start(bf16[64,32,128]{2,1,0:T(8,128)(2,1)S(1)} %collective-permute-done.6.refs_1_), channel_id=1, source_target_pairs={{0,1},{1,2},{2,3},{3,0},{4,5},{5,6},{6,7},{7,4},{8,9},{9,10},{10,1... | collective-permute-start | bytes 1572872 | tf_op jit(solution)/shard_map/ppermute | solution.py:259
  133.4 0.0 all-to-all-done.2
  133.5 0.7 broadcast_in_dim.7
  134.1 6.7 %all-to-all-start.3 = ((bf16[16,4,8,128]{3,2,1,0:T(8,128)(2,1)}), bf16[16,4,8,128]{3,2,1,0:T(8,128)(2,1)S(1)}, u32[]{:S(2)}, u32[]{:S(2)}) async-start(bf16[16,4,8,128]{3,2,1,0:T(8,128)(2,1)} %broadcast_in_dim.7), calls=%async_computation.3 | async-start | bytes 262144 | tf_op jit(solution)/shard_map/all_to_all | solution.py:269
  140.9 0.0 collective-permute-done.7.refs_2_
  140.9 0.0 collective-permute-done.11.refs_5_
  140.9 11.9 %all-to-all-done.3.refs_7_ = bf16[16,4,8,128]{3,2,1,0:T(8,128)(2,1)S(1)} async-done(((bf16[16,4,8,128]{3,2,1,0:T(8,128)(2,1)}), bf16[16,4,8,128]{3,2,1,0:T(8,128)(2,1)S(1)}, u32[]{:S(2)}, u32[]{:S(2)}) %all-to-all-start.3) | async-done | bytes 131104 | tf_op jit(solution)/shard_map/all_to_all | solution.py:269
  152.8 0.0 collective-permute-done.10.refs_4_
  152.8 0.0 collective-permute-done.8.refs_3_
  152.9 3.9 %theirs.1 = bf16[2,32,64,128]{3,2,1,0:T(8,128)(2,1)S(1)} custom-call(s32[2]{0:T(128)S(1)} %pad_add_fusion.at_ref, bf16[64,64,128]{2,1,0:T(8,128)(2,1)S(1)} %all-to-all-done.gen_ref.refs_0_, bf16[64,32,128]{2,1,0:T(8,128)(2,1)S(1)} %collective-permute-done.6.refs_1_, bf16[64,32,128]{2,1,0:T(8,128)(2,1)S(1)} %collective-permute-done.7.refs_2_, ...), custom_call_target="tpu_custom_call" | custom-call | flops 536870912 | bytes 4194304 | tf_op jit(solution)/shard_map/theirs/pallas_call | solution.py:241
  156.8 6.7 %collective-permute-start.14 = (bf16[2,32,64,128]{3,2,1,0:T(8,128)(2,1)S(1)}, bf16[2,32,64,128]{3,2,1,0:T(8,128)(2,1)S(1)}, u32[]{:S(2)}, u32[]{:S(2)}) collective-permute-start(bf16[2,32,64,128]{3,2,1,0:T(8,128)(2,1)S(1)} %theirs.1), channel_id=1, source_target_pairs={{0,256},{256,0},{1,257},{257,1},{2,258},{258,2},{3,259},{259,3},{4... | collective-permute-start | bytes 3145736 | tf_op jit(solution)/shard_map/ppermute | solution.py:259
  163.5 3.1 %collective-permute-start.12 = (bf16[8,64,128]{2,1,0:T(8,128)(2,1)S(1)}, bf16[8,64,128]{2,1,0:T(8,128)(2,1)S(1)}, u32[]{:S(2)}, u32[]{:S(2)}) collective-permute-start(bf16[8,64,128]{2,1,0:T(8,128)(2,1)S(1)} %get-tuple-element.36), channel_id=1, source_target_pairs={{0,4},{4,8},{8,12},{12,16},{16,20},{20,24},{24,28},{28,32},{32,36}... | collective-permute-start | bytes 393224 | tf_op jit(solution)/shard_map/ppermute | solution.py:265
  166.6 5.7 %collective-permute-start.13 = (bf16[8,64,128]{2,1,0:T(8,128)(2,1)S(1)}, bf16[8,64,128]{2,1,0:T(8,128)(2,1)S(1)}, u32[]{:S(2)}, u32[]{:S(2)}) collective-permute-start(bf16[8,64,128]{2,1,0:T(8,128)(2,1)S(1)} %get-tuple-element.37), channel_id=1, source_target_pairs={{4,0},{8,4},{12,8},{16,12},{20,16},{24,20},{28,24},{32,28},{36,32}... | collective-permute-start | bytes 393224 | tf_op jit(solution)/shard_map/ppermute | solution.py:265
  172.4 0.7 collective-permute-done.12.refs_10_
  173.1 1.2 collective-permute-done.13.refs_11_
  174.3 0.0 copy-done.3
  174.3 3.9 %mine.1 = (f32[32,64,128]{2,1,0:T(8,128)S(1)}, f32[32,64,128]{2,1,0:T(8,128)S(1)}) custom-call(s32[2]{0:T(128)S(1)} %pad_add_fusion.at_ref, bf16[64,64,128]{2,1,0:T(8,128)(2,1)S(1)} %all-to-all-done.gen_ref.refs_0_, bf16[64,32,128]{2,1,0:T(8,128)(2,1)S(1)} %collective-permute-done.6.refs_1_, bf16[64,32,128]{2,1,0:T(8,128)(2,1)S(1)} %collective-permute-done.7.refs_2_, ...), custom_call_target="tpu_custom_call" | custom-call | flops 536870912 | bytes 4194304 | tf_op jit(solution)/shard_map/mine/pallas_call | solution.py:241
  178.2 0.0 collective-permute-done.14
  178.2 1.3 fusion
  (11 shorter events, 0.1 us)
Async XLA Ops:
  0.6 22.1 %copy-start = (bf16[2048,128]{1,0:T(8,128)(2,1)S(1)}, bf16[2048,128]{1,0:T(8,128)(2,1)}, u32[]{:S(2)}) copy-start(bf16[2048,128]{1,0:T(8,128)(2,1)} %param.6) | copy-start | bytes 1572868
  0.6 42.7 %copy-start.8 = (s32[32,8]{0,1:T(8,128)S(1)}, s32[32,8]{0,1:T(8,128)}, u32[]{:S(2)}) copy-start(s32[32,8]{0,1:T(8,128)} %param.8) | copy-start | bytes 3076
  3.5 29.4 %copy-start.10 = (bf16[8,64,128]{2,1,0:T(8,128)(2,1)S(1)}, bf16[8,64,128]{2,1,0:T(8,128)(2,1)}, u32[]{:S(2)}) copy-start(bf16[8,64,128]{2,1,0:T(8,128)(2,1)} %get-tuple-element.22) | copy-start | bytes 393220
  3.5 32.3 %copy-start.9 = (bf16[8,64,128]{2,1,0:T(8,128)(2,1)S(1)}, bf16[8,64,128]{2,1,0:T(8,128)(2,1)}, u32[]{:S(2)}) copy-start(bf16[8,64,128]{2,1,0:T(8,128)(2,1)} %get-tuple-element.23) | copy-start | bytes 393220
  3.5 85.5 %all-to-all-start = ((bf16[64,64,128]{2,1,0:T(8,128)(2,1)}), bf16[64,64,128]{2,1,0:T(8,128)(2,1)S(1)}, u32[]{:S(2)}, u32[]{:S(2)}) async-start(bf16[64,64,128]{2,1,0:T(8,128)(2,1)} %get-tuple-element.21), calls=%async_computation | async-start | bytes 2097152 | tf_op jit(solution)/shard_map/all_to_all | solution.py:269
  22.8 57.3 %collective-permute-start = (bf16[2048,128]{1,0:T(8,128)(2,1)S(1)}, bf16[2048,128]{1,0:T(8,128)(2,1)S(1)}, u32[]{:S(2)}, u32[]{:S(2)}) collective-permute-start(bf16[2048,128]{1,0:T(8,128)(2,1)S(1)} %copy-done), channel_id=1, source_target_pairs={{0,1},{1,2},{2,3},{3,0},{4,5},{5,6},{6,7},{7,4},{8,9},{9,10},{10,1... | collective-permute-start | bytes 1572872 | tf_op jit(solution)/shard_map/ppermute | solution.py:259
  26.0 54.1 %collective-permute-start.2 = (bf16[2048,128]{1,0:T(8,128)(2,1)S(1)}, bf16[2048,128]{1,0:T(8,128)(2,1)S(1)}, u32[]{:S(2)}, u32[]{:S(2)}) collective-permute-start(bf16[2048,128]{1,0:T(8,128)(2,1)S(1)} %copy-done), channel_id=1, source_target_pairs={{0,3},{1,0},{2,1},{3,2},{4,7},{5,4},{6,5},{7,6},{8,11},{9,8},{10,9... | collective-permute-start | bytes 1572872 | tf_op jit(solution)/shard_map/ppermute | solution.py:259
  29.4 50.8 %collective-permute-start.1 = (bf16[2048,128]{1,0:T(8,128)(2,1)S(1)}, bf16[2048,128]{1,0:T(8,128)(2,1)}, u32[]{:S(2)}, u32[]{:S(2)}) collective-permute-start(bf16[2048,128]{1,0:T(8,128)(2,1)S(1)} %copy-done), channel_id=1, source_target_pairs={{0,2},{1,3},{2,0},{3,1},{4,6},{5,7},{6,4},{7,5},{8,10},{9,11},{10,... | collective-permute-start | bytes 1572872 | tf_op jit(solution)/shard_map/ppermute | solution.py:259
  32.9 40.0 %collective-permute-start.3 = (bf16[8,64,128]{2,1,0:T(8,128)(2,1)S(1)}, bf16[8,64,128]{2,1,0:T(8,128)(2,1)S(1)}, u32[]{:S(2)}, u32[]{:S(2)}) collective-permute-start(bf16[8,64,128]{2,1,0:T(8,128)(2,1)S(1)} %copy-done.10), channel_id=1, source_target_pairs={{0,4},{4,8},{8,12},{12,16},{16,20},{20,24},{24,28},{28,32},{32,36}... | collective-permute-start | bytes 393224 | tf_op jit(solution)/shard_map/ppermute | solution.py:265
  35.9 37.1 %collective-permute-start.4 = (bf16[8,64,128]{2,1,0:T(8,128)(2,1)S(1)}, bf16[8,64,128]{2,1,0:T(8,128)(2,1)S(1)}, u32[]{:S(2)}, u32[]{:S(2)}) collective-permute-start(bf16[8,64,128]{2,1,0:T(8,128)(2,1)S(1)} %copy-done.9), channel_id=1, source_target_pairs={{4,0},{8,4},{12,8},{16,12},{20,16},{24,20},{28,24},{32,28},{36,32}... | collective-permute-start | bytes 393224 | tf_op jit(solution)/shard_map/ppermute | solution.py:265
  72.9 1.6 copy-start.1
  78.1 1.0 copy-start.2
  79.1 1.0 copy-start.4
  80.1 0.8 copy-start.6
  80.1 1.0 copy-start.7
  82.8 6.2 %collective-permute-start.5 = (bf16[4,2048,128]{2,1,0:T(8,128)(2,1)S(1)}, bf16[4,2048,128]{2,1,0:T(8,128)(2,1)}, u32[]{:S(2)}, u32[]{:S(2)}) collective-permute-start(bf16[4,2048,128]{2,1,0:T(8,128)(2,1)S(1)} %pad_maximum_fusion.own_ref), channel_id=1, source_target_pairs={{0,256},{256,0},{1,257},{257,1},{2,258},{258,2},{3,259},{259,3},{4... | collective-permute-start | bytes 6291464 | tf_op jit(solution)/shard_map/ppermute | solution.py:259
  92.2 24.4 %all-to-all-start.1 = ((bf16[16,4,8,128]{3,2,1,0:T(8,128)(2,1)}), bf16[16,4,8,128]{3,2,1,0:T(8,128)(2,1)S(1)}, u32[]{:S(2)}, u32[]{:S(2)}) async-start(bf16[16,4,8,128]{3,2,1,0:T(8,128)(2,1)} %partials.1), calls=%async_computation.1 | async-start | bytes 262144 | tf_op jit(solution)/shard_map/all_to_all | solution.py:269
  105.6 22.5 %collective-permute-start.9 = (bf16[64,32,128]{2,1,0:T(8,128)(2,1)}, bf16[64,32,128]{2,1,0:T(8,128)(2,1)S(1)}, u32[]{:S(2)}, u32[]{:S(2)}) collective-permute-start(bf16[64,32,128]{2,1,0:T(8,128)(2,1)} %get-tuple-element.42), channel_id=1, source_target_pairs={{0,3},{1,0},{2,1},{3,2},{4,7},{5,4},{6,5},{7,6},{8,11},{9,8},{10,9... | collective-permute-start | bytes 1572872 | tf_op jit(solution)/shard_map/ppermute | solution.py:259
  110.2 21.2 %collective-permute-start.6 = (bf16[64,32,128]{2,1,0:T(8,128)(2,1)}, bf16[64,32,128]{2,1,0:T(8,128)(2,1)S(1)}, u32[]{:S(2)}, u32[]{:S(2)}) collective-permute-start(bf16[64,32,128]{2,1,0:T(8,128)(2,1)} %get-tuple-element.43), channel_id=1, source_target_pairs={{0,1},{1,2},{2,3},{3,0},{4,5},{5,6},{6,7},{7,4},{8,9},{9,10},{10,1... | collective-permute-start | bytes 1572872 | tf_op jit(solution)/shard_map/ppermute | solution.py:259
  117.3 16.1 %all-to-all-start.2 = ((f32[16,8,128]{2,1,0:T(8,128)}), f32[16,8,128]{2,1,0:T(8,128)S(1)}, u32[]{:S(2)}, u32[]{:S(2)}) async-start(f32[16,8,128]{2,1,0:T(8,128)} %bitcast.10), calls=%async_computation.2 | async-start | bytes 131072 | tf_op jit(solution)/shard_map/all_to_all | solution.py:269
  121.6 19.3 %collective-permute-start.7 = (bf16[64,32,128]{2,1,0:T(8,128)(2,1)}, bf16[64,32,128]{2,1,0:T(8,128)(2,1)S(1)}, u32[]{:S(2)}, u32[]{:S(2)}) collective-permute-start(bf16[64,32,128]{2,1,0:T(8,128)(2,1)} %get-tuple-element.42), channel_id=1, source_target_pairs={{0,1},{1,2},{2,3},{3,0},{4,5},{5,6},{6,7},{7,4},{8,9},{9,10},{10,1... | collective-permute-start | bytes 1572872 | tf_op jit(solution)/shard_map/ppermute | solution.py:259
  124.9 16.0 %collective-permute-start.11 = (bf16[64,32,128]{2,1,0:T(8,128)(2,1)}, bf16[64,32,128]{2,1,0:T(8,128)(2,1)S(1)}, u32[]{:S(2)}, u32[]{:S(2)}) collective-permute-start(bf16[64,32,128]{2,1,0:T(8,128)(2,1)} %get-tuple-element.43), channel_id=1, source_target_pairs={{0,3},{1,0},{2,1},{3,2},{4,7},{5,4},{6,5},{7,6},{8,11},{9,8},{10,9... | collective-permute-start | bytes 1572872 | tf_op jit(solution)/shard_map/ppermute | solution.py:259
  128.1 24.7 %collective-permute-start.10 = (bf16[64,32,128]{2,1,0:T(8,128)(2,1)S(1)}, bf16[64,32,128]{2,1,0:T(8,128)(2,1)}, u32[]{:S(2)}, u32[]{:S(2)}) collective-permute-start(bf16[64,32,128]{2,1,0:T(8,128)(2,1)S(1)} %collective-permute-done.9.refs_6_), channel_id=1, source_target_pairs={{0,3},{1,0},{2,1},{3,2},{4,7},{5,4},{6,5},{7,6},{8,11},{9,8},{10,9... | collective-permute-start | bytes 1572872 | tf_op jit(solution)/shard_map/ppermute | solution.py:259
  131.4 21.4 %collective-permute-start.8 = (bf16[64,32,128]{2,1,0:T(8,128)(2,1)S(1)}, bf16[64,32,128]{2,1,0:T(8,128)(2,1)}, u32[]{:S(2)}, u32[]{:S(2)}) collective-permute-start(bf16[64,32,128]{2,1,0:T(8,128)(2,1)S(1)} %collective-permute-done.6.refs_1_), channel_id=1, source_target_pairs={{0,1},{1,2},{2,3},{3,0},{4,5},{5,6},{6,7},{7,4},{8,9},{9,10},{10,1... | collective-permute-start | bytes 1572872 | tf_op jit(solution)/shard_map/ppermute | solution.py:259
  134.1 18.7 %all-to-all-start.3 = ((bf16[16,4,8,128]{3,2,1,0:T(8,128)(2,1)}), bf16[16,4,8,128]{3,2,1,0:T(8,128)(2,1)S(1)}, u32[]{:S(2)}, u32[]{:S(2)}) async-start(bf16[16,4,8,128]{3,2,1,0:T(8,128)(2,1)} %broadcast_in_dim.7), calls=%async_computation.3 | async-start | bytes 262144 | tf_op jit(solution)/shard_map/all_to_all | solution.py:269
  152.8 21.5 %copy-start.3 = (f32[32,64,128]{2,1,0:T(8,128)S(1)}, f32[32,64,128]{2,1,0:T(8,128)}, u32[]{:S(2)}) copy-start(f32[32,64,128]{2,1,0:T(8,128)} %copy-done.2) | copy-start | bytes 3145732
  152.8 21.5 %copy-start.5 = (f32[32,64,128]{2,1,0:T(8,128)S(1)}, f32[32,64,128]{2,1,0:T(8,128)}, u32[]{:S(2)}) copy-start(f32[32,64,128]{2,1,0:T(8,128)} %copy-done.4) | copy-start | bytes 3145732
  156.8 21.5 %collective-permute-start.14 = (bf16[2,32,64,128]{3,2,1,0:T(8,128)(2,1)S(1)}, bf16[2,32,64,128]{3,2,1,0:T(8,128)(2,1)S(1)}, u32[]{:S(2)}, u32[]{:S(2)}) collective-permute-start(bf16[2,32,64,128]{3,2,1,0:T(8,128)(2,1)S(1)} %theirs.1), channel_id=1, source_target_pairs={{0,256},{256,0},{1,257},{257,1},{2,258},{258,2},{3,259},{259,3},{4... | collective-permute-start | bytes 3145736 | tf_op jit(solution)/shard_map/ppermute | solution.py:259
  163.5 9.6 %collective-permute-start.12 = (bf16[8,64,128]{2,1,0:T(8,128)(2,1)S(1)}, bf16[8,64,128]{2,1,0:T(8,128)(2,1)S(1)}, u32[]{:S(2)}, u32[]{:S(2)}) collective-permute-start(bf16[8,64,128]{2,1,0:T(8,128)(2,1)S(1)} %get-tuple-element.36), channel_id=1, source_target_pairs={{0,4},{4,8},{8,12},{12,16},{16,20},{20,24},{24,28},{28,32},{32,36}... | collective-permute-start | bytes 393224 | tf_op jit(solution)/shard_map/ppermute | solution.py:265
  166.6 7.7 %collective-permute-start.13 = (bf16[8,64,128]{2,1,0:T(8,128)(2,1)S(1)}, bf16[8,64,128]{2,1,0:T(8,128)(2,1)S(1)}, u32[]{:S(2)}, u32[]{:S(2)}) collective-permute-start(bf16[8,64,128]{2,1,0:T(8,128)(2,1)S(1)} %get-tuple-element.37), channel_id=1, source_target_pairs={{4,0},{8,4},{12,8},{16,12},{20,16},{24,20},{28,24},{32,28},{36,32}... | collective-permute-start | bytes 393224 | tf_op jit(solution)/shard_map/ppermute | solution.py:265

commit v9 on v8

--- a/solution.py
+++ b/solution.py
@@ -208,8 +208,11 @@
                 sr_ref, sp_ref, below_ref, above_ref, range_ref, rows_ref = refs[:-1]
                 range_ref[b] = for_range + sr_ref[b]
                 for_rows += sp_ref[b]
-                for_rows += jnp.where(step == 0, below_ref[b].astype(F32), 0.0)
-                for_rows += jnp.where(step == steps - 1, above_ref[b].astype(F32), 0.0)
+                if b < HB:
+                    for_rows += jnp.where(step == 0, below_ref[b].astype(F32), 0.0)
+                if b >= per - HB:
+                    above = above_ref[b - (per - HB)].astype(F32)
+                    for_rows += jnp.where(step == steps - 1, above, 0.0)
                 rows_ref[b] = for_rows
             else:
                 refs[0][0, b] = for_range.astype(BF16)
@@ -218,7 +221,7 @@
 
 def low_rank(at, gens, w, added=()):
     blocks, _, _ = gens[0].shape
-    count, per = blocks // 2, HB
+    count, per = blocks // 2, 2 * HB
     steps = count // per
     mine = bool(added)
     depth = sum(g.shape[1] for g in gens)

time: 181 us -> 179 us (0.989)
  Pallas kernels: 17.5 us -> 15.6 us
    pallas_call x2, Pallas kernels: 7.79 us -> 5.96 us  [low_rank(): pl.pallas_call(functools.partial(low_rank_kernel, mine, len(gens)), grid_...]
where the time goes in v9:
time: 179 us; the launch traced here: 178 us
  starting transfers between devices  99 us (55%)
  waiting for transfers between devices  52 us (29%)
  Pallas kernels  15.6 us (9%)
  local copies, waits for them, and re-layouts  6.91 us (4%)
  other arithmetic  3.19 us (2%)
    all_to_all x4, starting transfers between devices, spread_out(): return lax.all_to_all(x, axis, split_axis=0, concat_axis=0, tiled=True)  42.6 us
    ppermute x11, starting transfers between devices, around(): return lax.ppermute(x, axis, [(i, (i + by) % count) for i in range(count)])  37.1 us
    ppermute x4, waiting for transfers between devices, along_front(): return lax.ppermute(x, FRONT, pairs)  31.4 us
    ppermute x4, starting transfers between devices, along_front(): return lax.ppermute(x, FRONT, pairs)  19.3 us
    all_to_all x4, waiting for transfers between devices, spread_out(): return lax.all_to_all(x, axis, split_axis=0, concat_axis=0, tiled=True)  16.4 us
    pallas_call x2, Pallas kernels, low_rank(): pl.pallas_call(functools.partial(low_rank_kernel, mine, len(gens)), grid_...  5.96 us
    unnamed x23, local copies, waits for them, and re-layouts  4.58 us
    ppermute x11, waiting for transfers between devices, around(): return lax.ppermute(x, axis, [(i, (i + by) % count) for i in range(count)])  4.2 us
  transfers between devices with their start and end apart: 19, of which 6 were waited for; matrix products, arithmetic and copies ran while one was open for 2% of the time, Pallas kernels for 4%

profile of v9, /device:TPU:1, one launch (start us, length us, event | category | flops | bytes accessed | tf_op | source)
XLA Modules:
  0.0 177.7 jit_solution(708540666155914677)
XLA Ops:
  0.6 0.0 copy-start
  0.6 0.0 copy-start.8
  0.7 2.9 %pack.1 = (bf16[8,64,128]{2,1,0:T(8,128)(2,1)}, bf16[8,64,128]{2,1,0:T(8,128)(2,1)}, bf16[64,64,128]{2,1,0:T(8,128)(2,1)}) custom-call(s32[64]{0:T(128)} %bitcast.34, bf16[64,4096]{1,0:T(8,128)(2,1)} %bitcast.27, bf16[64,4096]{1,0:T(8,128)(2,1)} %bitcast.28, bf16[32,64,128]{2,1,0:T(8,128)(2,1)} %bitcast.24), custom_call_target="tpu_custom_call" | custom-call | bytes 2097152 | tf_op jit(solution)/shard_map/pack/pallas_call | solution.py:62
  3.5 19.2 %all-to-all-start = ((bf16[64,64,128]{2,1,0:T(8,128)(2,1)}), bf16[64,64,128]{2,1,0:T(8,128)(2,1)S(1)}, u32[]{:S(2)}, u32[]{:S(2)}) async-start(bf16[64,64,128]{2,1,0:T(8,128)(2,1)} %get-tuple-element.21), calls=%async_computation | async-start | bytes 2097152 | tf_op jit(solution)/shard_map/all_to_all | solution.py:272
  22.8 0.0 copy-done
  22.8 3.2 %collective-permute-start = (bf16[2048,128]{1,0:T(8,128)(2,1)S(1)}, bf16[2048,128]{1,0:T(8,128)(2,1)S(1)}, u32[]{:S(2)}, u32[]{:S(2)}) collective-permute-start(bf16[2048,128]{1,0:T(8,128)(2,1)S(1)} %copy-done), channel_id=1, source_target_pairs={{0,1},{1,2},{2,3},{3,0},{4,5},{5,6},{6,7},{7,4},{8,9},{9,10},{10,1... | collective-permute-start | bytes 1572872 | tf_op jit(solution)/shard_map/ppermute | solution.py:262
  26.0 3.4 %collective-permute-start.2 = (bf16[2048,128]{1,0:T(8,128)(2,1)S(1)}, bf16[2048,128]{1,0:T(8,128)(2,1)S(1)}, u32[]{:S(2)}, u32[]{:S(2)}) collective-permute-start(bf16[2048,128]{1,0:T(8,128)(2,1)S(1)} %copy-done), channel_id=1, source_target_pairs={{0,3},{1,0},{2,1},{3,2},{4,7},{5,4},{6,5},{7,6},{8,11},{9,8},{10,9... | collective-permute-start | bytes 1572872 | tf_op jit(solution)/shard_map/ppermute | solution.py:262
  29.4 3.5 %collective-permute-start.1 = (bf16[2048,128]{1,0:T(8,128)(2,1)S(1)}, bf16[2048,128]{1,0:T(8,128)(2,1)}, u32[]{:S(2)}, u32[]{:S(2)}) collective-permute-start(bf16[2048,128]{1,0:T(8,128)(2,1)S(1)} %copy-done), channel_id=1, source_target_pairs={{0,2},{1,3},{2,0},{3,1},{4,6},{5,7},{6,4},{7,5},{8,10},{9,11},{10,... | collective-permute-start | bytes 1572872 | tf_op jit(solution)/shard_map/ppermute | solution.py:262
  32.9 0.0 copy-done.10
  32.9 2.9 %collective-permute-start.3 = (bf16[8,64,128]{2,1,0:T(8,128)(2,1)S(1)}, bf16[8,64,128]{2,1,0:T(8,128)(2,1)S(1)}, u32[]{:S(2)}, u32[]{:S(2)}) collective-permute-start(bf16[8,64,128]{2,1,0:T(8,128)(2,1)S(1)} %copy-done.10), channel_id=1, source_target_pairs={{0,4},{4,8},{8,12},{12,16},{16,20},{20,24},{24,28},{28,32},{32,36}... | collective-permute-start | bytes 393224 | tf_op jit(solution)/shard_map/ppermute | solution.py:268
  35.8 0.0 copy-done.9
  35.9 7.5 %collective-permute-start.4 = (bf16[8,64,128]{2,1,0:T(8,128)(2,1)S(1)}, bf16[8,64,128]{2,1,0:T(8,128)(2,1)S(1)}, u32[]{:S(2)}, u32[]{:S(2)}) collective-permute-start(bf16[8,64,128]{2,1,0:T(8,128)(2,1)S(1)} %copy-done.9), channel_id=1, source_target_pairs={{4,0},{8,4},{12,8},{16,12},{20,16},{24,20},{28,24},{32,28},{36,32}... | collective-permute-start | bytes 393224 | tf_op jit(solution)/shard_map/ppermute | solution.py:268
  43.4 0.0 copy-done.8
  43.4 0.1 copy.10
  43.5 29.4 %collective-permute-done.3.low_ref = bf16[8,64,128]{2,1,0:T(8,128)(2,1)S(1)} collective-permute-done((bf16[8,64,128]{2,1,0:T(8,128)(2,1)S(1)}, bf16[8,64,128]{2,1,0:T(8,128)(2,1)S(1)}, u32[]{:S(2)}, u32[]{:S(2)}) %collective-permute-start.3) | collective-permute-done | bytes 131104 | tf_op jit(solution)/shard_map/ppermute | solution.py:268
  72.9 0.0 collective-permute-done.4.high_ref
  72.9 1.6 copy-done.1
  74.5 3.6 %sparse.1 = (f32[32,64,128]{2,1,0:T(8,128)S(1)}, f32[32,64,128]{2,1,0:T(8,128)S(1)}, bf16[8,64,128]{2,1,0:T(8,128)(2,1)S(1)}, bf16[8,64,128]{2,1,0:T(8,128)(2,1)S(1)}) custom-call(s32[32,8]{1,0:T(8,128)S(1)} %subtract_add_fusion.cols_ref, bf16[32,64,512]{2,1,0:T(8,128)(2,1)S(1)} %copy-done.1, bf16[32,64,128]{2,1,0:T(8,128)(2,1)S(1)} %bitcast.26, ...), custom_call_target="tpu_custom_call" | custom-call | flops 536870912 | bytes 6291456 | tf_op jit(solution)/shard_map/sparse/pallas_call | solution.py:109
  78.1 0.0 copy-start.2
  78.1 1.0 copy-done.2
  79.1 1.0 copy-done.4
  80.1 0.0 collective-permute-done
  80.1 0.0 collective-permute-done.2
  80.1 0.0 copy-start.7
  80.1 0.0 collective-permute-done.1
  80.1 0.8 copy-done.6
  80.9 0.2 copy-done.7
  81.1 1.8 pad_maximum_fusion.own_ref
  82.8 1.9 %collective-permute-start.5 = (bf16[4,2048,128]{2,1,0:T(8,128)(2,1)S(1)}, bf16[4,2048,128]{2,1,0:T(8,128)(2,1)}, u32[]{:S(2)}, u32[]{:S(2)}) collective-permute-start(bf16[4,2048,128]{2,1,0:T(8,128)(2,1)S(1)} %pad_maximum_fusion.own_ref), channel_id=1, source_target_pairs={{0,256},{256,0},{1,257},{257,1},{2,258},{258,2},{3,259},{259,3},{4... | collective-permute-start | bytes 6291464 | tf_op jit(solution)/shard_map/ppermute | solution.py:262
  84.8 0.1 pad_add_fusion.at_ref
  84.8 4.2 %collective-permute-done.5.other_ref = bf16[4,2048,128]{2,1,0:T(8,128)(2,1)} collective-permute-done((bf16[4,2048,128]{2,1,0:T(8,128)(2,1)S(1)}, bf16[4,2048,128]{2,1,0:T(8,128)(2,1)}, u32[]{:S(2)}, u32[]{:S(2)}) %collective-permute-start.5) | collective-permute-done | bytes 2097184 | tf_op jit(solution)/shard_map/ppermute | solution.py:262
  89.0 0.0 all-to-all-done.gen_ref.refs_0_
  89.0 3.2 %partials.1 = bf16[16,4,8,128]{3,2,1,0:T(8,128)(2,1)} custom-call(s32[2]{0:T(128)S(1)} %pad_add_fusion.at_ref, bf16[64,64,128]{2,1,0:T(8,128)(2,1)S(1)} %all-to-all-done.gen_ref.refs_0_, bf16[4,2048,128]{2,1,0:T(8,128)(2,1)S(1)} %pad_maximum_fusion.own_ref, bf16[4,2048,128]{2,1,0:T(8,128)(2,1)} %collective-permute-done.5.other_ref), custom_call_target="tpu_custom_call" | custom-call | flops 536870912 | bytes 6291456 | tf_op jit(solution)/shard_map/partials/pallas_call | solution.py:168
  92.2 12.3 %all-to-all-start.1 = ((bf16[16,4,8,128]{3,2,1,0:T(8,128)(2,1)}), bf16[16,4,8,128]{3,2,1,0:T(8,128)(2,1)S(1)}, u32[]{:S(2)}, u32[]{:S(2)}) async-start(bf16[16,4,8,128]{3,2,1,0:T(8,128)(2,1)} %partials.1), calls=%async_computation.1 | async-start | bytes 262144 | tf_op jit(solution)/shard_map/all_to_all | solution.py:272
  104.5 1.0 fusion.2
  105.6 4.6 %collective-permute-start.9 = (bf16[64,32,128]{2,1,0:T(8,128)(2,1)}, bf16[64,32,128]{2,1,0:T(8,128)(2,1)S(1)}, u32[]{:S(2)}, u32[]{:S(2)}) collective-permute-start(bf16[64,32,128]{2,1,0:T(8,128)(2,1)} %get-tuple-element.42), channel_id=1, source_target_pairs={{0,3},{1,0},{2,1},{3,2},{4,7},{5,4},{6,5},{7,6},{8,11},{9,8},{10,9... | collective-permute-start | bytes 1572872 | tf_op jit(solution)/shard_map/ppermute | solution.py:262
  110.2 1.9 %collective-permute-start.6 = (bf16[64,32,128]{2,1,0:T(8,128)(2,1)}, bf16[64,32,128]{2,1,0:T(8,128)(2,1)S(1)}, u32[]{:S(2)}, u32[]{:S(2)}) collective-permute-start(bf16[64,32,128]{2,1,0:T(8,128)(2,1)} %get-tuple-element.43), channel_id=1, source_target_pairs={{0,1},{1,2},{2,3},{3,0},{4,5},{5,6},{6,7},{7,4},{8,9},{9,10},{10,1... | collective-permute-start | bytes 1572872 | tf_op jit(solution)/shard_map/ppermute | solution.py:262
  112.2 4.5 %all-to-all-done.1 = bf16[16,4,8,128]{3,2,1,0:T(8,128)(2,1)S(1)} async-done(((bf16[16,4,8,128]{3,2,1,0:T(8,128)(2,1)}), bf16[16,4,8,128]{3,2,1,0:T(8,128)(2,1)S(1)}, u32[]{:S(2)}, u32[]{:S(2)}) %all-to-all-start.1) | async-done | bytes 131104 | tf_op jit(solution)/shard_map/all_to_all | solution.py:272
  116.7 0.6 broadcast_in_dim.6
  117.3 4.3 %all-to-all-start.2 = ((f32[16,8,128]{2,1,0:T(8,128)}), f32[16,8,128]{2,1,0:T(8,128)S(1)}, u32[]{:S(2)}, u32[]{:S(2)}) async-start(f32[16,8,128]{2,1,0:T(8,128)} %bitcast.10), calls=%async_computation.2 | async-start | bytes 131072 | tf_op jit(solution)/shard_map/all_to_all | solution.py:272
  121.6 3.3 %collective-permute-start.7 = (bf16[64,32,128]{2,1,0:T(8,128)(2,1)}, bf16[64,32,128]{2,1,0:T(8,128)(2,1)S(1)}, u32[]{:S(2)}, u32[]{:S(2)}) collective-permute-start(bf16[64,32,128]{2,1,0:T(8,128)(2,1)} %get-tuple-element.42), channel_id=1, source_target_pairs={{0,1},{1,2},{2,3},{3,0},{4,5},{5,6},{6,7},{7,4},{8,9},{9,10},{10,1... | collective-permute-start | bytes 1572872 | tf_op jit(solution)/shard_map/ppermute | solution.py:262
  124.9 3.2 %collective-permute-start.11 = (bf16[64,32,128]{2,1,0:T(8,128)(2,1)}, bf16[64,32,128]{2,1,0:T(8,128)(2,1)S(1)}, u32[]{:S(2)}, u32[]{:S(2)}) collective-permute-start(bf16[64,32,128]{2,1,0:T(8,128)(2,1)} %get-tuple-element.43), channel_id=1, source_target_pairs={{0,3},{1,0},{2,1},{3,2},{4,7},{5,4},{6,5},{7,6},{8,11},{9,8},{10,9... | collective-permute-start | bytes 1572872 | tf_op jit(solution)/shard_map/ppermute | solution.py:262
  128.1 0.0 collective-permute-done.9.refs_6_
  128.1 3.3 %collective-permute-start.10 = (bf16[64,32,128]{2,1,0:T(8,128)(2,1)S(1)}, bf16[64,32,128]{2,1,0:T(8,128)(2,1)}, u32[]{:S(2)}, u32[]{:S(2)}) collective-permute-start(bf16[64,32,128]{2,1,0:T(8,128)(2,1)S(1)} %collective-permute-done.9.refs_6_), channel_id=1, source_target_pairs={{0,3},{1,0},{2,1},{3,2},{4,7},{5,4},{6,5},{7,6},{8,11},{9,8},{10,9... | collective-permute-start | bytes 1572872 | tf_op jit(solution)/shard_map/ppermute | solution.py:262
  131.4 0.0 collective-permute-done.6.refs_1_
  131.4 2.0 %collective-permute-start.8 = (bf16[64,32,128]{2,1,0:T(8,128)(2,1)S(1)}, bf16[64,32,128]{2,1,0:T(8,128)(2,1)}, u32[]{:S(2)}, u32[]{:S(2)}) collective-permute-start(bf16[64,32,128]{2,1,0:T(8,128)(2,1)S(1)} %collective-permute-done.6.refs_1_), channel_id=1, source_target_pairs={{0,1},{1,2},{2,3},{3,0},{4,5},{5,6},{6,7},{7,4},{8,9},{9,10},{10,1... | collective-permute-start | bytes 1572872 | tf_op jit(solution)/shard_map/ppermute | solution.py:262
  133.4 0.0 all-to-all-done.2
  133.5 0.7 broadcast_in_dim.7
  134.1 6.7 %all-to-all-start.3 = ((bf16[16,4,8,128]{3,2,1,0:T(8,128)(2,1)}), bf16[16,4,8,128]{3,2,1,0:T(8,128)(2,1)S(1)}, u32[]{:S(2)}, u32[]{:S(2)}) async-start(bf16[16,4,8,128]{3,2,1,0:T(8,128)(2,1)} %broadcast_in_dim.7), calls=%async_computation.3 | async-start | bytes 262144 | tf_op jit(solution)/shard_map/all_to_all | solution.py:272
  140.9 0.0 collective-permute-done.7.refs_2_
  140.9 0.0 collective-permute-done.11.refs_5_
  140.9 11.9 %all-to-all-done.3.refs_7_ = bf16[16,4,8,128]{3,2,1,0:T(8,128)(2,1)S(1)} async-done(((bf16[16,4,8,128]{3,2,1,0:T(8,128)(2,1)}), bf16[16,4,8,128]{3,2,1,0:T(8,128)(2,1)S(1)}, u32[]{:S(2)}, u32[]{:S(2)}) %all-to-all-start.3) | async-done | bytes 131104 | tf_op jit(solution)/shard_map/all_to_all | solution.py:272
  152.8 0.0 collective-permute-done.10.refs_4_
  152.8 0.0 collective-permute-done.8.refs_3_
  152.9 3.0 %theirs.1 = bf16[2,32,64,128]{3,2,1,0:T(8,128)(2,1)S(1)} custom-call(s32[2]{0:T(128)S(1)} %pad_add_fusion.at_ref, bf16[64,64,128]{2,1,0:T(8,128)(2,1)S(1)} %all-to-all-done.gen_ref.refs_0_, bf16[64,32,128]{2,1,0:T(8,128)(2,1)S(1)} %collective-permute-done.6.refs_1_, bf16[64,32,128]{2,1,0:T(8,128)(2,1)S(1)} %collective-permute-done.7.refs_2_, ...), custom_call_target="tpu_custom_call" | custom-call | flops 536870912 | bytes 4194304 | tf_op jit(solution)/shard_map/theirs/pallas_call | solution.py:244
  155.9 6.7 %collective-permute-start.14 = (bf16[2,32,64,128]{3,2,1,0:T(8,128)(2,1)S(1)}, bf16[2,32,64,128]{3,2,1,0:T(8,128)(2,1)S(1)}, u32[]{:S(2)}, u32[]{:S(2)}) collective-permute-start(bf16[2,32,64,128]{3,2,1,0:T(8,128)(2,1)S(1)} %theirs.1), channel_id=1, source_target_pairs={{0,256},{256,0},{1,257},{257,1},{2,258},{258,2},{3,259},{259,3},{4... | collective-permute-start | bytes 3145736 | tf_op jit(solution)/shard_map/ppermute | solution.py:262
  162.6 3.1 %collective-permute-start.12 = (bf16[8,64,128]{2,1,0:T(8,128)(2,1)S(1)}, bf16[8,64,128]{2,1,0:T(8,128)(2,1)S(1)}, u32[]{:S(2)}, u32[]{:S(2)}) collective-permute-start(bf16[8,64,128]{2,1,0:T(8,128)(2,1)S(1)} %get-tuple-element.36), channel_id=1, source_target_pairs={{0,4},{4,8},{8,12},{12,16},{16,20},{20,24},{24,28},{28,32},{32,36}... | collective-permute-start | bytes 393224 | tf_op jit(solution)/shard_map/ppermute | solution.py:268
  165.7 5.7 %collective-permute-start.13 = (bf16[8,64,128]{2,1,0:T(8,128)(2,1)S(1)}, bf16[8,64,128]{2,1,0:T(8,128)(2,1)S(1)}, u32[]{:S(2)}, u32[]{:S(2)}) collective-permute-start(bf16[8,64,128]{2,1,0:T(8,128)(2,1)S(1)} %get-tuple-element.37), channel_id=1, source_target_pairs={{4,0},{8,4},{12,8},{16,12},{20,16},{24,20},{28,24},{32,28},{36,32}... | collective-permute-start | bytes 393224 | tf_op jit(solution)/shard_map/ppermute | solution.py:268
  171.5 0.7 collective-permute-done.12.refs_10_
  172.2 1.2 collective-permute-done.13.refs_11_
  173.4 0.0 copy-done.3
  173.4 3.0 %mine.1 = (f32[32,64,128]{2,1,0:T(8,128)S(1)}, f32[32,64,128]{2,1,0:T(8,128)S(1)}) custom-call(s32[2]{0:T(128)S(1)} %pad_add_fusion.at_ref, bf16[64,64,128]{2,1,0:T(8,128)(2,1)S(1)} %all-to-all-done.gen_ref.refs_0_, bf16[64,32,128]{2,1,0:T(8,128)(2,1)S(1)} %collective-permute-done.6.refs_1_, bf16[64,32,128]{2,1,0:T(8,128)(2,1)S(1)} %collective-permute-done.7.refs_2_, ...), custom_call_target="tpu_custom_call" | custom-call | flops 536870912 | bytes 4194304 | tf_op jit(solution)/shard_map/mine/pallas_call | solution.py:244
  176.4 0.0 collective-permute-done.14
  176.4 1.3 fusion
  (11 shorter events, 0.1 us)
Async XLA Ops:
  0.6 22.1 %copy-start = (bf16[2048,128]{1,0:T(8,128)(2,1)S(1)}, bf16[2048,128]{1,0:T(8,128)(2,1)}, u32[]{:S(2)}) copy-start(bf16[2048,128]{1,0:T(8,128)(2,1)} %param.6) | copy-start | bytes 1572868
  0.6 42.7 %copy-start.8 = (s32[32,8]{0,1:T(8,128)S(1)}, s32[32,8]{0,1:T(8,128)}, u32[]{:S(2)}) copy-start(s32[32,8]{0,1:T(8,128)} %param.8) | copy-start | bytes 3076
  3.5 29.4 %copy-start.10 = (bf16[8,64,128]{2,1,0:T(8,128)(2,1)S(1)}, bf16[8,64,128]{2,1,0:T(8,128)(2,1)}, u32[]{:S(2)}) copy-start(bf16[8,64,128]{2,1,0:T(8,128)(2,1)} %get-tuple-element.22) | copy-start | bytes 393220
  3.5 32.3 %copy-start.9 = (bf16[8,64,128]{2,1,0:T(8,128)(2,1)S(1)}, bf16[8,64,128]{2,1,0:T(8,128)(2,1)}, u32[]{:S(2)}) copy-start(bf16[8,64,128]{2,1,0:T(8,128)(2,1)} %get-tuple-element.23) | copy-start | bytes 393220
  3.5 85.5 %all-to-all-start = ((bf16[64,64,128]{2,1,0:T(8,128)(2,1)}), bf16[64,64,128]{2,1,0:T(8,128)(2,1)S(1)}, u32[]{:S(2)}, u32[]{:S(2)}) async-start(bf16[64,64,128]{2,1,0:T(8,128)(2,1)} %get-tuple-element.21), calls=%async_computation | async-start | bytes 2097152 | tf_op jit(solution)/shard_map/all_to_all | solution.py:272
  22.8 57.3 %collective-permute-start = (bf16[2048,128]{1,0:T(8,128)(2,1)S(1)}, bf16[2048,128]{1,0:T(8,128)(2,1)S(1)}, u32[]{:S(2)}, u32[]{:S(2)}) collective-permute-start(bf16[2048,128]{1,0:T(8,128)(2,1)S(1)} %copy-done), channel_id=1, source_target_pairs={{0,1},{1,2},{2,3},{3,0},{4,5},{5,6},{6,7},{7,4},{8,9},{9,10},{10,1... | collective-permute-start | bytes 1572872 | tf_op jit(solution)/shard_map/ppermute | solution.py:262
  26.0 54.1 %collective-permute-start.2 = (bf16[2048,128]{1,0:T(8,128)(2,1)S(1)}, bf16[2048,128]{1,0:T(8,128)(2,1)S(1)}, u32[]{:S(2)}, u32[]{:S(2)}) collective-permute-start(bf16[2048,128]{1,0:T(8,128)(2,1)S(1)} %copy-done), channel_id=1, source_target_pairs={{0,3},{1,0},{2,1},{3,2},{4,7},{5,4},{6,5},{7,6},{8,11},{9,8},{10,9... | collective-permute-start | bytes 1572872 | tf_op jit(solution)/shard_map/ppermute | solution.py:262
  29.4 50.8 %collective-permute-start.1 = (bf16[2048,128]{1,0:T(8,128)(2,1)S(1)}, bf16[2048,128]{1,0:T(8,128)(2,1)}, u32[]{:S(2)}, u32[]{:S(2)}) collective-permute-start(bf16[2048,128]{1,0:T(8,128)(2,1)S(1)} %copy-done), channel_id=1, source_target_pairs={{0,2},{1,3},{2,0},{3,1},{4,6},{5,7},{6,4},{7,5},{8,10},{9,11},{10,... | collective-permute-start | bytes 1572872 | tf_op jit(solution)/shard_map/ppermute | solution.py:262
  32.9 40.0 %collective-permute-start.3 = (bf16[8,64,128]{2,1,0:T(8,128)(2,1)S(1)}, bf16[8,64,128]{2,1,0:T(8,128)(2,1)S(1)}, u32[]{:S(2)}, u32[]{:S(2)}) collective-permute-start(bf16[8,64,128]{2,1,0:T(8,128)(2,1)S(1)} %copy-done.10), channel_id=1, source_target_pairs={{0,4},{4,8},{8,12},{12,16},{16,20},{20,24},{24,28},{28,32},{32,36}... | collective-permute-start | bytes 393224 | tf_op jit(solution)/shard_map/ppermute | solution.py:268
  35.9 37.1 %collective-permute-start.4 = (bf16[8,64,128]{2,1,0:T(8,128)(2,1)S(1)}, bf16[8,64,128]{2,1,0:T(8,128)(2,1)S(1)}, u32[]{:S(2)}, u32[]{:S(2)}) collective-permute-start(bf16[8,64,128]{2,1,0:T(8,128)(2,1)S(1)} %copy-done.9), channel_id=1, source_target_pairs={{4,0},{8,4},{12,8},{16,12},{20,16},{24,20},{28,24},{32,28},{36,32}... | collective-permute-start | bytes 393224 | tf_op jit(solution)/shard_map/ppermute | solution.py:268
  72.9 1.6 copy-start.1
  78.1 1.0 copy-start.2
  79.1 1.0 copy-start.4
  80.1 0.8 copy-start.6
  80.1 1.0 copy-start.7
  82.8 6.2 %collective-permute-start.5 = (bf16[4,2048,128]{2,1,0:T(8,128)(2,1)S(1)}, bf16[4,2048,128]{2,1,0:T(8,128)(2,1)}, u32[]{:S(2)}, u32[]{:S(2)}) collective-permute-start(bf16[4,2048,128]{2,1,0:T(8,128)(2,1)S(1)} %pad_maximum_fusion.own_ref), channel_id=1, source_target_pairs={{0,256},{256,0},{1,257},{257,1},{2,258},{258,2},{3,259},{259,3},{4... | collective-permute-start | bytes 6291464 | tf_op jit(solution)/shard_map/ppermute | solution.py:262
  92.2 24.4 %all-to-all-start.1 = ((bf16[16,4,8,128]{3,2,1,0:T(8,128)(2,1)}), bf16[16,4,8,128]{3,2,1,0:T(8,128)(2,1)S(1)}, u32[]{:S(2)}, u32[]{:S(2)}) async-start(bf16[16,4,8,128]{3,2,1,0:T(8,128)(2,1)} %partials.1), calls=%async_computation.1 | async-start | bytes 262144 | tf_op jit(solution)/shard_map/all_to_all | solution.py:272
  105.6 22.5 %collective-permute-start.9 = (bf16[64,32,128]{2,1,0:T(8,128)(2,1)}, bf16[64,32,128]{2,1,0:T(8,128)(2,1)S(1)}, u32[]{:S(2)}, u32[]{:S(2)}) collective-permute-start(bf16[64,32,128]{2,1,0:T(8,128)(2,1)} %get-tuple-element.42), channel_id=1, source_target_pairs={{0,3},{1,0},{2,1},{3,2},{4,7},{5,4},{6,5},{7,6},{8,11},{9,8},{10,9... | collective-permute-start | bytes 1572872 | tf_op jit(solution)/shard_map/ppermute | solution.py:262
  110.2 21.2 %collective-permute-start.6 = (bf16[64,32,128]{2,1,0:T(8,128)(2,1)}, bf16[64,32,128]{2,1,0:T(8,128)(2,1)S(1)}, u32[]{:S(2)}, u32[]{:S(2)}) collective-permute-start(bf16[64,32,128]{2,1,0:T(8,128)(2,1)} %get-tuple-element.43), channel_id=1, source_target_pairs={{0,1},{1,2},{2,3},{3,0},{4,5},{5,6},{6,7},{7,4},{8,9},{9,10},{10,1... | collective-permute-start | bytes 1572872 | tf_op jit(solution)/shard_map/ppermute | solution.py:262
  117.3 16.1 %all-to-all-start.2 = ((f32[16,8,128]{2,1,0:T(8,128)}), f32[16,8,128]{2,1,0:T(8,128)S(1)}, u32[]{:S(2)}, u32[]{:S(2)}) async-start(f32[16,8,128]{2,1,0:T(8,128)} %bitcast.10), calls=%async_computation.2 | async-start | bytes 131072 | tf_op jit(solution)/shard_map/all_to_all | solution.py:272
  121.6 19.3 %collective-permute-start.7 = (bf16[64,32,128]{2,1,0:T(8,128)(2,1)}, bf16[64,32,128]{2,1,0:T(8,128)(2,1)S(1)}, u32[]{:S(2)}, u32[]{:S(2)}) collective-permute-start(bf16[64,32,128]{2,1,0:T(8,128)(2,1)} %get-tuple-element.42), channel_id=1, source_target_pairs={{0,1},{1,2},{2,3},{3,0},{4,5},{5,6},{6,7},{7,4},{8,9},{9,10},{10,1... | collective-permute-start | bytes 1572872 | tf_op jit(solution)/shard_map/ppermute | solution.py:262
  124.9 16.0 %collective-permute-start.11 = (bf16[64,32,128]{2,1,0:T(8,128)(2,1)}, bf16[64,32,128]{2,1,0:T(8,128)(2,1)S(1)}, u32[]{:S(2)}, u32[]{:S(2)}) collective-permute-start(bf16[64,32,128]{2,1,0:T(8,128)(2,1)} %get-tuple-element.43), channel_id=1, source_target_pairs={{0,3},{1,0},{2,1},{3,2},{4,7},{5,4},{6,5},{7,6},{8,11},{9,8},{10,9... | collective-permute-start | bytes 1572872 | tf_op jit(solution)/shard_map/ppermute | solution.py:262
  128.1 24.7 %collective-permute-start.10 = (bf16[64,32,128]{2,1,0:T(8,128)(2,1)S(1)}, bf16[64,32,128]{2,1,0:T(8,128)(2,1)}, u32[]{:S(2)}, u32[]{:S(2)}) collective-permute-start(bf16[64,32,128]{2,1,0:T(8,128)(2,1)S(1)} %collective-permute-done.9.refs_6_), channel_id=1, source_target_pairs={{0,3},{1,0},{2,1},{3,2},{4,7},{5,4},{6,5},{7,6},{8,11},{9,8},{10,9... | collective-permute-start | bytes 1572872 | tf_op jit(solution)/shard_map/ppermute | solution.py:262
  131.4 21.4 %collective-permute-start.8 = (bf16[64,32,128]{2,1,0:T(8,128)(2,1)S(1)}, bf16[64,32,128]{2,1,0:T(8,128)(2,1)}, u32[]{:S(2)}, u32[]{:S(2)}) collective-permute-start(bf16[64,32,128]{2,1,0:T(8,128)(2,1)S(1)} %collective-permute-done.6.refs_1_), channel_id=1, source_target_pairs={{0,1},{1,2},{2,3},{3,0},{4,5},{5,6},{6,7},{7,4},{8,9},{9,10},{10,1... | collective-permute-start | bytes 1572872 | tf_op jit(solution)/shard_map/ppermute | solution.py:262
  134.1 18.7 %all-to-all-start.3 = ((bf16[16,4,8,128]{3,2,1,0:T(8,128)(2,1)}), bf16[16,4,8,128]{3,2,1,0:T(8,128)(2,1)S(1)}, u32[]{:S(2)}, u32[]{:S(2)}) async-start(bf16[16,4,8,128]{3,2,1,0:T(8,128)(2,1)} %broadcast_in_dim.7), calls=%async_computation.3 | async-start | bytes 262144 | tf_op jit(solution)/shard_map/all_to_all | solution.py:272
  152.8 20.6 %copy-start.3 = (f32[32,64,128]{2,1,0:T(8,128)S(1)}, f32[32,64,128]{2,1,0:T(8,128)}, u32[]{:S(2)}) copy-start(f32[32,64,128]{2,1,0:T(8,128)} %copy-done.2) | copy-start | bytes 3145732
  152.8 20.6 %copy-start.5 = (f32[32,64,128]{2,1,0:T(8,128)S(1)}, f32[32,64,128]{2,1,0:T(8,128)}, u32[]{:S(2)}) copy-start(f32[32,64,128]{2,1,0:T(8,128)} %copy-done.4) | copy-start | bytes 3145732
  155.9 20.5 %collective-permute-start.14 = (bf16[2,32,64,128]{3,2,1,0:T(8,128)(2,1)S(1)}, bf16[2,32,64,128]{3,2,1,0:T(8,128)(2,1)S(1)}, u32[]{:S(2)}, u32[]{:S(2)}) collective-permute-start(bf16[2,32,64,128]{3,2,1,0:T(8,128)(2,1)S(1)} %theirs.1), channel_id=1, source_target_pairs={{0,256},{256,0},{1,257},{257,1},{2,258},{258,2},{3,259},{259,3},{4... | collective-permute-start | bytes 3145736 | tf_op jit(solution)/shard_map/ppermute | solution.py:262
  162.6 9.6 %collective-permute-start.12 = (bf16[8,64,128]{2,1,0:T(8,128)(2,1)S(1)}, bf16[8,64,128]{2,1,0:T(8,128)(2,1)S(1)}, u32[]{:S(2)}, u32[]{:S(2)}) collective-permute-start(bf16[8,64,128]{2,1,0:T(8,128)(2,1)S(1)} %get-tuple-element.36), channel_id=1, source_target_pairs={{0,4},{4,8},{8,12},{12,16},{16,20},{20,24},{24,28},{28,32},{32,36}... | collective-permute-start | bytes 393224 | tf_op jit(solution)/shard_map/ppermute | solution.py:268
  165.7 7.7 %collective-permute-start.13 = (bf16[8,64,128]{2,1,0:T(8,128)(2,1)S(1)}, bf16[8,64,128]{2,1,0:T(8,128)(2,1)S(1)}, u32[]{:S(2)}, u32[]{:S(2)}) collective-permute-start(bf16[8,64,128]{2,1,0:T(8,128)(2,1)S(1)} %get-tuple-element.37), channel_id=1, source_target_pairs={{4,0},{8,4},{12,8},{16,12},{20,16},{24,20},{28,24},{32,28},{36,32}... | collective-permute-start | bytes 393224 | tf_op jit(solution)/shard_map/ppermute | solution.py:268
